TPU v7x, 32 devices: a whole 2x2x4 slice. The times are simulated.
32 devices in a mesh: dp: 2 (over y), tok: 8 (over z, core), col: 2 (over x).
Axes of the slice: x: 2, y: 2, z: 4, core: 2. Of those that a mesh axis runs over, the one named last changes fastest.
Arguments:
- tokens: bfloat16 [2, 4096, 1024], P('dp', 'tok'), may hold values from -6 to 6
- ln_gain: bfloat16 [1024], replicated, may hold values from 0.099609375 to 1.8984375
- qkv_weight: bfloat16 [3, 1024, 512], P(None, None, 'col'), may hold values from -0.375 to 0.375
- out_weight: bfloat16 [512, 1024], P('col'), may hold values from -0.25 to 0.25
- readout_weight: bfloat16 [1024, 64], replicated, may hold values from -0.1875 to 0.1875
- conv_weight: bfloat16 [2, 64, 576], replicated, may hold values from -0.25 to 0.25
- head_weight: bfloat16 [2, 64], replicated, may hold values from -0.75 to 0.75
- holo_cot: float32 [2, 2, 16, 256], P('dp', None, 'tok', 'col'), may hold values from -2.5 to 2.5
Outputs:
- hologram: float32 [2, 2, 16, 256], P('dp', None, 'tok', 'col')
- conv_grad: float32 [2, 64, 576], replicated
- out_grad: float32 [512, 1024], P('col')
All inputs are finite; a program needn't handle non-finite values.
Results may differ from a plain program's by a relative error of at most 0.017.
The roundings to bfloat16 on the way count: a program that leaves them out, or rounds other values in their place, can miss the bound.
Values may be sent and summed in bfloat16 or wider, within the bound.
No kernel may reach another device: no remote copies, remote signals or barrier semaphores. Data moves between devices by JAX's collectives and lax.ppermute only.
A program may use at most 128 MiB of HBM per device.

v0:
```python
import jax
import jax.numpy as jnp
from jax import lax
from jax.sharding import PartitionSpec as P

HEAD = 64


EPSILON = 1e-05


def extended(shard, sides, width):
    for axis, dim in sides:
        size, length = (lax.axis_size(axis), shard.shape[dim])
        up = [(i, (i + 1) % size) for i in range(size - 1)]
        down = [(j, i) for i, j in up]
        last = lax.slice_in_dim(shard, length - width, length, axis=dim)
        initial = lax.slice_in_dim(shard, 0, width, axis=dim)
        before = lax.ppermute(last, axis, up)
        after = lax.ppermute(initial, axis, down)
        shard = jnp.concatenate([before, shard, after], axis=dim)
    return shard


def normalize(rows_in, ln_gain):
    values = rows_in.astype(jnp.float32)
    center = values - jnp.mean(values, axis=-1, keepdims=True)
    spread = jnp.mean(center * center, axis=-1, keepdims=True)
    return (center * lax.rsqrt(spread + EPSILON) * ln_gain.astype(jnp.float32)).astype(jnp.bfloat16)


def project(normed, weights_all):
    return tuple(
        (
            jnp.dot(normed, weights_all[member], preferred_element_type=jnp.float32).astype(
                jnp.bfloat16
            )
            for member in range(3)
        )
    )


def empty_state(queries):
    query_count = queries.shape[0]
    head_count = queries.shape[1] // HEAD
    return (
        jnp.zeros((query_count, head_count, HEAD), jnp.float32),
        jnp.full((head_count, query_count), -1e30, jnp.float32),
        jnp.zeros((head_count, query_count), jnp.float32),
    )


def absorb(queries, running, key_rows, value_rows):
    summed, row_top, row_total = running
    head_count = summed.shape[1]
    query_view = queries.reshape(queries.shape[0], head_count, HEAD)
    key_view = key_rows.reshape(key_rows.shape[0], head_count, HEAD)
    value_view = value_rows.reshape(value_rows.shape[0], head_count, HEAD)
    scores = jnp.einsum(
        "qhd,khd->hqk", query_view, key_view, preferred_element_type=jnp.float32
    ) * (1.0 / HEAD**0.5)
    new_top = jnp.maximum(row_top, jnp.max(scores, axis=-1))
    rescale = jnp.exp(row_top - new_top)
    raised = jnp.exp(scores - new_top[:, :, None])
    row_total = row_total * rescale + jnp.sum(raised, axis=-1)
    weighted = jnp.einsum(
        "hqk,khd->qhd", raised.astype(jnp.bfloat16), value_view, preferred_element_type=jnp.float32
    )
    summed = summed * jnp.transpose(rescale)[:, :, None] + weighted
    return (summed, new_top, row_total)


def absorb_keys(queries, running, arrived):
    key_rows, value_rows = arrived
    total_rows = key_rows.shape[0]
    block_rows = 512
    block_count = total_rows // block_rows

    def advance(turn_at, carried):
        key_block = lax.dynamic_slice_in_dim(key_rows, turn_at * block_rows, block_rows, 0)
        value_block = lax.dynamic_slice_in_dim(value_rows, turn_at * block_rows, block_rows, 0)
        return absorb(queries, carried, key_block, value_block)

    return lax.fori_loop(0, block_count, advance, running)


def finish(running):
    summed, row_top, row_total = running
    return (
        (summed / jnp.transpose(row_total)[:, :, None])
        .reshape(summed.shape[0], -1)
        .astype(jnp.bfloat16)
    )


def neighbourhood(padded, grid_rows, grid_cols):
    pieces = [
        padded[:, row_off : row_off + grid_rows, col_off : col_off + grid_cols]
        for row_off in range(3)
        for col_off in range(3)
    ]
    return jnp.concatenate(pieces, axis=0).reshape(9 * padded.shape[0], grid_rows * grid_cols)


def flipped(padded, grid_rows, grid_cols):
    pieces = [
        padded[:, 2 - row_off : 2 - row_off + grid_rows, 2 - col_off : 2 - col_off + grid_cols]
        for row_off in range(3)
        for col_off in range(3)
    ]
    return jnp.concatenate(pieces, axis=0).reshape(9 * padded.shape[0], grid_rows * grid_cols)


def transposed(weight):
    channels = weight.shape[0]
    return jnp.transpose(weight.reshape(channels, 9, channels), (2, 1, 0)).reshape(
        channels, 9 * channels
    )


def with_rims(field):
    return extended(field, (("tok", 1), ("col", 2)), 1)


def shards(
    tokens, ln_gain, qkv_weight, out_weight, readout_weight, conv_weight, head_weight, holo_cot
):
    frame_rows = tokens[0]
    cotangent = holo_cot[0]
    rows_dev = cotangent.shape[1]
    cols_dev = cotangent.shape[2]
    col_count = lax.axis_size("col")
    col_at = lax.axis_index("col")
    channels = conv_weight.shape[1]
    layer_count = conv_weight.shape[0]
    width = frame_rows.shape[1]
    own_rows = lax.dynamic_index_in_dim(
        frame_rows.reshape(rows_dev, col_count, cols_dev, width), col_at, 1, keepdims=False
    ).reshape(rows_dev * cols_dev, width)
    own_values = own_rows.astype(jnp.float32)
    readout_wide = readout_weight.astype(jnp.float32)
    readout_back = jnp.transpose(readout_wide)
    all_projections = lax.all_gather(qkv_weight, "col", axis=2, tiled=True)
    all_outputs = lax.all_gather(out_weight, "col", axis=0, tiled=True)
    normed = normalize(own_rows, ln_gain)
    queries, key_rows, value_rows = project(normed, all_projections)
    running = absorb_keys(
        queries,
        empty_state(queries),
        (
            lax.all_gather(key_rows, ("tok", "col"), axis=0, tiled=True),
            lax.all_gather(value_rows, ("tok", "col"), axis=0, tiled=True),
        ),
    )
    context = finish(running)
    mixed = own_values + jnp.dot(context, all_outputs, preferred_element_type=jnp.float32)
    readout = jnp.dot(mixed, readout_wide, precision=lax.Precision.HIGHEST)
    hidden = jnp.transpose(readout.astype(jnp.bfloat16)).reshape(channels, rows_dev, cols_dev)
    inputs = []
    pre_acts = []
    for layer_at in range(layer_count):
        stacked = neighbourhood(with_rims(hidden), rows_dev, cols_dev)
        pre_act = jnp.dot(conv_weight[layer_at], stacked, preferred_element_type=jnp.float32)
        inputs.append(stacked)
        pre_acts.append(pre_act)
        hidden = jax.nn.silu(pre_act).astype(jnp.bfloat16).reshape(channels, rows_dev, cols_dev)
    hologram = jnp.dot(
        head_weight, hidden.reshape(channels, -1), preferred_element_type=jnp.float32
    )
    grad_hidden = jnp.dot(
        jnp.transpose(head_weight.astype(jnp.float32)),
        cotangent.reshape(cotangent.shape[0], -1),
        precision=lax.Precision.HIGHEST,
    ).astype(jnp.bfloat16)
    conv_terms = [None] * layer_count
    for layer_at in reversed(range(layer_count)):
        pre_act = pre_acts[layer_at]
        sigmoid_pre = jax.nn.sigmoid(pre_act)
        grad_pre = (
            grad_hidden.astype(jnp.float32) * sigmoid_pre * (1.0 + pre_act * (1.0 - sigmoid_pre))
        ).astype(jnp.bfloat16)
        conv_terms[layer_at] = lax.dot_general(
            grad_pre, inputs[layer_at], (((1,), (1,)), ((), ())), preferred_element_type=jnp.float32
        )
        padded = with_rims(grad_pre.reshape(channels, rows_dev, cols_dev))
        grad_hidden = jnp.dot(
            transposed(conv_weight[layer_at]),
            flipped(padded, rows_dev, cols_dev),
            preferred_element_type=jnp.float32,
        ).astype(jnp.bfloat16)
    conv_grad = lax.psum(jnp.stack(conv_terms), ("dp", "tok", "col"))
    shard_rows = out_weight.shape[0]
    small_term = lax.dot_general(
        context, grad_hidden, (((0,), (1,)), ((), ())), preferred_element_type=jnp.float32
    )
    grad_small = lax.psum(small_term, ("dp", "tok", "col"))
    own_small = lax.dynamic_slice_in_dim(grad_small, col_at * shard_rows, shard_rows, 0)
    out_grad = jnp.dot(own_small, readout_back, precision=lax.Precision.HIGHEST)
    return (hologram.reshape(1, cotangent.shape[0], rows_dev, cols_dev), conv_grad, out_grad)


def solution(mesh):
    in_specs = (
        P("dp", "tok", None),
        P(),
        P(None, None, "col"),
        P("col", None),
        P(),
        P(),
        P(),
        P("dp", None, "tok", "col"),
    )
    out_specs = (P("dp", None, "tok", "col"), P(), P("col", None))
    return jax.shard_map(shards, mesh=mesh, in_specs=in_specs, out_specs=out_specs, check_vma=False)
```

profile of v0, /device:TPU:0, one launch (start us, length us, event | category | flops | bytes accessed | tf_op | source)
XLA Modules:
  0.0 457.9 jit_solution(10940003317655362925)
XLA Ops:
  12.6 44.5 %all-gather.5.cloned.1.call-done = bf16[3,1024,512]{2,1,0:T(8,128)(2,1)} async-done(((bf16[3,1024,256]{2,1,0:T(8,128)(2,1)}), bf16[3,1024,512]{2,1,0:T(8,128)(2,1)}) %all-gather.5.cloned.1.call-update) | async-done | bytes 3145744 | tf_op jit(solution)/shard_map/all_gather | solution.py:143
  64.6 45.8 %all-gather.7.cloned.1.call-done = bf16[4096,512]{1,0:T(8,128)(2,1)} async-done(((bf16[256,512]{1,0:T(8,128)(2,1)}), bf16[4096,512]{1,0:T(8,128)(2,1)}) %all-gather.7.cloned.1.call-update) | async-done | bytes 4194320 | tf_op jit(solution)/shard_map/all_gather | solution.py:151
  110.3 51.7 %all-gather.9.cloned.1.call-done = bf16[4096,512]{1,0:T(8,128)(2,1)} async-done(((bf16[256,512]{1,0:T(8,128)(2,1)}), bf16[4096,512]{1,0:T(8,128)(2,1)}) %all-gather.9.cloned.1.call-update) | async-done | bytes 4194320 | tf_op jit(solution)/shard_map/all_gather | solution.py:152
  162.1 84.8 %while.18 = (s32[]{:T(128)}, f32[256,8,64]{0,2,1:T(8,128)S(1)}, f32[8,256]{1,0:T(8,128)S(1)}, f32[8,256]{1,0:T(8,128)S(1)}, bf16[4096,512]{1,0:T(8,128)(2,1)}, /...) while((s32[]{:T(128)}, f32[256,8,64]{0,2,1:T(8,128)S(1)}, ...), condition=%wide.region_5.6_spmd.clone, body=%wide.region_2.5_spmd.clone.sunk | while | flops 277229568 | bytes 19267752 | solution.py:84
  163.5 2.8 bitcast_reduce_fusion.2
  166.4 3.0 fusion.84
  169.6 3.2 fusion.83
  177.2 2.9 fusion.84
  180.3 3.1 fusion.83
  187.7 2.9 fusion.84
  190.9 3.1 fusion.83
  195.5 2.8 bitcast_reduce_fusion.2
  198.3 2.9 fusion.84
  201.4 3.1 fusion.83
  208.9 2.9 fusion.84
  212.0 3.1 fusion.83
  219.5 2.9 fusion.84
  222.6 3.1 fusion.83
  227.3 2.8 bitcast_reduce_fusion.2
  230.1 2.9 fusion.84
  233.2 3.1 fusion.83
  240.6 2.9 fusion.84
  243.8 3.1 fusion.83
  260.9 3.6 collective-permute-done.3
  265.8 3.1 collective-permute-start.4
  270.2 3.2 collective-permute-done.5
  277.6 3.6 collective-permute-done.7
  282.7 3.2 collective-permute-start.8
  291.8 4.7 %collective-permute-start.11 = (bf16[64,4,1]{2,1,0:T(4,128)(2,1)S(1)}, bf16[64,4,1]{2,1,0:T(4,128)(2,1)S(1)}, u32[]{:S(2)}, u32[]{:S(2)}) collective-permute-start(bf16[64,4,1]{2,1,0:T(4,128)(2,1)S(1)} %get-tuple-element.222), channel_id=1, source_target_pairs={{0,1},{2,3},{4,5},{6,7},{8,9},{10,11},{12,13},{14,15},{16,17},{18,... | collective-permute-start | bytes 1544 | tf_op jit(solution)/shard_map/ppermute | solution.py:19
  299.4 3.4 collective-permute-start.12
  308.9 4.5 collective-permute-start.15
  318.1 129.1 %all-reduce.3.cloned.1.call-done = (f32[2,64,576]{2,1,0:T(8,128)}, f32[512,64]{1,0:T(8,128)}) async-done(((f32[2,64,576]{2,1,0:T(8,128)}, f32[512,64]{1,0:T(8,128)}), (f32[2,64,576]{2,1,0:T(8,128)}, f32[512,64]{1,0:T(8,128)})) %all-reduce.3.cloned.1.call-update) | async-done | bytes 426000 | tf_op jit(solution)/shard_map/psum | solution.py:191
  (192 shorter events, 85.7 us)
Async XLA Ops:
  7.2 241.6 %copy-start = (bf16[1024,64]{0,1:T(8,128)(2,1)S(1)}, bf16[1024,64]{0,1:T(8,128)(2,1)}, u32[]{:S(2)}) copy-start(bf16[1024,64]{0,1:T(8,128)(2,1)} %param.14) | copy-start | bytes 393220
  7.2 50.0 %all-gather.5.cloned.1.call-start = ((), (), s32[]{:S(2)}) async-start(), calls=%async_computation | async-start | bytes 4718592 | tf_op jit(solution)/shard_map/all_gather | solution.py:143
  7.9 54.7 %copy-start.1 = (bf16[1,512,1024]{2,1,0:T(8,128)(2,1)S(1)}, bf16[1,512,1024]{2,1,0:T(8,128)(2,1)}, u32[]{:S(2)}) copy-start(bf16[1,512,1024]{2,1,0:T(8,128)(2,1)} %param.10) | copy-start | bytes 3145732
  7.9 102.4 %all-gather.7.cloned.1.call-start = ((), (), s32[]{:S(2)}) async-start(), calls=%async_computation.1 | async-start | bytes 4456448 | tf_op jit(solution)/shard_map/all_gather | solution.py:151
  59.5 102.5 %all-gather.9.cloned.1.call-start = ((), (), s32[]{:S(2)}) async-start(), calls=%async_computation.2 | async-start | bytes 4456448 | tf_op jit(solution)/shard_map/all_gather | solution.py:152
  62.0 185.0 %all-gather.11.cloned.1.call-start = ((), (), s32[]{:S(2)}) async-start(), calls=%async_computation.3 | async-start | bytes 1572864 | tf_op jit(solution)/shard_map/all_gather | solution.py:144
  62.6 384.7 %all-reduce.3.cloned.1.call-start = ((), (), s32[]{:S(2)}) async-start(), calls=%async_computation.4 | async-start | bytes 1179648 | tf_op jit(solution)/shard_map/psum | solution.py:191
  246.9 18.6 %copy-start.2 = (bf16[2,64,576]{2,1,0:T(8,128)(2,1)S(1)}, bf16[2,64,576]{2,1,0:T(8,128)(2,1)}, u32[]{:S(2)}) copy-start(bf16[2,64,576]{2,1,0:T(8,128)(2,1)} %param.15) | copy-start | bytes 442372
  247.0 35.3 %copy-start.3 = (f32[1,2,2,128]{3,2,1,0:T(2,128)S(1)}, f32[1,2,2,128]{3,2,1,0:T(2,128)}, u32[]{:S(2)}) copy-start(f32[1,2,2,128]{3,2,1,0:T(2,128)} %param.17) | copy-start | bytes 6148
  247.0 35.3 %copy-start.4 = (bf16[2,64]{1,0:T(2,128)(2,1)S(1)}, bf16[2,64]{1,0:T(2,128)(2,1)}, u32[]{:S(2)}) copy-start(bf16[2,64]{1,0:T(2,128)(2,1)} %param.16) | copy-start | bytes 772
  249.5 3.5 collective-permute-start
  251.7 4.0 collective-permute-start.1
  255.9 4.4 collective-permute-start.2
  258.4 6.2 %collective-permute-start.3 = (bf16[64,4,1]{2,1,0:T(4,128)(2,1)S(1)}, bf16[64,4,1]{2,1,0:T(4,128)(2,1)S(1)}, u32[]{:S(2)}, u32[]{:S(2)}) collective-permute-start(bf16[64,4,1]{2,1,0:T(4,128)(2,1)S(1)} %get-tuple-element.230), channel_id=1, source_target_pairs={{1,0},{3,2},{5,4},{7,6},{9,8},{11,10},{13,12},{15,14},{17,16},{19,... | collective-permute-start | bytes 1544 | tf_op jit(solution)/shard_map/ppermute | solution.py:20
  265.8 4.4 collective-permute-start.4
  268.9 4.5 collective-permute-start.5
  273.6 3.3 collective-permute-start.6
  275.0 6.2 %collective-permute-start.7 = (bf16[64,4,1]{2,1,0:T(4,128)(2,1)S(1)}, bf16[64,4,1]{2,1,0:T(4,128)(2,1)S(1)}, u32[]{:S(2)}, u32[]{:S(2)}) collective-permute-start(bf16[64,4,1]{2,1,0:T(4,128)(2,1)S(1)} %get-tuple-element.226), channel_id=1, source_target_pairs={{1,0},{3,2},{5,4},{7,6},{9,8},{11,10},{13,12},{15,14},{17,16},{19,... | collective-permute-start | bytes 1544 | tf_op jit(solution)/shard_map/ppermute | solution.py:20
  282.7 5.2 %collective-permute-start.8 = (bf16[64,1,128]{2,1,0:T(2,128)(2,1)S(1)}, bf16[64,1,128]{2,1,0:T(2,128)(2,1)S(1)}, u32[]{:S(2)}, u32[]{:S(2)}) collective-permute-start(bf16[64,1,128]{2,1,0:T(2,128)(2,1)S(1)} %get-tuple-element.234), channel_id=1, source_target_pairs={{0,2},{2,4},{4,6},{6,8},{8,10},{10,12},{12,14},{1,3},{3,5},{5,7},{... | collective-permute-start | bytes 49160 | tf_op jit(solution)/shard_map/ppermute | solution.py:19
  285.9 4.2 collective-permute-start.9
  290.3 6.2 %collective-permute-start.10 = (bf16[64,4,1]{2,1,0:T(4,128)(2,1)S(1)}, bf16[64,4,1]{2,1,0:T(4,128)(2,1)S(1)}, u32[]{:S(2)}, u32[]{:S(2)}) collective-permute-start(bf16[64,4,1]{2,1,0:T(4,128)(2,1)S(1)} %get-tuple-element.223), channel_id=1, source_target_pairs={{1,0},{3,2},{5,4},{7,6},{9,8},{11,10},{13,12},{15,14},{17,16},{19,... | collective-permute-start | bytes 1544 | tf_op jit(solution)/shard_map/ppermute | solution.py:20
  291.8 6.4 %collective-permute-start.11 = (bf16[64,4,1]{2,1,0:T(4,128)(2,1)S(1)}, bf16[64,4,1]{2,1,0:T(4,128)(2,1)S(1)}, u32[]{:S(2)}, u32[]{:S(2)}) collective-permute-start(bf16[64,4,1]{2,1,0:T(4,128)(2,1)S(1)} %get-tuple-element.222), channel_id=1, source_target_pairs={{0,1},{2,3},{4,5},{6,7},{8,9},{10,11},{12,13},{14,15},{16,17},{18,... | collective-permute-start | bytes 1544 | tf_op jit(solution)/shard_map/ppermute | solution.py:19
  299.4 4.9 %collective-permute-start.12 = (bf16[64,1,128]{2,1,0:T(2,128)(2,1)S(1)}, bf16[64,1,128]{2,1,0:T(2,128)(2,1)S(1)}, u32[]{:S(2)}, u32[]{:S(2)}) collective-permute-start(bf16[64,1,128]{2,1,0:T(2,128)(2,1)S(1)} %get-tuple-element.232), channel_id=1, source_target_pairs={{0,2},{2,4},{4,6},{6,8},{8,10},{10,12},{12,14},{1,3},{3,5},{5,7},{... | collective-permute-start | bytes 49160 | tf_op jit(solution)/shard_map/ppermute | solution.py:19
  302.8 3.7 collective-permute-start.13
  306.8 6.6 %collective-permute-start.14 = (bf16[64,4,1]{2,1,0:T(4,128)(2,1)S(1)}, bf16[64,4,1]{2,1,0:T(4,128)(2,1)S(1)}, u32[]{:S(2)}, u32[]{:S(2)}) collective-permute-start(bf16[64,4,1]{2,1,0:T(4,128)(2,1)S(1)} %get-tuple-element.219), channel_id=1, source_target_pairs={{1,0},{3,2},{5,4},{7,6},{9,8},{11,10},{13,12},{15,14},{17,16},{19,... | collective-permute-start | bytes 1544 | tf_op jit(solution)/shard_map/ppermute | solution.py:20
  308.9 6.4 %collective-permute-start.15 = (bf16[64,4,1]{2,1,0:T(4,128)(2,1)S(1)}, bf16[64,4,1]{2,1,0:T(4,128)(2,1)S(1)}, u32[]{:S(2)}, u32[]{:S(2)}) collective-permute-start(bf16[64,4,1]{2,1,0:T(4,128)(2,1)S(1)} %get-tuple-element.218), channel_id=1, source_target_pairs={{0,1},{2,3},{4,5},{6,7},{8,9},{10,11},{12,13},{14,15},{16,17},{18,... | collective-permute-start | bytes 1544 | tf_op jit(solution)/shard_map/ppermute | solution.py:19
Sparse Core Ops, SparseCore 0:
  9.5 47.5 all-gather.4
  59.9 50.3 all-gather.6
  113.1 48.8 all-gather.8
  163.5 19.7 all-gather.10
  317.5 129.6 all-reduce.2
where the time goes:
time: 459 us; the launch traced here: 458 us
  waiting for transfers between devices  293 us (64%)
  matrix products  61.2 us (13%)
  starting transfers between devices  35.6 us (8%)
  other arithmetic  35.1 us (8%)
  local copies, waits for them, and re-layouts  17.7 us (4%)
  between operations  14.5 us (3%)
    psum x1, waiting for transfers between devices, shards(): conv_grad = lax.psum(jnp.stack(conv_terms), ('dp', 'tok', 'col'))  129 us
    all_gather x1, waiting for transfers between devices, shards(): lax.all_gather(value_rows, ('tok', 'col'), axis=0, tiled=True)  51.7 us
    all_gather x1, waiting for transfers between devices, shards(): lax.all_gather(key_rows, ('tok', 'col'), axis=0, tiled=True)  45.8 us
    all_gather x1, waiting for transfers between devices, shards(): all_projections = lax.all_gather(qkv_weight, 'col', axis=2, tiled=True)  44.5 us
    ppermute x8, starting transfers between devices, extended(): before = lax.ppermute(last, axis, up)  25.1 us
    dot_general x8, matrix products, absorb(): jnp.einsum('hqk,khd->qhd', raised.astype(jnp.bfloat16), value_view, prefe...  25 us
    reduce_sum x8, other arithmetic, absorb(): row_total = row_total * rescale + jnp.sum(raised, axis=-1)  23.2 us
    dot_general x8, matrix products, absorb(): jnp.einsum('qhd,khd->hqk', query_view, key_view, preferred_element_type=j...  22.4 us
  transfers between devices with their start and end apart: 21, of which 14 were waited for; matrix products, arithmetic and copies ran while one was open for 22% of the time, Pallas kernels for 0%

commit v1 on v0

v1 whole, which is shorter than its diff:
```python
import functools

import jax
import jax.numpy as jnp
from jax import lax
from jax.experimental import pallas as pl
from jax.experimental.pallas import tpu as pltpu
from jax.sharding import PartitionSpec as P

HEAD = 64
EPSILON = 1e-05
BF16 = jnp.bfloat16
F32 = jnp.float32
VMEM = pl.BlockSpec(memory_space=pltpu.VMEM)
SMEM = pl.BlockSpec(memory_space=pltpu.SMEM)
PARAMS = pltpu.CompilerParams(vmem_limit_bytes=48 * 2**20)
NT = (((1,), (1,)), ((), ()))
TN = (((0,), (0,)), ((), ()))


def dot(a, b):
    return jnp.dot(a, b, preferred_element_type=F32)


def split3(values):
    high = values.astype(BF16)
    rest = values - high.astype(F32)
    mid = rest.astype(BF16)
    low = (rest - mid.astype(F32)).astype(BF16)
    return high, mid, low


def project_kernel(place, tokens, gain, weight, mine, theirs):
    core = place[0]
    values = tokens[...].astype(F32)
    center = values - jnp.mean(values, axis=-1, keepdims=True)
    spread = jnp.mean(center * center, axis=-1, keepdims=True)
    normed = (center * lax.rsqrt(spread + EPSILON) * gain[...].astype(F32)).astype(BF16)
    kept = mine.shape[0] * HEAD
    for which, out in ((core, mine), (1 - core, theirs)):
        for member in range(3):
            part = weight[member, :, pl.ds(pl.multiple_of(which * kept, 128), kept)]
            rows = dot(normed, part).astype(BF16)
            if member == 0:
                rows = rows * jnp.asarray(1.0 / HEAD**0.5, BF16)
            turned = rows.T
            for head in range(mine.shape[0]):
                out[head, member * HEAD : (member + 1) * HEAD, :] = turned[head * HEAD : (head + 1) * HEAD, :]


def project(place, tokens, gain, weight):
    count, length = weight.shape[2] // HEAD // 2, tokens.shape[0]
    shape = jax.ShapeDtypeStruct((count, 3 * HEAD, length), BF16)
    return pl.pallas_call(
        project_kernel,
        out_shape=(shape, shape),
        in_specs=[SMEM, VMEM, VMEM, VMEM],
        out_specs=(VMEM, VMEM),
        compiler_params=PARAMS,
        name="project",
    )(place, tokens, gain, weight)


def absorb_kernel(first, *refs):
    if first:
        queries, block, out, top = refs
    else:
        queries, block, carried, carried_top, out, top = refs
    keys = block[:HEAD, :].T
    length = block.shape[1]
    values = jnp.concatenate([block[HEAD:, :], jnp.ones((16, length), BF16)], axis=0)
    width = min(512, queries.shape[1])
    depth = min(512, length)
    for at in range(0, queries.shape[1], width):
        part = queries[:, at : at + width]
        running = None if first else carried[:, at : at + width]
        best = None if first else carried_top[0:1, at : at + width]
        for below in range(0, length, depth):
            scores = dot(keys[below : below + depth], part)
            raised_top = jnp.max(scores, axis=0, keepdims=True)
            if best is not None:
                raised_top = jnp.maximum(best, raised_top)
            weights = jnp.exp(scores - raised_top).astype(BF16)
            added = dot(values[:, below : below + depth], weights)
            running = added if best is None else running * jnp.exp(best - raised_top) + added
            best = raised_top
        out[:, at : at + width] = running
        top[:, at : at + width] = jnp.broadcast_to(best, (8, width))


def absorb(queries, block, state):
    count = queries.shape[1]
    shapes = (jax.ShapeDtypeStruct((HEAD + 16, count), F32), jax.ShapeDtypeStruct((8, count), F32))
    first = state is None
    return pl.pallas_call(
        functools.partial(absorb_kernel, first),
        out_shape=shapes,
        in_specs=[VMEM] * (2 if first else 4),
        out_specs=(VMEM, VMEM),
        input_output_aliases={} if first else {2: 0, 3: 1},
        compiler_params=PARAMS,
        name="absorb",
    )(queries, block, *(() if first else state))


def finish_kernel(*refs):
    states, (folded, context, share) = refs[:-3], refs[-3:]
    for head, state in enumerate(states):
        context[head * HEAD : (head + 1) * HEAD, :] = (state[:HEAD, :] / state[HEAD : HEAD + 1, :]).astype(BF16)
    whole = context[...]
    share[...] = sum(dot(part, whole) for part in split3(folded[...]))


def finish(states, folded):
    count = states[0].shape[1]
    return pl.pallas_call(
        finish_kernel,
        out_shape=(
            jax.ShapeDtypeStruct((len(states) * HEAD, count), BF16),
            jax.ShapeDtypeStruct((folded.shape[0], count), F32),
        ),
        in_specs=[VMEM] * (len(states) + 1),
        out_specs=(VMEM, VMEM),
        compiler_params=PARAMS,
        name="finish",
    )(*states, folded)


def turned(values, step):
    return pltpu.roll(values, step % values.shape[1], 1)


def three_columns(values, cols):
    cells = values.shape[1]
    column = lax.rem(lax.broadcasted_iota(jnp.int32, (1, cells), 1), cols)
    wide = values.astype(F32)
    left = jnp.where(column == 0, 0.0, turned(wide, 1)).astype(BF16)
    right = jnp.where(column == cols - 1, 0.0, turned(wide, -1)).astype(BF16)
    return jnp.concatenate([left, values.astype(BF16), right], axis=0)


def three_rows(weights, columns, cols):
    cells = columns.shape[1] - 2 * cols
    return sum(dot(weights[a], columns[:, a * cols : a * cols + cells]) for a in range(3))


def network_kernel(
    cols, frame_rows, place, hidden, cotangent, forward, backward, head, context, holo, sums, gradient, pre_one, pre_two
):
    core, half, row_at = place[0], place[1], place[2]
    own = context.shape[1]
    cells = hidden.shape[1]
    rim = (cells - own) // 2
    row_count = cells // cols
    above = rim // cols
    first_row = row_at - above

    def inside(start_row, rows):
        lane = lax.broadcasted_iota(jnp.int32, (1, rows * cols), 1)
        frame_lane = lane + (first_row + start_row) * cols
        return jnp.logical_and(frame_lane >= 0, frame_lane < frame_rows * cols)

    columns_zero = three_columns(hidden[...], cols)
    first = three_rows(forward[0], columns_zero, cols)
    rows_one = row_count - 2
    one = jnp.where(inside(1, rows_one), first * jax.nn.sigmoid(first), 0.0)
    columns_one = three_columns(one, cols)
    second = three_rows(forward[1], columns_one, cols)
    rows_two = row_count - 4
    sigmoid_two = jax.nn.sigmoid(second)
    two = (second * sigmoid_two).astype(BF16)
    holo[...] = dot(head[...], two[:, rim - 2 * cols : rim - 2 * cols + own])
    grad_two = lax.dot_general(
        head[...].astype(F32), cotangent[...], TN, precision=lax.Precision.HIGHEST, preferred_element_type=F32
    ).astype(BF16)
    slope = grad_two.astype(F32) * sigmoid_two * (1.0 + second * (1.0 - sigmoid_two))
    pre_grad_two = jnp.where(inside(2, rows_two), slope, 0.0)
    grad_one = three_rows(backward[1], three_columns(pre_grad_two, cols), cols).astype(BF16)
    rows_grad = row_count - 6
    middle = first[:, 2 * cols : 2 * cols + rows_grad * cols]
    sigmoid_one = jax.nn.sigmoid(middle)
    slope = grad_one.astype(F32) * sigmoid_one * (1.0 + middle * (1.0 - sigmoid_one))
    pre_grad_one = jnp.where(inside(3, rows_grad), slope, 0.0)
    grad_zero = three_rows(backward[0], three_columns(pre_grad_one, cols), cols).astype(BF16)
    pre_one[...] = pre_grad_one[:, rim - 3 * cols : rim - 3 * cols + own].astype(BF16)
    pre_two[...] = pre_grad_two[:, rim - 2 * cols : rim - 2 * cols + own].astype(BF16)

    share = sums.shape[0]
    taps = 9 * hidden.shape[0]
    for layer, (pre, columns, offset) in enumerate(((pre_one, columns_zero, rim), (pre_two, columns_one, rim - cols))):

        @pl.when(core == layer)
        def _(pre=pre, columns=columns, offset=offset):
            stacked = jnp.concatenate(
                [columns[:, offset + (a - 1) * cols : offset + (a - 1) * cols + own] for a in range(3)], axis=0
            )
            rows = pre[pl.ds(pl.multiple_of(half * share, 16), share), :]
            sums[:, :taps] = lax.dot_general(rows, stacked, NT, preferred_element_type=F32)

    piece = own // 2
    total = None
    for side in range(2):
        where = lax.rem(core + side, 2)
        seen = context[:, pl.ds(pl.multiple_of(where * piece, 128), piece)]
        term = lax.dot_general(
            grad_zero[:, side * piece : (side + 1) * piece], seen, NT, preferred_element_type=F32
        )
        total = term if total is None else total + term
    gradient[...] = total


def network(place, hidden, cotangent, forward, backward, head, context, cols, frame_rows, col_count):
    own = context.shape[1]
    channels = hidden.shape[0]
    return pl.pallas_call(
        functools.partial(network_kernel, cols, frame_rows),
        out_shape=(
            jax.ShapeDtypeStruct((head.shape[0], own), F32),
            jax.ShapeDtypeStruct((channels // col_count, 9 * channels), F32),
            jax.ShapeDtypeStruct((channels, context.shape[0]), F32),
        ),
        in_specs=[SMEM] + [VMEM] * 6,
        out_specs=(VMEM,) * 3,
        scratch_shapes=[pltpu.VMEM((channels, own), BF16)] * 2,
        compiler_params=PARAMS,
        name="network",
    )(place, hidden, cotangent, forward, backward, head, context)


def swapped(values, axis):
    size = lax.axis_size(axis)
    return lax.ppermute(values, axis, [(i, i ^ 1) for i in range(size)])


def passed(values, axis, step, wrap):
    size = lax.axis_size(axis)
    pairs = [(i, (i + step) % size) for i in range(size) if wrap or 0 <= i + step < size]
    return lax.ppermute(values, axis, pairs)


def in_order(core, mine, theirs, axis):
    return jnp.where(
        core == 0, jnp.concatenate([mine, theirs], axis=axis), jnp.concatenate([theirs, mine], axis=axis)
    )


def shards(
    tokens, ln_gain, qkv_weight, out_weight, readout_weight, conv_weight, head_weight, holo_cot
):
    frame_rows = tokens[0]
    cotangent = holo_cot[0]
    rows_dev, cols_dev = cotangent.shape[1:]
    tok_count, col_count, dp_count = (lax.axis_size(axis) for axis in ("tok", "col", "dp"))
    chips = tok_count // 2
    tok_at, half = lax.axis_index("tok"), lax.axis_index("col")
    core = lax.rem(tok_at, 2)
    chip_row = (tok_at - core) * rows_dev
    place = jnp.stack([core, half, chip_row]).astype(jnp.int32)
    layers, channels = conv_weight.shape[:2]
    cols = cols_dev * col_count
    length = frame_rows.shape[0]

    mine, theirs = project(place, frame_rows, ln_gain.reshape(1, -1), qkv_weight)
    joined = jnp.concatenate([mine, swapped(theirs, "tok")], axis=2)
    count = joined.shape[0]
    queries = [joined[head, :HEAD] for head in range(count)]
    blocks = [joined[head, HEAD:] for head in range(count)]
    states = [None] * count
    for turn in range(chips):
        arriving = [passed(block, "tok", 2, True) for block in blocks] if turn < chips - 1 else None
        states = [absorb(queries[head], blocks[head], states[head]) for head in range(count)]
        blocks = arriving

    kept = count * HEAD
    own_out = lax.dynamic_slice_in_dim(out_weight, core * kept, kept, 0)
    folded = lax.dot_general(readout_weight, own_out, (((0,), (1,)), ((), ())), preferred_element_type=F32)
    direct = lax.dot_general(readout_weight, frame_rows, (((0,), (1,)), ((), ())), preferred_element_type=F32)
    context, share = finish([state[0] for state in states], folded)
    partial = share[:, :length] + swapped(share[:, length:], "tok")
    own_map = (partial + swapped(partial, "col") + direct).astype(BF16)
    chip_map = in_order(core, own_map, swapped(own_map, "tok"), 1)
    rows_chip = 2 * rows_dev
    hidden = jnp.concatenate(
        [passed(chip_map, "tok", 2, False), chip_map, passed(chip_map, "tok", -2, False)], axis=1
    )

    wide_cot = in_order(half, cotangent, swapped(cotangent, "col"), 2)
    chip_cot = in_order(core, wide_cot, swapped(wide_cot, "tok"), 1)
    edge = chip_cot.shape[1] - 2
    cot_rows = jnp.concatenate(
        [passed(chip_cot[:, edge:], "tok", 2, False), chip_cot, passed(chip_cot[:, :2], "tok", -2, False)], axis=1
    )
    taps = conv_weight.reshape(layers, channels, 3, 3, channels)
    forward = jnp.transpose(taps.reshape(layers, channels, 3, 3 * channels), (0, 2, 1, 3))
    backward = jnp.transpose(taps[:, :, ::-1, ::-1, :], (0, 2, 4, 3, 1)).reshape(layers, 3, channels, 3 * channels)
    holo, sums, gradient = network(
        place, hidden, cot_rows.reshape(cot_rows.shape[0], -1), forward, backward, head_weight, context, cols,
        tok_count * rows_dev, col_count,
    )
    holo = holo.reshape(-1, rows_chip, cols)
    hologram = lax.dynamic_slice(
        holo, (0, core * rows_dev, half * cols_dev), (holo.shape[0], rows_dev, cols_dev)
    )

    taps_wide = sums.shape[1]
    lanes = 128 * ((taps_wide + 127) // 128)
    rows = sums.shape[0]
    pieces = gradient.shape[0] // rows
    folded_gradient = [gradient[at * rows : (at + 1) * rows] for at in range(pieces)]
    sent = jnp.concatenate([jnp.pad(sums, ((0, 0), (0, lanes - taps_wide))), *folded_gradient], axis=1)
    summed = sent
    for step in range(1, dp_count):
        summed = summed + passed(sent, "dp", step, True)
    total = summed
    for step in range(1, chips):
        total = total + passed(summed, "tok", 2 * step, True)
    own_grad = total[:, :taps_wide]
    layer_grad = in_order(half, own_grad, swapped(own_grad, "col"), 0)
    other_grad = swapped(layer_grad, "tok")
    conv_grad = in_order(core, layer_grad[None], other_grad[None], 0)
    wide = gradient.shape[1]
    own_small = jnp.concatenate(
        [total[:, lanes + at * wide : lanes + (at + 1) * wide] for at in range(pieces)], axis=0
    )
    small = in_order(core, own_small, swapped(own_small, "tok"), 1)
    out_grad = lax.dot_general(
        small, readout_weight.astype(F32), (((0,), (1,)), ((), ())), precision=lax.Precision.HIGHEST
    )
    return (hologram[None], conv_grad, out_grad)


def solution(mesh):
    in_specs = (
        P("dp", "tok", None),
        P(),
        P(None, None, "col"),
        P("col", None),
        P(),
        P(),
        P(),
        P("dp", None, "tok", "col"),
    )
    out_specs = (P("dp", None, "tok", "col"), P(), P("col", None))
    return jax.shard_map(shards, mesh=mesh, in_specs=in_specs, out_specs=out_specs, check_vma=False)
```

time: 459 us -> 108 us (0.24)
  waiting for transfers between devices: 293 us -> 46.2 us
  matrix products: 61.2 us -> 2.25 us
  other arithmetic: 35.1 us -> 1.05 us
  Pallas kernels: 0 us -> 23.2 us
  between operations: 14.5 us -> 1.11 us
  local copies, waits for them, and re-layouts: 17.7 us -> 5.05 us
  starting transfers between devices: 35.6 us -> 28.7 us
    all_gather x4 -> x0, waiting for transfers between devices: 142 us -> none  [the longest x1 51.7 us: shards(): lax.all_gather(value_rows, ('tok', 'col'), axis=0, tiled=True)]
    psum x1 -> x0, waiting for transfers between devices: 129 us -> none  [shards(): conv_grad = lax.psum(jnp.stack(conv_terms), ('dp', 'tok', 'col'))]
    dot_general x30 -> x3, matrix products: 61.2 us -> 2.25 us  [the longest x1 1.6 us: shards(): lax.dot_general(small, readout_weight.astype(F32), (((0,), (1,)), ((), ()...]
    reduce_sum x10 -> x0, other arithmetic: 25.7 us -> none  [the longest x8 23.2 us: absorb(): row_total = row_total * rescale + jnp.sum(raised, axis=-1)]
    ppermute x16 -> x23, waiting for transfers between devices: 20.9 us -> 46.2 us  [the longest x14 36.8 us: passed(): return lax.ppermute(values, axis, pairs)]
    pallas_call x0 -> x11, Pallas kernels: none -> 23.2 us  [the longest x8 16.3 us: absorb(): pl.pallas_call(functools.partial(absorb_kernel, first), out_shape=shapes,...]
    dynamic_slice x24 -> x0, local copies, waits for them, and re-layouts: 13.6 us -> none  [the longest x16 11.9 us: advance(): lax.dynamic_slice_in_dim(value_rows, turn_at * block_rows, block_rows, 0)]
    ppermute x16 -> x23, starting transfers between devices: 35.4 us -> 28.7 us  [the longest x14 22.7 us: passed(): return lax.ppermute(values, axis, pairs)]
  transfers between devices with their start and end apart: 21 -> 23, of which waited for: 14 -> 13; matrix products, arithmetic and copies ran while one was open for 22% -> 4% of each run, Pallas kernels for 0% -> 13%
where the time goes in v1:
time: 108 us
  waiting for transfers between devices  46.2 us (43%)
  starting transfers between devices  28.7 us (27%)
  Pallas kernels  23.2 us (21%)
  local copies, waits for them, and re-layouts  5.05 us (5%)
  matrix products  2.25 us (2%)
  between operations  1.11 us (1%)
    ppermute x14, waiting for transfers between devices, passed(): return lax.ppermute(values, axis, pairs)  36.8 us
    ppermute x14, starting transfers between devices, passed(): return lax.ppermute(values, axis, pairs)  22.7 us
    pallas_call x8, Pallas kernels, absorb(): pl.pallas_call(functools.partial(absorb_kernel, first), out_shape=shapes,...  16.3 us
    ppermute x9, waiting for transfers between devices, swapped(): return lax.ppermute(values, axis, [(i, i ^ 1) for i in range(size)])  9.46 us
    ppermute x9, starting transfers between devices, swapped(): return lax.ppermute(values, axis, [(i, i ^ 1) for i in range(size)])  6.05 us
    pallas_call x1, Pallas kernels, network(): pl.pallas_call(functools.partial(network_kernel, cols, frame_rows), out_s...  3.75 us
    unnamed x19, local copies, waits for them, and re-layouts  2.92 us
    pallas_call x1, Pallas kernels, project(): pl.pallas_call(project_kernel, out_shape=(shape, shape), in_specs=[SMEM,...  2.86 us
  transfers between devices with their start and end apart: 23, of which 13 were waited for; matrix products, arithmetic and copies ran while one was open for 4% of the time, Pallas kernels for 13%

profile of v1, /device:TPU:0, one launch (start us, length us, event | category | flops | bytes accessed | tf_op | source)
XLA Modules:
  0.0 107.6 jit_solution(1105416599507606818)
XLA Ops:
  2.7 1.4 %copy-done.3 = bf16[3,1024,256]{2,1,0:T(8,128)(2,1)S(1)} copy-done((bf16[3,1024,256]{2,1,0:T(8,128)(2,1)S(1)}, bf16[3,1024,256]{2,1,0:T(8,128)(2,1)}, u32[]{:S(2)}) %copy-start.3) | copy-done | bytes 1572888
  4.1 2.9 %project.1 = (bf16[2,192,512]{2,1,0:T(8,128)(2,1)S(1)}, bf16[2,192,512]{2,1,0:T(8,128)(2,1)S(1)}) custom-call(s32[3]{0:T(128)S(1)} %pad_add_fusion.place, bf16[512,1024]{1,0:T(8,128)(2,1)S(1)} %bitcast.36, bf16[1,1024]{1,0:T(2,128)(2,1)S(1)} %reshape.76.gain, bf16[3,1024,256]{2,1,0:T(8,128)(2,1)S(1)} %copy-done.3), custom_call_target="tpu_custom_call" | custom-call | tf_op jit(solution)/shard_map/project/pallas_call | solution.py:54
  9.0 3.0 %collective-permute-start.4 = (bf16[128,1024]{1,0:T(8,128)(2,1)S(1)}, bf16[128,1024]{1,0:T(8,128)(2,1)S(1)}, u32[]{:S(2)}, u32[]{:S(2)}) collective-permute-start(bf16[128,1024]{1,0:T(8,128)(2,1)S(1)} %get-tuple-element.45.refs_1_), channel_id=1, source_target_pairs={{0,4},{2,6},{4,8},{6,10},{8,12},{10,14},{12,0},{14,2},{1,5},{3,7},... | collective-permute-start | bytes 786440 | tf_op jit(solution)/shard_map/ppermute | solution.py:238
  12.0 1.6 %collective-permute-start.1 = (bf16[128,1024]{1,0:T(8,128)(2,1)S(1)}, bf16[128,1024]{1,0:T(8,128)(2,1)S(1)}, u32[]{:S(2)}, u32[]{:S(2)}) collective-permute-start(bf16[128,1024]{1,0:T(8,128)(2,1)S(1)} %get-tuple-element.46.refs_1_), channel_id=1, source_target_pairs={{0,4},{2,6},{4,8},{6,10},{8,12},{10,14},{12,0},{14,2},{1,5},{3,7},... | collective-permute-start | bytes 786440 | tf_op jit(solution)/shard_map/ppermute | solution.py:238
  13.6 7.6 %collective-permute-done.4.refs_1_ = bf16[128,1024]{1,0:T(8,128)(2,1)S(1)} collective-permute-done((bf16[128,1024]{1,0:T(8,128)(2,1)S(1)}, bf16[128,1024]{1,0:T(8,128)(2,1)S(1)}, u32[]{:S(2)}, u32[]{:S(2)}) %collective-permute-start.4) | collective-permute-done | bytes 262176 | tf_op jit(solution)/shard_map/ppermute | solution.py:238
  21.2 5.6 %collective-permute-done.1.refs_1_ = bf16[128,1024]{1,0:T(8,128)(2,1)S(1)} collective-permute-done((bf16[128,1024]{1,0:T(8,128)(2,1)S(1)}, bf16[128,1024]{1,0:T(8,128)(2,1)S(1)}, u32[]{:S(2)}, u32[]{:S(2)}) %collective-permute-start.1) | collective-permute-done | bytes 262176 | tf_op jit(solution)/shard_map/ppermute | solution.py:238
  26.8 5.6 %collective-permute-done.5.refs_1_ = bf16[128,1024]{1,0:T(8,128)(2,1)S(1)} collective-permute-done((bf16[128,1024]{1,0:T(8,128)(2,1)S(1)}, bf16[128,1024]{1,0:T(8,128)(2,1)S(1)}, u32[]{:S(2)}, u32[]{:S(2)}) %collective-permute-start.5) | collective-permute-done | bytes 262176 | tf_op jit(solution)/shard_map/ppermute | solution.py:238
  32.4 5.6 %collective-permute-done.2.refs_1_ = bf16[128,1024]{1,0:T(8,128)(2,1)S(1)} collective-permute-done((bf16[128,1024]{1,0:T(8,128)(2,1)S(1)}, bf16[128,1024]{1,0:T(8,128)(2,1)S(1)}, u32[]{:S(2)}, u32[]{:S(2)}) %collective-permute-start.2) | collective-permute-done | bytes 262176 | tf_op jit(solution)/shard_map/ppermute | solution.py:238
  38.3 2.0 %absorb.12 = (f32[80,1024]{1,0:T(8,128)S(1)}, f32[8,1024]{1,0:T(8,128)S(1)}) custom-call(bf16[64,1024]{1,0:T(8,128)(2,1)S(1)} %get-tuple-element.47.refs_0_, bf16[128,1024]{1,0:T(8,128)(2,1)S(1)} %get-tuple-element.45.refs_1_), custom_call_target="tpu_custom_call" | custom-call | tf_op jit(solution)/shard_map/absorb/pallas_call | solution.py:95
  40.3 2.0 %absorb.8 = (f32[80,1024]{1,0:T(8,128)S(1)}, f32[8,1024]{1,0:T(8,128)S(1)}) custom-call(bf16[64,1024]{1,0:T(8,128)(2,1)S(1)} %get-tuple-element.48.refs_0_, bf16[128,1024]{1,0:T(8,128)(2,1)S(1)} %get-tuple-element.46.refs_1_), custom_call_target="tpu_custom_call" | custom-call | tf_op jit(solution)/shard_map/absorb/pallas_call | solution.py:95
  42.3 2.1 %absorb.13 = (f32[80,1024]{1,0:T(8,128)S(1)}, f32[8,1024]{1,0:T(8,128)S(1)}) custom-call(bf16[64,1024]{1,0:T(8,128)(2,1)S(1)} %get-tuple-element.47.refs_0_, bf16[128,1024]{1,0:T(8,128)(2,1)S(1)} %collective-permute-done.4.refs_1_, f32[80,1024]{1,0:T(8,128)S(1)} %get-tuple-element.33.refs_2_, ...), custom_call_target="tpu_custom_call", output_to_operand_aliasing={{0}: (2, {}), {1}: (3, {})} | custom-call | tf_op jit(solution)/shard_map/absorb/pallas_call | solution.py:95
  44.3 2.1 %absorb.9 = (f32[80,1024]{1,0:T(8,128)S(1)}, f32[8,1024]{1,0:T(8,128)S(1)}) custom-call(bf16[64,1024]{1,0:T(8,128)(2,1)S(1)} %get-tuple-element.48.refs_0_, bf16[128,1024]{1,0:T(8,128)(2,1)S(1)} %collective-permute-done.1.refs_1_, f32[80,1024]{1,0:T(8,128)S(1)} %get-tuple-element.26.refs_2_, ...), custom_call_target="tpu_custom_call", output_to_operand_aliasing={{0}: (2, {}), {1}: (3, {})} | custom-call | tf_op jit(solution)/shard_map/absorb/pallas_call | solution.py:95
  46.4 2.1 %absorb.14 = (f32[80,1024]{1,0:T(8,128)S(1)}, f32[8,1024]{1,0:T(8,128)S(1)}) custom-call(bf16[64,1024]{1,0:T(8,128)(2,1)S(1)} %get-tuple-element.47.refs_0_, bf16[128,1024]{1,0:T(8,128)(2,1)S(1)} %collective-permute-done.5.refs_1_, f32[80,1024]{1,0:T(8,128)S(1)} %get-tuple-element.35.refs_2_, ...), custom_call_target="tpu_custom_call", output_to_operand_aliasing={{0}: (2, {}), {1}: (3, {})} | custom-call | tf_op jit(solution)/shard_map/absorb/pallas_call | solution.py:95
  48.5 2.1 %absorb.10 = (f32[80,1024]{1,0:T(8,128)S(1)}, f32[8,1024]{1,0:T(8,128)S(1)}) custom-call(bf16[64,1024]{1,0:T(8,128)(2,1)S(1)} %get-tuple-element.48.refs_0_, bf16[128,1024]{1,0:T(8,128)(2,1)S(1)} %collective-permute-done.2.refs_1_, f32[80,1024]{1,0:T(8,128)S(1)} %get-tuple-element.28.refs_2_, ...), custom_call_target="tpu_custom_call", output_to_operand_aliasing={{0}: (2, {}), {1}: (3, {})} | custom-call | tf_op jit(solution)/shard_map/absorb/pallas_call | solution.py:95
  50.5 2.1 %absorb.15 = (f32[80,1024]{1,0:T(8,128)S(1)}, f32[8,1024]{1,0:T(8,128)S(1)}) custom-call(bf16[64,1024]{1,0:T(8,128)(2,1)S(1)} %get-tuple-element.47.refs_0_, bf16[128,1024]{1,0:T(8,128)(2,1)S(1)} %collective-permute-done.6.refs_1_, f32[80,1024]{1,0:T(8,128)S(1)} %get-tuple-element.37.refs_2_, ...), custom_call_target="tpu_custom_call", output_to_operand_aliasing={{0}: (2, {}), {1}: (3, {})} | custom-call | tf_op jit(solution)/shard_map/absorb/pallas_call | solution.py:95
  52.6 2.1 %absorb.11 = (f32[80,1024]{1,0:T(8,128)S(1)}, f32[8,1024]{1,0:T(8,128)S(1)}) custom-call(bf16[64,1024]{1,0:T(8,128)(2,1)S(1)} %get-tuple-element.48.refs_0_, bf16[128,1024]{1,0:T(8,128)(2,1)S(1)} %collective-permute-done.3.refs_1_, f32[80,1024]{1,0:T(8,128)S(1)} %get-tuple-element.30.refs_2_, ...), custom_call_target="tpu_custom_call", output_to_operand_aliasing={{0}: (2, {}), {1}: (3, {})} | custom-call | tf_op jit(solution)/shard_map/absorb/pallas_call | solution.py:95
  55.1 1.8 %collective-permute-start.12 = (f32[2,2,128]{2,1,0:T(2,128)S(1)}, f32[2,2,128]{2,1,0:T(2,128)S(1)}, u32[]{:S(2)}, u32[]{:S(2)}) collective-permute-start(f32[2,2,128]{2,1,0:T(2,128)S(1)} %bitcast.43), channel_id=1, source_target_pairs={{0,1},{1,0},{2,3},{3,2},{4,5},{5,4},{6,7},{7,6},{8,9},{9,8},{10,11... | collective-permute-start | bytes 6152 | tf_op jit(solution)/shard_map/ppermute | solution.py:232
  56.8 1.9 %collective-permute-done.12 = f32[2,2,128]{2,1,0:T(2,128)S(1)} collective-permute-done((f32[2,2,128]{2,1,0:T(2,128)S(1)}, f32[2,2,128]{2,1,0:T(2,128)S(1)}, u32[]{:S(2)}, u32[]{:S(2)}) %collective-permute-start.12) | collective-permute-done | bytes 2080 | tf_op jit(solution)/shard_map/ppermute | solution.py:232
  58.8 1.8 %collective-permute-start.8 = (f32[64,512]{1,0:T(8,128)S(1)}, f32[64,512]{1,0:T(8,128)S(1)}, u32[]{:S(2)}, u32[]{:S(2)}) collective-permute-start(f32[64,512]{1,0:T(8,128)S(1)} %slice_add_fusion), channel_id=1, source_target_pairs={{0,1},{1,0},{2,3},{3,2},{4,5},{5,4},{6,7},{7,6},{8,9},{9,8},{10,11... | collective-permute-start | bytes 393224 | tf_op jit(solution)/shard_map/ppermute | solution.py:232
  61.3 3.5 %collective-permute-done.8 = f32[64,512]{1,0:T(8,128)S(1)} collective-permute-done((f32[64,512]{1,0:T(8,128)S(1)}, f32[64,512]{1,0:T(8,128)S(1)}, u32[]{:S(2)}, u32[]{:S(2)}) %collective-permute-start.8) | collective-permute-done | bytes 131104 | tf_op jit(solution)/shard_map/ppermute | solution.py:232
  64.9 3.5 %collective-permute-start.14 = (f32[2,2,256]{2,1,0:T(2,128)S(1)}, f32[2,2,256]{2,1,0:T(2,128)S(1)}, u32[]{:S(2)}, u32[]{:S(2)}) collective-permute-start(f32[2,2,256]{2,1,0:T(2,128)S(1)} %get-tuple-element.55), channel_id=1, source_target_pairs={{0,4},{2,6},{4,8},{6,10},{8,12},{10,14},{1,5},{3,7},{5,9},{7,11},{... | collective-permute-start | bytes 12296 | tf_op jit(solution)/shard_map/ppermute | solution.py:238
  69.7 4.6 %collective-permute-start.10 = (bf16[64,1024]{1,0:T(8,128)(2,1)S(1)}, bf16[64,1024]{1,0:T(8,128)(2,1)S(1)}, u32[]{:S(2)}, u32[]{:S(2)}) collective-permute-start(bf16[64,1024]{1,0:T(8,128)(2,1)S(1)} %maximum_select_fusion.3), channel_id=1, source_target_pairs={{0,4},{2,6},{4,8},{6,10},{8,12},{10,14},{1,5},{3,7},{5,9},{7,11},{... | collective-permute-start | bytes 393224 | tf_op jit(solution)/shard_map/ppermute | solution.py:238
  77.0 4.1 %collective-permute-done.11 = bf16[64,1024]{1,0:T(8,128)(2,1)S(1)} collective-permute-done((bf16[64,1024]{1,0:T(8,128)(2,1)S(1)}, bf16[64,1024]{1,0:T(8,128)(2,1)S(1)}, u32[]{:S(2)}, u32[]{:S(2)}) %collective-permute-start.11) | collective-permute-done | bytes 131104 | tf_op jit(solution)/shard_map/ppermute | solution.py:238
  81.2 3.7 %network.1 = (f32[2,1024]{1,0:T(2,128)S(1)}, f32[32,576]{1,0:T(8,128)S(1)}, f32[64,128]{1,0:T(8,128)S(1)}) custom-call(s32[3]{0:T(128)S(1)} %pad_add_fusion.place, bf16[64,3072]{1,0:T(8,128)(2,1)S(1)} %pad_maximum_fusion.hidden, f32[2,2048]{1,0:T(2,128)S(1)} %bitcast.38, bf16[2,3,64,192]{3,2,1,0:T(8,128)(2,1)S(1)} %bitcast.37, ...), custom_call_target="tpu_custom_call" | custom-call | tf_op jit(solution)/shard_map/network/pallas_call | solution.py:215
  85.0 1.7 %collective-permute-start.16 = (f32[32,896]{1,0:T(8,128)S(1)}, f32[32,896]{1,0:T(8,128)S(1)}, u32[]{:S(2)}, u32[]{:S(2)}) collective-permute-start(f32[32,896]{1,0:T(8,128)S(1)} %fusion.1), channel_id=1, source_target_pairs={{0,16},{16,0},{1,17},{17,1},{2,18},{18,2},{3,19},{19,3},{4,20},{20... | collective-permute-start | bytes 344072 | tf_op jit(solution)/shard_map/ppermute | solution.py:238
  86.7 3.1 %collective-permute-done.16 = f32[32,896]{1,0:T(8,128)S(1)} collective-permute-done((f32[32,896]{1,0:T(8,128)S(1)}, f32[32,896]{1,0:T(8,128)S(1)}, u32[]{:S(2)}, u32[]{:S(2)}) %collective-permute-start.16) | collective-permute-done | bytes 114720 | tf_op jit(solution)/shard_map/ppermute | solution.py:238
  89.9 1.7 %collective-permute-start.17 = (f32[32,896]{1,0:T(8,128)S(1)}, f32[32,896]{1,0:T(8,128)S(1)}, u32[]{:S(2)}, u32[]{:S(2)}) collective-permute-start(f32[32,896]{1,0:T(8,128)S(1)} %fusion.17), channel_id=1, source_target_pairs={{0,4},{2,6},{4,8},{6,10},{8,12},{10,14},{12,0},{14,2},{1,5},{3,7},... | collective-permute-start | bytes 344072 | tf_op jit(solution)/shard_map/ppermute | solution.py:238
  92.8 2.8 %collective-permute-start.19 = (f32[32,896]{1,0:T(8,128)S(1)}, f32[32,896]{1,0:T(8,128)S(1)}, u32[]{:S(2)}, u32[]{:S(2)}) collective-permute-start(f32[32,896]{1,0:T(8,128)S(1)} %fusion.17), channel_id=1, source_target_pairs={{0,12},{2,14},{4,0},{6,2},{8,4},{10,6},{12,8},{14,10},{1,13},{3,15... | collective-permute-start | bytes 344072 | tf_op jit(solution)/shard_map/ppermute | solution.py:238
  97.4 3.2 %collective-permute-done.18 = f32[32,896]{1,0:T(8,128)S(1)} collective-permute-done((f32[32,896]{1,0:T(8,128)S(1)}, f32[32,896]{1,0:T(8,128)S(1)}, u32[]{:S(2)}, u32[]{:S(2)}) %collective-permute-start.18) | collective-permute-done | bytes 114720 | tf_op jit(solution)/shard_map/ppermute | solution.py:238
  100.6 1.7 %collective-permute-start.20 = (f32[32,576]{1,0:T(8,128)S(1)}, f32[32,576]{1,0:T(8,128)S(1)}, u32[]{:S(2)}, u32[]{:S(2)}) collective-permute-start(f32[32,576]{1,0:T(8,128)S(1)} %get-tuple-element.52), channel_id=1, source_target_pairs={{0,1},{1,0},{2,3},{3,2},{4,5},{5,4},{6,7},{7,6},{8,9},{9,8},{10,11... | collective-permute-start | bytes 221192 | tf_op jit(solution)/shard_map/ppermute | solution.py:232
  102.4 2.8 %collective-permute-done.20 = f32[32,576]{1,0:T(8,128)S(1)} collective-permute-done((f32[32,576]{1,0:T(8,128)S(1)}, f32[32,576]{1,0:T(8,128)S(1)}, u32[]{:S(2)}, u32[]{:S(2)}) %collective-permute-start.20) | collective-permute-done | bytes 73760 | tf_op jit(solution)/shard_map/ppermute | solution.py:232
  105.3 1.6 %fusion.2 = f32[256,1024]{1,0:T(8,128)} fusion(bf16[1024,64]{0,1:T(8,128)(2,1)S(1)} %copy-done.5, f32[64,128]{1,0:T(8,128)S(1)} %collective-permute-done.22, f32[32,128]{1,0:T(8,128)S(1)} %get-tuple-element.50, f32[32,128]{1,0:T(8,128)S(1)} %get-tuple-element.49, pred[]{:T(512)S(6)} %eq.4), kind=kOutput, calls=%fused_computation.20 | convolution fusion | flops 201408512 | bytes 1245185 | tf_op jit(solution)/shard_map/dot_general | solution.py:326
  (78 shorter events, 13.5 us)
Async XLA Ops:
  0.6 37.4 %copy-start = (bf16[256,1024]{1,0:T(8,128)(2,1)S(1)}, bf16[256,1024]{1,0:T(8,128)(2,1)}, u32[]{:S(2)}) copy-start(bf16[256,1024]{1,0:T(8,128)(2,1)} %param.11) | copy-start | bytes 1572868
  1.5 1.2 %copy-start.1 = (bf16[1,512,1024]{2,1,0:T(8,128)(2,1)S(1)}, bf16[1,512,1024]{2,1,0:T(8,128)(2,1)}, u32[]{:S(2)}) copy-start(bf16[1,512,1024]{2,1,0:T(8,128)(2,1)} %param.8) | copy-start | bytes 3145732
  2.7 1.4 %copy-start.3 = (bf16[3,1024,256]{2,1,0:T(8,128)(2,1)S(1)}, bf16[3,1024,256]{2,1,0:T(8,128)(2,1)}, u32[]{:S(2)}) copy-start(bf16[3,1024,256]{2,1,0:T(8,128)(2,1)} %weight.1) | copy-start | bytes 4718596
  7.0 31.1 %copy-start.5 = (bf16[1024,64]{0,1:T(8,128)(2,1)S(1)}, bf16[1024,64]{0,1:T(8,128)(2,1)}, u32[]{:S(2)}) copy-start(bf16[1024,64]{0,1:T(8,128)(2,1)} %param.12) | copy-start | bytes 393220
  7.0 1.9 %collective-permute-start = (bf16[2,192,512]{2,1,0:T(8,128)(2,1)S(1)}, bf16[2,192,512]{2,1,0:T(8,128)(2,1)S(1)}, u32[]{:S(2)}, u32[]{:S(2)}) collective-permute-start(bf16[2,192,512]{2,1,0:T(8,128)(2,1)S(1)} %get-tuple-element.25), channel_id=1, source_target_pairs={{0,2},{2,0},{4,6},{6,4},{8,10},{10,8},{12,14},{14,12},{1,3},{3,1},... | collective-permute-start | bytes 1179656 | tf_op jit(solution)/shard_map/ppermute | solution.py:232
  9.0 12.2 %collective-permute-start.4 = (bf16[128,1024]{1,0:T(8,128)(2,1)S(1)}, bf16[128,1024]{1,0:T(8,128)(2,1)S(1)}, u32[]{:S(2)}, u32[]{:S(2)}) collective-permute-start(bf16[128,1024]{1,0:T(8,128)(2,1)S(1)} %get-tuple-element.45.refs_1_), channel_id=1, source_target_pairs={{0,4},{2,6},{4,8},{6,10},{8,12},{10,14},{12,0},{14,2},{1,5},{3,7},... | collective-permute-start | bytes 786440 | tf_op jit(solution)/shard_map/ppermute | solution.py:238
  12.0 14.8 %collective-permute-start.1 = (bf16[128,1024]{1,0:T(8,128)(2,1)S(1)}, bf16[128,1024]{1,0:T(8,128)(2,1)S(1)}, u32[]{:S(2)}, u32[]{:S(2)}) collective-permute-start(bf16[128,1024]{1,0:T(8,128)(2,1)S(1)} %get-tuple-element.46.refs_1_), channel_id=1, source_target_pairs={{0,4},{2,6},{4,8},{6,10},{8,12},{10,14},{12,0},{14,2},{1,5},{3,7},... | collective-permute-start | bytes 786440 | tf_op jit(solution)/shard_map/ppermute | solution.py:238
  21.2 11.2 %collective-permute-start.5 = (bf16[128,1024]{1,0:T(8,128)(2,1)S(1)}, bf16[128,1024]{1,0:T(8,128)(2,1)S(1)}, u32[]{:S(2)}, u32[]{:S(2)}) collective-permute-start(bf16[128,1024]{1,0:T(8,128)(2,1)S(1)} %collective-permute-done.4.refs_1_), channel_id=1, source_target_pairs={{0,4},{2,6},{4,8},{6,10},{8,12},{10,14},{12,0},{14,2},{1,5},{3,7},... | collective-permute-start | bytes 786440 | tf_op jit(solution)/shard_map/ppermute | solution.py:238
  26.8 11.2 %collective-permute-start.2 = (bf16[128,1024]{1,0:T(8,128)(2,1)S(1)}, bf16[128,1024]{1,0:T(8,128)(2,1)S(1)}, u32[]{:S(2)}, u32[]{:S(2)}) collective-permute-start(bf16[128,1024]{1,0:T(8,128)(2,1)S(1)} %collective-permute-done.1.refs_1_), channel_id=1, source_target_pairs={{0,4},{2,6},{4,8},{6,10},{8,12},{10,14},{12,0},{14,2},{1,5},{3,7},... | collective-permute-start | bytes 786440 | tf_op jit(solution)/shard_map/ppermute | solution.py:238
  32.4 18.1 %collective-permute-start.6 = (bf16[128,1024]{1,0:T(8,128)(2,1)S(1)}, bf16[128,1024]{1,0:T(8,128)(2,1)S(1)}, u32[]{:S(2)}, u32[]{:S(2)}) collective-permute-start(bf16[128,1024]{1,0:T(8,128)(2,1)S(1)} %collective-permute-done.5.refs_1_), channel_id=1, source_target_pairs={{0,4},{2,6},{4,8},{6,10},{8,12},{10,14},{12,0},{14,2},{1,5},{3,7},... | collective-permute-start | bytes 786440 | tf_op jit(solution)/shard_map/ppermute | solution.py:238
  38.0 14.6 %collective-permute-start.3 = (bf16[128,1024]{1,0:T(8,128)(2,1)S(1)}, bf16[128,1024]{1,0:T(8,128)(2,1)S(1)}, u32[]{:S(2)}, u32[]{:S(2)}) collective-permute-start(bf16[128,1024]{1,0:T(8,128)(2,1)S(1)} %collective-permute-done.2.refs_1_), channel_id=1, source_target_pairs={{0,4},{2,6},{4,8},{6,10},{8,12},{10,14},{12,0},{14,2},{1,5},{3,7},... | collective-permute-start | bytes 786440 | tf_op jit(solution)/shard_map/ppermute | solution.py:238
  48.4 6.6 %copy-start.7 = (f32[1,2,2,128]{3,2,1,0:T(2,128)S(1)}, f32[1,2,2,128]{3,2,1,0:T(2,128)}, u32[]{:S(2)}) copy-start(f32[1,2,2,128]{3,2,1,0:T(2,128)} %param.15) | copy-start | bytes 6148
  50.5 10.0 %copy-start.2 = (bf16[1,512,1024]{2,1,0:T(8,128)(2,1)S(1)}, bf16[1,512,1024]{2,1,0:T(8,128)(2,1)}, u32[]{:S(2)}) copy-start(bf16[1,512,1024]{2,1,0:T(8,128)(2,1)} %param.8) | copy-start | bytes 3145732
  52.6 8.4 %copy-start.6 = (bf16[2,64,576]{2,1,0:T(8,128)(2,1)S(1)}, bf16[2,64,576]{2,1,0:T(8,128)(2,1)}, u32[]{:S(2)}) copy-start(bf16[2,64,576]{2,1,0:T(8,128)(2,1)} %param.13) | copy-start | bytes 442372
  55.0 3.8 %collective-permute-start.7 = (f32[64,512]{1,0:T(8,128)S(1)}, f32[64,512]{1,0:T(8,128)S(1)}, u32[]{:S(2)}, u32[]{:S(2)}) collective-permute-start(f32[64,512]{1,0:T(8,128)S(1)} %slice.44), channel_id=1, source_target_pairs={{0,2},{2,0},{4,6},{6,4},{8,10},{10,8},{12,14},{14,12},{1,3},{3,1},... | collective-permute-start | bytes 393224 | tf_op jit(solution)/shard_map/ppermute | solution.py:232
  55.1 3.7 %collective-permute-start.12 = (f32[2,2,128]{2,1,0:T(2,128)S(1)}, f32[2,2,128]{2,1,0:T(2,128)S(1)}, u32[]{:S(2)}, u32[]{:S(2)}) collective-permute-start(f32[2,2,128]{2,1,0:T(2,128)S(1)} %bitcast.43), channel_id=1, source_target_pairs={{0,1},{1,0},{2,3},{3,2},{4,5},{5,4},{6,7},{7,6},{8,9},{9,8},{10,11... | collective-permute-start | bytes 6152 | tf_op jit(solution)/shard_map/ppermute | solution.py:232
  58.7 2.5 %collective-permute-start.13 = (f32[2,2,256]{2,1,0:T(2,128)S(1)}, f32[2,2,256]{2,1,0:T(2,128)S(1)}, u32[]{:S(2)}, u32[]{:S(2)}) collective-permute-start(f32[2,2,256]{2,1,0:T(2,128)S(1)} %maximum_select_fusion.7), channel_id=1, source_target_pairs={{0,2},{2,0},{4,6},{6,4},{8,10},{10,8},{12,14},{14,12},{1,3},{3,1},... | collective-permute-start | bytes 12296 | tf_op jit(solution)/shard_map/ppermute | solution.py:232
  58.8 6.0 %collective-permute-start.8 = (f32[64,512]{1,0:T(8,128)S(1)}, f32[64,512]{1,0:T(8,128)S(1)}, u32[]{:S(2)}, u32[]{:S(2)}) collective-permute-start(f32[64,512]{1,0:T(8,128)S(1)} %slice_add_fusion), channel_id=1, source_target_pairs={{0,1},{1,0},{2,3},{3,2},{4,5},{5,4},{6,7},{7,6},{8,9},{9,8},{10,11... | collective-permute-start | bytes 393224 | tf_op jit(solution)/shard_map/ppermute | solution.py:232
  64.8 4.9 %collective-permute-start.9 = (bf16[64,512]{1,0:T(8,128)(2,1)S(1)}, bf16[64,512]{1,0:T(8,128)(2,1)S(1)}, u32[]{:S(2)}, u32[]{:S(2)}) collective-permute-start(bf16[64,512]{1,0:T(8,128)(2,1)S(1)} %add_convert_fusion), channel_id=1, source_target_pairs={{0,2},{2,0},{4,6},{6,4},{8,10},{10,8},{12,14},{14,12},{1,3},{3,1},... | collective-permute-start | bytes 196616 | tf_op jit(solution)/shard_map/ppermute | solution.py:232
  64.9 11.3 %collective-permute-start.14 = (f32[2,2,256]{2,1,0:T(2,128)S(1)}, f32[2,2,256]{2,1,0:T(2,128)S(1)}, u32[]{:S(2)}, u32[]{:S(2)}) collective-permute-start(f32[2,2,256]{2,1,0:T(2,128)S(1)} %get-tuple-element.55), channel_id=1, source_target_pairs={{0,4},{2,6},{4,8},{6,10},{8,12},{10,14},{1,5},{3,7},{5,9},{7,11},{... | collective-permute-start | bytes 12296 | tf_op jit(solution)/shard_map/ppermute | solution.py:238
  68.3 7.8 %collective-permute-start.15 = (f32[2,2,256]{2,1,0:T(2,128)S(1)}, f32[2,2,256]{2,1,0:T(2,128)S(1)}, u32[]{:S(2)}, u32[]{:S(2)}) collective-permute-start(f32[2,2,256]{2,1,0:T(2,128)S(1)} %get-tuple-element.56), channel_id=1, source_target_pairs={{4,0},{6,2},{8,4},{10,6},{12,8},{14,10},{5,1},{7,3},{9,5},{11,7},{... | collective-permute-start | bytes 12296 | tf_op jit(solution)/shard_map/ppermute | solution.py:238
  69.7 7.4 %collective-permute-start.10 = (bf16[64,1024]{1,0:T(8,128)(2,1)S(1)}, bf16[64,1024]{1,0:T(8,128)(2,1)S(1)}, u32[]{:S(2)}, u32[]{:S(2)}) collective-permute-start(bf16[64,1024]{1,0:T(8,128)(2,1)S(1)} %maximum_select_fusion.3), channel_id=1, source_target_pairs={{0,4},{2,6},{4,8},{6,10},{8,12},{10,14},{1,5},{3,7},{5,9},{7,11},{... | collective-permute-start | bytes 393224 | tf_op jit(solution)/shard_map/ppermute | solution.py:238
  74.2 6.9 %collective-permute-start.11 = (bf16[64,1024]{1,0:T(8,128)(2,1)S(1)}, bf16[64,1024]{1,0:T(8,128)(2,1)S(1)}, u32[]{:S(2)}, u32[]{:S(2)}) collective-permute-start(bf16[64,1024]{1,0:T(8,128)(2,1)S(1)} %maximum_select_fusion.3), channel_id=1, source_target_pairs={{4,0},{6,2},{8,4},{10,6},{12,8},{14,10},{5,1},{7,3},{9,5},{11,7},{... | collective-permute-start | bytes 393224 | tf_op jit(solution)/shard_map/ppermute | solution.py:238
  75.5 5.7 %copy-start.4 = (bf16[2,64]{1,0:T(2,128)(2,1)S(1)}, bf16[2,64]{1,0:T(2,128)(2,1)}, u32[]{:S(2)}) copy-start(bf16[2,64]{1,0:T(2,128)(2,1)} %head.1) | copy-start | bytes 772
  85.0 4.9 %collective-permute-start.16 = (f32[32,896]{1,0:T(8,128)S(1)}, f32[32,896]{1,0:T(8,128)S(1)}, u32[]{:S(2)}, u32[]{:S(2)}) collective-permute-start(f32[32,896]{1,0:T(8,128)S(1)} %fusion.1), channel_id=1, source_target_pairs={{0,16},{16,0},{1,17},{17,1},{2,18},{18,2},{3,19},{19,3},{4,20},{20... | collective-permute-start | bytes 344072 | tf_op jit(solution)/shard_map/ppermute | solution.py:238
  89.9 7.5 %collective-permute-start.17 = (f32[32,896]{1,0:T(8,128)S(1)}, f32[32,896]{1,0:T(8,128)S(1)}, u32[]{:S(2)}, u32[]{:S(2)}) collective-permute-start(f32[32,896]{1,0:T(8,128)S(1)} %fusion.17), channel_id=1, source_target_pairs={{0,4},{2,6},{4,8},{6,10},{8,12},{10,14},{12,0},{14,2},{1,5},{3,7},... | collective-permute-start | bytes 344072 | tf_op jit(solution)/shard_map/ppermute | solution.py:238
  91.6 9.0 %collective-permute-start.18 = (f32[32,896]{1,0:T(8,128)S(1)}, f32[32,896]{1,0:T(8,128)S(1)}, u32[]{:S(2)}, u32[]{:S(2)}) collective-permute-start(f32[32,896]{1,0:T(8,128)S(1)} %fusion.17), channel_id=1, source_target_pairs={{0,8},{2,10},{4,12},{6,14},{8,0},{10,2},{12,4},{14,6},{1,9},{3,11}... | collective-permute-start | bytes 344072 | tf_op jit(solution)/shard_map/ppermute | solution.py:238
  92.8 7.8 %collective-permute-start.19 = (f32[32,896]{1,0:T(8,128)S(1)}, f32[32,896]{1,0:T(8,128)S(1)}, u32[]{:S(2)}, u32[]{:S(2)}) collective-permute-start(f32[32,896]{1,0:T(8,128)S(1)} %fusion.17), channel_id=1, source_target_pairs={{0,12},{2,14},{4,0},{6,2},{8,4},{10,6},{12,8},{14,10},{1,13},{3,15... | collective-permute-start | bytes 344072 | tf_op jit(solution)/shard_map/ppermute | solution.py:238
  100.6 4.5 %collective-permute-start.20 = (f32[32,576]{1,0:T(8,128)S(1)}, f32[32,576]{1,0:T(8,128)S(1)}, u32[]{:S(2)}, u32[]{:S(2)}) collective-permute-start(f32[32,576]{1,0:T(8,128)S(1)} %get-tuple-element.52), channel_id=1, source_target_pairs={{0,1},{1,0},{2,3},{3,2},{4,5},{5,4},{6,7},{7,6},{8,9},{9,8},{10,11... | collective-permute-start | bytes 221192 | tf_op jit(solution)/shard_map/ppermute | solution.py:232
  102.4 2.9 %collective-permute-start.22 = (f32[64,128]{1,0:T(8,128)S(1)}, f32[64,128]{1,0:T(8,128)S(1)}, u32[]{:S(2)}, u32[]{:S(2)}) collective-permute-start(f32[64,128]{1,0:T(8,128)S(1)} %pad_maximum_fusion.1), channel_id=1, source_target_pairs={{0,2},{2,0},{4,6},{6,4},{8,10},{10,8},{12,14},{14,12},{1,3},{3,1},... | collective-permute-start | bytes 98312 | tf_op jit(solution)/shard_map/ppermute | solution.py:232
  105.2 1.7 %collective-permute-start.21 = (f32[64,576]{1,0:T(8,128)S(1)}, f32[64,576]{1,0:T(8,128)S(1)}, u32[]{:S(2)}, u32[]{:S(2)}) collective-permute-start(f32[64,576]{1,0:T(8,128)S(1)} %maximum_select_fusion.2), channel_id=1, source_target_pairs={{0,2},{2,0},{4,6},{6,4},{8,10},{10,8},{12,14},{14,12},{1,3},{3,1},... | collective-permute-start | bytes 442376 | tf_op jit(solution)/shard_map/ppermute | solution.py:232

commit v2 on v1

--- a/solution.py
+++ b/solution.py
@@ -30,20 +30,37 @@
     return high, mid, low
 
 
-def project_kernel(place, tokens, gain, weight, mine, theirs):
+def project_kernel(place, tokens, gain, weight, mine, theirs, rows, parts, normed, token_sems, weight_sems):
     core = place[0]
-    values = tokens[...].astype(F32)
-    center = values - jnp.mean(values, axis=-1, keepdims=True)
-    spread = jnp.mean(center * center, axis=-1, keepdims=True)
-    normed = (center * lax.rsqrt(spread + EPSILON) * gain[...].astype(F32)).astype(BF16)
+    pieces = token_sems.shape[0]
+    size = rows.shape[0] // pieces
+    token_copies = [
+        pltpu.make_async_copy(
+            tokens.at[pl.ds(at * size, size)], rows.at[pl.ds(at * size, size)], token_sems.at[at]
+        )
+        for at in range(pieces)
+    ]
+    weight_copies = [
+        pltpu.make_async_copy(weight.at[member], parts.at[member], weight_sems.at[member]) for member in range(3)
+    ]
+    for copy in token_copies + weight_copies:
+        copy.start()
+    wide_gain = gain[...].astype(F32)
+    for at, copy in enumerate(token_copies):
+        copy.wait()
+        values = rows[at * size : (at + 1) * size, :].astype(F32)
+        center = values - jnp.mean(values, axis=-1, keepdims=True)
+        spread = jnp.mean(center * center, axis=-1, keepdims=True)
+        normed[at * size : (at + 1) * size, :] = (center * lax.rsqrt(spread + EPSILON) * wide_gain).astype(BF16)
     kept = mine.shape[0] * HEAD
-    for which, out in ((core, mine), (1 - core, theirs)):
-        for member in range(3):
-            part = weight[member, :, pl.ds(pl.multiple_of(which * kept, 128), kept)]
-            rows = dot(normed, part).astype(BF16)
+    for member, copy in enumerate(weight_copies):
+        copy.wait()
+        for which, out in ((core, mine), (1 - core, theirs)):
+            part = parts[member, :, pl.ds(pl.multiple_of(which * kept, 128), kept)]
+            product = dot(normed[...], part).astype(BF16)
             if member == 0:
-                rows = rows * jnp.asarray(1.0 / HEAD**0.5, BF16)
-            turned = rows.T
+                product = product * jnp.asarray(1.0 / HEAD**0.5, BF16)
+            turned = product.T
             for head in range(mine.shape[0]):
                 out[head, member * HEAD : (member + 1) * HEAD, :] = turned[head * HEAD : (head + 1) * HEAD, :]
 
@@ -51,11 +68,20 @@
 def project(place, tokens, gain, weight):
     count, length = weight.shape[2] // HEAD // 2, tokens.shape[0]
     shape = jax.ShapeDtypeStruct((count, 3 * HEAD, length), BF16)
+    pieces = 4 if length % 64 == 0 else 1
+    anywhere = pl.BlockSpec(memory_space=pltpu.HBM)
     return pl.pallas_call(
         project_kernel,
         out_shape=(shape, shape),
-        in_specs=[SMEM, VMEM, VMEM, VMEM],
+        in_specs=[SMEM, anywhere, VMEM, anywhere],
         out_specs=(VMEM, VMEM),
+        scratch_shapes=[
+            pltpu.VMEM(tokens.shape, BF16),
+            pltpu.VMEM(weight.shape, BF16),
+            pltpu.VMEM(tokens.shape, BF16),
+            pltpu.SemaphoreType.DMA((pieces,)),
+            pltpu.SemaphoreType.DMA((3,)),
+        ],
         compiler_params=PARAMS,
         name="project",
     )(place, tokens, gain, weight)
@@ -263,18 +289,51 @@
     mine, theirs = project(place, frame_rows, ln_gain.reshape(1, -1), qkv_weight)
     joined = jnp.concatenate([mine, swapped(theirs, "tok")], axis=2)
     count = joined.shape[0]
+    kept = count * HEAD
     queries = [joined[head, :HEAD] for head in range(count)]
     blocks = [joined[head, HEAD:] for head in range(count)]
     states = [None] * count
+
+    def weights_stage(_):
+        taps = conv_weight.reshape(layers, channels, 3, 3, channels)
+        forward = jnp.transpose(taps.reshape(layers, channels, 3, 3 * channels), (0, 2, 1, 3))
+        backward = jnp.transpose(taps[:, :, ::-1, ::-1, :], (0, 2, 4, 3, 1)).reshape(
+            layers, 3, channels, 3 * channels
+        )
+        own_out = lax.dynamic_slice_in_dim(out_weight, core * kept, kept, 0)
+        folded = lax.dot_general(readout_weight, own_out, (((0,), (1,)), ((), ())), preferred_element_type=F32)
+        direct = lax.dot_general(readout_weight, frame_rows, (((0,), (1,)), ((), ())), preferred_element_type=F32)
+        return (forward, backward, folded, direct)
+
+    def cotangent_stage(_):
+        wide = in_order(half, cotangent, swapped(cotangent, "col"), 2)
+        return in_order(core, wide, swapped(wide, "tok"), 1)
+
+    def rim_stage(chip_cot):
+        edge = chip_cot.shape[1] - 2
+        before, after = passed(chip_cot[:, edge:], "tok", 2, False), passed(chip_cot[:, :2], "tok", -2, False)
+        return jnp.concatenate([before, chip_cot, after], axis=1)
+
+    stages = [weights_stage, cotangent_stage, rim_stage]
+    results, held = [], None
     for turn in range(chips):
         arriving = [passed(block, "tok", 2, True) for block in blocks] if turn < chips - 1 else None
         states = [absorb(queries[head], blocks[head], states[head]) for head in range(count)]
-        blocks = arriving
-
-    kept = count * HEAD
-    own_out = lax.dynamic_slice_in_dim(out_weight, core * kept, kept, 0)
-    folded = lax.dot_general(readout_weight, own_out, (((0,), (1,)), ((), ())), preferred_element_type=F32)
-    direct = lax.dot_general(readout_weight, frame_rows, (((0,), (1,)), ((), ())), preferred_element_type=F32)
+        if stages:
+            held = stages.pop(0)(held)
+            results.append(held)
+        if arriving is not None:
+            tied = [lax.optimization_barrier((arriving[head], states[head])) for head in range(count)]
+            blocks, states = [pair[0] for pair in tied], [pair[1] for pair in tied]
+            if held is not None and turn < len(results):
+                blocks[-1], held = lax.optimization_barrier((blocks[-1], held))
+                results[-1] = held
+    for stage in stages:
+        held = stage(held)
+        results.append(held)
+    forward, backward, folded, direct = results[0]
+    cot_rows = results[2]
+
     context, share = finish([state[0] for state in states], folded)
     partial = share[:, :length] + swapped(share[:, length:], "tok")
     own_map = (partial + swapped(partial, "col") + direct).astype(BF16)
@@ -284,15 +343,6 @@
         [passed(chip_map, "tok", 2, False), chip_map, passed(chip_map, "tok", -2, False)], axis=1
     )
 
-    wide_cot = in_order(half, cotangent, swapped(cotangent, "col"), 2)
-    chip_cot = in_order(core, wide_cot, swapped(wide_cot, "tok"), 1)
-    edge = chip_cot.shape[1] - 2
-    cot_rows = jnp.concatenate(
-        [passed(chip_cot[:, edge:], "tok", 2, False), chip_cot, passed(chip_cot[:, :2], "tok", -2, False)], axis=1
-    )
-    taps = conv_weight.reshape(layers, channels, 3, 3, channels)
-    forward = jnp.transpose(taps.reshape(layers, channels, 3, 3 * channels), (0, 2, 1, 3))
-    backward = jnp.transpose(taps[:, :, ::-1, ::-1, :], (0, 2, 4, 3, 1)).reshape(layers, 3, channels, 3 * channels)
     holo, sums, gradient = network(
         place, hidden, cot_rows.reshape(cot_rows.shape[0], -1), forward, backward, head_weight, context, cols,
         tok_count * rows_dev, col_count,
@@ -315,9 +365,7 @@
     for step in range(1, chips):
         total = total + passed(summed, "tok", 2 * step, True)
     own_grad = total[:, :taps_wide]
-    layer_grad = in_order(half, own_grad, swapped(own_grad, "col"), 0)
-    other_grad = swapped(layer_grad, "tok")
-    conv_grad = in_order(core, layer_grad[None], other_grad[None], 0)
+    col_grad = swapped(own_grad, "col")
     wide = gradient.shape[1]
     own_small = jnp.concatenate(
         [total[:, lanes + at * wide : lanes + (at + 1) * wide] for at in range(pieces)], axis=0
@@ -326,6 +374,10 @@
     out_grad = lax.dot_general(
         small, readout_weight.astype(F32), (((0,), (1,)), ((), ())), precision=lax.Precision.HIGHEST
     )
+    col_grad, out_grad = lax.optimization_barrier((col_grad, out_grad))
+    layer_grad = in_order(half, own_grad, col_grad, 0)
+    other_grad = swapped(layer_grad, "tok")
+    conv_grad = in_order(core, layer_grad[None], other_grad[None], 0)
     return (hologram[None], conv_grad, out_grad)
 
 

time: 108 us -> 103 us (0.954)
  waiting for transfers between devices: 46.2 us -> 36.8 us
  local copies, waits for them, and re-layouts: 5.05 us -> 7.02 us
  Pallas kernels: 23.2 us -> 24.5 us
  starting transfers between devices: 28.7 us -> 29.9 us
    ppermute x14, waiting for transfers between devices: 36.8 us -> 24.6 us  [passed(): return lax.ppermute(values, axis, pairs)]
    ppermute x9, waiting for transfers between devices: 9.46 us -> 12.2 us  [swapped(): return lax.ppermute(values, axis, [(i, i ^ 1) for i in range(size)])]
    pallas_call x1, Pallas kernels: 2.86 us -> 4.09 us  [project(): pl.pallas_call(project_kernel, out_shape=(shape, shape), in_specs=[SMEM,...]
    ppermute x14, starting transfers between devices: 22.7 us -> 23.8 us  [passed(): return lax.ppermute(values, axis, pairs)]
    unnamed x19 -> x21, local copies, waits for them, and re-layouts: 2.92 us -> 2.93 us
  transfers between devices with their start and end apart: 23 -> 23, of which waited for: 13 -> 17; matrix products, arithmetic and copies ran while one was open for 4% -> 5% of each run, Pallas kernels for 13% -> 12%
where the time goes in v2:
time: 103 us
  waiting for transfers between devices  36.8 us (36%)
  starting transfers between devices  29.9 us (29%)
  Pallas kernels  24.5 us (24%)
  local copies, waits for them, and re-layouts  7.02 us (7%)
  matrix products  2.25 us (2%)
  other arithmetic  1.05 us (1%)
  between operations  1.05 us (1%)
    ppermute x14, waiting for transfers between devices, passed(): return lax.ppermute(values, axis, pairs)  24.6 us
    ppermute x14, starting transfers between devices, passed(): return lax.ppermute(values, axis, pairs)  23.8 us
    pallas_call x8, Pallas kernels, absorb(): pl.pallas_call(functools.partial(absorb_kernel, first), out_shape=shapes,...  16.4 us
    ppermute x9, waiting for transfers between devices, swapped(): return lax.ppermute(values, axis, [(i, i ^ 1) for i in range(size)])  12.2 us
    ppermute x9, starting transfers between devices, swapped(): return lax.ppermute(values, axis, [(i, i ^ 1) for i in range(size)])  6.1 us
    pallas_call x1, Pallas kernels, project(): pl.pallas_call(project_kernel, out_shape=(shape, shape), in_specs=[SMEM,...  4.09 us
    pallas_call x1, Pallas kernels, network(): pl.pallas_call(functools.partial(network_kernel, cols, frame_rows), out_s...  3.76 us
    unnamed x21, local copies, waits for them, and re-layouts  2.93 us
  transfers between devices with their start and end apart: 23, of which 17 were waited for; matrix products, arithmetic and copies ran while one was open for 5% of the time, Pallas kernels for 12%

profile of v2, /device:TPU:0, one launch (start us, length us, event | category | flops | bytes accessed | tf_op | source)
XLA Modules:
  0.0 102.6 jit_solution(3590361129001288236)
XLA Ops:
  4.1 4.1 %project.1 = (bf16[2,192,512]{2,1,0:T(8,128)(2,1)S(1)}, bf16[2,192,512]{2,1,0:T(8,128)(2,1)S(1)}) custom-call(s32[3]{0:T(128)S(1)} %pad_add_fusion.place, bf16[512,1024]{1,0:T(8,128)(2,1)S(1)} %bitcast.35, bf16[1,1024]{1,0:T(2,128)(2,1)S(1)} %reshape.76.gain, bf16[3,1024,256]{2,1,0:T(8,128)(2,1)S(1)} %copy-done.3), custom_call_target="tpu_custom_call" | custom-call | tf_op jit(solution)/shard_map/project/pallas_call | solution.py:73
  11.4 3.0 %collective-permute-start.4 = (bf16[128,1024]{1,0:T(8,128)(2,1)S(1)}, bf16[128,1024]{1,0:T(8,128)(2,1)S(1)}, u32[]{:S(2)}, u32[]{:S(2)}) collective-permute-start(bf16[128,1024]{1,0:T(8,128)(2,1)S(1)} %get-tuple-element.104.refs_1_), channel_id=1, source_target_pairs={{0,4},{2,6},{4,8},{6,10},{8,12},{10,14},{12,0},{14,2},{1,5},{3,7},... | collective-permute-start | bytes 786440 | tf_op jit(solution)/shard_map/ppermute | solution.py:264
  14.3 1.6 %collective-permute-start.1 = (bf16[128,1024]{1,0:T(8,128)(2,1)S(1)}, bf16[128,1024]{1,0:T(8,128)(2,1)S(1)}, u32[]{:S(2)}, u32[]{:S(2)}) collective-permute-start(bf16[128,1024]{1,0:T(8,128)(2,1)S(1)} %get-tuple-element.103.refs_1_), channel_id=1, source_target_pairs={{0,4},{2,6},{4,8},{6,10},{8,12},{10,14},{12,0},{14,2},{1,5},{3,7},... | collective-permute-start | bytes 786440 | tf_op jit(solution)/shard_map/ppermute | solution.py:264
  17.3 2.0 %absorb.12 = (f32[80,1024]{1,0:T(8,128)S(1)}, f32[8,1024]{1,0:T(8,128)S(1)}) custom-call(bf16[64,1024]{1,0:T(8,128)(2,1)S(1)} %get-tuple-element.106.refs_0_, bf16[128,1024]{1,0:T(8,128)(2,1)S(1)} %get-tuple-element.104.refs_1_), custom_call_target="tpu_custom_call" | custom-call | tf_op jit(solution)/shard_map/absorb/pallas_call | solution.py:121
  19.4 4.2 %collective-permute-done.4.refs_1_ = bf16[128,1024]{1,0:T(8,128)(2,1)S(1)} collective-permute-done((bf16[128,1024]{1,0:T(8,128)(2,1)S(1)}, bf16[128,1024]{1,0:T(8,128)(2,1)S(1)}, u32[]{:S(2)}, u32[]{:S(2)}) %collective-permute-start.4) | collective-permute-done | bytes 262176 | tf_op jit(solution)/shard_map/ppermute | solution.py:264
  23.5 2.0 %absorb.8 = (f32[80,1024]{1,0:T(8,128)S(1)}, f32[8,1024]{1,0:T(8,128)S(1)}) custom-call(bf16[64,1024]{1,0:T(8,128)(2,1)S(1)} %get-tuple-element.105.refs_0_, bf16[128,1024]{1,0:T(8,128)(2,1)S(1)} %get-tuple-element.103.refs_1_), custom_call_target="tpu_custom_call" | custom-call | tf_op jit(solution)/shard_map/absorb/pallas_call | solution.py:121
  25.5 3.6 %collective-permute-done.1.refs_1_ = bf16[128,1024]{1,0:T(8,128)(2,1)S(1)} collective-permute-done((bf16[128,1024]{1,0:T(8,128)(2,1)S(1)}, bf16[128,1024]{1,0:T(8,128)(2,1)S(1)}, u32[]{:S(2)}, u32[]{:S(2)}) %collective-permute-start.1) | collective-permute-done | bytes 262176 | tf_op jit(solution)/shard_map/ppermute | solution.py:264
  29.1 1.7 %collective-permute-start.6 = (f32[2,2,128]{2,1,0:T(2,128)S(1)}, f32[2,2,128]{2,1,0:T(2,128)S(1)}, u32[]{:S(2)}, u32[]{:S(2)}) collective-permute-start(f32[2,2,128]{2,1,0:T(2,128)S(1)} %bitcast.43), channel_id=1, source_target_pairs={{0,1},{1,0},{2,3},{3,2},{4,5},{5,4},{6,7},{7,6},{8,9},{9,8},{10,11... | collective-permute-start | bytes 6152 | tf_op jit(solution)/shard_map/ppermute | solution.py:258
  30.9 1.9 %collective-permute-done.6 = f32[2,2,128]{2,1,0:T(2,128)S(1)} collective-permute-done((f32[2,2,128]{2,1,0:T(2,128)S(1)}, f32[2,2,128]{2,1,0:T(2,128)S(1)}, u32[]{:S(2)}, u32[]{:S(2)}) %collective-permute-start.6) | collective-permute-done | bytes 2080 | tf_op jit(solution)/shard_map/ppermute | solution.py:258
  33.9 2.1 %absorb.13 = (f32[80,1024]{1,0:T(8,128)S(1)}, f32[8,1024]{1,0:T(8,128)S(1)}) custom-call(bf16[64,1024]{1,0:T(8,128)(2,1)S(1)} %get-tuple-element.106.refs_0_, bf16[128,1024]{1,0:T(8,128)(2,1)S(1)} %collective-permute-done.4.refs_1_, f32[80,1024]{1,0:T(8,128)S(1)} %get-tuple-element.75.refs_2_, ...), custom_call_target="tpu_custom_call", output_to_operand_aliasing={{0}: (2, {}), {1}: (3, {})} | custom-call | tf_op jit(solution)/shard_map/absorb/pallas_call | solution.py:121
  36.0 2.1 %absorb.9 = (f32[80,1024]{1,0:T(8,128)S(1)}, f32[8,1024]{1,0:T(8,128)S(1)}) custom-call(bf16[64,1024]{1,0:T(8,128)(2,1)S(1)} %get-tuple-element.105.refs_0_, bf16[128,1024]{1,0:T(8,128)(2,1)S(1)} %collective-permute-done.1.refs_1_, f32[80,1024]{1,0:T(8,128)S(1)} %get-tuple-element.58.refs_2_, ...), custom_call_target="tpu_custom_call", output_to_operand_aliasing={{0}: (2, {}), {1}: (3, {})} | custom-call | tf_op jit(solution)/shard_map/absorb/pallas_call | solution.py:121
  38.1 1.6 %collective-permute-start.8 = (bf16[128,1024]{1,0:T(8,128)(2,1)S(1)}, bf16[128,1024]{1,0:T(8,128)(2,1)S(1)}, u32[]{:S(2)}, u32[]{:S(2)}) collective-permute-start(bf16[128,1024]{1,0:T(8,128)(2,1)S(1)} %collective-permute-done.5.refs_1_), channel_id=1, source_target_pairs={{0,4},{2,6},{4,8},{6,10},{8,12},{10,14},{12,0},{14,2},{1,5},{3,7},... | collective-permute-start | bytes 786440 | tf_op jit(solution)/shard_map/ppermute | solution.py:264
  42.6 4.7 %collective-permute-start.9 = (f32[2,2,256]{2,1,0:T(2,128)S(1)}, f32[2,2,256]{2,1,0:T(2,128)S(1)}, u32[]{:S(2)}, u32[]{:S(2)}) collective-permute-start(f32[2,2,256]{2,1,0:T(2,128)S(1)} %get-tuple-element.113), channel_id=1, source_target_pairs={{0,4},{2,6},{4,8},{6,10},{8,12},{10,14},{1,5},{3,7},{5,9},{7,11},{... | collective-permute-start | bytes 12296 | tf_op jit(solution)/shard_map/ppermute | solution.py:264
  47.3 2.1 %absorb.14 = (f32[80,1024]{1,0:T(8,128)S(1)}, f32[8,1024]{1,0:T(8,128)S(1)}) custom-call(bf16[64,1024]{1,0:T(8,128)(2,1)S(1)} %get-tuple-element.106.refs_0_, bf16[128,1024]{1,0:T(8,128)(2,1)S(1)} %collective-permute-done.5.refs_1_, f32[80,1024]{1,0:T(8,128)S(1)} %get-tuple-element.81.refs_2_, ...), custom_call_target="tpu_custom_call", output_to_operand_aliasing={{0}: (2, {}), {1}: (3, {})} | custom-call | tf_op jit(solution)/shard_map/absorb/pallas_call | solution.py:121
  49.4 2.1 %absorb.10 = (f32[80,1024]{1,0:T(8,128)S(1)}, f32[8,1024]{1,0:T(8,128)S(1)}) custom-call(bf16[64,1024]{1,0:T(8,128)(2,1)S(1)} %get-tuple-element.105.refs_0_, bf16[128,1024]{1,0:T(8,128)(2,1)S(1)} %collective-permute-done.2.refs_1_, f32[80,1024]{1,0:T(8,128)S(1)} %get-tuple-element.63.refs_2_, ...), custom_call_target="tpu_custom_call", output_to_operand_aliasing={{0}: (2, {}), {1}: (3, {})} | custom-call | tf_op jit(solution)/shard_map/absorb/pallas_call | solution.py:121
  51.5 2.8 %collective-permute-done.3.refs_1_ = bf16[128,1024]{1,0:T(8,128)(2,1)S(1)} collective-permute-done((bf16[128,1024]{1,0:T(8,128)(2,1)S(1)}, bf16[128,1024]{1,0:T(8,128)(2,1)S(1)}, u32[]{:S(2)}, u32[]{:S(2)}) %collective-permute-start.3) | collective-permute-done | bytes 262176 | tf_op jit(solution)/shard_map/ppermute | solution.py:264
  54.3 2.1 %absorb.15 = (f32[80,1024]{1,0:T(8,128)S(1)}, f32[8,1024]{1,0:T(8,128)S(1)}) custom-call(bf16[64,1024]{1,0:T(8,128)(2,1)S(1)} %get-tuple-element.106.refs_0_, bf16[128,1024]{1,0:T(8,128)(2,1)S(1)} %collective-permute-done.8.refs_1_, f32[80,1024]{1,0:T(8,128)S(1)} %get-tuple-element.88.refs_2_, ...), custom_call_target="tpu_custom_call", output_to_operand_aliasing={{0}: (2, {}), {1}: (3, {})} | custom-call | tf_op jit(solution)/shard_map/absorb/pallas_call | solution.py:121
  56.4 2.1 %absorb.11 = (f32[80,1024]{1,0:T(8,128)S(1)}, f32[8,1024]{1,0:T(8,128)S(1)}) custom-call(bf16[64,1024]{1,0:T(8,128)(2,1)S(1)} %get-tuple-element.105.refs_0_, bf16[128,1024]{1,0:T(8,128)(2,1)S(1)} %collective-permute-done.3.refs_1_, f32[80,1024]{1,0:T(8,128)S(1)} %get-tuple-element.68.refs_2_, ...), custom_call_target="tpu_custom_call", output_to_operand_aliasing={{0}: (2, {}), {1}: (3, {})} | custom-call | tf_op jit(solution)/shard_map/absorb/pallas_call | solution.py:121
  60.2 1.8 %collective-permute-start.12 = (f32[64,512]{1,0:T(8,128)S(1)}, f32[64,512]{1,0:T(8,128)S(1)}, u32[]{:S(2)}, u32[]{:S(2)}) collective-permute-start(f32[64,512]{1,0:T(8,128)S(1)} %slice_add_fusion), channel_id=1, source_target_pairs={{0,1},{1,0},{2,3},{3,2},{4,5},{5,4},{6,7},{7,6},{8,9},{9,8},{10,11... | collective-permute-start | bytes 393224 | tf_op jit(solution)/shard_map/ppermute | solution.py:258
  62.0 3.8 %collective-permute-done.12 = f32[64,512]{1,0:T(8,128)S(1)} collective-permute-done((f32[64,512]{1,0:T(8,128)S(1)}, f32[64,512]{1,0:T(8,128)S(1)}, u32[]{:S(2)}, u32[]{:S(2)}) %collective-permute-start.12) | collective-permute-done | bytes 131104 | tf_op jit(solution)/shard_map/ppermute | solution.py:258
  70.1 1.7 %collective-permute-done.14 = bf16[64,1024]{1,0:T(8,128)(2,1)S(1)} collective-permute-done((bf16[64,1024]{1,0:T(8,128)(2,1)S(1)}, bf16[64,1024]{1,0:T(8,128)(2,1)S(1)}, u32[]{:S(2)}, u32[]{:S(2)}) %collective-permute-start.14) | collective-permute-done | bytes 131104 | tf_op jit(solution)/shard_map/ppermute | solution.py:264
  71.8 4.1 %collective-permute-done.15 = bf16[64,1024]{1,0:T(8,128)(2,1)S(1)} collective-permute-done((bf16[64,1024]{1,0:T(8,128)(2,1)S(1)}, bf16[64,1024]{1,0:T(8,128)(2,1)S(1)}, u32[]{:S(2)}, u32[]{:S(2)}) %collective-permute-start.15) | collective-permute-done | bytes 131104 | tf_op jit(solution)/shard_map/ppermute | solution.py:264
  76.0 3.8 %network.1 = (f32[2,1024]{1,0:T(2,128)S(1)}, f32[32,576]{1,0:T(8,128)S(1)}, f32[64,128]{1,0:T(8,128)S(1)}) custom-call(s32[3]{0:T(128)S(1)} %pad_add_fusion.place, bf16[64,3072]{1,0:T(8,128)(2,1)S(1)} %pad_maximum_fusion.hidden, f32[2,2048]{1,0:T(2,128)S(1)} %bitcast.37, bf16[2,3,64,192]{3,2,1,0:T(8,128)(2,1)S(1)} %bitcast.36, ...), custom_call_target="tpu_custom_call" | custom-call | tf_op jit(solution)/shard_map/network/pallas_call | solution.py:241
  79.8 1.8 %collective-permute-start.16 = (f32[32,896]{1,0:T(8,128)S(1)}, f32[32,896]{1,0:T(8,128)S(1)}, u32[]{:S(2)}, u32[]{:S(2)}) collective-permute-start(f32[32,896]{1,0:T(8,128)S(1)} %fusion.1), channel_id=1, source_target_pairs={{0,16},{16,0},{1,17},{17,1},{2,18},{18,2},{3,19},{19,3},{4,20},{20... | collective-permute-start | bytes 344072 | tf_op jit(solution)/shard_map/ppermute | solution.py:264
  81.6 3.1 %collective-permute-done.16 = f32[32,896]{1,0:T(8,128)S(1)} collective-permute-done((f32[32,896]{1,0:T(8,128)S(1)}, f32[32,896]{1,0:T(8,128)S(1)}, u32[]{:S(2)}, u32[]{:S(2)}) %collective-permute-start.16) | collective-permute-done | bytes 114720 | tf_op jit(solution)/shard_map/ppermute | solution.py:264
  84.7 1.6 %collective-permute-start.17 = (f32[32,896]{1,0:T(8,128)S(1)}, f32[32,896]{1,0:T(8,128)S(1)}, u32[]{:S(2)}, u32[]{:S(2)}) collective-permute-start(f32[32,896]{1,0:T(8,128)S(1)} %fusion.17), channel_id=1, source_target_pairs={{0,4},{2,6},{4,8},{6,10},{8,12},{10,14},{12,0},{14,2},{1,5},{3,7},... | collective-permute-start | bytes 344072 | tf_op jit(solution)/shard_map/ppermute | solution.py:264
  87.5 2.8 %collective-permute-start.19 = (f32[32,896]{1,0:T(8,128)S(1)}, f32[32,896]{1,0:T(8,128)S(1)}, u32[]{:S(2)}, u32[]{:S(2)}) collective-permute-start(f32[32,896]{1,0:T(8,128)S(1)} %fusion.17), channel_id=1, source_target_pairs={{0,12},{2,14},{4,0},{6,2},{8,4},{10,6},{12,8},{14,10},{1,13},{3,15... | collective-permute-start | bytes 344072 | tf_op jit(solution)/shard_map/ppermute | solution.py:264
  90.3 2.0 %collective-permute-done.17 = f32[32,896]{1,0:T(8,128)S(1)} collective-permute-done((f32[32,896]{1,0:T(8,128)S(1)}, f32[32,896]{1,0:T(8,128)S(1)}, u32[]{:S(2)}, u32[]{:S(2)}) %collective-permute-start.17) | collective-permute-done | bytes 114720 | tf_op jit(solution)/shard_map/ppermute | solution.py:264
  92.3 3.0 %collective-permute-done.18 = f32[32,896]{1,0:T(8,128)S(1)} collective-permute-done((f32[32,896]{1,0:T(8,128)S(1)}, f32[32,896]{1,0:T(8,128)S(1)}, u32[]{:S(2)}, u32[]{:S(2)}) %collective-permute-start.18) | collective-permute-done | bytes 114720 | tf_op jit(solution)/shard_map/ppermute | solution.py:264
  95.5 1.8 %collective-permute-start.20 = (f32[32,576]{1,0:T(8,128)S(1)}, f32[32,576]{1,0:T(8,128)S(1)}, u32[]{:S(2)}, u32[]{:S(2)}) collective-permute-start(f32[32,576]{1,0:T(8,128)S(1)} %get-tuple-element.108), channel_id=1, source_target_pairs={{0,1},{1,0},{2,3},{3,2},{4,5},{5,4},{6,7},{7,6},{8,9},{9,8},{10,11... | collective-permute-start | bytes 221192 | tf_op jit(solution)/shard_map/ppermute | solution.py:258
  97.2 1.6 %fusion.2 = f32[256,1024]{1,0:T(8,128)} fusion(bf16[1024,64]{0,1:T(8,128)(2,1)S(1)} %copy-done.6, f32[64,128]{1,0:T(8,128)S(1)} %collective-permute-done.21, f32[32,128]{1,0:T(8,128)S(1)} %get-tuple-element.110, f32[32,128]{1,0:T(8,128)S(1)} %get-tuple-element.109, pred[]{:T(512)S(6)} %eq.4), kind=kOutput, calls=%fused_computation.20 | convolution fusion | flops 201408512 | bytes 1245185 | tf_op jit(solution)/shard_map/dot_general | solution.py:374
  98.8 1.5 %collective-permute-done.20 = f32[32,576]{1,0:T(8,128)S(1)} collective-permute-done((f32[32,576]{1,0:T(8,128)S(1)}, f32[32,576]{1,0:T(8,128)S(1)}, u32[]{:S(2)}, u32[]{:S(2)}) %collective-permute-start.20) | collective-permute-done | bytes 73760 | tf_op jit(solution)/shard_map/ppermute | solution.py:258
  (80 shorter events, 21.6 us)
Async XLA Ops:
  0.6 8.1 %copy-start = (bf16[256,1024]{1,0:T(8,128)(2,1)S(1)}, bf16[256,1024]{1,0:T(8,128)(2,1)}, u32[]{:S(2)}) copy-start(bf16[256,1024]{1,0:T(8,128)(2,1)} %param.11) | copy-start | bytes 1572868
  1.5 1.2 %copy-start.1 = (bf16[1,512,1024]{2,1,0:T(8,128)(2,1)S(1)}, bf16[1,512,1024]{2,1,0:T(8,128)(2,1)}, u32[]{:S(2)}) copy-start(bf16[1,512,1024]{2,1,0:T(8,128)(2,1)} %param.8) | copy-start | bytes 3145732
  2.7 1.4 %copy-start.3 = (bf16[3,1024,256]{2,1,0:T(8,128)(2,1)S(1)}, bf16[3,1024,256]{2,1,0:T(8,128)(2,1)}, u32[]{:S(2)}) copy-start(bf16[3,1024,256]{2,1,0:T(8,128)(2,1)} %weight.1) | copy-start | bytes 4718596
  4.1 4.7 %copy-start.6 = (bf16[1024,64]{0,1:T(8,128)(2,1)S(1)}, bf16[1024,64]{0,1:T(8,128)(2,1)}, u32[]{:S(2)}) copy-start(bf16[1024,64]{0,1:T(8,128)(2,1)} %param.12) | copy-start | bytes 393220
  4.1 4.9 %copy-start.7 = (bf16[2,64,576]{2,1,0:T(8,128)(2,1)S(1)}, bf16[2,64,576]{2,1,0:T(8,128)(2,1)}, u32[]{:S(2)}) copy-start(bf16[2,64,576]{2,1,0:T(8,128)(2,1)} %param.13) | copy-start | bytes 442372
  4.1 5.2 %copy-start.2 = (bf16[1,512,1024]{2,1,0:T(8,128)(2,1)S(1)}, bf16[1,512,1024]{2,1,0:T(8,128)(2,1)}, u32[]{:S(2)}) copy-start(bf16[1,512,1024]{2,1,0:T(8,128)(2,1)} %param.8) | copy-start | bytes 3145732
  8.2 2.0 %collective-permute-start = (bf16[2,192,512]{2,1,0:T(8,128)(2,1)S(1)}, bf16[2,192,512]{2,1,0:T(8,128)(2,1)}, u32[]{:S(2)}, u32[]{:S(2)}) collective-permute-start(bf16[2,192,512]{2,1,0:T(8,128)(2,1)S(1)} %get-tuple-element.54), channel_id=1, source_target_pairs={{0,2},{2,0},{4,6},{6,4},{8,10},{10,8},{12,14},{14,12},{1,3},{3,1},... | collective-permute-start | bytes 1179656 | tf_op jit(solution)/shard_map/ppermute | solution.py:258
  11.3 3.0 %copy-start.5 = (bf16[2,192,1024]{2,1,0:T(8,128)(2,1)}, bf16[2,192,1024]{2,1,0:T(8,128)(2,1)S(1)}, u32[]{:S(2)}) copy-start(bf16[2,192,1024]{2,1,0:T(8,128)(2,1)S(1)} %constant_dynamic-update-slice_fusion) | copy-start | bytes 2359300
  11.4 12.2 %collective-permute-start.4 = (bf16[128,1024]{1,0:T(8,128)(2,1)S(1)}, bf16[128,1024]{1,0:T(8,128)(2,1)S(1)}, u32[]{:S(2)}, u32[]{:S(2)}) collective-permute-start(bf16[128,1024]{1,0:T(8,128)(2,1)S(1)} %get-tuple-element.104.refs_1_), channel_id=1, source_target_pairs={{0,4},{2,6},{4,8},{6,10},{8,12},{10,14},{12,0},{14,2},{1,5},{3,7},... | collective-permute-start | bytes 786440 | tf_op jit(solution)/shard_map/ppermute | solution.py:264
  14.3 14.8 %collective-permute-start.1 = (bf16[128,1024]{1,0:T(8,128)(2,1)S(1)}, bf16[128,1024]{1,0:T(8,128)(2,1)S(1)}, u32[]{:S(2)}, u32[]{:S(2)}) collective-permute-start(bf16[128,1024]{1,0:T(8,128)(2,1)S(1)} %get-tuple-element.103.refs_1_), channel_id=1, source_target_pairs={{0,4},{2,6},{4,8},{6,10},{8,12},{10,14},{12,0},{14,2},{1,5},{3,7},... | collective-permute-start | bytes 786440 | tf_op jit(solution)/shard_map/ppermute | solution.py:264
  15.9 13.2 %copy-start.8 = (f32[1,2,2,128]{3,2,1,0:T(2,128)S(1)}, f32[1,2,2,128]{3,2,1,0:T(2,128)}, u32[]{:S(2)}) copy-start(f32[1,2,2,128]{3,2,1,0:T(2,128)} %param.15) | copy-start | bytes 6148
  23.5 14.5 %collective-permute-start.5 = (bf16[128,1024]{1,0:T(8,128)(2,1)S(1)}, bf16[128,1024]{1,0:T(8,128)(2,1)S(1)}, u32[]{:S(2)}, u32[]{:S(2)}) collective-permute-start(bf16[128,1024]{1,0:T(8,128)(2,1)S(1)} %collective-permute-done.4.refs_1_), channel_id=1, source_target_pairs={{0,4},{2,6},{4,8},{6,10},{8,12},{10,14},{12,0},{14,2},{1,5},{3,7},... | collective-permute-start | bytes 786440 | tf_op jit(solution)/shard_map/ppermute | solution.py:264
  29.1 10.7 %collective-permute-start.2 = (bf16[128,1024]{1,0:T(8,128)(2,1)S(1)}, bf16[128,1024]{1,0:T(8,128)(2,1)S(1)}, u32[]{:S(2)}, u32[]{:S(2)}) collective-permute-start(bf16[128,1024]{1,0:T(8,128)(2,1)S(1)} %collective-permute-done.1.refs_1_), channel_id=1, source_target_pairs={{0,4},{2,6},{4,8},{6,10},{8,12},{10,14},{12,0},{14,2},{1,5},{3,7},... | collective-permute-start | bytes 786440 | tf_op jit(solution)/shard_map/ppermute | solution.py:264
  29.1 3.6 %collective-permute-start.6 = (f32[2,2,128]{2,1,0:T(2,128)S(1)}, f32[2,2,128]{2,1,0:T(2,128)S(1)}, u32[]{:S(2)}, u32[]{:S(2)}) collective-permute-start(f32[2,2,128]{2,1,0:T(2,128)S(1)} %bitcast.43), channel_id=1, source_target_pairs={{0,1},{1,0},{2,3},{3,2},{4,5},{5,4},{6,7},{7,6},{8,9},{9,8},{10,11... | collective-permute-start | bytes 6152 | tf_op jit(solution)/shard_map/ppermute | solution.py:258
  32.7 1.2 %collective-permute-start.7 = (f32[2,2,256]{2,1,0:T(2,128)S(1)}, f32[2,2,256]{2,1,0:T(2,128)S(1)}, u32[]{:S(2)}, u32[]{:S(2)}) collective-permute-start(f32[2,2,256]{2,1,0:T(2,128)S(1)} %maximum_select_fusion.7), channel_id=1, source_target_pairs={{0,2},{2,0},{4,6},{6,4},{8,10},{10,8},{12,14},{14,12},{1,3},{3,1},... | collective-permute-start | bytes 12296 | tf_op jit(solution)/shard_map/ppermute | solution.py:258
  38.1 13.4 %collective-permute-start.8 = (bf16[128,1024]{1,0:T(8,128)(2,1)S(1)}, bf16[128,1024]{1,0:T(8,128)(2,1)S(1)}, u32[]{:S(2)}, u32[]{:S(2)}) collective-permute-start(bf16[128,1024]{1,0:T(8,128)(2,1)S(1)} %collective-permute-done.5.refs_1_), channel_id=1, source_target_pairs={{0,4},{2,6},{4,8},{6,10},{8,12},{10,14},{12,0},{14,2},{1,5},{3,7},... | collective-permute-start | bytes 786440 | tf_op jit(solution)/shard_map/ppermute | solution.py:264
  39.8 14.5 %collective-permute-start.3 = (bf16[128,1024]{1,0:T(8,128)(2,1)S(1)}, bf16[128,1024]{1,0:T(8,128)(2,1)S(1)}, u32[]{:S(2)}, u32[]{:S(2)}) collective-permute-start(bf16[128,1024]{1,0:T(8,128)(2,1)S(1)} %collective-permute-done.2.refs_1_), channel_id=1, source_target_pairs={{0,4},{2,6},{4,8},{6,10},{8,12},{10,14},{12,0},{14,2},{1,5},{3,7},... | collective-permute-start | bytes 786440 | tf_op jit(solution)/shard_map/ppermute | solution.py:264
  41.3 10.2 %collective-permute-start.10 = (f32[2,2,256]{2,1,0:T(2,128)S(1)}, f32[2,2,256]{2,1,0:T(2,128)S(1)}, u32[]{:S(2)}, u32[]{:S(2)}) collective-permute-start(f32[2,2,256]{2,1,0:T(2,128)S(1)} %get-tuple-element.114), channel_id=1, source_target_pairs={{4,0},{6,2},{8,4},{10,6},{12,8},{14,10},{5,1},{7,3},{9,5},{11,7},{... | collective-permute-start | bytes 12296 | tf_op jit(solution)/shard_map/ppermute | solution.py:264
  42.6 8.9 %collective-permute-start.9 = (f32[2,2,256]{2,1,0:T(2,128)S(1)}, f32[2,2,256]{2,1,0:T(2,128)S(1)}, u32[]{:S(2)}, u32[]{:S(2)}) collective-permute-start(f32[2,2,256]{2,1,0:T(2,128)S(1)} %get-tuple-element.113), channel_id=1, source_target_pairs={{0,4},{2,6},{4,8},{6,10},{8,12},{10,14},{1,5},{3,7},{5,9},{7,11},{... | collective-permute-start | bytes 12296 | tf_op jit(solution)/shard_map/ppermute | solution.py:264
  58.4 17.6 %copy-start.4 = (bf16[2,64]{1,0:T(2,128)(2,1)S(1)}, bf16[2,64]{1,0:T(2,128)(2,1)}, u32[]{:S(2)}) copy-start(bf16[2,64]{1,0:T(2,128)(2,1)} %head.1) | copy-start | bytes 772
  58.8 1.4 %collective-permute-start.11 = (f32[64,512]{1,0:T(8,128)S(1)}, f32[64,512]{1,0:T(8,128)S(1)}, u32[]{:S(2)}, u32[]{:S(2)}) collective-permute-start(f32[64,512]{1,0:T(8,128)S(1)} %slice.46), channel_id=1, source_target_pairs={{0,2},{2,0},{4,6},{6,4},{8,10},{10,8},{12,14},{14,12},{1,3},{3,1},... | collective-permute-start | bytes 393224 | tf_op jit(solution)/shard_map/ppermute | solution.py:258
  60.2 5.6 %collective-permute-start.12 = (f32[64,512]{1,0:T(8,128)S(1)}, f32[64,512]{1,0:T(8,128)S(1)}, u32[]{:S(2)}, u32[]{:S(2)}) collective-permute-start(f32[64,512]{1,0:T(8,128)S(1)} %slice_add_fusion), channel_id=1, source_target_pairs={{0,1},{1,0},{2,3},{3,2},{4,5},{5,4},{6,7},{7,6},{8,9},{9,8},{10,11... | collective-permute-start | bytes 393224 | tf_op jit(solution)/shard_map/ppermute | solution.py:258
  65.8 1.3 %collective-permute-start.13 = (bf16[64,512]{1,0:T(8,128)(2,1)S(1)}, bf16[64,512]{1,0:T(8,128)(2,1)S(1)}, u32[]{:S(2)}, u32[]{:S(2)}) collective-permute-start(bf16[64,512]{1,0:T(8,128)(2,1)S(1)} %add_convert_fusion), channel_id=1, source_target_pairs={{0,2},{2,0},{4,6},{6,4},{8,10},{10,8},{12,14},{14,12},{1,3},{3,1},... | collective-permute-start | bytes 196616 | tf_op jit(solution)/shard_map/ppermute | solution.py:258
  67.2 4.6 %collective-permute-start.14 = (bf16[64,1024]{1,0:T(8,128)(2,1)S(1)}, bf16[64,1024]{1,0:T(8,128)(2,1)S(1)}, u32[]{:S(2)}, u32[]{:S(2)}) collective-permute-start(bf16[64,1024]{1,0:T(8,128)(2,1)S(1)} %maximum_select_fusion.3), channel_id=1, source_target_pairs={{0,4},{2,6},{4,8},{6,10},{8,12},{10,14},{1,5},{3,7},{5,9},{7,11},{... | collective-permute-start | bytes 393224 | tf_op jit(solution)/shard_map/ppermute | solution.py:264
  68.6 7.3 %collective-permute-start.15 = (bf16[64,1024]{1,0:T(8,128)(2,1)S(1)}, bf16[64,1024]{1,0:T(8,128)(2,1)S(1)}, u32[]{:S(2)}, u32[]{:S(2)}) collective-permute-start(bf16[64,1024]{1,0:T(8,128)(2,1)S(1)} %maximum_select_fusion.3), channel_id=1, source_target_pairs={{4,0},{6,2},{8,4},{10,6},{12,8},{14,10},{5,1},{7,3},{9,5},{11,7},{... | collective-permute-start | bytes 393224 | tf_op jit(solution)/shard_map/ppermute | solution.py:264
  79.8 4.9 %collective-permute-start.16 = (f32[32,896]{1,0:T(8,128)S(1)}, f32[32,896]{1,0:T(8,128)S(1)}, u32[]{:S(2)}, u32[]{:S(2)}) collective-permute-start(f32[32,896]{1,0:T(8,128)S(1)} %fusion.1), channel_id=1, source_target_pairs={{0,16},{16,0},{1,17},{17,1},{2,18},{18,2},{3,19},{19,3},{4,20},{20... | collective-permute-start | bytes 344072 | tf_op jit(solution)/shard_map/ppermute | solution.py:264
  84.7 7.7 %collective-permute-start.17 = (f32[32,896]{1,0:T(8,128)S(1)}, f32[32,896]{1,0:T(8,128)S(1)}, u32[]{:S(2)}, u32[]{:S(2)}) collective-permute-start(f32[32,896]{1,0:T(8,128)S(1)} %fusion.17), channel_id=1, source_target_pairs={{0,4},{2,6},{4,8},{6,10},{8,12},{10,14},{12,0},{14,2},{1,5},{3,7},... | collective-permute-start | bytes 344072 | tf_op jit(solution)/shard_map/ppermute | solution.py:264
  86.3 9.1 %collective-permute-start.18 = (f32[32,896]{1,0:T(8,128)S(1)}, f32[32,896]{1,0:T(8,128)S(1)}, u32[]{:S(2)}, u32[]{:S(2)}) collective-permute-start(f32[32,896]{1,0:T(8,128)S(1)} %fusion.17), channel_id=1, source_target_pairs={{0,8},{2,10},{4,12},{6,14},{8,0},{10,2},{12,4},{14,6},{1,9},{3,11}... | collective-permute-start | bytes 344072 | tf_op jit(solution)/shard_map/ppermute | solution.py:264
  87.5 7.8 %collective-permute-start.19 = (f32[32,896]{1,0:T(8,128)S(1)}, f32[32,896]{1,0:T(8,128)S(1)}, u32[]{:S(2)}, u32[]{:S(2)}) collective-permute-start(f32[32,896]{1,0:T(8,128)S(1)} %fusion.17), channel_id=1, source_target_pairs={{0,12},{2,14},{4,0},{6,2},{8,4},{10,6},{12,8},{14,10},{1,13},{3,15... | collective-permute-start | bytes 344072 | tf_op jit(solution)/shard_map/ppermute | solution.py:264
  95.4 1.9 %collective-permute-start.21 = (f32[64,128]{1,0:T(8,128)S(1)}, f32[64,128]{1,0:T(8,128)S(1)}, u32[]{:S(2)}, u32[]{:S(2)}) collective-permute-start(f32[64,128]{1,0:T(8,128)S(1)} %pad_maximum_fusion.1), channel_id=1, source_target_pairs={{0,2},{2,0},{4,6},{6,4},{8,10},{10,8},{12,14},{14,12},{1,3},{3,1},... | collective-permute-start | bytes 98312 | tf_op jit(solution)/shard_map/ppermute | solution.py:258
  95.5 4.9 %collective-permute-start.20 = (f32[32,576]{1,0:T(8,128)S(1)}, f32[32,576]{1,0:T(8,128)S(1)}, u32[]{:S(2)}, u32[]{:S(2)}) collective-permute-start(f32[32,576]{1,0:T(8,128)S(1)} %get-tuple-element.108), channel_id=1, source_target_pairs={{0,1},{1,0},{2,3},{3,2},{4,5},{5,4},{6,7},{7,6},{8,9},{9,8},{10,11... | collective-permute-start | bytes 221192 | tf_op jit(solution)/shard_map/ppermute | solution.py:258
  100.4 1.5 %collective-permute-start.22 = (f32[64,576]{1,0:T(8,128)S(1)}, f32[64,576]{1,0:T(8,128)S(1)}, u32[]{:S(2)}, u32[]{:S(2)}) collective-permute-start(f32[64,576]{1,0:T(8,128)S(1)} %maximum_select_fusion.2), channel_id=1, source_target_pairs={{0,2},{2,0},{4,6},{6,4},{8,10},{10,8},{12,14},{14,12},{1,3},{3,1},... | collective-permute-start | bytes 442376 | tf_op jit(solution)/shard_map/ppermute | solution.py:258

commit v3 on v1

--- a/solution.py
+++ b/solution.py
@@ -30,35 +30,57 @@
     return high, mid, low
 
 
-def project_kernel(place, tokens, gain, weight, mine, theirs):
-    core = place[0]
+def normalize_kernel(tokens, gain, normed):
     values = tokens[...].astype(F32)
     center = values - jnp.mean(values, axis=-1, keepdims=True)
     spread = jnp.mean(center * center, axis=-1, keepdims=True)
-    normed = (center * lax.rsqrt(spread + EPSILON) * gain[...].astype(F32)).astype(BF16)
-    kept = mine.shape[0] * HEAD
-    for which, out in ((core, mine), (1 - core, theirs)):
+    wide_gain = gain[...].astype(F32)[None, :]
+    normed[...] = (center * lax.rsqrt(spread + EPSILON) * wide_gain).astype(BF16)
+
+
+def normalize(tokens, gain):
+    return pl.pallas_call(
+        normalize_kernel,
+        out_shape=jax.ShapeDtypeStruct(tokens.shape, BF16),
+        in_specs=[VMEM, VMEM],
+        out_specs=VMEM,
+        compiler_params=PARAMS,
+        name="normalize",
+    )(tokens, gain)
+
+
+def project_kernel(place, normed, weight, queries, keyed, theirs):
+    core = place[0]
+    kept = keyed.shape[0] * HEAD
+    rows = normed[...]
+    for which in range(2):
+        start = core if which == 0 else 1 - core
         for member in range(3):
-            part = weight[member, :, pl.ds(pl.multiple_of(which * kept, 128), kept)]
-            rows = dot(normed, part).astype(BF16)
+            part = weight[member, :, pl.ds(pl.multiple_of(start * kept, 128), kept)]
+            product = dot(rows, part).astype(BF16)
             if member == 0:
-                rows = rows * jnp.asarray(1.0 / HEAD**0.5, BF16)
-            turned = rows.T
-            for head in range(mine.shape[0]):
-                out[head, member * HEAD : (member + 1) * HEAD, :] = turned[head * HEAD : (head + 1) * HEAD, :]
-
-
-def project(place, tokens, gain, weight):
-    count, length = weight.shape[2] // HEAD // 2, tokens.shape[0]
-    shape = jax.ShapeDtypeStruct((count, 3 * HEAD, length), BF16)
+                product = product * jnp.asarray(1.0 / HEAD**0.5, BF16)
+            turned = product.T
+            for head in range(keyed.shape[0]):
+                piece = turned[head * HEAD : (head + 1) * HEAD, :]
+                if which == 1:
+                    theirs[head, member * HEAD : (member + 1) * HEAD, :] = piece
+                elif member == 0:
+                    queries[head] = piece
+                else:
+                    keyed[head, (member - 1) * HEAD : member * HEAD, :] = piece
+
+
+def project(place, normed, weight):
+    count, length = weight.shape[2] // HEAD // 2, normed.shape[0]
     return pl.pallas_call(
         project_kernel,
-        out_shape=(shape, shape),
-        in_specs=[SMEM, VMEM, VMEM, VMEM],
-        out_specs=(VMEM, VMEM),
+        out_shape=tuple(jax.ShapeDtypeStruct((count, many * HEAD, length), BF16) for many in (1, 2, 3)),
+        in_specs=[SMEM, VMEM, VMEM],
+        out_specs=(VMEM,) * 3,
         compiler_params=PARAMS,
         name="project",
-    )(place, tokens, gain, weight)
+    )(place, normed, weight)
 
 
 def absorb_kernel(first, *refs):
@@ -145,7 +167,7 @@
 
 
 def network_kernel(
-    cols, frame_rows, place, hidden, cotangent, forward, backward, head, context, holo, sums, gradient, pre_one, pre_two
+    cols, frame_rows, place, hidden, forward, backward, head, context, holo, sums, gradient, pre_one, pre_two
 ):
     core, half, row_at = place[0], place[1], place[2]
     own = context.shape[1]
@@ -160,7 +182,8 @@
         frame_lane = lane + (first_row + start_row) * cols
         return jnp.logical_and(frame_lane >= 0, frame_lane < frame_rows * cols)
 
-    columns_zero = three_columns(hidden[...], cols)
+    channels, outputs = forward.shape[2], head.shape[0]
+    columns_zero = three_columns(hidden[:channels, :], cols)
     first = three_rows(forward[0], columns_zero, cols)
     rows_one = row_count - 2
     one = jnp.where(inside(1, rows_one), first * jax.nn.sigmoid(first), 0.0)
@@ -170,8 +193,10 @@
     sigmoid_two = jax.nn.sigmoid(second)
     two = (second * sigmoid_two).astype(BF16)
     holo[...] = dot(head[...], two[:, rim - 2 * cols : rim - 2 * cols + own])
+    pieces = hidden[channels:, 2 * cols : cells - 2 * cols].astype(F32)
+    cotangent = pieces[:outputs] + pieces[outputs : 2 * outputs] + pieces[2 * outputs : 3 * outputs]
     grad_two = lax.dot_general(
-        head[...].astype(F32), cotangent[...], TN, precision=lax.Precision.HIGHEST, preferred_element_type=F32
+        head[...].astype(F32), cotangent, TN, precision=lax.Precision.HIGHEST, preferred_element_type=F32
     ).astype(BF16)
     slope = grad_two.astype(F32) * sigmoid_two * (1.0 + second * (1.0 - sigmoid_two))
     pre_grad_two = jnp.where(inside(2, rows_two), slope, 0.0)
@@ -186,7 +211,7 @@
     pre_two[...] = pre_grad_two[:, rim - 2 * cols : rim - 2 * cols + own].astype(BF16)
 
     share = sums.shape[0]
-    taps = 9 * hidden.shape[0]
+    taps = 9 * channels
     for layer, (pre, columns, offset) in enumerate(((pre_one, columns_zero, rim), (pre_two, columns_one, rim - cols))):
 
         @pl.when(core == layer)
@@ -209,9 +234,9 @@
     gradient[...] = total
 
 
-def network(place, hidden, cotangent, forward, backward, head, context, cols, frame_rows, col_count):
+def network(place, hidden, forward, backward, head, context, cols, frame_rows, col_count):
     own = context.shape[1]
-    channels = hidden.shape[0]
+    channels = forward.shape[2]
     return pl.pallas_call(
         functools.partial(network_kernel, cols, frame_rows),
         out_shape=(
@@ -219,12 +244,12 @@
             jax.ShapeDtypeStruct((channels // col_count, 9 * channels), F32),
             jax.ShapeDtypeStruct((channels, context.shape[0]), F32),
         ),
-        in_specs=[SMEM] + [VMEM] * 6,
+        in_specs=[SMEM] + [VMEM] * 5,
         out_specs=(VMEM,) * 3,
         scratch_shapes=[pltpu.VMEM((channels, own), BF16)] * 2,
         compiler_params=PARAMS,
         name="network",
-    )(place, hidden, cotangent, forward, backward, head, context)
+    )(place, hidden, forward, backward, head, context)
 
 
 def swapped(values, axis):
@@ -260,42 +285,62 @@
     cols = cols_dev * col_count
     length = frame_rows.shape[0]
 
-    mine, theirs = project(place, frame_rows, ln_gain.reshape(1, -1), qkv_weight)
-    joined = jnp.concatenate([mine, swapped(theirs, "tok")], axis=2)
-    count = joined.shape[0]
-    queries = [joined[head, :HEAD] for head in range(count)]
-    blocks = [joined[head, HEAD:] for head in range(count)]
+    own_queries, own_keyed, theirs = project(place, normalize(frame_rows, ln_gain), qkv_weight)
+    received = swapped(theirs, "tok")
+    count = received.shape[0]
+    kept = count * HEAD
+    blocks = [jnp.concatenate([own_keyed[head], received[head, HEAD:]], axis=1) for head in range(count)]
+    queries = [jnp.concatenate([own_queries[head], received[head, :HEAD]], axis=1) for head in range(count)]
     states = [None] * count
+
+    def prepare(conv_weight, out_weight, readout_weight, frame_rows, other_cot):
+        taps = conv_weight.reshape(layers, channels, 3, 3, channels)
+        forward = jnp.transpose(taps.reshape(layers, channels, 3, 3 * channels), (0, 2, 1, 3))
+        backward = jnp.transpose(taps[:, :, ::-1, ::-1, :], (0, 2, 4, 3, 1)).reshape(
+            layers, 3, channels, 3 * channels
+        )
+        own_out = lax.dynamic_slice_in_dim(out_weight, core * kept, kept, 0)
+        folded = lax.dot_general(readout_weight, own_out, (((0,), (1,)), ((), ())), preferred_element_type=F32)
+        direct = lax.dot_general(readout_weight, frame_rows, (((0,), (1,)), ((), ())), preferred_element_type=F32)
+        wide_cot = in_order(half, cotangent, other_cot, 2)
+        exact_cot = jnp.concatenate(split3(wide_cot.reshape(wide_cot.shape[0], -1)), axis=0)
+        exact_cot = jnp.pad(exact_cot, ((0, -exact_cot.shape[0] % 16), (0, 0)))
+        return (forward, backward, folded, direct, exact_cot)
+
     for turn in range(chips):
-        arriving = [passed(block, "tok", 2, True) for block in blocks] if turn < chips - 1 else None
-        states = [absorb(queries[head], blocks[head], states[head]) for head in range(count)]
+        arriving = [passed(block, "tok", 2, True) for block in blocks] if turn < chips - 1 else blocks
+        for head in range(count):
+            states[head] = absorb(queries[head], blocks[head], states[head])
+            if turn == 0 and head == 0:
+                states[head], given = lax.optimization_barrier(
+                    (states[head], (conv_weight, out_weight, readout_weight, frame_rows, swapped(cotangent, "col")))
+                )
+                prepared = prepare(*given)
+            if turn == min(1, chips - 1) and head == count - 1:
+                states[head], prepared = lax.optimization_barrier((states[head], prepared))
+            arriving[head], states[head] = lax.optimization_barrier((arriving[head], states[head]))
+            if head + 1 < count:
+                gate = arriving[head] if turn < chips - 1 else states[head]
+                blocks[head + 1], gate = lax.optimization_barrier((blocks[head + 1], gate))
+                if turn < chips - 1:
+                    arriving[head] = gate
+                else:
+                    states[head] = gate
         blocks = arriving
-
-    kept = count * HEAD
-    own_out = lax.dynamic_slice_in_dim(out_weight, core * kept, kept, 0)
-    folded = lax.dot_general(readout_weight, own_out, (((0,), (1,)), ((), ())), preferred_element_type=F32)
-    direct = lax.dot_general(readout_weight, frame_rows, (((0,), (1,)), ((), ())), preferred_element_type=F32)
+    forward, backward, folded, direct, exact_cot = prepared
+
     context, share = finish([state[0] for state in states], folded)
     partial = share[:, :length] + swapped(share[:, length:], "tok")
     own_map = (partial + swapped(partial, "col") + direct).astype(BF16)
+    own_map = jnp.concatenate([own_map, exact_cot], axis=0)
     chip_map = in_order(core, own_map, swapped(own_map, "tok"), 1)
     rows_chip = 2 * rows_dev
     hidden = jnp.concatenate(
         [passed(chip_map, "tok", 2, False), chip_map, passed(chip_map, "tok", -2, False)], axis=1
     )
 
-    wide_cot = in_order(half, cotangent, swapped(cotangent, "col"), 2)
-    chip_cot = in_order(core, wide_cot, swapped(wide_cot, "tok"), 1)
-    edge = chip_cot.shape[1] - 2
-    cot_rows = jnp.concatenate(
-        [passed(chip_cot[:, edge:], "tok", 2, False), chip_cot, passed(chip_cot[:, :2], "tok", -2, False)], axis=1
-    )
-    taps = conv_weight.reshape(layers, channels, 3, 3, channels)
-    forward = jnp.transpose(taps.reshape(layers, channels, 3, 3 * channels), (0, 2, 1, 3))
-    backward = jnp.transpose(taps[:, :, ::-1, ::-1, :], (0, 2, 4, 3, 1)).reshape(layers, 3, channels, 3 * channels)
     holo, sums, gradient = network(
-        place, hidden, cot_rows.reshape(cot_rows.shape[0], -1), forward, backward, head_weight, context, cols,
-        tok_count * rows_dev, col_count,
+        place, hidden, forward, backward, head_weight, context, cols, tok_count * rows_dev, col_count
     )
     holo = holo.reshape(-1, rows_chip, cols)
     hologram = lax.dynamic_slice(
@@ -315,9 +360,7 @@
     for step in range(1, chips):
         total = total + passed(summed, "tok", 2 * step, True)
     own_grad = total[:, :taps_wide]
-    layer_grad = in_order(half, own_grad, swapped(own_grad, "col"), 0)
-    other_grad = swapped(layer_grad, "tok")
-    conv_grad = in_order(core, layer_grad[None], other_grad[None], 0)
+    col_grad = swapped(own_grad, "col")
     wide = gradient.shape[1]
     own_small = jnp.concatenate(
         [total[:, lanes + at * wide : lanes + (at + 1) * wide] for at in range(pieces)], axis=0
@@ -326,6 +369,10 @@
     out_grad = lax.dot_general(
         small, readout_weight.astype(F32), (((0,), (1,)), ((), ())), precision=lax.Precision.HIGHEST
     )
+    col_grad, out_grad = lax.optimization_barrier((col_grad, out_grad))
+    layer_grad = in_order(half, own_grad, col_grad, 0)
+    other_grad = swapped(layer_grad, "tok")
+    conv_grad = in_order(core, layer_grad[None], other_grad[None], 0)
     return (hologram[None], conv_grad, out_grad)
 
 

time: 108 us -> 95.6 us (0.89)
  waiting for transfers between devices: 46.2 us -> 32.8 us
  starting transfers between devices: 28.7 us -> 22 us
  local copies, waits for them, and re-layouts: 5.05 us -> 10.9 us
  Pallas kernels: 23.2 us -> 24.4 us
    ppermute x14 -> x12, waiting for transfers between devices: 36.8 us -> 23.7 us  [passed(): return lax.ppermute(values, axis, pairs)]
    ppermute x14 -> x12, starting transfers between devices: 22.7 us -> 15.5 us  [passed(): return lax.ppermute(values, axis, pairs)]
    transpose x2, local copies, waits for them, and re-layouts: 0.23 us -> 2.84 us  [prepare(): jnp.transpose(taps[:, :, ::-1, ::-1, :], (0, 2, 4, 3, 1))]
    another operation x2, local copies, waits for them, and re-layouts: 0.17 us -> 2.75 us  [prepare(): taps.reshape(layers, channels, 3, 3 * channels)]
    optimization_barrier x0 -> x2, local copies, waits for them, and re-layouts: none -> 1.95 us  [the longest x1 1.79 us: shards(): lax.optimization_barrier((states[head], (conv_weight, out_weight, readout...]
    ppermute x9 -> x8, starting transfers between devices: 6.05 us -> 6.56 us  [swapped(): return lax.ppermute(values, axis, [(i, i ^ 1) for i in range(size)])]
    ppermute x9 -> x8, waiting for transfers between devices: 9.46 us -> 9.07 us  [swapped(): return lax.ppermute(values, axis, [(i, i ^ 1) for i in range(size)])]
    pallas_call x1 -> x2, Pallas kernels: 2.86 us -> 3.09 us  [the longest x1 2.4 us: project(): pl.pallas_call(project_kernel, out_shape=tuple((jax.ShapeDtypeStruct((cou...]
  transfers between devices with their start and end apart: 23 -> 20, of which waited for: 13 -> 16; matrix products, arithmetic and copies ran while one was open for 4% -> 12% of each run, Pallas kernels for 13% -> 16%
where the time goes in v3:
time: 95.6 us; the launch traced here: 95.2 us
  waiting for transfers between devices  32.8 us (34%)
  Pallas kernels  24.4 us (26%)
  starting transfers between devices  22 us (23%)
  local copies, waits for them, and re-layouts  10.9 us (11%)
  matrix products  2.91 us (3%)
  other arithmetic  1.13 us (1%)
  between operations  1.01 us (1%)
    ppermute x12, waiting for transfers between devices, passed(): return lax.ppermute(values, axis, pairs)  23.7 us
    pallas_call x8, Pallas kernels, absorb(): pl.pallas_call(functools.partial(absorb_kernel, first), out_shape=shapes,...  17.2 us
    ppermute x12, starting transfers between devices, passed(): return lax.ppermute(values, axis, pairs)  15.5 us
    ppermute x8, waiting for transfers between devices, swapped(): return lax.ppermute(values, axis, [(i, i ^ 1) for i in range(size)])  9.07 us
    ppermute x8, starting transfers between devices, swapped(): return lax.ppermute(values, axis, [(i, i ^ 1) for i in range(size)])  6.56 us
    pallas_call x1, Pallas kernels, network(): pl.pallas_call(functools.partial(network_kernel, cols, frame_rows), out_s...  3.75 us
    transpose x2, local copies, waits for them, and re-layouts, prepare(): jnp.transpose(taps[:, :, ::-1, ::-1, :], (0, 2, 4, 3, 1))  2.84 us
    another operation x2, local copies, waits for them, and re-layouts, prepare(): taps.reshape(layers, channels, 3, 3 * channels)  2.75 us
  transfers between devices with their start and end apart: 20, of which 16 were waited for; matrix products, arithmetic and copies ran while one was open for 12% of the time, Pallas kernels for 16%

profile of v3, /device:TPU:0, one launch (start us, length us, event | category | flops | bytes accessed | tf_op | source)
XLA Modules:
  0.0 95.2 jit_solution(3087111827328108088)
XLA Ops:
  4.0 2.4 %project.1 = (bf16[2,64,512]{2,1,0:T(8,128)(2,1)S(1)}, bf16[2,128,512]{2,1,0:T(8,128)(2,1)S(1)}, bf16[2,192,512]{2,1,0:T(8,128)(2,1)S(1)}) custom-call(s32[3]{0:T(128)S(1)} %pad_add_fusion.place, bf16[512,1024]{1,0:T(8,128)(2,1)S(1)} %normalize.1.normed, bf16[3,1024,256]{2,1,0:T(8,128)(2,1)S(1)} %copy-done.3), custom_call_target="tpu_custom_call" | custom-call | tf_op jit(solution)/shard_map/project/pallas_call | solution.py:76
  7.0 2.6 %collective-permute-start.3 = (f32[2,2,128]{2,1,0:T(2,128)S(1)}, f32[2,2,128]{2,1,0:T(2,128)S(1)}, u32[]{:S(2)}, u32[]{:S(2)}) collective-permute-start(f32[2,2,128]{2,1,0:T(2,128)S(1)} %bitcast.50), channel_id=1, source_target_pairs={{0,1},{1,0},{2,3},{3,2},{4,5},{5,4},{6,7},{7,6},{8,9},{9,8},{10,11... | collective-permute-start | bytes 6152 | tf_op jit(solution)/shard_map/ppermute | solution.py:257
  9.7 1.7 %collective-permute-start.2 = (bf16[128,1024]{1,0:T(8,128)(2,1)S(1)}, bf16[128,1024]{1,0:T(8,128)(2,1)S(1)}, u32[]{:S(2)}, u32[]{:S(2)}) collective-permute-start(bf16[128,1024]{1,0:T(8,128)(2,1)S(1)} %pad_maximum_fusion.2.refs_1_), channel_id=1, source_target_pairs={{0,4},{2,6},{4,8},{6,10},{8,12},{10,14},{12,0},{14,2},{1,5},{3,7},... | collective-permute-start | bytes 786440 | tf_op jit(solution)/shard_map/ppermute | solution.py:263
  11.4 2.0 %absorb.8 = (f32[80,1024]{1,0:T(8,128)S(1)}, f32[8,1024]{1,0:T(8,128)S(1)}) custom-call(bf16[64,1024]{1,0:T(8,128)(2,1)S(1)} %get-tuple-element.152.refs_0_, bf16[128,1024]{1,0:T(8,128)(2,1)S(1)} %pad_maximum_fusion.2.refs_1_), custom_call_target="tpu_custom_call" | custom-call | tf_op jit(solution)/shard_map/absorb/pallas_call | solution.py:117
  13.5 1.6 %collective-permute-start.1 = (bf16[128,1024]{1,0:T(8,128)(2,1)S(1)}, bf16[128,1024]{1,0:T(8,128)(2,1)S(1)}, u32[]{:S(2)}, u32[]{:S(2)}) collective-permute-start(bf16[128,1024]{1,0:T(8,128)(2,1)S(1)} %pad_maximum_fusion.1.refs_1_), channel_id=1, source_target_pairs={{0,4},{2,6},{4,8},{6,10},{8,12},{10,14},{12,0},{14,2},{1,5},{3,7},... | collective-permute-start | bytes 786440 | tf_op jit(solution)/shard_map/ppermute | solution.py:263
  15.1 1.8 %copy.25 = bf16[2,64,576]{1,2,0:T(8,128)(2,1)} copy(bf16[2,64,576]{2,1,0:T(8,128)(2,1)} %param.13) | data formatting | bytes 294912 | tf_op jit(solution)/shard_map/optimization_barrier | solution.py:315
  16.9 1.7 %reverse_bitcast_fusion = bf16[2,3,64,3,64]{4,2,3,1,0:T(8,128)(2,1)} fusion(bf16[2,64,3,3,64]{1,4,3,2,0:T(8,128)(2,1)} %bitcast.44), kind=kLoop, calls=%fused_computation.2 | loop fusion | bytes 294912 | tf_op jit(solution)/shard_map/transpose | solution.py:299
  18.8 1.9 %collective-permute-done.2.refs_1_ = bf16[128,1024]{1,0:T(8,128)(2,1)S(1)} collective-permute-done((bf16[128,1024]{1,0:T(8,128)(2,1)S(1)}, bf16[128,1024]{1,0:T(8,128)(2,1)S(1)}, u32[]{:S(2)}, u32[]{:S(2)}) %collective-permute-start.2) | collective-permute-done | bytes 262176 | tf_op jit(solution)/shard_map/ppermute | solution.py:263
  20.7 2.0 %absorb.9 = (f32[80,1024]{1,0:T(8,128)S(1)}, f32[8,1024]{1,0:T(8,128)S(1)}) custom-call(bf16[64,1024]{1,0:T(8,128)(2,1)S(1)} %get-tuple-element.151.refs_0_, bf16[128,1024]{1,0:T(8,128)(2,1)S(1)} %pad_maximum_fusion.1.refs_1_), custom_call_target="tpu_custom_call" | custom-call | tf_op jit(solution)/shard_map/absorb/pallas_call | solution.py:117
  22.7 3.6 %collective-permute-done.1.refs_1_ = bf16[128,1024]{1,0:T(8,128)(2,1)S(1)} collective-permute-done((bf16[128,1024]{1,0:T(8,128)(2,1)S(1)}, bf16[128,1024]{1,0:T(8,128)(2,1)S(1)}, u32[]{:S(2)}, u32[]{:S(2)}) %collective-permute-start.1) | collective-permute-done | bytes 262176 | tf_op jit(solution)/shard_map/ppermute | solution.py:263
  26.3 1.8 %reshape_reshape.3 = bf16[2,64,3,192]{3,2,1,0:T(4,128)(2,1)} reshape(bf16[2,64,576]{2,1,0:T(8,128)(2,1)} %param.13) | data formatting | bytes 294912 | tf_op jit(solution)/shard_map/reshape;reshape | solution.py:298
  29.2 2.1 %absorb.10 = (f32[80,1024]{1,0:T(8,128)S(1)}, f32[8,1024]{1,0:T(8,128)S(1)}) custom-call(bf16[64,1024]{1,0:T(8,128)(2,1)S(1)} %get-tuple-element.152.refs_0_, bf16[128,1024]{1,0:T(8,128)(2,1)S(1)} %collective-permute-done.2.refs_1_, f32[80,1024]{1,0:T(8,128)S(1)} %get-tuple-element.82.refs_2_, ...), custom_call_target="tpu_custom_call", output_to_operand_aliasing={{0}: (2, {}), {1}: (3, {})} | custom-call | tf_op jit(solution)/shard_map/absorb/pallas_call | solution.py:117
  34.9 2.1 %absorb.11 = (f32[80,1024]{1,0:T(8,128)S(1)}, f32[8,1024]{1,0:T(8,128)S(1)}) custom-call(bf16[64,1024]{1,0:T(8,128)(2,1)S(1)} %get-tuple-element.151.refs_0_, bf16[128,1024]{1,0:T(8,128)(2,1)S(1)} %collective-permute-done.1.refs_1_, f32[80,1024]{1,0:T(8,128)S(1)} %get-tuple-element.88.refs_2_, ...), custom_call_target="tpu_custom_call", output_to_operand_aliasing={{0}: (2, {}), {1}: (3, {})} | custom-call | tf_op jit(solution)/shard_map/absorb/pallas_call | solution.py:117
  38.8 3.0 %absorb.12 = (f32[80,1024]{1,0:T(8,128)S(1)}, f32[8,1024]{1,0:T(8,128)S(1)}) custom-call(bf16[64,1024]{1,0:T(8,128)(2,1)S(1)} %get-tuple-element.152.refs_0_, bf16[128,1024]{1,0:T(8,128)(2,1)} %collective-permute-done.5.refs_1_, f32[80,1024]{1,0:T(8,128)S(1)} %get-tuple-element.101.refs_2_, ...), custom_call_target="tpu_custom_call", output_to_operand_aliasing={{0}: (2, {}), {1}: (3, {})} | custom-call | tf_op jit(solution)/shard_map/absorb/pallas_call | solution.py:117
  43.2 2.1 %absorb.14 = (f32[80,1024]{1,0:T(8,128)S(1)}, f32[8,1024]{1,0:T(8,128)S(1)}) custom-call(bf16[64,1024]{1,0:T(8,128)(2,1)S(1)} %get-tuple-element.152.refs_0_, bf16[128,1024]{1,0:T(8,128)(2,1)S(1)} %collective-permute-done.7.refs_1_, f32[80,1024]{1,0:T(8,128)S(1)} %get-tuple-element.113.refs_2_, ...), custom_call_target="tpu_custom_call", output_to_operand_aliasing={{0}: (2, {}), {1}: (3, {})} | custom-call | tf_op jit(solution)/shard_map/absorb/pallas_call | solution.py:117
  45.3 2.1 %absorb.13 = (f32[80,1024]{1,0:T(8,128)S(1)}, f32[8,1024]{1,0:T(8,128)S(1)}) custom-call(bf16[64,1024]{1,0:T(8,128)(2,1)S(1)} %get-tuple-element.151.refs_0_, bf16[128,1024]{1,0:T(8,128)(2,1)S(1)} %collective-permute-done.4.refs_1_, f32[80,1024]{1,0:T(8,128)S(1)} %get-tuple-element.107.refs_2_, ...), custom_call_target="tpu_custom_call", output_to_operand_aliasing={{0}: (2, {}), {1}: (3, {})} | custom-call | tf_op jit(solution)/shard_map/absorb/pallas_call | solution.py:117
  48.1 2.1 %absorb.15 = (f32[80,1024]{1,0:T(8,128)S(1)}, f32[8,1024]{1,0:T(8,128)S(1)}) custom-call(bf16[64,1024]{1,0:T(8,128)(2,1)S(1)} %get-tuple-element.151.refs_0_, bf16[128,1024]{1,0:T(8,128)(2,1)S(1)} %collective-permute-done.6.refs_1_, f32[80,1024]{1,0:T(8,128)S(1)} %get-tuple-element.119.refs_2_, ...), custom_call_target="tpu_custom_call", output_to_operand_aliasing={{0}: (2, {}), {1}: (3, {})} | custom-call | tf_op jit(solution)/shard_map/absorb/pallas_call | solution.py:117
  51.9 1.6 %collective-permute-start.9 = (f32[64,512]{1,0:T(8,128)S(1)}, f32[64,512]{1,0:T(8,128)S(1)}, u32[]{:S(2)}, u32[]{:S(2)}) collective-permute-start(f32[64,512]{1,0:T(8,128)S(1)} %slice_add_fusion), channel_id=1, source_target_pairs={{0,1},{1,0},{2,3},{3,2},{4,5},{5,4},{6,7},{7,6},{8,9},{9,8},{10,11... | collective-permute-start | bytes 393224 | tf_op jit(solution)/shard_map/ppermute | solution.py:257
  53.5 4.1 %collective-permute-done.9 = f32[64,512]{1,0:T(8,128)S(1)} collective-permute-done((f32[64,512]{1,0:T(8,128)S(1)}, f32[64,512]{1,0:T(8,128)S(1)}, u32[]{:S(2)}, u32[]{:S(2)}) %collective-permute-start.9) | collective-permute-done | bytes 131104 | tf_op jit(solution)/shard_map/ppermute | solution.py:257
  59.0 1.7 %collective-permute-start.11 = (bf16[80,1024]{1,0:T(8,128)(2,1)S(1)}, bf16[80,1024]{1,0:T(8,128)(2,1)S(1)}, u32[]{:S(2)}, u32[]{:S(2)}) collective-permute-start(bf16[80,1024]{1,0:T(8,128)(2,1)S(1)} %maximum_select_fusion.1), channel_id=1, source_target_pairs={{0,4},{2,6},{4,8},{6,10},{8,12},{10,14},{1,5},{3,7},{5,9},{7,11},{... | collective-permute-start | bytes 491528 | tf_op jit(solution)/shard_map/ppermute | solution.py:263
  62.1 2.3 %collective-permute-done.11 = bf16[80,1024]{1,0:T(8,128)(2,1)S(1)} collective-permute-done((bf16[80,1024]{1,0:T(8,128)(2,1)S(1)}, bf16[80,1024]{1,0:T(8,128)(2,1)S(1)}, u32[]{:S(2)}, u32[]{:S(2)}) %collective-permute-start.11) | collective-permute-done | bytes 163872 | tf_op jit(solution)/shard_map/ppermute | solution.py:263
  64.4 4.1 %collective-permute-done.12 = bf16[80,1024]{1,0:T(8,128)(2,1)S(1)} collective-permute-done((bf16[80,1024]{1,0:T(8,128)(2,1)S(1)}, bf16[80,1024]{1,0:T(8,128)(2,1)S(1)}, u32[]{:S(2)}, u32[]{:S(2)}) %collective-permute-start.12) | collective-permute-done | bytes 163872 | tf_op jit(solution)/shard_map/ppermute | solution.py:263
  68.6 3.7 %network.1 = (f32[2,1024]{1,0:T(2,128)S(1)}, f32[32,576]{1,0:T(8,128)S(1)}, f32[64,128]{1,0:T(8,128)S(1)}) custom-call(s32[3]{0:T(128)S(1)} %pad_add_fusion.place, bf16[80,3072]{1,0:T(8,128)(2,1)S(1)} %pad_maximum_fusion.hidden, bf16[2,3,64,192]{3,2,1,0:T(8,128)(2,1)S(1)} %bitcast.43, bf16[2,3,64,192]{3,2,1,0:T(8,128)(2,1)S(1)} %copy.27.backward, ...), custom_call_target="tpu_custom_call" | custom-call | tf_op jit(solution)/shard_map/network/pallas_call | solution.py:240
  72.4 1.7 %collective-permute-start.13 = (f32[32,896]{1,0:T(8,128)S(1)}, f32[32,896]{1,0:T(8,128)S(1)}, u32[]{:S(2)}, u32[]{:S(2)}) collective-permute-start(f32[32,896]{1,0:T(8,128)S(1)} %fusion.2), channel_id=1, source_target_pairs={{0,16},{16,0},{1,17},{17,1},{2,18},{18,2},{3,19},{19,3},{4,20},{20... | collective-permute-start | bytes 344072 | tf_op jit(solution)/shard_map/ppermute | solution.py:263
  74.0 3.2 %collective-permute-done.13 = f32[32,896]{1,0:T(8,128)S(1)} collective-permute-done((f32[32,896]{1,0:T(8,128)S(1)}, f32[32,896]{1,0:T(8,128)S(1)}, u32[]{:S(2)}, u32[]{:S(2)}) %collective-permute-start.13) | collective-permute-done | bytes 114720 | tf_op jit(solution)/shard_map/ppermute | solution.py:263
  77.2 1.6 %collective-permute-start.14 = (f32[32,896]{1,0:T(8,128)S(1)}, f32[32,896]{1,0:T(8,128)S(1)}, u32[]{:S(2)}, u32[]{:S(2)}) collective-permute-start(f32[32,896]{1,0:T(8,128)S(1)} %fusion.23), channel_id=1, source_target_pairs={{0,4},{2,6},{4,8},{6,10},{8,12},{10,14},{12,0},{14,2},{1,5},{3,7},... | collective-permute-start | bytes 344072 | tf_op jit(solution)/shard_map/ppermute | solution.py:263
  79.9 2.8 %collective-permute-start.16 = (f32[32,896]{1,0:T(8,128)S(1)}, f32[32,896]{1,0:T(8,128)S(1)}, u32[]{:S(2)}, u32[]{:S(2)}) collective-permute-start(f32[32,896]{1,0:T(8,128)S(1)} %fusion.23), channel_id=1, source_target_pairs={{0,12},{2,14},{4,0},{6,2},{8,4},{10,6},{12,8},{14,10},{1,13},{3,15... | collective-permute-start | bytes 344072 | tf_op jit(solution)/shard_map/ppermute | solution.py:263
  82.8 2.0 %collective-permute-done.14 = f32[32,896]{1,0:T(8,128)S(1)} collective-permute-done((f32[32,896]{1,0:T(8,128)S(1)}, f32[32,896]{1,0:T(8,128)S(1)}, u32[]{:S(2)}, u32[]{:S(2)}) %collective-permute-start.14) | collective-permute-done | bytes 114720 | tf_op jit(solution)/shard_map/ppermute | solution.py:263
  84.8 3.1 %collective-permute-done.15 = f32[32,896]{1,0:T(8,128)S(1)} collective-permute-done((f32[32,896]{1,0:T(8,128)S(1)}, f32[32,896]{1,0:T(8,128)S(1)}, u32[]{:S(2)}, u32[]{:S(2)}) %collective-permute-start.15) | collective-permute-done | bytes 114720 | tf_op jit(solution)/shard_map/ppermute | solution.py:263
  88.0 1.6 %collective-permute-start.17 = (f32[32,576]{1,0:T(8,128)S(1)}, f32[32,576]{1,0:T(8,128)S(1)}, u32[]{:S(2)}, u32[]{:S(2)}) collective-permute-start(f32[32,576]{1,0:T(8,128)S(1)} %get-tuple-element.144), channel_id=1, source_target_pairs={{0,1},{1,0},{2,3},{3,2},{4,5},{5,4},{6,7},{7,6},{8,9},{9,8},{10,11... | collective-permute-start | bytes 221192 | tf_op jit(solution)/shard_map/ppermute | solution.py:257
  89.7 1.6 %fusion.3 = f32[256,1024]{1,0:T(8,128)} fusion(bf16[1024,64]{0,1:T(8,128)(2,1)S(1)} %copy-done.6, f32[64,128]{1,0:T(8,128)S(1)} %collective-permute-done.18, f32[32,128]{1,0:T(8,128)S(1)} %get-tuple-element.146, f32[32,128]{1,0:T(8,128)S(1)} %get-tuple-element.145, pred[]{:T(512)S(6)} %eq.4), kind=kOutput, calls=%fused_computation.27 | convolution fusion | flops 201408512 | bytes 1245185 | tf_op jit(solution)/shard_map/dot_general | solution.py:369
  91.2 1.7 %collective-permute-done.17 = f32[32,576]{1,0:T(8,128)S(1)} collective-permute-done((f32[32,576]{1,0:T(8,128)S(1)}, f32[32,576]{1,0:T(8,128)S(1)}, u32[]{:S(2)}, u32[]{:S(2)}) %collective-permute-start.17) | collective-permute-done | bytes 73760 | tf_op jit(solution)/shard_map/ppermute | solution.py:257
  (78 shorter events, 21.2 us)
Async XLA Ops:
  0.6 18.0 %copy-start = (bf16[256,1024]{1,0:T(8,128)(2,1)S(1)}, bf16[256,1024]{1,0:T(8,128)(2,1)}, u32[]{:S(2)}) copy-start(bf16[256,1024]{1,0:T(8,128)(2,1)} %param.11) | copy-start | bytes 1572868
  0.7 1.3 %copy-start.1 = (bf16[1,512,1024]{2,1,0:T(8,128)(2,1)S(1)}, bf16[1,512,1024]{2,1,0:T(8,128)(2,1)}, u32[]{:S(2)}) copy-start(bf16[1,512,1024]{2,1,0:T(8,128)(2,1)} %param.8) | copy-start | bytes 3145732
  1.9 0.7 copy-start.4
  2.6 1.4 %copy-start.3 = (bf16[3,1024,256]{2,1,0:T(8,128)(2,1)S(1)}, bf16[3,1024,256]{2,1,0:T(8,128)(2,1)}, u32[]{:S(2)}) copy-start(bf16[3,1024,256]{2,1,0:T(8,128)(2,1)} %weight.1) | copy-start | bytes 4718596
  3.3 3.7 %copy-start.8 = (f32[1,2,2,128]{3,2,1,0:T(2,128)S(1)}, f32[1,2,2,128]{3,2,1,0:T(2,128)}, u32[]{:S(2)}) copy-start(f32[1,2,2,128]{3,2,1,0:T(2,128)} %param.15) | copy-start | bytes 6148
  6.4 3.2 %collective-permute-start = (bf16[2,192,512]{2,1,0:T(8,128)(2,1)S(1)}, bf16[2,192,512]{2,1,0:T(8,128)(2,1)S(1)}, u32[]{:S(2)}, u32[]{:S(2)}) collective-permute-start(bf16[2,192,512]{2,1,0:T(8,128)(2,1)S(1)} %get-tuple-element.70), channel_id=1, source_target_pairs={{0,2},{2,0},{4,6},{6,4},{8,10},{10,8},{12,14},{14,12},{1,3},{3,1},... | collective-permute-start | bytes 1179656 | tf_op jit(solution)/shard_map/ppermute | solution.py:257
  7.0 6.4 %collective-permute-start.3 = (f32[2,2,128]{2,1,0:T(2,128)S(1)}, f32[2,2,128]{2,1,0:T(2,128)S(1)}, u32[]{:S(2)}, u32[]{:S(2)}) collective-permute-start(f32[2,2,128]{2,1,0:T(2,128)S(1)} %bitcast.50), channel_id=1, source_target_pairs={{0,1},{1,0},{2,3},{3,2},{4,5},{5,4},{6,7},{7,6},{8,9},{9,8},{10,11... | collective-permute-start | bytes 6152 | tf_op jit(solution)/shard_map/ppermute | solution.py:257
  9.6 9.0 %copy-start.6 = (bf16[1024,64]{0,1:T(8,128)(2,1)S(1)}, bf16[1024,64]{0,1:T(8,128)(2,1)}, u32[]{:S(2)}) copy-start(bf16[1024,64]{0,1:T(8,128)(2,1)} %param.12) | copy-start | bytes 393220
  9.7 11.0 %collective-permute-start.2 = (bf16[128,1024]{1,0:T(8,128)(2,1)S(1)}, bf16[128,1024]{1,0:T(8,128)(2,1)S(1)}, u32[]{:S(2)}, u32[]{:S(2)}) collective-permute-start(bf16[128,1024]{1,0:T(8,128)(2,1)S(1)} %pad_maximum_fusion.2.refs_1_), channel_id=1, source_target_pairs={{0,4},{2,6},{4,8},{6,10},{8,12},{10,14},{12,0},{14,2},{1,5},{3,7},... | collective-permute-start | bytes 786440 | tf_op jit(solution)/shard_map/ppermute | solution.py:263
  11.4 16.7 %copy-start.2 = (bf16[1,512,1024]{2,1,0:T(8,128)(2,1)S(1)}, bf16[1,512,1024]{2,1,0:T(8,128)(2,1)}, u32[]{:S(2)}) copy-start(bf16[1,512,1024]{2,1,0:T(8,128)(2,1)} %param.8) | copy-start | bytes 3145732
  13.5 12.8 %collective-permute-start.1 = (bf16[128,1024]{1,0:T(8,128)(2,1)S(1)}, bf16[128,1024]{1,0:T(8,128)(2,1)S(1)}, u32[]{:S(2)}, u32[]{:S(2)}) collective-permute-start(bf16[128,1024]{1,0:T(8,128)(2,1)S(1)} %pad_maximum_fusion.1.refs_1_), channel_id=1, source_target_pairs={{0,4},{2,6},{4,8},{6,10},{8,12},{10,14},{12,0},{14,2},{1,5},{3,7},... | collective-permute-start | bytes 786440 | tf_op jit(solution)/shard_map/ppermute | solution.py:263
  20.7 11.3 %collective-permute-start.5 = (bf16[128,1024]{1,0:T(8,128)(2,1)S(1)}, bf16[128,1024]{1,0:T(8,128)(2,1)}, u32[]{:S(2)}, u32[]{:S(2)}) collective-permute-start(bf16[128,1024]{1,0:T(8,128)(2,1)S(1)} %collective-permute-done.2.refs_1_), channel_id=1, source_target_pairs={{0,4},{2,6},{4,8},{6,10},{8,12},{10,14},{12,0},{14,2},{1,5},{3,7},... | collective-permute-start | bytes 786440 | tf_op jit(solution)/shard_map/ppermute | solution.py:263
  26.3 11.2 %collective-permute-start.4 = (bf16[128,1024]{1,0:T(8,128)(2,1)S(1)}, bf16[128,1024]{1,0:T(8,128)(2,1)S(1)}, u32[]{:S(2)}, u32[]{:S(2)}) collective-permute-start(bf16[128,1024]{1,0:T(8,128)(2,1)S(1)} %collective-permute-done.1.refs_1_), channel_id=1, source_target_pairs={{0,4},{2,6},{4,8},{6,10},{8,12},{10,14},{12,0},{14,2},{1,5},{3,7},... | collective-permute-start | bytes 786440 | tf_op jit(solution)/shard_map/ppermute | solution.py:263
  32.0 11.2 %collective-permute-start.7 = (bf16[128,1024]{1,0:T(8,128)(2,1)}, bf16[128,1024]{1,0:T(8,128)(2,1)S(1)}, u32[]{:S(2)}, u32[]{:S(2)}) collective-permute-start(bf16[128,1024]{1,0:T(8,128)(2,1)} %collective-permute-done.5.refs_1_), channel_id=1, source_target_pairs={{0,4},{2,6},{4,8},{6,10},{8,12},{10,14},{12,0},{14,2},{1,5},{3,7},... | collective-permute-start | bytes 786440 | tf_op jit(solution)/shard_map/ppermute | solution.py:263
  37.6 10.6 %collective-permute-start.6 = (bf16[128,1024]{1,0:T(8,128)(2,1)S(1)}, bf16[128,1024]{1,0:T(8,128)(2,1)S(1)}, u32[]{:S(2)}, u32[]{:S(2)}) collective-permute-start(bf16[128,1024]{1,0:T(8,128)(2,1)S(1)} %collective-permute-done.4.refs_1_), channel_id=1, source_target_pairs={{0,4},{2,6},{4,8},{6,10},{8,12},{10,14},{12,0},{14,2},{1,5},{3,7},... | collective-permute-start | bytes 786440 | tf_op jit(solution)/shard_map/ppermute | solution.py:263
  45.3 12.3 %copy-start.7 = (f32[64,512]{1,0:T(8,128)S(1)}, f32[64,512]{1,0:T(8,128)}, u32[]{:S(2)}) copy-start(f32[64,512]{1,0:T(8,128)} %fusion.26) | copy-start | bytes 393220
  50.5 18.1 %copy-start.5 = (bf16[2,64]{1,0:T(2,128)(2,1)S(1)}, bf16[2,64]{1,0:T(2,128)(2,1)}, u32[]{:S(2)}) copy-start(bf16[2,64]{1,0:T(2,128)(2,1)} %head.1) | copy-start | bytes 772
  50.5 1.4 %collective-permute-start.8 = (f32[64,512]{1,0:T(8,128)S(1)}, f32[64,512]{1,0:T(8,128)S(1)}, u32[]{:S(2)}, u32[]{:S(2)}) collective-permute-start(f32[64,512]{1,0:T(8,128)S(1)} %slice.54), channel_id=1, source_target_pairs={{0,2},{2,0},{4,6},{6,4},{8,10},{10,8},{12,14},{14,12},{1,3},{3,1},... | collective-permute-start | bytes 393224 | tf_op jit(solution)/shard_map/ppermute | solution.py:257
  51.9 5.6 %collective-permute-start.9 = (f32[64,512]{1,0:T(8,128)S(1)}, f32[64,512]{1,0:T(8,128)S(1)}, u32[]{:S(2)}, u32[]{:S(2)}) collective-permute-start(f32[64,512]{1,0:T(8,128)S(1)} %slice_add_fusion), channel_id=1, source_target_pairs={{0,1},{1,0},{2,3},{3,2},{4,5},{5,4},{6,7},{7,6},{8,9},{9,8},{10,11... | collective-permute-start | bytes 393224 | tf_op jit(solution)/shard_map/ppermute | solution.py:257
  57.6 1.3 %collective-permute-start.10 = (bf16[80,512]{1,0:T(8,128)(2,1)S(1)}, bf16[80,512]{1,0:T(8,128)(2,1)S(1)}, u32[]{:S(2)}, u32[]{:S(2)}) collective-permute-start(bf16[80,512]{1,0:T(8,128)(2,1)S(1)} %pad_maximum_fusion.5), channel_id=1, source_target_pairs={{0,2},{2,0},{4,6},{6,4},{8,10},{10,8},{12,14},{14,12},{1,3},{3,1},... | collective-permute-start | bytes 245768 | tf_op jit(solution)/shard_map/ppermute | solution.py:257
  59.0 5.4 %collective-permute-start.11 = (bf16[80,1024]{1,0:T(8,128)(2,1)S(1)}, bf16[80,1024]{1,0:T(8,128)(2,1)S(1)}, u32[]{:S(2)}, u32[]{:S(2)}) collective-permute-start(bf16[80,1024]{1,0:T(8,128)(2,1)S(1)} %maximum_select_fusion.1), channel_id=1, source_target_pairs={{0,4},{2,6},{4,8},{6,10},{8,12},{10,14},{1,5},{3,7},{5,9},{7,11},{... | collective-permute-start | bytes 491528 | tf_op jit(solution)/shard_map/ppermute | solution.py:263
  60.7 7.9 %collective-permute-start.12 = (bf16[80,1024]{1,0:T(8,128)(2,1)S(1)}, bf16[80,1024]{1,0:T(8,128)(2,1)S(1)}, u32[]{:S(2)}, u32[]{:S(2)}) collective-permute-start(bf16[80,1024]{1,0:T(8,128)(2,1)S(1)} %maximum_select_fusion.1), channel_id=1, source_target_pairs={{4,0},{6,2},{8,4},{10,6},{12,8},{14,10},{5,1},{7,3},{9,5},{11,7},{... | collective-permute-start | bytes 491528 | tf_op jit(solution)/shard_map/ppermute | solution.py:263
  72.4 4.9 %collective-permute-start.13 = (f32[32,896]{1,0:T(8,128)S(1)}, f32[32,896]{1,0:T(8,128)S(1)}, u32[]{:S(2)}, u32[]{:S(2)}) collective-permute-start(f32[32,896]{1,0:T(8,128)S(1)} %fusion.2), channel_id=1, source_target_pairs={{0,16},{16,0},{1,17},{17,1},{2,18},{18,2},{3,19},{19,3},{4,20},{20... | collective-permute-start | bytes 344072 | tf_op jit(solution)/shard_map/ppermute | solution.py:263
  77.2 7.6 %collective-permute-start.14 = (f32[32,896]{1,0:T(8,128)S(1)}, f32[32,896]{1,0:T(8,128)S(1)}, u32[]{:S(2)}, u32[]{:S(2)}) collective-permute-start(f32[32,896]{1,0:T(8,128)S(1)} %fusion.23), channel_id=1, source_target_pairs={{0,4},{2,6},{4,8},{6,10},{8,12},{10,14},{12,0},{14,2},{1,5},{3,7},... | collective-permute-start | bytes 344072 | tf_op jit(solution)/shard_map/ppermute | solution.py:263
  78.8 9.1 %collective-permute-start.15 = (f32[32,896]{1,0:T(8,128)S(1)}, f32[32,896]{1,0:T(8,128)S(1)}, u32[]{:S(2)}, u32[]{:S(2)}) collective-permute-start(f32[32,896]{1,0:T(8,128)S(1)} %fusion.23), channel_id=1, source_target_pairs={{0,8},{2,10},{4,12},{6,14},{8,0},{10,2},{12,4},{14,6},{1,9},{3,11}... | collective-permute-start | bytes 344072 | tf_op jit(solution)/shard_map/ppermute | solution.py:263
  79.9 8.0 %collective-permute-start.16 = (f32[32,896]{1,0:T(8,128)S(1)}, f32[32,896]{1,0:T(8,128)S(1)}, u32[]{:S(2)}, u32[]{:S(2)}) collective-permute-start(f32[32,896]{1,0:T(8,128)S(1)} %fusion.23), channel_id=1, source_target_pairs={{0,12},{2,14},{4,0},{6,2},{8,4},{10,6},{12,8},{14,10},{1,13},{3,15... | collective-permute-start | bytes 344072 | tf_op jit(solution)/shard_map/ppermute | solution.py:263
  87.9 1.7 %collective-permute-start.18 = (f32[64,128]{1,0:T(8,128)S(1)}, f32[64,128]{1,0:T(8,128)S(1)}, u32[]{:S(2)}, u32[]{:S(2)}) collective-permute-start(f32[64,128]{1,0:T(8,128)S(1)} %pad_maximum_fusion.6), channel_id=1, source_target_pairs={{0,2},{2,0},{4,6},{6,4},{8,10},{10,8},{12,14},{14,12},{1,3},{3,1},... | collective-permute-start | bytes 98312 | tf_op jit(solution)/shard_map/ppermute | solution.py:257
  88.0 4.9 %collective-permute-start.17 = (f32[32,576]{1,0:T(8,128)S(1)}, f32[32,576]{1,0:T(8,128)S(1)}, u32[]{:S(2)}, u32[]{:S(2)}) collective-permute-start(f32[32,576]{1,0:T(8,128)S(1)} %get-tuple-element.144), channel_id=1, source_target_pairs={{0,1},{1,0},{2,3},{3,2},{4,5},{5,4},{6,7},{7,6},{8,9},{9,8},{10,11... | collective-permute-start | bytes 221192 | tf_op jit(solution)/shard_map/ppermute | solution.py:257
  93.0 1.5 %collective-permute-start.19 = (f32[64,576]{1,0:T(8,128)S(1)}, f32[64,576]{1,0:T(8,128)S(1)}, u32[]{:S(2)}, u32[]{:S(2)}) collective-permute-start(f32[64,576]{1,0:T(8,128)S(1)} %maximum_select_fusion.3), channel_id=1, source_target_pairs={{0,2},{2,0},{4,6},{6,4},{8,10},{10,8},{12,14},{14,12},{1,3},{3,1},... | collective-permute-start | bytes 442376 | tf_op jit(solution)/shard_map/ppermute | solution.py:257

commit v4 on v3

--- a/solution.py
+++ b/solution.py
@@ -49,35 +49,29 @@
     )(tokens, gain)
 
 
-def project_kernel(place, normed, weight, queries, keyed, theirs):
+def project_kernel(members, place, normed, weight, mine, theirs):
     core = place[0]
-    kept = keyed.shape[0] * HEAD
+    kept = mine.shape[0] * HEAD
     rows = normed[...]
-    for which in range(2):
-        start = core if which == 0 else 1 - core
-        for member in range(3):
-            part = weight[member, :, pl.ds(pl.multiple_of(start * kept, 128), kept)]
+    for which, out in ((1 - core, theirs), (core, mine)):
+        for at, member in enumerate(members):
+            part = weight[member, :, pl.ds(pl.multiple_of(which * kept, 128), kept)]
             product = dot(rows, part).astype(BF16)
             if member == 0:
                 product = product * jnp.asarray(1.0 / HEAD**0.5, BF16)
             turned = product.T
-            for head in range(keyed.shape[0]):
-                piece = turned[head * HEAD : (head + 1) * HEAD, :]
-                if which == 1:
-                    theirs[head, member * HEAD : (member + 1) * HEAD, :] = piece
-                elif member == 0:
-                    queries[head] = piece
-                else:
-                    keyed[head, (member - 1) * HEAD : member * HEAD, :] = piece
-
-
-def project(place, normed, weight):
+            for head in range(mine.shape[0]):
+                out[head, at * HEAD : (at + 1) * HEAD, :] = turned[head * HEAD : (head + 1) * HEAD, :]
+
+
+def project(members, place, normed, weight):
     count, length = weight.shape[2] // HEAD // 2, normed.shape[0]
-    return pl.pallas_call(
-        project_kernel,
-        out_shape=tuple(jax.ShapeDtypeStruct((count, many * HEAD, length), BF16) for many in (1, 2, 3)),
+    shape = jax.ShapeDtypeStruct((count, len(members) * HEAD, length), BF16)
+    return pl.pallas_call(
+        functools.partial(project_kernel, members),
+        out_shape=(shape, shape),
         in_specs=[SMEM, VMEM, VMEM],
-        out_specs=(VMEM,) * 3,
+        out_specs=(VMEM,) * 2,
         compiler_params=PARAMS,
         name="project",
     )(place, normed, weight)
@@ -167,7 +161,8 @@
 
 
 def network_kernel(
-    cols, frame_rows, place, hidden, forward, backward, head, context, holo, sums, gradient, pre_one, pre_two
+    cols, frame_rows, place, own_map, other_map, rims, other_rims, forward, backward, head, context, holo, sums,
+    gradient, hidden, pre_one, pre_two,
 ):
     core, half, row_at = place[0], place[1], place[2]
     own = context.shape[1]
@@ -176,6 +171,13 @@
     row_count = cells // cols
     above = rim // cols
     first_row = row_at - above
+    piece = own // 2
+    for order, (mine, theirs, at) in enumerate(
+        ((rims, other_rims, 0), (own_map, other_map, 0), (rims, other_rims, piece))
+    ):
+        for which, source in ((core, mine), (1 - core, theirs)):
+            start = pl.multiple_of(order * own + which * piece, 128)
+            hidden[:, pl.ds(start, piece)] = source[:, at : at + piece]
 
     def inside(start_row, rows):
         lane = lax.broadcasted_iota(jnp.int32, (1, rows * cols), 1)
@@ -222,7 +224,6 @@
             rows = pre[pl.ds(pl.multiple_of(half * share, 16), share), :]
             sums[:, :taps] = lax.dot_general(rows, stacked, NT, preferred_element_type=F32)
 
-    piece = own // 2
     total = None
     for side in range(2):
         where = lax.rem(core + side, 2)
@@ -234,7 +235,7 @@
     gradient[...] = total
 
 
-def network(place, hidden, forward, backward, head, context, cols, frame_rows, col_count):
+def network(place, maps, forward, backward, head, context, cols, frame_rows, col_count):
     own = context.shape[1]
     channels = forward.shape[2]
     return pl.pallas_call(
@@ -244,12 +245,12 @@
             jax.ShapeDtypeStruct((channels // col_count, 9 * channels), F32),
             jax.ShapeDtypeStruct((channels, context.shape[0]), F32),
         ),
-        in_specs=[SMEM] + [VMEM] * 5,
+        in_specs=[SMEM] + [VMEM] * 8,
         out_specs=(VMEM,) * 3,
-        scratch_shapes=[pltpu.VMEM((channels, own), BF16)] * 2,
+        scratch_shapes=[pltpu.VMEM((maps[0].shape[0], 3 * own), BF16)] + [pltpu.VMEM((channels, own), BF16)] * 2,
         compiler_params=PARAMS,
         name="network",
-    )(place, hidden, forward, backward, head, context)
+    )(place, *maps, forward, backward, head, context)
 
 
 def swapped(values, axis):
@@ -261,6 +262,14 @@
     size = lax.axis_size(axis)
     pairs = [(i, (i + step) % size) for i in range(size) if wrap or 0 <= i + step < size]
     return lax.ppermute(values, axis, pairs)
+
+
+def everyone(values, axis, stride, count):
+    sent = values.astype(BF16)
+    total = sent.astype(F32)
+    for step in range(1, count):
+        total = total + passed(sent, axis, stride * step, True).astype(F32)
+    return total
 
 
 def in_order(core, mine, theirs, axis):
@@ -285,15 +294,19 @@
     cols = cols_dev * col_count
     length = frame_rows.shape[0]
 
-    own_queries, own_keyed, theirs = project(place, normalize(frame_rows, ln_gain), qkv_weight)
-    received = swapped(theirs, "tok")
-    count = received.shape[0]
+    normed = normalize(frame_rows, ln_gain)
+    own_keyed, their_keyed = project((1, 2), place, normed, qkv_weight)
+    own_keyed, their_keyed, normed = lax.optimization_barrier((own_keyed, their_keyed, normed))
+    got_keyed = swapped(their_keyed, "tok")
+    own_queries, their_queries = project((0,), place, normed, qkv_weight)
+    got_queries = swapped(their_queries, "tok")
+    count = got_keyed.shape[0]
     kept = count * HEAD
-    blocks = [jnp.concatenate([own_keyed[head], received[head, HEAD:]], axis=1) for head in range(count)]
-    queries = [jnp.concatenate([own_queries[head], received[head, :HEAD]], axis=1) for head in range(count)]
+    blocks = [jnp.concatenate([own_keyed[head], got_keyed[head]], axis=1) for head in range(count)]
+    queries = [jnp.concatenate([own_queries[head], got_queries[head]], axis=1) for head in range(count)]
     states = [None] * count
 
-    def prepare(conv_weight, out_weight, readout_weight, frame_rows, other_cot):
+    def prepare(conv_weight, out_weight, readout_weight, frame_rows, cotangent):
         taps = conv_weight.reshape(layers, channels, 3, 3, channels)
         forward = jnp.transpose(taps.reshape(layers, channels, 3, 3 * channels), (0, 2, 1, 3))
         backward = jnp.transpose(taps[:, :, ::-1, ::-1, :], (0, 2, 4, 3, 1)).reshape(
@@ -302,7 +315,7 @@
         own_out = lax.dynamic_slice_in_dim(out_weight, core * kept, kept, 0)
         folded = lax.dot_general(readout_weight, own_out, (((0,), (1,)), ((), ())), preferred_element_type=F32)
         direct = lax.dot_general(readout_weight, frame_rows, (((0,), (1,)), ((), ())), preferred_element_type=F32)
-        wide_cot = in_order(half, cotangent, other_cot, 2)
+        wide_cot = in_order(half, cotangent, swapped(cotangent, "col"), 2)
         exact_cot = jnp.concatenate(split3(wide_cot.reshape(wide_cot.shape[0], -1)), axis=0)
         exact_cot = jnp.pad(exact_cot, ((0, -exact_cot.shape[0] % 16), (0, 0)))
         return (forward, backward, folded, direct, exact_cot)
@@ -313,7 +326,7 @@
             states[head] = absorb(queries[head], blocks[head], states[head])
             if turn == 0 and head == 0:
                 states[head], given = lax.optimization_barrier(
-                    (states[head], (conv_weight, out_weight, readout_weight, frame_rows, swapped(cotangent, "col")))
+                    (states[head], (conv_weight, out_weight, readout_weight, frame_rows, cotangent))
                 )
                 prepared = prepare(*given)
             if turn == min(1, chips - 1) and head == count - 1:
@@ -333,14 +346,11 @@
     partial = share[:, :length] + swapped(share[:, length:], "tok")
     own_map = (partial + swapped(partial, "col") + direct).astype(BF16)
     own_map = jnp.concatenate([own_map, exact_cot], axis=0)
-    chip_map = in_order(core, own_map, swapped(own_map, "tok"), 1)
+    rims = jnp.concatenate([passed(own_map, "tok", 2, False), passed(own_map, "tok", -2, False)], axis=1)
     rows_chip = 2 * rows_dev
-    hidden = jnp.concatenate(
-        [passed(chip_map, "tok", 2, False), chip_map, passed(chip_map, "tok", -2, False)], axis=1
-    )
-
+    maps = (own_map, swapped(own_map, "tok"), rims, swapped(rims, "tok"))
     holo, sums, gradient = network(
-        place, hidden, forward, backward, head_weight, context, cols, tok_count * rows_dev, col_count
+        place, maps, forward, backward, head_weight, context, cols, tok_count * rows_dev, col_count
     )
     holo = holo.reshape(-1, rows_chip, cols)
     hologram = lax.dynamic_slice(
@@ -353,12 +363,8 @@
     pieces = gradient.shape[0] // rows
     folded_gradient = [gradient[at * rows : (at + 1) * rows] for at in range(pieces)]
     sent = jnp.concatenate([jnp.pad(sums, ((0, 0), (0, lanes - taps_wide))), *folded_gradient], axis=1)
-    summed = sent
-    for step in range(1, dp_count):
-        summed = summed + passed(sent, "dp", step, True)
-    total = summed
-    for step in range(1, chips):
-        total = total + passed(summed, "tok", 2 * step, True)
+    summed = everyone(sent, "dp", 1, dp_count)
+    total = everyone(summed, "tok", 2, chips)
     own_grad = total[:, :taps_wide]
     col_grad = swapped(own_grad, "col")
     wide = gradient.shape[1]
@@ -369,9 +375,11 @@
     out_grad = lax.dot_general(
         small, readout_weight.astype(F32), (((0,), (1,)), ((), ())), precision=lax.Precision.HIGHEST
     )
-    col_grad, out_grad = lax.optimization_barrier((col_grad, out_grad))
+    core_grad = swapped(own_grad, "tok")
+    col_grad, out_grad, core_grad = lax.optimization_barrier((col_grad, out_grad, core_grad))
+    far_grad = swapped(col_grad, "tok")
     layer_grad = in_order(half, own_grad, col_grad, 0)
-    other_grad = swapped(layer_grad, "tok")
+    other_grad = in_order(half, core_grad, far_grad, 0)
     conv_grad = in_order(core, layer_grad[None], other_grad[None], 0)
     return (hologram[None], conv_grad, out_grad)
 

time: 95.6 us -> 90.9 us (0.951)
  local copies, waits for them, and re-layouts: 10.9 us -> 4.95 us
  waiting for transfers between devices: 32.8 us -> 35.7 us
  starting transfers between devices: 22 us -> 20.8 us
    another operation x2, local copies, waits for them, and re-layouts: 2.75 us -> 0.17 us  [prepare(): taps.reshape(layers, channels, 3, 3 * channels)]
    ppermute x12, waiting for transfers between devices: 23.7 us -> 26 us  [passed(): return lax.ppermute(values, axis, pairs)]
    transpose x2, local copies, waits for them, and re-layouts: 2.84 us -> 0.9 us  [prepare(): jnp.transpose(taps[:, :, ::-1, ::-1, :], (0, 2, 4, 3, 1))]
    optimization_barrier x1, local copies, waits for them, and re-layouts: 1.79 us -> 0.19 us  [shards(): lax.optimization_barrier((states[head], (conv_weight, out_weight, readout...]
    pallas_call x1 -> x2, Pallas kernels: 2.4 us -> 3.19 us  [project(): pl.pallas_call(functools.partial(project_kernel, members), out_shape=(sha...]
    ppermute x8 -> x11, waiting for transfers between devices: 9.07 us -> 9.66 us  [swapped(): return lax.ppermute(values, axis, [(i, i ^ 1) for i in range(size)])]
    unnamed x19 -> x26, local copies, waits for them, and re-layouts: 2.63 us -> 2.11 us
    ppermute x8 -> x11, starting transfers between devices: 6.56 us -> 6.1 us  [swapped(): return lax.ppermute(values, axis, [(i, i ^ 1) for i in range(size)])]
  transfers between devices with their start and end apart: 20 -> 23, of which waited for: 16 -> 17; matrix products, arithmetic and copies ran while one was open for 12% -> 6% of each run, Pallas kernels for 16% -> 17%
where the time goes in v4:
time: 90.9 us; the launch traced here: 90.7 us
  waiting for transfers between devices  35.7 us (39%)
  Pallas kernels  24.2 us (27%)
  starting transfers between devices  20.8 us (23%)
  local copies, waits for them, and re-layouts  4.95 us (5%)
  matrix products  2.91 us (3%)
  other arithmetic  1.09 us (1%)
  between operations  1.06 us (1%)
    ppermute x12, waiting for transfers between devices, passed(): return lax.ppermute(values, axis, pairs)  26 us
    pallas_call x8, Pallas kernels, absorb(): pl.pallas_call(functools.partial(absorb_kernel, first), out_shape=shapes,...  16.3 us
    ppermute x12, starting transfers between devices, passed(): return lax.ppermute(values, axis, pairs)  14.7 us
    ppermute x11, waiting for transfers between devices, swapped(): return lax.ppermute(values, axis, [(i, i ^ 1) for i in range(size)])  9.66 us
    ppermute x11, starting transfers between devices, swapped(): return lax.ppermute(values, axis, [(i, i ^ 1) for i in range(size)])  6.1 us
    pallas_call x1, Pallas kernels, network(): pl.pallas_call(functools.partial(network_kernel, cols, frame_rows), out_s...  3.78 us
    pallas_call x2, Pallas kernels, project(): pl.pallas_call(functools.partial(project_kernel, members), out_shape=(sha...  3.19 us
    unnamed x26, local copies, waits for them, and re-layouts  2.11 us
  transfers between devices with their start and end apart: 23, of which 17 were waited for; matrix products, arithmetic and copies ran while one was open for 6% of the time, Pallas kernels for 17%

profile of v4, /device:TPU:0, one launch (start us, length us, event | category | flops | bytes accessed | tf_op | source)
XLA Modules:
  0.0 90.7 jit_solution(13447693004803729845)
XLA Ops:
  0.7 1.4 %copy-done.2 = bf16[1,512,1024]{2,1,0:T(8,128)(2,1)S(1)} copy-done((bf16[1,512,1024]{2,1,0:T(8,128)(2,1)S(1)}, bf16[1,512,1024]{2,1,0:T(8,128)(2,1)}, u32[]{:S(2)}) %copy-start.2) | copy-done | bytes 1048600
  3.5 1.9 %project.2 = (bf16[2,128,512]{2,1,0:T(8,128)(2,1)S(1)}, bf16[2,128,512]{2,1,0:T(8,128)(2,1)S(1)}) custom-call(s32[3]{0:T(128)S(1)} %pad_add_fusion.place, bf16[512,1024]{1,0:T(8,128)(2,1)S(1)} %normalize.1.normed, bf16[3,1024,256]{2,1,0:T(8,128)(2,1)S(1)} %copy-done.1), custom_call_target="tpu_custom_call" | custom-call | tf_op jit(solution)/shard_map/project/pallas_call | solution.py:70
  8.8 2.8 %collective-permute-start.3 = (bf16[128,1024]{1,0:T(8,128)(2,1)S(1)}, bf16[128,1024]{1,0:T(8,128)(2,1)S(1)}, u32[]{:S(2)}, u32[]{:S(2)}) collective-permute-start(bf16[128,1024]{1,0:T(8,128)(2,1)S(1)} %pad_maximum_fusion.1.refs_1_), channel_id=1, source_target_pairs={{0,4},{2,6},{4,8},{6,10},{8,12},{10,14},{12,0},{14,2},{1,5},{3,7},... | collective-permute-start | bytes 786440 | tf_op jit(solution)/shard_map/ppermute | solution.py:264
  11.5 2.0 %absorb.8 = (f32[80,1024]{1,0:T(8,128)S(1)}, f32[8,1024]{1,0:T(8,128)S(1)}) custom-call(bf16[64,1024]{1,0:T(8,128)(2,1)S(1)} %get-tuple-element.162.refs_0_, bf16[128,1024]{1,0:T(8,128)(2,1)S(1)} %pad_maximum_fusion.1.refs_1_), custom_call_target="tpu_custom_call" | custom-call | tf_op jit(solution)/shard_map/absorb/pallas_call | solution.py:111
  13.6 1.6 %collective-permute-start.1 = (bf16[128,1024]{1,0:T(8,128)(2,1)S(1)}, bf16[128,1024]{1,0:T(8,128)(2,1)S(1)}, u32[]{:S(2)}, u32[]{:S(2)}) collective-permute-start(bf16[128,1024]{1,0:T(8,128)(2,1)S(1)} %pad_maximum_fusion.refs_1_), channel_id=1, source_target_pairs={{0,4},{2,6},{4,8},{6,10},{8,12},{10,14},{12,0},{14,2},{1,5},{3,7},... | collective-permute-start | bytes 786440 | tf_op jit(solution)/shard_map/ppermute | solution.py:264
  15.2 1.5 %collective-permute-start.6 = (f32[2,2,128]{2,1,0:T(2,128)S(1)}, f32[2,2,128]{2,1,0:T(2,128)S(1)}, u32[]{:S(2)}, u32[]{:S(2)}) collective-permute-start(f32[2,2,128]{2,1,0:T(2,128)S(1)} %bitcast.52), channel_id=1, source_target_pairs={{0,1},{1,0},{2,3},{3,2},{4,5},{5,4},{6,7},{7,6},{8,9},{9,8},{10,11... | collective-permute-start | bytes 6152 | tf_op jit(solution)/shard_map/ppermute | solution.py:258
  19.3 1.4 %collective-permute-done.3.refs_1_ = bf16[128,1024]{1,0:T(8,128)(2,1)S(1)} collective-permute-done((bf16[128,1024]{1,0:T(8,128)(2,1)S(1)}, bf16[128,1024]{1,0:T(8,128)(2,1)S(1)}, u32[]{:S(2)}, u32[]{:S(2)}) %collective-permute-start.3) | collective-permute-done | bytes 262176 | tf_op jit(solution)/shard_map/ppermute | solution.py:264
  21.0 2.0 %absorb.9 = (f32[80,1024]{1,0:T(8,128)S(1)}, f32[8,1024]{1,0:T(8,128)S(1)}) custom-call(bf16[64,1024]{1,0:T(8,128)(2,1)S(1)} %get-tuple-element.161.refs_0_, bf16[128,1024]{1,0:T(8,128)(2,1)S(1)} %pad_maximum_fusion.refs_1_), custom_call_target="tpu_custom_call" | custom-call | tf_op jit(solution)/shard_map/absorb/pallas_call | solution.py:111
  23.0 3.4 %collective-permute-done.1.refs_1_ = bf16[128,1024]{1,0:T(8,128)(2,1)S(1)} collective-permute-done((bf16[128,1024]{1,0:T(8,128)(2,1)S(1)}, bf16[128,1024]{1,0:T(8,128)(2,1)S(1)}, u32[]{:S(2)}, u32[]{:S(2)}) %collective-permute-start.1) | collective-permute-done | bytes 262176 | tf_op jit(solution)/shard_map/ppermute | solution.py:264
  26.4 2.1 %absorb.10 = (f32[80,1024]{1,0:T(8,128)S(1)}, f32[8,1024]{1,0:T(8,128)S(1)}) custom-call(bf16[64,1024]{1,0:T(8,128)(2,1)S(1)} %get-tuple-element.162.refs_0_, bf16[128,1024]{1,0:T(8,128)(2,1)S(1)} %collective-permute-done.3.refs_1_, f32[80,1024]{1,0:T(8,128)S(1)} %get-tuple-element.91.refs_2_, ...), custom_call_target="tpu_custom_call", output_to_operand_aliasing={{0}: (2, {}), {1}: (3, {})} | custom-call | tf_op jit(solution)/shard_map/absorb/pallas_call | solution.py:111
  28.4 3.5 %collective-permute-done.5.refs_1_ = bf16[128,1024]{1,0:T(8,128)(2,1)S(1)} collective-permute-done((bf16[128,1024]{1,0:T(8,128)(2,1)S(1)}, bf16[128,1024]{1,0:T(8,128)(2,1)S(1)}, u32[]{:S(2)}, u32[]{:S(2)}) %collective-permute-start.5) | collective-permute-done | bytes 262176 | tf_op jit(solution)/shard_map/ppermute | solution.py:264
  32.0 2.1 %absorb.11 = (f32[80,1024]{1,0:T(8,128)S(1)}, f32[8,1024]{1,0:T(8,128)S(1)}) custom-call(bf16[64,1024]{1,0:T(8,128)(2,1)S(1)} %get-tuple-element.161.refs_0_, bf16[128,1024]{1,0:T(8,128)(2,1)S(1)} %collective-permute-done.1.refs_1_, f32[80,1024]{1,0:T(8,128)S(1)} %get-tuple-element.97.refs_2_, ...), custom_call_target="tpu_custom_call", output_to_operand_aliasing={{0}: (2, {}), {1}: (3, {})} | custom-call | tf_op jit(solution)/shard_map/absorb/pallas_call | solution.py:111
  34.0 3.5 %collective-permute-done.4.refs_1_ = bf16[128,1024]{1,0:T(8,128)(2,1)S(1)} collective-permute-done((bf16[128,1024]{1,0:T(8,128)(2,1)S(1)}, bf16[128,1024]{1,0:T(8,128)(2,1)S(1)}, u32[]{:S(2)}, u32[]{:S(2)}) %collective-permute-start.4) | collective-permute-done | bytes 262176 | tf_op jit(solution)/shard_map/ppermute | solution.py:264
  37.6 2.1 %absorb.12 = (f32[80,1024]{1,0:T(8,128)S(1)}, f32[8,1024]{1,0:T(8,128)S(1)}) custom-call(bf16[64,1024]{1,0:T(8,128)(2,1)S(1)} %get-tuple-element.162.refs_0_, bf16[128,1024]{1,0:T(8,128)(2,1)S(1)} %collective-permute-done.5.refs_1_, f32[80,1024]{1,0:T(8,128)S(1)} %get-tuple-element.110.refs_2_, ...), custom_call_target="tpu_custom_call", output_to_operand_aliasing={{0}: (2, {}), {1}: (3, {})} | custom-call | tf_op jit(solution)/shard_map/absorb/pallas_call | solution.py:111
  39.6 3.6 %collective-permute-done.8.refs_1_ = bf16[128,1024]{1,0:T(8,128)(2,1)S(1)} collective-permute-done((bf16[128,1024]{1,0:T(8,128)(2,1)S(1)}, bf16[128,1024]{1,0:T(8,128)(2,1)S(1)}, u32[]{:S(2)}, u32[]{:S(2)}) %collective-permute-start.8) | collective-permute-done | bytes 262176 | tf_op jit(solution)/shard_map/ppermute | solution.py:264
  43.2 2.1 %absorb.14 = (f32[80,1024]{1,0:T(8,128)S(1)}, f32[8,1024]{1,0:T(8,128)S(1)}) custom-call(bf16[64,1024]{1,0:T(8,128)(2,1)S(1)} %get-tuple-element.162.refs_0_, bf16[128,1024]{1,0:T(8,128)(2,1)S(1)} %collective-permute-done.8.refs_1_, f32[80,1024]{1,0:T(8,128)S(1)} %get-tuple-element.122.refs_2_, ...), custom_call_target="tpu_custom_call", output_to_operand_aliasing={{0}: (2, {}), {1}: (3, {})} | custom-call | tf_op jit(solution)/shard_map/absorb/pallas_call | solution.py:111
  45.3 2.1 %absorb.13 = (f32[80,1024]{1,0:T(8,128)S(1)}, f32[8,1024]{1,0:T(8,128)S(1)}) custom-call(bf16[64,1024]{1,0:T(8,128)(2,1)S(1)} %get-tuple-element.161.refs_0_, bf16[128,1024]{1,0:T(8,128)(2,1)S(1)} %collective-permute-done.4.refs_1_, f32[80,1024]{1,0:T(8,128)S(1)} %get-tuple-element.116.refs_2_, ...), custom_call_target="tpu_custom_call", output_to_operand_aliasing={{0}: (2, {}), {1}: (3, {})} | custom-call | tf_op jit(solution)/shard_map/absorb/pallas_call | solution.py:111
  48.5 2.1 %absorb.15 = (f32[80,1024]{1,0:T(8,128)S(1)}, f32[8,1024]{1,0:T(8,128)S(1)}) custom-call(bf16[64,1024]{1,0:T(8,128)(2,1)S(1)} %get-tuple-element.161.refs_0_, bf16[128,1024]{1,0:T(8,128)(2,1)S(1)} %collective-permute-done.7.refs_1_, f32[80,1024]{1,0:T(8,128)S(1)} %get-tuple-element.128.refs_2_, ...), custom_call_target="tpu_custom_call", output_to_operand_aliasing={{0}: (2, {}), {1}: (3, {})} | custom-call | tf_op jit(solution)/shard_map/absorb/pallas_call | solution.py:111
  51.0 1.3 %collective-permute-done.9 = f32[64,512]{1,0:T(8,128)S(1)} collective-permute-done((f32[64,512]{1,0:T(8,128)S(1)}, f32[64,512]{1,0:T(8,128)S(1)}, u32[]{:S(2)}, u32[]{:S(2)}) %collective-permute-start.9) | collective-permute-done | bytes 131104 | tf_op jit(solution)/shard_map/ppermute | solution.py:258
  52.3 1.5 %collective-permute-start.10 = (f32[64,512]{1,0:T(8,128)S(1)}, f32[64,512]{1,0:T(8,128)S(1)}, u32[]{:S(2)}, u32[]{:S(2)}) collective-permute-start(f32[64,512]{1,0:T(8,128)S(1)} %slice_add_fusion), channel_id=1, source_target_pairs={{0,1},{1,0},{2,3},{3,2},{4,5},{5,4},{6,7},{7,6},{8,9},{9,8},{10,11... | collective-permute-start | bytes 393224 | tf_op jit(solution)/shard_map/ppermute | solution.py:258
  53.9 4.1 %collective-permute-done.10 = f32[64,512]{1,0:T(8,128)S(1)} collective-permute-done((f32[64,512]{1,0:T(8,128)S(1)}, f32[64,512]{1,0:T(8,128)S(1)}, u32[]{:S(2)}, u32[]{:S(2)}) %collective-permute-start.10) | collective-permute-done | bytes 131104 | tf_op jit(solution)/shard_map/ppermute | solution.py:258
  58.0 1.6 %collective-permute-start.12 = (bf16[80,512]{1,0:T(8,128)(2,1)S(1)}, bf16[80,512]{1,0:T(8,128)(2,1)S(1)}, u32[]{:S(2)}, u32[]{:S(2)}) collective-permute-start(bf16[80,512]{1,0:T(8,128)(2,1)S(1)} %pad_maximum_fusion.4.own_map), channel_id=1, source_target_pairs={{0,4},{2,6},{4,8},{6,10},{8,12},{10,14},{1,5},{3,7},{5,9},{7,11},{... | collective-permute-start | bytes 245768 | tf_op jit(solution)/shard_map/ppermute | solution.py:264
  61.7 4.3 %collective-permute-done.13 = bf16[80,512]{1,0:T(8,128)(2,1)S(1)} collective-permute-done((bf16[80,512]{1,0:T(8,128)(2,1)S(1)}, bf16[80,512]{1,0:T(8,128)(2,1)S(1)}, u32[]{:S(2)}, u32[]{:S(2)}) %collective-permute-start.13) | collective-permute-done | bytes 81952 | tf_op jit(solution)/shard_map/ppermute | solution.py:264
  67.5 3.8 %network.1 = (f32[2,1024]{1,0:T(2,128)S(1)}, f32[32,576]{1,0:T(8,128)S(1)}, f32[64,128]{1,0:T(8,128)S(1)}) custom-call(s32[3]{0:T(128)S(1)} %pad_add_fusion.place, bf16[80,512]{1,0:T(8,128)(2,1)S(1)} %pad_maximum_fusion.4.own_map, bf16[80,512]{1,0:T(8,128)(2,1)S(1)} %collective-permute-done.11.other_map, ...), custom_call_target="tpu_custom_call" | custom-call | tf_op jit(solution)/shard_map/network/pallas_call | solution.py:241
  71.3 1.6 %collective-permute-start.15 = (bf16[32,896]{1,0:T(8,128)(2,1)S(1)}, bf16[32,896]{1,0:T(8,128)(2,1)S(1)}, u32[]{:S(2)}, u32[]{:S(2)}) collective-permute-start(bf16[32,896]{1,0:T(8,128)(2,1)S(1)} %fusion.14), channel_id=1, source_target_pairs={{0,16},{16,0},{1,17},{17,1},{2,18},{18,2},{3,19},{19,3},{4,20},{20... | collective-permute-start | bytes 172040 | tf_op jit(solution)/shard_map/ppermute | solution.py:264
  72.9 2.6 %collective-permute-done.15 = bf16[32,896]{1,0:T(8,128)(2,1)S(1)} collective-permute-done((bf16[32,896]{1,0:T(8,128)(2,1)S(1)}, bf16[32,896]{1,0:T(8,128)(2,1)S(1)}, u32[]{:S(2)}, u32[]{:S(2)}) %collective-permute-start.15) | collective-permute-done | bytes 57376 | tf_op jit(solution)/shard_map/ppermute | solution.py:264
  75.6 1.6 %collective-permute-start.16 = (bf16[32,896]{1,0:T(8,128)(2,1)S(1)}, bf16[32,896]{1,0:T(8,128)(2,1)S(1)}, u32[]{:S(2)}, u32[]{:S(2)}) collective-permute-start(bf16[32,896]{1,0:T(8,128)(2,1)S(1)} %add_convert_fusion.1), channel_id=1, source_target_pairs={{0,4},{2,6},{4,8},{6,10},{8,12},{10,14},{12,0},{14,2},{1,5},{3,7},... | collective-permute-start | bytes 172040 | tf_op jit(solution)/shard_map/ppermute | solution.py:264
  78.3 2.8 %collective-permute-start.18 = (bf16[32,896]{1,0:T(8,128)(2,1)S(1)}, bf16[32,896]{1,0:T(8,128)(2,1)S(1)}, u32[]{:S(2)}, u32[]{:S(2)}) collective-permute-start(bf16[32,896]{1,0:T(8,128)(2,1)S(1)} %add_convert_fusion.1), channel_id=1, source_target_pairs={{0,12},{2,14},{4,0},{6,2},{8,4},{10,6},{12,8},{14,10},{1,13},{3,15... | collective-permute-start | bytes 172040 | tf_op jit(solution)/shard_map/ppermute | solution.py:264
  82.2 1.4 %collective-permute-done.17 = bf16[32,896]{1,0:T(8,128)(2,1)S(1)} collective-permute-done((bf16[32,896]{1,0:T(8,128)(2,1)S(1)}, bf16[32,896]{1,0:T(8,128)(2,1)S(1)}, u32[]{:S(2)}, u32[]{:S(2)}) %collective-permute-start.17) | collective-permute-done | bytes 57376 | tf_op jit(solution)/shard_map/ppermute | solution.py:264
  83.8 1.6 %collective-permute-start.19 = (f32[32,576]{1,0:T(8,128)S(1)}, f32[32,576]{1,0:T(8,128)S(1)}, u32[]{:S(2)}, u32[]{:S(2)}) collective-permute-start(f32[32,576]{1,0:T(8,128)S(1)} %get-tuple-element.154), channel_id=1, source_target_pairs={{0,1},{1,0},{2,3},{3,2},{4,5},{5,4},{6,7},{7,6},{8,9},{9,8},{10,11... | collective-permute-start | bytes 221192 | tf_op jit(solution)/shard_map/ppermute | solution.py:258
  85.6 1.6 %fusion.3 = f32[256,1024]{1,0:T(8,128)} fusion(bf16[1024,64]{0,1:T(8,128)(2,1)S(1)} %copy-done.6, f32[64,128]{1,0:T(8,128)S(1)} %collective-permute-done.20, f32[32,128]{1,0:T(8,128)S(1)} %get-tuple-element.156, f32[32,128]{1,0:T(8,128)S(1)} %get-tuple-element.155, pred[]{:T(512)S(6)} %eq.10), kind=kOutput, calls=%fused_computation.25 | convolution fusion | flops 201408512 | bytes 1245185 | tf_op jit(solution)/shard_map/dot_general | solution.py:375
  87.2 1.5 %collective-permute-done.19 = f32[32,576]{1,0:T(8,128)S(1)} collective-permute-done((f32[32,576]{1,0:T(8,128)S(1)}, f32[32,576]{1,0:T(8,128)S(1)}, u32[]{:S(2)}, u32[]{:S(2)}) %collective-permute-start.19) | collective-permute-done | bytes 73760 | tf_op jit(solution)/shard_map/ppermute | solution.py:258
  (93 shorter events, 17.5 us)
Async XLA Ops:
  0.6 17.2 %copy-start = (bf16[256,1024]{1,0:T(8,128)(2,1)S(1)}, bf16[256,1024]{1,0:T(8,128)(2,1)}, u32[]{:S(2)}) copy-start(bf16[256,1024]{1,0:T(8,128)(2,1)} %param.11) | copy-start | bytes 1572868
  5.4 3.4 %collective-permute-start = (bf16[2,128,512]{2,1,0:T(8,128)(2,1)S(1)}, bf16[2,128,512]{2,1,0:T(8,128)(2,1)S(1)}, u32[]{:S(2)}, u32[]{:S(2)}) collective-permute-start(bf16[2,128,512]{2,1,0:T(8,128)(2,1)S(1)} %get-tuple-element.77), channel_id=1, source_target_pairs={{0,2},{2,0},{4,6},{6,4},{8,10},{10,8},{12,14},{14,12},{1,3},{3,1},... | collective-permute-start | bytes 786440 | tf_op jit(solution)/shard_map/ppermute | solution.py:258
  7.3 1.4 %collective-permute-start.2 = (bf16[2,64,512]{2,1,0:T(8,128)(2,1)S(1)}, bf16[2,64,512]{2,1,0:T(8,128)(2,1)S(1)}, u32[]{:S(2)}, u32[]{:S(2)}) collective-permute-start(bf16[2,64,512]{2,1,0:T(8,128)(2,1)S(1)} %get-tuple-element.80), channel_id=1, source_target_pairs={{0,2},{2,0},{4,6},{6,4},{8,10},{10,8},{12,14},{14,12},{1,3},{3,1},... | collective-permute-start | bytes 393224 | tf_op jit(solution)/shard_map/ppermute | solution.py:258
  8.0 7.2 %copy-start.11 = (f32[1,2,2,128]{3,2,1,0:T(2,128)S(1)}, f32[1,2,2,128]{3,2,1,0:T(2,128)}, u32[]{:S(2)}) copy-start(f32[1,2,2,128]{3,2,1,0:T(2,128)} %param.15) | copy-start | bytes 6148
  8.0 8.7 %copy-start.3 = (bf16[1,512,1024]{2,1,0:T(8,128)(2,1)S(1)}, bf16[1,512,1024]{2,1,0:T(8,128)(2,1)}, u32[]{:S(2)}) copy-start(bf16[1,512,1024]{2,1,0:T(8,128)(2,1)} %param.8) | copy-start | bytes 3145732
  8.0 8.7 %copy-start.6 = (bf16[1024,64]{0,1:T(8,128)(2,1)S(1)}, bf16[1024,64]{0,1:T(8,128)(2,1)}, u32[]{:S(2)}) copy-start(bf16[1024,64]{0,1:T(8,128)(2,1)} %param.12) | copy-start | bytes 393220
  8.0 5.5 %copy-start.10 = (bf16[128,512]{1,0:T(8,128)(2,1)S(1)}, bf16[128,512]{1,0:T(8,128)(2,1)}, u32[]{:S(2)}) copy-start(bf16[128,512]{1,0:T(8,128)(2,1)} %get-tuple-element.146) | copy-start | bytes 393220
  8.7 9.3 %copy-start.8 = (bf16[2,64,576]{2,1,0:T(8,128)(2,1)S(1)}, bf16[2,64,576]{2,1,0:T(8,128)(2,1)}, u32[]{:S(2)}) copy-start(bf16[2,64,576]{2,1,0:T(8,128)(2,1)} %param.13) | copy-start | bytes 442372
  8.8 11.9 %collective-permute-start.3 = (bf16[128,1024]{1,0:T(8,128)(2,1)S(1)}, bf16[128,1024]{1,0:T(8,128)(2,1)S(1)}, u32[]{:S(2)}, u32[]{:S(2)}) collective-permute-start(bf16[128,1024]{1,0:T(8,128)(2,1)S(1)} %pad_maximum_fusion.1.refs_1_), channel_id=1, source_target_pairs={{0,4},{2,6},{4,8},{6,10},{8,12},{10,14},{12,0},{14,2},{1,5},{3,7},... | collective-permute-start | bytes 786440 | tf_op jit(solution)/shard_map/ppermute | solution.py:264
  13.6 12.8 %collective-permute-start.1 = (bf16[128,1024]{1,0:T(8,128)(2,1)S(1)}, bf16[128,1024]{1,0:T(8,128)(2,1)S(1)}, u32[]{:S(2)}, u32[]{:S(2)}) collective-permute-start(bf16[128,1024]{1,0:T(8,128)(2,1)S(1)} %pad_maximum_fusion.refs_1_), channel_id=1, source_target_pairs={{0,4},{2,6},{4,8},{6,10},{8,12},{10,14},{12,0},{14,2},{1,5},{3,7},... | collective-permute-start | bytes 786440 | tf_op jit(solution)/shard_map/ppermute | solution.py:264
  15.2 5.8 %collective-permute-start.6 = (f32[2,2,128]{2,1,0:T(2,128)S(1)}, f32[2,2,128]{2,1,0:T(2,128)S(1)}, u32[]{:S(2)}, u32[]{:S(2)}) collective-permute-start(f32[2,2,128]{2,1,0:T(2,128)S(1)} %bitcast.52), channel_id=1, source_target_pairs={{0,1},{1,0},{2,3},{3,2},{4,5},{5,4},{6,7},{7,6},{8,9},{9,8},{10,11... | collective-permute-start | bytes 6152 | tf_op jit(solution)/shard_map/ppermute | solution.py:258
  20.7 11.2 %collective-permute-start.5 = (bf16[128,1024]{1,0:T(8,128)(2,1)S(1)}, bf16[128,1024]{1,0:T(8,128)(2,1)S(1)}, u32[]{:S(2)}, u32[]{:S(2)}) collective-permute-start(bf16[128,1024]{1,0:T(8,128)(2,1)S(1)} %collective-permute-done.3.refs_1_), channel_id=1, source_target_pairs={{0,4},{2,6},{4,8},{6,10},{8,12},{10,14},{12,0},{14,2},{1,5},{3,7},... | collective-permute-start | bytes 786440 | tf_op jit(solution)/shard_map/ppermute | solution.py:264
  26.3 11.2 %collective-permute-start.4 = (bf16[128,1024]{1,0:T(8,128)(2,1)S(1)}, bf16[128,1024]{1,0:T(8,128)(2,1)S(1)}, u32[]{:S(2)}, u32[]{:S(2)}) collective-permute-start(bf16[128,1024]{1,0:T(8,128)(2,1)S(1)} %collective-permute-done.1.refs_1_), channel_id=1, source_target_pairs={{0,4},{2,6},{4,8},{6,10},{8,12},{10,14},{12,0},{14,2},{1,5},{3,7},... | collective-permute-start | bytes 786440 | tf_op jit(solution)/shard_map/ppermute | solution.py:264
  32.0 11.2 %collective-permute-start.8 = (bf16[128,1024]{1,0:T(8,128)(2,1)S(1)}, bf16[128,1024]{1,0:T(8,128)(2,1)S(1)}, u32[]{:S(2)}, u32[]{:S(2)}) collective-permute-start(bf16[128,1024]{1,0:T(8,128)(2,1)S(1)} %collective-permute-done.5.refs_1_), channel_id=1, source_target_pairs={{0,4},{2,6},{4,8},{6,10},{8,12},{10,14},{12,0},{14,2},{1,5},{3,7},... | collective-permute-start | bytes 786440 | tf_op jit(solution)/shard_map/ppermute | solution.py:264
  37.6 10.9 %collective-permute-start.7 = (bf16[128,1024]{1,0:T(8,128)(2,1)S(1)}, bf16[128,1024]{1,0:T(8,128)(2,1)S(1)}, u32[]{:S(2)}, u32[]{:S(2)}) collective-permute-start(bf16[128,1024]{1,0:T(8,128)(2,1)S(1)} %collective-permute-done.4.refs_1_), channel_id=1, source_target_pairs={{0,4},{2,6},{4,8},{6,10},{8,12},{10,14},{12,0},{14,2},{1,5},{3,7},... | collective-permute-start | bytes 786440 | tf_op jit(solution)/shard_map/ppermute | solution.py:264
  45.3 12.7 %copy-start.9 = (f32[64,512]{1,0:T(8,128)S(1)}, f32[64,512]{1,0:T(8,128)}, u32[]{:S(2)}) copy-start(f32[64,512]{1,0:T(8,128)} %fusion.27) | copy-start | bytes 393220
  47.3 19.1 %copy-start.7 = (bf16[2,3,64,3,64]{2,4,3,1,0:T(8,128)(2,1)S(1)}, bf16[2,3,64,3,64]{2,4,3,1,0:T(8,128)(2,1)}, u32[]{:S(2)}) copy-start(bf16[2,3,64,3,64]{2,4,3,1,0:T(8,128)(2,1)} %copy.26) | copy-start | bytes 442372
  50.6 16.9 %copy-start.5 = (bf16[2,64]{1,0:T(2,128)(2,1)S(1)}, bf16[2,64]{1,0:T(2,128)(2,1)}, u32[]{:S(2)}) copy-start(bf16[2,64]{1,0:T(2,128)(2,1)} %head.1) | copy-start | bytes 772
  50.9 1.4 %collective-permute-start.9 = (f32[64,512]{1,0:T(8,128)S(1)}, f32[64,512]{1,0:T(8,128)S(1)}, u32[]{:S(2)}, u32[]{:S(2)}) collective-permute-start(f32[64,512]{1,0:T(8,128)S(1)} %slice.56), channel_id=1, source_target_pairs={{0,2},{2,0},{4,6},{6,4},{8,10},{10,8},{12,14},{14,12},{1,3},{3,1},... | collective-permute-start | bytes 393224 | tf_op jit(solution)/shard_map/ppermute | solution.py:258
  52.3 5.6 %collective-permute-start.10 = (f32[64,512]{1,0:T(8,128)S(1)}, f32[64,512]{1,0:T(8,128)S(1)}, u32[]{:S(2)}, u32[]{:S(2)}) collective-permute-start(f32[64,512]{1,0:T(8,128)S(1)} %slice_add_fusion), channel_id=1, source_target_pairs={{0,1},{1,0},{2,3},{3,2},{4,5},{5,4},{6,7},{7,6},{8,9},{9,8},{10,11... | collective-permute-start | bytes 393224 | tf_op jit(solution)/shard_map/ppermute | solution.py:258
  58.0 3.7 %collective-permute-start.12 = (bf16[80,512]{1,0:T(8,128)(2,1)S(1)}, bf16[80,512]{1,0:T(8,128)(2,1)S(1)}, u32[]{:S(2)}, u32[]{:S(2)}) collective-permute-start(bf16[80,512]{1,0:T(8,128)(2,1)S(1)} %pad_maximum_fusion.4.own_map), channel_id=1, source_target_pairs={{0,4},{2,6},{4,8},{6,10},{8,12},{10,14},{1,5},{3,7},{5,9},{7,11},{... | collective-permute-start | bytes 245768 | tf_op jit(solution)/shard_map/ppermute | solution.py:264
  59.6 6.3 %collective-permute-start.13 = (bf16[80,512]{1,0:T(8,128)(2,1)S(1)}, bf16[80,512]{1,0:T(8,128)(2,1)S(1)}, u32[]{:S(2)}, u32[]{:S(2)}) collective-permute-start(bf16[80,512]{1,0:T(8,128)(2,1)S(1)} %pad_maximum_fusion.4.own_map), channel_id=1, source_target_pairs={{4,0},{6,2},{8,4},{10,6},{12,8},{14,10},{5,1},{7,3},{9,5},{11,7},{... | collective-permute-start | bytes 245768 | tf_op jit(solution)/shard_map/ppermute | solution.py:264
  66.0 1.5 %collective-permute-start.14 = (bf16[80,1024]{1,0:T(8,128)(2,1)S(1)}, bf16[80,1024]{1,0:T(8,128)(2,1)S(1)}, u32[]{:S(2)}, u32[]{:S(2)}) collective-permute-start(bf16[80,1024]{1,0:T(8,128)(2,1)S(1)} %constant_dynamic-update-slice_fusion.rims), channel_id=1, source_target_pairs={{0,2},{2,0},{4,6},{6,4},{8,10},{10,8},{12,14},{14,12},{1,3},{3,1},... | collective-permute-start | bytes 491528 | tf_op jit(solution)/shard_map/ppermute | solution.py:258
  66.0 1.5 %collective-permute-start.11 = (bf16[80,512]{1,0:T(8,128)(2,1)S(1)}, bf16[80,512]{1,0:T(8,128)(2,1)S(1)}, u32[]{:S(2)}, u32[]{:S(2)}) collective-permute-start(bf16[80,512]{1,0:T(8,128)(2,1)S(1)} %pad_maximum_fusion.4.own_map), channel_id=1, source_target_pairs={{0,2},{2,0},{4,6},{6,4},{8,10},{10,8},{12,14},{14,12},{1,3},{3,1},... | collective-permute-start | bytes 245768 | tf_op jit(solution)/shard_map/ppermute | solution.py:258
  71.3 4.2 %collective-permute-start.15 = (bf16[32,896]{1,0:T(8,128)(2,1)S(1)}, bf16[32,896]{1,0:T(8,128)(2,1)S(1)}, u32[]{:S(2)}, u32[]{:S(2)}) collective-permute-start(bf16[32,896]{1,0:T(8,128)(2,1)S(1)} %fusion.14), channel_id=1, source_target_pairs={{0,16},{16,0},{1,17},{17,1},{2,18},{18,2},{3,19},{19,3},{4,20},{20... | collective-permute-start | bytes 172040 | tf_op jit(solution)/shard_map/ppermute | solution.py:264
  75.6 6.7 %collective-permute-start.16 = (bf16[32,896]{1,0:T(8,128)(2,1)S(1)}, bf16[32,896]{1,0:T(8,128)(2,1)S(1)}, u32[]{:S(2)}, u32[]{:S(2)}) collective-permute-start(bf16[32,896]{1,0:T(8,128)(2,1)S(1)} %add_convert_fusion.1), channel_id=1, source_target_pairs={{0,4},{2,6},{4,8},{6,10},{8,12},{10,14},{12,0},{14,2},{1,5},{3,7},... | collective-permute-start | bytes 172040 | tf_op jit(solution)/shard_map/ppermute | solution.py:264
  77.2 6.4 %collective-permute-start.17 = (bf16[32,896]{1,0:T(8,128)(2,1)S(1)}, bf16[32,896]{1,0:T(8,128)(2,1)S(1)}, u32[]{:S(2)}, u32[]{:S(2)}) collective-permute-start(bf16[32,896]{1,0:T(8,128)(2,1)S(1)} %add_convert_fusion.1), channel_id=1, source_target_pairs={{0,8},{2,10},{4,12},{6,14},{8,0},{10,2},{12,4},{14,6},{1,9},{3,11}... | collective-permute-start | bytes 172040 | tf_op jit(solution)/shard_map/ppermute | solution.py:264
  78.3 5.3 %collective-permute-start.18 = (bf16[32,896]{1,0:T(8,128)(2,1)S(1)}, bf16[32,896]{1,0:T(8,128)(2,1)S(1)}, u32[]{:S(2)}, u32[]{:S(2)}) collective-permute-start(bf16[32,896]{1,0:T(8,128)(2,1)S(1)} %add_convert_fusion.1), channel_id=1, source_target_pairs={{0,12},{2,14},{4,0},{6,2},{8,4},{10,6},{12,8},{14,10},{1,13},{3,15... | collective-permute-start | bytes 172040 | tf_op jit(solution)/shard_map/ppermute | solution.py:264
  83.7 1.9 %collective-permute-start.20 = (f32[64,128]{1,0:T(8,128)S(1)}, f32[64,128]{1,0:T(8,128)S(1)}, u32[]{:S(2)}, u32[]{:S(2)}) collective-permute-start(f32[64,128]{1,0:T(8,128)S(1)} %pad_maximum_fusion.5), channel_id=1, source_target_pairs={{0,2},{2,0},{4,6},{6,4},{8,10},{10,8},{12,14},{14,12},{1,3},{3,1},... | collective-permute-start | bytes 98312 | tf_op jit(solution)/shard_map/ppermute | solution.py:258
  83.8 4.9 %collective-permute-start.19 = (f32[32,576]{1,0:T(8,128)S(1)}, f32[32,576]{1,0:T(8,128)S(1)}, u32[]{:S(2)}, u32[]{:S(2)}) collective-permute-start(f32[32,576]{1,0:T(8,128)S(1)} %get-tuple-element.154), channel_id=1, source_target_pairs={{0,1},{1,0},{2,3},{3,2},{4,5},{5,4},{6,7},{7,6},{8,9},{9,8},{10,11... | collective-permute-start | bytes 221192 | tf_op jit(solution)/shard_map/ppermute | solution.py:258
  85.4 3.3 %collective-permute-start.21 = (f32[32,576]{1,0:T(8,128)S(1)}, f32[32,576]{1,0:T(8,128)S(1)}, u32[]{:S(2)}, u32[]{:S(2)}) collective-permute-start(f32[32,576]{1,0:T(8,128)S(1)} %get-tuple-element.154), channel_id=1, source_target_pairs={{0,2},{2,0},{4,6},{6,4},{8,10},{10,8},{12,14},{14,12},{1,3},{3,1},... | collective-permute-start | bytes 221192 | tf_op jit(solution)/shard_map/ppermute | solution.py:258
  88.7 1.3 %collective-permute-start.22 = (f32[32,576]{1,0:T(8,128)S(1)}, f32[32,576]{1,0:T(8,128)S(1)}, u32[]{:S(2)}, u32[]{:S(2)}) collective-permute-start(f32[32,576]{1,0:T(8,128)S(1)} %collective-permute-done.19), channel_id=1, source_target_pairs={{0,2},{2,0},{4,6},{6,4},{8,10},{10,8},{12,14},{14,12},{1,3},{3,1},... | collective-permute-start | bytes 221192 | tf_op jit(solution)/shard_map/ppermute | solution.py:258
  (3 other events, 4.9 us)

commit v5 on v4

--- a/solution.py
+++ b/solution.py
@@ -49,19 +49,19 @@
     )(tokens, gain)
 
 
-def project_kernel(members, place, normed, weight, mine, theirs):
+def project_kernel(members, place, normed, weight, mine, theirs, turned):
     core = place[0]
     kept = mine.shape[0] * HEAD
     rows = normed[...]
-    for which, out in ((1 - core, theirs), (core, mine)):
-        for at, member in enumerate(members):
-            part = weight[member, :, pl.ds(pl.multiple_of(which * kept, 128), kept)]
-            product = dot(rows, part).astype(BF16)
-            if member == 0:
-                product = product * jnp.asarray(1.0 / HEAD**0.5, BF16)
-            turned = product.T
+    for at, member in enumerate(members):
+        product = dot(rows, weight[member]).astype(BF16)
+        if member == 0:
+            product = product * jnp.asarray(1.0 / HEAD**0.5, BF16)
+        turned[at] = product.T
+        for which, out in ((1 - core, theirs), (core, mine)):
             for head in range(mine.shape[0]):
-                out[head, at * HEAD : (at + 1) * HEAD, :] = turned[head * HEAD : (head + 1) * HEAD, :]
+                start = pl.multiple_of(which * kept + head * HEAD, HEAD)
+                out[head, at * HEAD : (at + 1) * HEAD, :] = turned[at, pl.ds(start, HEAD), :]
 
 
 def project(members, place, normed, weight):
@@ -72,6 +72,7 @@
         out_shape=(shape, shape),
         in_specs=[SMEM, VMEM, VMEM],
         out_specs=(VMEM,) * 2,
+        scratch_shapes=[pltpu.VMEM((len(members), weight.shape[2], length), BF16)],
         compiler_params=PARAMS,
         name="project",
     )(place, normed, weight)
@@ -161,7 +162,7 @@
 
 
 def network_kernel(
-    cols, frame_rows, place, own_map, other_map, rims, other_rims, forward, backward, head, context, holo, sums,
+    cols, frame_rows, place, mine, theirs, forward, backward, head, context, holo, sums,
     gradient, hidden, pre_one, pre_two,
 ):
     core, half, row_at = place[0], place[1], place[2]
@@ -172,12 +173,10 @@
     above = rim // cols
     first_row = row_at - above
     piece = own // 2
-    for order, (mine, theirs, at) in enumerate(
-        ((rims, other_rims, 0), (own_map, other_map, 0), (rims, other_rims, piece))
-    ):
+    for order in range(3):
         for which, source in ((core, mine), (1 - core, theirs)):
             start = pl.multiple_of(order * own + which * piece, 128)
-            hidden[:, pl.ds(start, piece)] = source[:, at : at + piece]
+            hidden[:, pl.ds(start, piece)] = source[:, order * piece : (order + 1) * piece]
 
     def inside(start_row, rows):
         lane = lax.broadcasted_iota(jnp.int32, (1, rows * cols), 1)
@@ -245,7 +244,7 @@
             jax.ShapeDtypeStruct((channels // col_count, 9 * channels), F32),
             jax.ShapeDtypeStruct((channels, context.shape[0]), F32),
         ),
-        in_specs=[SMEM] + [VMEM] * 8,
+        in_specs=[SMEM] + [VMEM] * 6,
         out_specs=(VMEM,) * 3,
         scratch_shapes=[pltpu.VMEM((maps[0].shape[0], 3 * own), BF16)] + [pltpu.VMEM((channels, own), BF16)] * 2,
         compiler_params=PARAMS,
@@ -258,18 +257,59 @@
     return lax.ppermute(values, axis, [(i, i ^ 1) for i in range(size)])
 
 
-def passed(values, axis, step, wrap):
-    size = lax.axis_size(axis)
-    pairs = [(i, (i + step) % size) for i in range(size) if wrap or 0 <= i + step < size]
-    return lax.ppermute(values, axis, pairs)
-
-
-def everyone(values, axis, stride, count):
-    sent = values.astype(BF16)
-    total = sent.astype(F32)
-    for step in range(1, count):
-        total = total + passed(sent, axis, stride * step, True).astype(F32)
-    return total
+def passed(values, step, across):
+    size, cols = lax.axis_size("tok"), lax.axis_size("col")
+    pairs = [
+        (i * cols + j, (i + step) * cols + (j ^ 1 if across else j))
+        for i in range(size)
+        for j in range(cols)
+        if 0 <= i + step < size
+    ]
+    return lax.ppermute(values, ("tok", "col"), pairs)
+
+
+def round_ring(values):
+    size = lax.axis_size("tok")
+    chips = size // 2
+    order = [at for at in range(chips) if at == 0 or at % 2 == 1] + [
+        at for at in reversed(range(chips)) if at and at % 2 == 0
+    ]
+    following = {order[at]: order[(at + 1) % chips] for at in range(chips)}
+    return lax.ppermute(values, "tok", [(i, 2 * following[i // 2] + i % 2) for i in range(size)])
+
+
+def tree_sum(terms):
+    while len(terms) > 1:
+        terms = [sum(terms[at : at + 2][1:], terms[at]) for at in range(0, len(terms), 2)]
+    return terms[0]
+
+
+def other_place(at, step, count):
+    return at ^ step if count & (count - 1) == 0 else (at + step) % count
+
+
+def sum_chips(values):
+    size = lax.axis_size("tok")
+    chips = size // 2
+    terms = [values.astype(F32)]
+    for step in range(1, chips):
+        pairs = [(i, 2 * other_place(i // 2, step, chips) + i % 2) for i in range(size)]
+        terms.append(lax.ppermute(values, "tok", pairs).astype(F32))
+    return tree_sum(terms)
+
+
+def sum_frames(values, across):
+    size, cols = lax.axis_size("dp"), lax.axis_size("col")
+    terms = []
+    for step in range(size):
+        pairs = [
+            (i * cols + j, other_place(i, step, size) * cols + (j ^ 1 if across else j))
+            for i in range(size)
+            for j in range(cols)
+        ]
+        moved = lax.ppermute(values, ("dp", "col"), pairs) if step or across else values
+        terms.append(moved.astype(F32))
+    return tree_sum(terms)
 
 
 def in_order(core, mine, theirs, axis):
@@ -321,7 +361,7 @@
         return (forward, backward, folded, direct, exact_cot)
 
     for turn in range(chips):
-        arriving = [passed(block, "tok", 2, True) for block in blocks] if turn < chips - 1 else blocks
+        arriving = [round_ring(block) for block in blocks] if turn < chips - 1 else blocks
         for head in range(count):
             states[head] = absorb(queries[head], blocks[head], states[head])
             if turn == 0 and head == 0:
@@ -344,11 +384,21 @@
 
     context, share = finish([state[0] for state in states], folded)
     partial = share[:, :length] + swapped(share[:, length:], "tok")
-    own_map = (partial + swapped(partial, "col") + direct).astype(BF16)
-    own_map = jnp.concatenate([own_map, exact_cot], axis=0)
-    rims = jnp.concatenate([passed(own_map, "tok", 2, False), passed(own_map, "tok", -2, False)], axis=1)
+    partial = (partial + jnp.where(half == 0, direct, 0.0)).astype(BF16)
+    with_cot = jnp.concatenate([partial, exact_cot], axis=0)
+    near = (passed(with_cot, 2, False), with_cot, passed(with_cot, -2, False))
+    far = (passed(partial, 2, True), swapped(partial, "col"), passed(partial, -2, True))
+    maps = jnp.concatenate(
+        [
+            jnp.concatenate(
+                [(ours[:channels].astype(F32) + others.astype(F32)).astype(BF16), ours[channels:]], axis=0
+            )
+            for ours, others in zip(near, far)
+        ],
+        axis=1,
+    )
     rows_chip = 2 * rows_dev
-    maps = (own_map, swapped(own_map, "tok"), rims, swapped(rims, "tok"))
+    maps = (maps, swapped(maps, "tok"))
     holo, sums, gradient = network(
         place, maps, forward, backward, head_weight, context, cols, tok_count * rows_dev, col_count
     )
@@ -363,24 +413,19 @@
     pieces = gradient.shape[0] // rows
     folded_gradient = [gradient[at * rows : (at + 1) * rows] for at in range(pieces)]
     sent = jnp.concatenate([jnp.pad(sums, ((0, 0), (0, lanes - taps_wide))), *folded_gradient], axis=1)
-    summed = everyone(sent, "dp", 1, dp_count)
-    total = everyone(summed, "tok", 2, chips)
-    own_grad = total[:, :taps_wide]
-    col_grad = swapped(own_grad, "col")
+    summed = sum_chips(sent.astype(BF16)).astype(BF16)
+    summed_taps = summed[:, :taps_wide]
+    own_terms, far_terms = sum_frames(summed, False), sum_frames(summed_taps, True)
     wide = gradient.shape[1]
     own_small = jnp.concatenate(
-        [total[:, lanes + at * wide : lanes + (at + 1) * wide] for at in range(pieces)], axis=0
+        [own_terms[:, lanes + at * wide : lanes + (at + 1) * wide] for at in range(pieces)], axis=0
     )
     small = in_order(core, own_small, swapped(own_small, "tok"), 1)
     out_grad = lax.dot_general(
         small, readout_weight.astype(F32), (((0,), (1,)), ((), ())), precision=lax.Precision.HIGHEST
     )
-    core_grad = swapped(own_grad, "tok")
-    col_grad, out_grad, core_grad = lax.optimization_barrier((col_grad, out_grad, core_grad))
-    far_grad = swapped(col_grad, "tok")
-    layer_grad = in_order(half, own_grad, col_grad, 0)
-    other_grad = in_order(half, core_grad, far_grad, 0)
-    conv_grad = in_order(core, layer_grad[None], other_grad[None], 0)
+    layer_grad = in_order(half, own_terms[:, :taps_wide], far_terms, 0)
+    conv_grad = in_order(core, layer_grad[None], swapped(layer_grad, "tok")[None], 0)
     return (hologram[None], conv_grad, out_grad)
 
 

time: 90.9 us -> 94.7 us (1.042)
  starting transfers between devices: 20.8 us -> 31 us
  waiting for transfers between devices: 35.7 us -> 29.9 us
    ppermute x12 -> x16, starting transfers between devices: 14.7 us -> 27.5 us  [the longest x4 9.64 us: passed(): return lax.ppermute(values, ('tok', 'col'), pairs)]
    ppermute x11 -> x8, waiting for transfers between devices: 9.66 us -> 3.89 us  [swapped(): return lax.ppermute(values, axis, [(i, i ^ 1) for i in range(size)])]
    ppermute x11 -> x8, starting transfers between devices: 6.1 us -> 3.48 us  [swapped(): return lax.ppermute(values, axis, [(i, i ^ 1) for i in range(size)])]
    ppermute x12 -> x16, waiting for transfers between devices: 26 us -> 26 us  [the longest x6 10.8 us: round_ring(): lax.ppermute(values, 'tok', [(i, 2 * following[i // 2] + i % 2) for i in...]
    unnamed x26 -> x25, local copies, waits for them, and re-layouts: 2.11 us -> 2.1 us
  transfers between devices with their start and end apart: 23 -> 24, of which waited for: 17 -> 15; matrix products, arithmetic and copies ran while one was open for 6% -> 6% of each run, Pallas kernels for 17% -> 16%
where the time goes in v5:
time: 94.7 us; the launch traced here: 94.5 us
  starting transfers between devices  31 us (33%)
  waiting for transfers between devices  29.9 us (32%)
  Pallas kernels  23.5 us (25%)
  local copies, waits for them, and re-layouts  4.95 us (5%)
  matrix products  2.91 us (3%)
  other arithmetic  1.16 us (1%)
  between operations  1.13 us (1%)
    pallas_call x8, Pallas kernels, absorb(): pl.pallas_call(functools.partial(absorb_kernel, first), out_shape=shapes,...  16.3 us
    ppermute x6, waiting for transfers between devices, round_ring(): lax.ppermute(values, 'tok', [(i, 2 * following[i // 2] + i % 2) for i in...  10.8 us
    ppermute x4, starting transfers between devices, passed(): return lax.ppermute(values, ('tok', 'col'), pairs)  9.64 us
    ppermute x6, starting transfers between devices, round_ring(): lax.ppermute(values, 'tok', [(i, 2 * following[i // 2] + i % 2) for i in...  9.34 us
    ppermute x4, waiting for transfers between devices, passed(): return lax.ppermute(values, ('tok', 'col'), pairs)  6.79 us
    ppermute x3, starting transfers between devices, sum_chips(): terms.append(lax.ppermute(values, 'tok', pairs).astype(F32))  4.97 us
    ppermute x3, waiting for transfers between devices, sum_chips(): terms.append(lax.ppermute(values, 'tok', pairs).astype(F32))  4.7 us
    ppermute x8, waiting for transfers between devices, swapped(): return lax.ppermute(values, axis, [(i, i ^ 1) for i in range(size)])  3.89 us
  transfers between devices with their start and end apart: 24, of which 15 were waited for; matrix products, arithmetic and copies ran while one was open for 6% of the time, Pallas kernels for 16%

profile of v5, /device:TPU:0, one launch (start us, length us, event | category | flops | bytes accessed | tf_op | source)
XLA Modules:
  0.0 94.5 jit_solution(10698001427726809753)
XLA Ops:
  0.7 1.4 %copy-done.2 = bf16[1,512,1024]{2,1,0:T(8,128)(2,1)S(1)} copy-done((bf16[1,512,1024]{2,1,0:T(8,128)(2,1)S(1)}, bf16[1,512,1024]{2,1,0:T(8,128)(2,1)}, u32[]{:S(2)}) %copy-start.2) | copy-done | bytes 1048600
  3.5 1.4 %project.2 = (bf16[2,128,512]{2,1,0:T(8,128)(2,1)S(1)}, bf16[2,128,512]{2,1,0:T(8,128)(2,1)S(1)}) custom-call(s32[3]{0:T(128)S(1)} %pad_add_fusion.place, bf16[512,1024]{1,0:T(8,128)(2,1)S(1)} %normalize.1.normed, bf16[3,1024,256]{2,1,0:T(8,128)(2,1)S(1)} %copy-done.1), custom_call_target="tpu_custom_call" | custom-call | tf_op jit(solution)/shard_map/project/pallas_call | solution.py:70
  8.0 2.8 %collective-permute-start.3 = (bf16[128,1024]{1,0:T(8,128)(2,1)S(1)}, bf16[128,1024]{1,0:T(8,128)(2,1)S(1)}, u32[]{:S(2)}, u32[]{:S(2)}) collective-permute-start(bf16[128,1024]{1,0:T(8,128)(2,1)S(1)} %pad_maximum_fusion.1.refs_1_), channel_id=1, source_target_pairs={{0,4},{2,6},{4,12},{6,14},{8,0},{10,2},{12,8},{14,10},{1,5},{3,7},... | collective-permute-start | bytes 786440 | tf_op jit(solution)/shard_map/ppermute | solution.py:278
  10.8 2.0 %absorb.8 = (f32[80,1024]{1,0:T(8,128)S(1)}, f32[8,1024]{1,0:T(8,128)S(1)}) custom-call(bf16[64,1024]{1,0:T(8,128)(2,1)S(1)} %get-tuple-element.158.refs_0_, bf16[128,1024]{1,0:T(8,128)(2,1)S(1)} %pad_maximum_fusion.1.refs_1_), custom_call_target="tpu_custom_call" | custom-call | tf_op jit(solution)/shard_map/absorb/pallas_call | solution.py:112
  12.8 2.6 %collective-permute-start.1 = (bf16[128,1024]{1,0:T(8,128)(2,1)S(1)}, bf16[128,1024]{1,0:T(8,128)(2,1)S(1)}, u32[]{:S(2)}, u32[]{:S(2)}) collective-permute-start(bf16[128,1024]{1,0:T(8,128)(2,1)S(1)} %pad_maximum_fusion.refs_1_), channel_id=1, source_target_pairs={{0,4},{2,6},{4,12},{6,14},{8,0},{10,2},{12,8},{14,10},{1,5},{3,7},... | collective-permute-start | bytes 786440 | tf_op jit(solution)/shard_map/ppermute | solution.py:278
  15.4 1.5 %collective-permute-start.6 = (f32[2,2,128]{2,1,0:T(2,128)S(1)}, f32[2,2,128]{2,1,0:T(2,128)S(1)}, u32[]{:S(2)}, u32[]{:S(2)}) collective-permute-start(f32[2,2,128]{2,1,0:T(2,128)S(1)} %bitcast.50), channel_id=1, source_target_pairs={{0,1},{1,0},{2,3},{3,2},{4,5},{5,4},{6,7},{7,6},{8,9},{9,8},{10,11... | collective-permute-start | bytes 6152 | tf_op jit(solution)/shard_map/ppermute | solution.py:257
  20.1 2.0 %absorb.9 = (f32[80,1024]{1,0:T(8,128)S(1)}, f32[8,1024]{1,0:T(8,128)S(1)}) custom-call(bf16[64,1024]{1,0:T(8,128)(2,1)S(1)} %get-tuple-element.157.refs_0_, bf16[128,1024]{1,0:T(8,128)(2,1)S(1)} %pad_maximum_fusion.refs_1_), custom_call_target="tpu_custom_call" | custom-call | tf_op jit(solution)/shard_map/absorb/pallas_call | solution.py:112
  22.1 2.5 %collective-permute-done.1.refs_1_ = bf16[128,1024]{1,0:T(8,128)(2,1)S(1)} collective-permute-done((bf16[128,1024]{1,0:T(8,128)(2,1)S(1)}, bf16[128,1024]{1,0:T(8,128)(2,1)S(1)}, u32[]{:S(2)}, u32[]{:S(2)}) %collective-permute-start.1) | collective-permute-done | bytes 262176 | tf_op jit(solution)/shard_map/ppermute | solution.py:278
  25.7 2.1 %absorb.10 = (f32[80,1024]{1,0:T(8,128)S(1)}, f32[8,1024]{1,0:T(8,128)S(1)}) custom-call(bf16[64,1024]{1,0:T(8,128)(2,1)S(1)} %get-tuple-element.158.refs_0_, bf16[128,1024]{1,0:T(8,128)(2,1)S(1)} %collective-permute-done.3.refs_1_, f32[80,1024]{1,0:T(8,128)S(1)} %get-tuple-element.88.refs_2_, ...), custom_call_target="tpu_custom_call", output_to_operand_aliasing={{0}: (2, {}), {1}: (3, {})} | custom-call | tf_op jit(solution)/shard_map/absorb/pallas_call | solution.py:112
  27.7 2.4 %collective-permute-done.5.refs_1_ = bf16[128,1024]{1,0:T(8,128)(2,1)S(1)} collective-permute-done((bf16[128,1024]{1,0:T(8,128)(2,1)S(1)}, bf16[128,1024]{1,0:T(8,128)(2,1)S(1)}, u32[]{:S(2)}, u32[]{:S(2)}) %collective-permute-start.5) | collective-permute-done | bytes 262176 | tf_op jit(solution)/shard_map/ppermute | solution.py:278
  31.3 2.1 %absorb.11 = (f32[80,1024]{1,0:T(8,128)S(1)}, f32[8,1024]{1,0:T(8,128)S(1)}) custom-call(bf16[64,1024]{1,0:T(8,128)(2,1)S(1)} %get-tuple-element.157.refs_0_, bf16[128,1024]{1,0:T(8,128)(2,1)S(1)} %collective-permute-done.1.refs_1_, f32[80,1024]{1,0:T(8,128)S(1)} %get-tuple-element.94.refs_2_, ...), custom_call_target="tpu_custom_call", output_to_operand_aliasing={{0}: (2, {}), {1}: (3, {})} | custom-call | tf_op jit(solution)/shard_map/absorb/pallas_call | solution.py:112
  33.4 2.4 %collective-permute-done.4.refs_1_ = bf16[128,1024]{1,0:T(8,128)(2,1)S(1)} collective-permute-done((bf16[128,1024]{1,0:T(8,128)(2,1)S(1)}, bf16[128,1024]{1,0:T(8,128)(2,1)S(1)}, u32[]{:S(2)}, u32[]{:S(2)}) %collective-permute-start.4) | collective-permute-done | bytes 262176 | tf_op jit(solution)/shard_map/ppermute | solution.py:278
  37.0 2.1 %absorb.12 = (f32[80,1024]{1,0:T(8,128)S(1)}, f32[8,1024]{1,0:T(8,128)S(1)}) custom-call(bf16[64,1024]{1,0:T(8,128)(2,1)S(1)} %get-tuple-element.158.refs_0_, bf16[128,1024]{1,0:T(8,128)(2,1)S(1)} %collective-permute-done.5.refs_1_, f32[80,1024]{1,0:T(8,128)S(1)} %get-tuple-element.107.refs_2_, ...), custom_call_target="tpu_custom_call", output_to_operand_aliasing={{0}: (2, {}), {1}: (3, {})} | custom-call | tf_op jit(solution)/shard_map/absorb/pallas_call | solution.py:112
  39.1 2.4 %collective-permute-done.8.refs_1_ = bf16[128,1024]{1,0:T(8,128)(2,1)S(1)} collective-permute-done((bf16[128,1024]{1,0:T(8,128)(2,1)S(1)}, bf16[128,1024]{1,0:T(8,128)(2,1)S(1)}, u32[]{:S(2)}, u32[]{:S(2)}) %collective-permute-start.8) | collective-permute-done | bytes 262176 | tf_op jit(solution)/shard_map/ppermute | solution.py:278
  41.4 2.1 %absorb.14 = (f32[80,1024]{1,0:T(8,128)S(1)}, f32[8,1024]{1,0:T(8,128)S(1)}) custom-call(bf16[64,1024]{1,0:T(8,128)(2,1)S(1)} %get-tuple-element.158.refs_0_, bf16[128,1024]{1,0:T(8,128)(2,1)S(1)} %collective-permute-done.8.refs_1_, f32[80,1024]{1,0:T(8,128)S(1)} %get-tuple-element.119.refs_2_, ...), custom_call_target="tpu_custom_call", output_to_operand_aliasing={{0}: (2, {}), {1}: (3, {})} | custom-call | tf_op jit(solution)/shard_map/absorb/pallas_call | solution.py:112
  43.5 2.1 %absorb.13 = (f32[80,1024]{1,0:T(8,128)S(1)}, f32[8,1024]{1,0:T(8,128)S(1)}) custom-call(bf16[64,1024]{1,0:T(8,128)(2,1)S(1)} %get-tuple-element.157.refs_0_, bf16[128,1024]{1,0:T(8,128)(2,1)S(1)} %collective-permute-done.4.refs_1_, f32[80,1024]{1,0:T(8,128)S(1)} %get-tuple-element.113.refs_2_, ...), custom_call_target="tpu_custom_call", output_to_operand_aliasing={{0}: (2, {}), {1}: (3, {})} | custom-call | tf_op jit(solution)/shard_map/absorb/pallas_call | solution.py:112
  46.7 2.1 %absorb.15 = (f32[80,1024]{1,0:T(8,128)S(1)}, f32[8,1024]{1,0:T(8,128)S(1)}) custom-call(bf16[64,1024]{1,0:T(8,128)(2,1)S(1)} %get-tuple-element.157.refs_0_, bf16[128,1024]{1,0:T(8,128)(2,1)S(1)} %collective-permute-done.7.refs_1_, f32[80,1024]{1,0:T(8,128)S(1)} %get-tuple-element.125.refs_2_, ...), custom_call_target="tpu_custom_call", output_to_operand_aliasing={{0}: (2, {}), {1}: (3, {})} | custom-call | tf_op jit(solution)/shard_map/absorb/pallas_call | solution.py:112
  49.2 1.3 %collective-permute-done.9 = f32[64,512]{1,0:T(8,128)S(1)} collective-permute-done((f32[64,512]{1,0:T(8,128)S(1)}, f32[64,512]{1,0:T(8,128)S(1)}, u32[]{:S(2)}, u32[]{:S(2)}) %collective-permute-start.9) | collective-permute-done | bytes 131104 | tf_op jit(solution)/shard_map/ppermute | solution.py:257
  50.5 3.7 %collective-permute-start.11 = (bf16[64,512]{1,0:T(8,128)(2,1)S(1)}, bf16[64,512]{1,0:T(8,128)(2,1)S(1)}, u32[]{:S(2)}, u32[]{:S(2)}) collective-permute-start(bf16[64,512]{1,0:T(8,128)(2,1)S(1)} %add_convert_fusion.3), channel_id=1, source_target_pairs={{0,5},{1,4},{2,7},{3,6},{4,9},{5,8},{6,11},{7,10},{8,13},{9,12},{1... | collective-permute-start | bytes 196616 | tf_op jit(solution)/shard_map/ppermute | solution.py:268
  54.8 3.4 %collective-permute-start.10 = (bf16[80,512]{1,0:T(8,128)(2,1)S(1)}, bf16[80,512]{1,0:T(8,128)(2,1)S(1)}, u32[]{:S(2)}, u32[]{:S(2)}) collective-permute-start(bf16[80,512]{1,0:T(8,128)(2,1)S(1)} %pad_maximum_fusion.4), channel_id=1, source_target_pairs={{0,4},{1,5},{2,6},{3,7},{4,8},{5,9},{6,10},{7,11},{8,12},{9,13},{1... | collective-permute-start | bytes 245768 | tf_op jit(solution)/shard_map/ppermute | solution.py:268
  60.9 4.4 %collective-permute-done.13 = bf16[80,512]{1,0:T(8,128)(2,1)S(1)} collective-permute-done((bf16[80,512]{1,0:T(8,128)(2,1)S(1)}, bf16[80,512]{1,0:T(8,128)(2,1)S(1)}, u32[]{:S(2)}, u32[]{:S(2)}) %collective-permute-start.13) | collective-permute-done | bytes 81952 | tf_op jit(solution)/shard_map/ppermute | solution.py:268
  65.3 2.3 %collective-permute-done.14 = bf16[64,512]{1,0:T(8,128)(2,1)S(1)} collective-permute-done((bf16[64,512]{1,0:T(8,128)(2,1)S(1)}, bf16[64,512]{1,0:T(8,128)(2,1)S(1)}, u32[]{:S(2)}, u32[]{:S(2)}) %collective-permute-start.14) | collective-permute-done | bytes 65568 | tf_op jit(solution)/shard_map/ppermute | solution.py:268
  69.3 3.8 %network.1 = (f32[2,1024]{1,0:T(2,128)S(1)}, f32[32,576]{1,0:T(8,128)S(1)}, f32[64,128]{1,0:T(8,128)S(1)}) custom-call(s32[3]{0:T(128)S(1)} %pad_add_fusion.place, bf16[80,1536]{1,0:T(8,128)(2,1)S(1)} %maximum_maximum_fusion.mine, bf16[80,1536]{1,0:T(8,128)(2,1)S(1)} %collective-permute-done.15.theirs, bf16[2,3,64,192]{3,2,1,0:T(8,128)(2,1)S(1)} %bitcast.44, ...), custom_call_target="tpu_custom_call" | custom-call | tf_op jit(solution)/shard_map/network/pallas_call | solution.py:240
  73.1 2.1 %collective-permute-start.16 = (bf16[32,896]{1,0:T(8,128)(2,1)S(1)}, bf16[32,896]{1,0:T(8,128)(2,1)S(1)}, u32[]{:S(2)}, u32[]{:S(2)}) collective-permute-start(bf16[32,896]{1,0:T(8,128)(2,1)S(1)} %fusion.14), channel_id=1, source_target_pairs={{0,4},{2,6},{4,0},{6,2},{8,12},{10,14},{12,8},{14,10},{1,5},{3,7},... | collective-permute-start | bytes 172040 | tf_op jit(solution)/shard_map/ppermute | solution.py:297
  75.2 1.5 %collective-permute-start.17 = (bf16[32,896]{1,0:T(8,128)(2,1)S(1)}, bf16[32,896]{1,0:T(8,128)(2,1)S(1)}, u32[]{:S(2)}, u32[]{:S(2)}) collective-permute-start(bf16[32,896]{1,0:T(8,128)(2,1)S(1)} %fusion.14), channel_id=1, source_target_pairs={{0,8},{2,10},{4,12},{6,14},{8,0},{10,2},{12,4},{14,6},{1,9},{3,11}... | collective-permute-start | bytes 172040 | tf_op jit(solution)/shard_map/ppermute | solution.py:297
  76.7 1.4 %collective-permute-start.18 = (bf16[32,896]{1,0:T(8,128)(2,1)S(1)}, bf16[32,896]{1,0:T(8,128)(2,1)S(1)}, u32[]{:S(2)}, u32[]{:S(2)}) collective-permute-start(bf16[32,896]{1,0:T(8,128)(2,1)S(1)} %fusion.14), channel_id=1, source_target_pairs={{0,12},{2,14},{4,8},{6,10},{8,4},{10,6},{12,0},{14,2},{1,13},{3,15... | collective-permute-start | bytes 172040 | tf_op jit(solution)/shard_map/ppermute | solution.py:297
  78.1 4.7 %collective-permute-done.17 = bf16[32,896]{1,0:T(8,128)(2,1)S(1)} collective-permute-done((bf16[32,896]{1,0:T(8,128)(2,1)S(1)}, bf16[32,896]{1,0:T(8,128)(2,1)S(1)}, u32[]{:S(2)}, u32[]{:S(2)}) %collective-permute-start.17) | collective-permute-done | bytes 57376 | tf_op jit(solution)/shard_map/ppermute | solution.py:297
  82.9 1.5 %collective-permute-start.20 = (bf16[32,576]{1,0:T(8,128)(2,1)S(1)}, bf16[32,576]{1,0:T(8,128)(2,1)S(1)}, u32[]{:S(2)}, u32[]{:S(2)}) collective-permute-start(bf16[32,576]{1,0:T(8,128)(2,1)S(1)} %slice.93), channel_id=1, source_target_pairs={{0,1},{1,0},{16,17},{17,16},{2,3},{3,2},{18,19},{19,18},{4,5},{5,4... | collective-permute-start | bytes 110600 | tf_op jit(solution)/shard_map/ppermute | solution.py:310
  84.4 1.5 %collective-permute-start.21 = (bf16[32,576]{1,0:T(8,128)(2,1)S(1)}, bf16[32,576]{1,0:T(8,128)(2,1)S(1)}, u32[]{:S(2)}, u32[]{:S(2)}) collective-permute-start(bf16[32,576]{1,0:T(8,128)(2,1)S(1)} %slice.93), channel_id=1, source_target_pairs={{0,17},{1,16},{16,1},{17,0},{2,19},{3,18},{18,3},{19,2},{4,21},{5,... | collective-permute-start | bytes 110600 | tf_op jit(solution)/shard_map/ppermute | solution.py:310
  87.2 2.1 %collective-permute-done.21 = bf16[32,576]{1,0:T(8,128)(2,1)S(1)} collective-permute-done((bf16[32,576]{1,0:T(8,128)(2,1)S(1)}, bf16[32,576]{1,0:T(8,128)(2,1)S(1)}, u32[]{:S(2)}, u32[]{:S(2)}) %collective-permute-start.21) | collective-permute-done | bytes 36896 | tf_op jit(solution)/shard_map/ppermute | solution.py:310
  89.3 1.4 %collective-permute-done.19 = bf16[32,896]{1,0:T(8,128)(2,1)S(1)} collective-permute-done((bf16[32,896]{1,0:T(8,128)(2,1)S(1)}, bf16[32,896]{1,0:T(8,128)(2,1)S(1)}, u32[]{:S(2)}, u32[]{:S(2)}) %collective-permute-start.19) | collective-permute-done | bytes 57376 | tf_op jit(solution)/shard_map/ppermute | solution.py:310
  92.1 1.6 %fusion.3 = f32[256,1024]{1,0:T(8,128)} fusion(bf16[1024,64]{0,1:T(8,128)(2,1)S(1)} %copy-done.6, f32[64,128]{1,0:T(8,128)S(1)} %collective-permute-done.23, f32[32,128]{1,0:T(8,128)S(1)} %get-tuple-element.148, f32[32,128]{1,0:T(8,128)S(1)} %get-tuple-element.147, pred[]{:T(512)S(6)} %eq.10), kind=kOutput, calls=%fused_computation.29 | convolution fusion | flops 201408512 | bytes 1245185 | tf_op jit(solution)/shard_map/dot_general | solution.py:424
  (100 shorter events, 21.0 us)
Async XLA Ops:
  0.6 17.4 %copy-start = (bf16[256,1024]{1,0:T(8,128)(2,1)S(1)}, bf16[256,1024]{1,0:T(8,128)(2,1)}, u32[]{:S(2)}) copy-start(bf16[256,1024]{1,0:T(8,128)(2,1)} %param.11) | copy-start | bytes 1572868
  4.9 3.1 %collective-permute-start = (bf16[2,128,512]{2,1,0:T(8,128)(2,1)S(1)}, bf16[2,128,512]{2,1,0:T(8,128)(2,1)S(1)}, u32[]{:S(2)}, u32[]{:S(2)}) collective-permute-start(bf16[2,128,512]{2,1,0:T(8,128)(2,1)S(1)} %get-tuple-element.74), channel_id=1, source_target_pairs={{0,2},{2,0},{4,6},{6,4},{8,10},{10,8},{12,14},{14,12},{1,3},{3,1},... | collective-permute-start | bytes 786440 | tf_op jit(solution)/shard_map/ppermute | solution.py:257
  6.5 1.4 %collective-permute-start.2 = (bf16[2,64,512]{2,1,0:T(8,128)(2,1)S(1)}, bf16[2,64,512]{2,1,0:T(8,128)(2,1)S(1)}, u32[]{:S(2)}, u32[]{:S(2)}) collective-permute-start(bf16[2,64,512]{2,1,0:T(8,128)(2,1)S(1)} %get-tuple-element.77), channel_id=1, source_target_pairs={{0,2},{2,0},{4,6},{6,4},{8,10},{10,8},{12,14},{14,12},{1,3},{3,1},... | collective-permute-start | bytes 393224 | tf_op jit(solution)/shard_map/ppermute | solution.py:257
  7.2 8.2 %copy-start.11 = (f32[1,2,2,128]{3,2,1,0:T(2,128)S(1)}, f32[1,2,2,128]{3,2,1,0:T(2,128)}, u32[]{:S(2)}) copy-start(f32[1,2,2,128]{3,2,1,0:T(2,128)} %param.15) | copy-start | bytes 6148
  7.2 9.7 %copy-start.3 = (bf16[1,512,1024]{2,1,0:T(8,128)(2,1)S(1)}, bf16[1,512,1024]{2,1,0:T(8,128)(2,1)}, u32[]{:S(2)}) copy-start(bf16[1,512,1024]{2,1,0:T(8,128)(2,1)} %param.8) | copy-start | bytes 3145732
  7.2 9.7 %copy-start.6 = (bf16[1024,64]{0,1:T(8,128)(2,1)S(1)}, bf16[1024,64]{0,1:T(8,128)(2,1)}, u32[]{:S(2)}) copy-start(bf16[1024,64]{0,1:T(8,128)(2,1)} %param.12) | copy-start | bytes 393220
  8.0 10.3 %copy-start.8 = (bf16[2,64,576]{2,1,0:T(8,128)(2,1)S(1)}, bf16[2,64,576]{2,1,0:T(8,128)(2,1)}, u32[]{:S(2)}) copy-start(bf16[2,64,576]{2,1,0:T(8,128)(2,1)} %param.13) | copy-start | bytes 442372
  8.0 11.6 %collective-permute-start.3 = (bf16[128,1024]{1,0:T(8,128)(2,1)S(1)}, bf16[128,1024]{1,0:T(8,128)(2,1)S(1)}, u32[]{:S(2)}, u32[]{:S(2)}) collective-permute-start(bf16[128,1024]{1,0:T(8,128)(2,1)S(1)} %pad_maximum_fusion.1.refs_1_), channel_id=1, source_target_pairs={{0,4},{2,6},{4,12},{6,14},{8,0},{10,2},{12,8},{14,10},{1,5},{3,7},... | collective-permute-start | bytes 786440 | tf_op jit(solution)/shard_map/ppermute | solution.py:278
  12.8 11.8 %collective-permute-start.1 = (bf16[128,1024]{1,0:T(8,128)(2,1)S(1)}, bf16[128,1024]{1,0:T(8,128)(2,1)S(1)}, u32[]{:S(2)}, u32[]{:S(2)}) collective-permute-start(bf16[128,1024]{1,0:T(8,128)(2,1)S(1)} %pad_maximum_fusion.refs_1_), channel_id=1, source_target_pairs={{0,4},{2,6},{4,12},{6,14},{8,0},{10,2},{12,8},{14,10},{1,5},{3,7},... | collective-permute-start | bytes 786440 | tf_op jit(solution)/shard_map/ppermute | solution.py:278
  15.4 4.6 %collective-permute-start.6 = (f32[2,2,128]{2,1,0:T(2,128)S(1)}, f32[2,2,128]{2,1,0:T(2,128)S(1)}, u32[]{:S(2)}, u32[]{:S(2)}) collective-permute-start(f32[2,2,128]{2,1,0:T(2,128)S(1)} %bitcast.50), channel_id=1, source_target_pairs={{0,1},{1,0},{2,3},{3,2},{4,5},{5,4},{6,7},{7,6},{8,9},{9,8},{10,11... | collective-permute-start | bytes 6152 | tf_op jit(solution)/shard_map/ppermute | solution.py:257
  19.6 10.6 %collective-permute-start.5 = (bf16[128,1024]{1,0:T(8,128)(2,1)S(1)}, bf16[128,1024]{1,0:T(8,128)(2,1)S(1)}, u32[]{:S(2)}, u32[]{:S(2)}) collective-permute-start(bf16[128,1024]{1,0:T(8,128)(2,1)S(1)} %collective-permute-done.3.refs_1_), channel_id=1, source_target_pairs={{0,4},{2,6},{4,12},{6,14},{8,0},{10,2},{12,8},{14,10},{1,5},{3,7},... | collective-permute-start | bytes 786440 | tf_op jit(solution)/shard_map/ppermute | solution.py:278
  24.6 11.2 %collective-permute-start.4 = (bf16[128,1024]{1,0:T(8,128)(2,1)S(1)}, bf16[128,1024]{1,0:T(8,128)(2,1)S(1)}, u32[]{:S(2)}, u32[]{:S(2)}) collective-permute-start(bf16[128,1024]{1,0:T(8,128)(2,1)S(1)} %collective-permute-done.1.refs_1_), channel_id=1, source_target_pairs={{0,4},{2,6},{4,12},{6,14},{8,0},{10,2},{12,8},{14,10},{1,5},{3,7},... | collective-permute-start | bytes 786440 | tf_op jit(solution)/shard_map/ppermute | solution.py:278
  30.2 11.2 %collective-permute-start.8 = (bf16[128,1024]{1,0:T(8,128)(2,1)S(1)}, bf16[128,1024]{1,0:T(8,128)(2,1)S(1)}, u32[]{:S(2)}, u32[]{:S(2)}) collective-permute-start(bf16[128,1024]{1,0:T(8,128)(2,1)S(1)} %collective-permute-done.5.refs_1_), channel_id=1, source_target_pairs={{0,4},{2,6},{4,12},{6,14},{8,0},{10,2},{12,8},{14,10},{1,5},{3,7},... | collective-permute-start | bytes 786440 | tf_op jit(solution)/shard_map/ppermute | solution.py:278
  35.8 10.9 %collective-permute-start.7 = (bf16[128,1024]{1,0:T(8,128)(2,1)S(1)}, bf16[128,1024]{1,0:T(8,128)(2,1)S(1)}, u32[]{:S(2)}, u32[]{:S(2)}) collective-permute-start(bf16[128,1024]{1,0:T(8,128)(2,1)S(1)} %collective-permute-done.4.refs_1_), channel_id=1, source_target_pairs={{0,4},{2,6},{4,12},{6,14},{8,0},{10,2},{12,8},{14,10},{1,5},{3,7},... | collective-permute-start | bytes 786440 | tf_op jit(solution)/shard_map/ppermute | solution.py:278
  41.4 9.1 %copy-start.9 = (f32[64,512]{1,0:T(8,128)S(1)}, f32[64,512]{1,0:T(8,128)}, u32[]{:S(2)}) copy-start(f32[64,512]{1,0:T(8,128)} %fusion.28) | copy-start | bytes 393220
  46.7 21.1 %copy-start.7 = (bf16[2,3,64,3,64]{2,4,3,1,0:T(8,128)(2,1)S(1)}, bf16[2,3,64,3,64]{2,4,3,1,0:T(8,128)(2,1)}, u32[]{:S(2)}) copy-start(bf16[2,3,64,3,64]{2,4,3,1,0:T(8,128)(2,1)} %copy.26) | copy-start | bytes 442372
  48.8 20.6 %copy-start.5 = (bf16[2,64]{1,0:T(2,128)(2,1)S(1)}, bf16[2,64]{1,0:T(2,128)(2,1)}, u32[]{:S(2)}) copy-start(bf16[2,64]{1,0:T(2,128)(2,1)} %head.1) | copy-start | bytes 772
  49.1 1.4 %collective-permute-start.9 = (f32[64,512]{1,0:T(8,128)S(1)}, f32[64,512]{1,0:T(8,128)S(1)}, u32[]{:S(2)}, u32[]{:S(2)}) collective-permute-start(f32[64,512]{1,0:T(8,128)S(1)} %slice.71), channel_id=1, source_target_pairs={{0,2},{2,0},{4,6},{6,4},{8,10},{10,8},{12,14},{14,12},{1,3},{3,1},... | collective-permute-start | bytes 393224 | tf_op jit(solution)/shard_map/ppermute | solution.py:257
  50.5 10.3 %collective-permute-start.11 = (bf16[64,512]{1,0:T(8,128)(2,1)S(1)}, bf16[64,512]{1,0:T(8,128)(2,1)S(1)}, u32[]{:S(2)}, u32[]{:S(2)}) collective-permute-start(bf16[64,512]{1,0:T(8,128)(2,1)S(1)} %add_convert_fusion.3), channel_id=1, source_target_pairs={{0,5},{1,4},{2,7},{3,6},{4,9},{5,8},{6,11},{7,10},{8,13},{9,12},{1... | collective-permute-start | bytes 196616 | tf_op jit(solution)/shard_map/ppermute | solution.py:268
  54.2 6.6 %collective-permute-start.12 = (bf16[64,512]{1,0:T(8,128)(2,1)S(1)}, bf16[64,512]{1,0:T(8,128)(2,1)S(1)}, u32[]{:S(2)}, u32[]{:S(2)}) collective-permute-start(bf16[64,512]{1,0:T(8,128)(2,1)S(1)} %add_convert_fusion.3), channel_id=1, source_target_pairs={{0,1},{1,0},{2,3},{3,2},{4,5},{5,4},{6,7},{7,6},{8,9},{9,8},{10,11... | collective-permute-start | bytes 196616 | tf_op jit(solution)/shard_map/ppermute | solution.py:257
  54.8 6.0 %collective-permute-start.10 = (bf16[80,512]{1,0:T(8,128)(2,1)S(1)}, bf16[80,512]{1,0:T(8,128)(2,1)S(1)}, u32[]{:S(2)}, u32[]{:S(2)}) collective-permute-start(bf16[80,512]{1,0:T(8,128)(2,1)S(1)} %pad_maximum_fusion.4), channel_id=1, source_target_pairs={{0,4},{1,5},{2,6},{3,7},{4,8},{5,9},{6,10},{7,11},{8,12},{9,13},{1... | collective-permute-start | bytes 245768 | tf_op jit(solution)/shard_map/ppermute | solution.py:268
  58.2 7.1 %collective-permute-start.13 = (bf16[80,512]{1,0:T(8,128)(2,1)S(1)}, bf16[80,512]{1,0:T(8,128)(2,1)S(1)}, u32[]{:S(2)}, u32[]{:S(2)}) collective-permute-start(bf16[80,512]{1,0:T(8,128)(2,1)S(1)} %pad_maximum_fusion.4), channel_id=1, source_target_pairs={{4,0},{5,1},{6,2},{7,3},{8,4},{9,5},{10,6},{11,7},{12,8},{13,9},{1... | collective-permute-start | bytes 245768 | tf_op jit(solution)/shard_map/ppermute | solution.py:268
  59.5 8.2 %collective-permute-start.14 = (bf16[64,512]{1,0:T(8,128)(2,1)S(1)}, bf16[64,512]{1,0:T(8,128)(2,1)S(1)}, u32[]{:S(2)}, u32[]{:S(2)}) collective-permute-start(bf16[64,512]{1,0:T(8,128)(2,1)S(1)} %add_convert_fusion.3), channel_id=1, source_target_pairs={{4,1},{5,0},{6,3},{7,2},{8,5},{9,4},{10,7},{11,6},{12,9},{13,8},{1... | collective-permute-start | bytes 196616 | tf_op jit(solution)/shard_map/ppermute | solution.py:268
  67.7 1.6 %collective-permute-start.15 = (bf16[80,1536]{1,0:T(8,128)(2,1)S(1)}, bf16[80,1536]{1,0:T(8,128)(2,1)S(1)}, u32[]{:S(2)}, u32[]{:S(2)}) collective-permute-start(bf16[80,1536]{1,0:T(8,128)(2,1)S(1)} %maximum_maximum_fusion.mine), channel_id=1, source_target_pairs={{0,2},{2,0},{4,6},{6,4},{8,10},{10,8},{12,14},{14,12},{1,3},{3,1},... | collective-permute-start | bytes 737288 | tf_op jit(solution)/shard_map/ppermute | solution.py:257
  73.1 5.0 %collective-permute-start.16 = (bf16[32,896]{1,0:T(8,128)(2,1)S(1)}, bf16[32,896]{1,0:T(8,128)(2,1)S(1)}, u32[]{:S(2)}, u32[]{:S(2)}) collective-permute-start(bf16[32,896]{1,0:T(8,128)(2,1)S(1)} %fusion.14), channel_id=1, source_target_pairs={{0,4},{2,6},{4,0},{6,2},{8,12},{10,14},{12,8},{14,10},{1,5},{3,7},... | collective-permute-start | bytes 172040 | tf_op jit(solution)/shard_map/ppermute | solution.py:297
  75.2 7.6 %collective-permute-start.17 = (bf16[32,896]{1,0:T(8,128)(2,1)S(1)}, bf16[32,896]{1,0:T(8,128)(2,1)S(1)}, u32[]{:S(2)}, u32[]{:S(2)}) collective-permute-start(bf16[32,896]{1,0:T(8,128)(2,1)S(1)} %fusion.14), channel_id=1, source_target_pairs={{0,8},{2,10},{4,12},{6,14},{8,0},{10,2},{12,4},{14,6},{1,9},{3,11}... | collective-permute-start | bytes 172040 | tf_op jit(solution)/shard_map/ppermute | solution.py:297
  76.7 6.1 %collective-permute-start.18 = (bf16[32,896]{1,0:T(8,128)(2,1)S(1)}, bf16[32,896]{1,0:T(8,128)(2,1)S(1)}, u32[]{:S(2)}, u32[]{:S(2)}) collective-permute-start(bf16[32,896]{1,0:T(8,128)(2,1)S(1)} %fusion.14), channel_id=1, source_target_pairs={{0,12},{2,14},{4,8},{6,10},{8,4},{10,6},{12,0},{14,2},{1,13},{3,15... | collective-permute-start | bytes 172040 | tf_op jit(solution)/shard_map/ppermute | solution.py:297
  82.9 4.3 %collective-permute-start.20 = (bf16[32,576]{1,0:T(8,128)(2,1)S(1)}, bf16[32,576]{1,0:T(8,128)(2,1)S(1)}, u32[]{:S(2)}, u32[]{:S(2)}) collective-permute-start(bf16[32,576]{1,0:T(8,128)(2,1)S(1)} %slice.93), channel_id=1, source_target_pairs={{0,1},{1,0},{16,17},{17,16},{2,3},{3,2},{18,19},{19,18},{4,5},{5,4... | collective-permute-start | bytes 110600 | tf_op jit(solution)/shard_map/ppermute | solution.py:310
  84.4 4.9 %collective-permute-start.21 = (bf16[32,576]{1,0:T(8,128)(2,1)S(1)}, bf16[32,576]{1,0:T(8,128)(2,1)S(1)}, u32[]{:S(2)}, u32[]{:S(2)}) collective-permute-start(bf16[32,576]{1,0:T(8,128)(2,1)S(1)} %slice.93), channel_id=1, source_target_pairs={{0,17},{1,16},{16,1},{17,0},{2,19},{3,18},{18,3},{19,2},{4,21},{5,... | collective-permute-start | bytes 110600 | tf_op jit(solution)/shard_map/ppermute | solution.py:310
  86.6 4.2 %collective-permute-start.19 = (bf16[32,896]{1,0:T(8,128)(2,1)S(1)}, bf16[32,896]{1,0:T(8,128)(2,1)S(1)}, u32[]{:S(2)}, u32[]{:S(2)}) collective-permute-start(bf16[32,896]{1,0:T(8,128)(2,1)S(1)} %add_convert_fusion.4), channel_id=1, source_target_pairs={{0,16},{1,17},{16,0},{17,1},{2,18},{3,19},{18,2},{19,3},{4,20},{5,... | collective-permute-start | bytes 172040 | tf_op jit(solution)/shard_map/ppermute | solution.py:310
  90.8 1.3 %collective-permute-start.23 = (f32[64,128]{1,0:T(8,128)S(1)}, f32[64,128]{1,0:T(8,128)S(1)}, u32[]{:S(2)}, u32[]{:S(2)}) collective-permute-start(f32[64,128]{1,0:T(8,128)S(1)} %pad_maximum_fusion.5), channel_id=1, source_target_pairs={{0,2},{2,0},{4,6},{6,4},{8,10},{10,8},{12,14},{14,12},{1,3},{3,1},... | collective-permute-start | bytes 98312 | tf_op jit(solution)/shard_map/ppermute | solution.py:257
  90.9 2.8 %collective-permute-start.22 = (f32[64,576]{1,0:T(8,128)S(1)}, f32[64,576]{1,0:T(8,128)S(1)}, u32[]{:S(2)}, u32[]{:S(2)}) collective-permute-start(f32[64,576]{1,0:T(8,128)S(1)} %maximum_select_fusion.2), channel_id=1, source_target_pairs={{0,2},{2,0},{4,6},{6,4},{8,10},{10,8},{12,14},{14,12},{1,3},{3,1},... | collective-permute-start | bytes 442376 | tf_op jit(solution)/shard_map/ppermute | solution.py:257
  (4 other events, 10.4 us)

commit v6 on v4

--- a/solution.py
+++ b/solution.py
@@ -49,19 +49,19 @@
     )(tokens, gain)
 
 
-def project_kernel(members, place, normed, weight, mine, theirs):
+def project_kernel(members, place, normed, weight, mine, theirs, turned):
     core = place[0]
     kept = mine.shape[0] * HEAD
     rows = normed[...]
-    for which, out in ((1 - core, theirs), (core, mine)):
-        for at, member in enumerate(members):
-            part = weight[member, :, pl.ds(pl.multiple_of(which * kept, 128), kept)]
-            product = dot(rows, part).astype(BF16)
-            if member == 0:
-                product = product * jnp.asarray(1.0 / HEAD**0.5, BF16)
-            turned = product.T
+    for at, member in enumerate(members):
+        product = dot(rows, weight[member]).astype(BF16)
+        if member == 0:
+            product = product * jnp.asarray(1.0 / HEAD**0.5, BF16)
+        turned[at] = product.T
+        for which, out in ((1 - core, theirs), (core, mine)):
             for head in range(mine.shape[0]):
-                out[head, at * HEAD : (at + 1) * HEAD, :] = turned[head * HEAD : (head + 1) * HEAD, :]
+                start = pl.multiple_of(which * kept + head * HEAD, HEAD)
+                out[head, at * HEAD : (at + 1) * HEAD, :] = turned[at, pl.ds(start, HEAD), :]
 
 
 def project(members, place, normed, weight):
@@ -72,6 +72,7 @@
         out_shape=(shape, shape),
         in_specs=[SMEM, VMEM, VMEM],
         out_specs=(VMEM,) * 2,
+        scratch_shapes=[pltpu.VMEM((len(members), weight.shape[2], length), BF16)],
         compiler_params=PARAMS,
         name="project",
     )(place, normed, weight)
@@ -264,12 +265,23 @@
     return lax.ppermute(values, axis, pairs)
 
 
+def round_ring(values):
+    size = lax.axis_size("tok")
+    chips = size // 2
+    order = [at for at in range(chips) if at == 0 or at % 2 == 1] + [
+        at for at in reversed(range(chips)) if at and at % 2 == 0
+    ]
+    following = {order[at]: order[(at + 1) % chips] for at in range(chips)}
+    return lax.ppermute(values, "tok", [(i, 2 * following[i // 2] + i % 2) for i in range(size)])
+
+
 def everyone(values, axis, stride, count):
     sent = values.astype(BF16)
-    total = sent.astype(F32)
-    for step in range(1, count):
-        total = total + passed(sent, axis, stride * step, True).astype(F32)
-    return total
+    terms = [(passed(sent, axis, stride * step, True) if step else sent).astype(F32) for step in range(count)]
+    while len(terms) > 1:
+        apart = len(terms) // 2
+        terms = [terms[at] + terms[at + apart] for at in range(apart)]
+    return terms[0]
 
 
 def in_order(core, mine, theirs, axis):
@@ -321,7 +333,7 @@
         return (forward, backward, folded, direct, exact_cot)
 
     for turn in range(chips):
-        arriving = [passed(block, "tok", 2, True) for block in blocks] if turn < chips - 1 else blocks
+        arriving = [round_ring(block) for block in blocks] if turn < chips - 1 else blocks
         for head in range(count):
             states[head] = absorb(queries[head], blocks[head], states[head])
             if turn == 0 and head == 0:
@@ -344,7 +356,8 @@
 
     context, share = finish([state[0] for state in states], folded)
     partial = share[:, :length] + swapped(share[:, length:], "tok")
-    own_map = (partial + swapped(partial, "col") + direct).astype(BF16)
+    partial = (partial + jnp.where(half == 0, direct, 0.0)).astype(BF16)
+    own_map = (partial.astype(F32) + swapped(partial, "col").astype(F32)).astype(BF16)
     own_map = jnp.concatenate([own_map, exact_cot], axis=0)
     rims = jnp.concatenate([passed(own_map, "tok", 2, False), passed(own_map, "tok", -2, False)], axis=1)
     rows_chip = 2 * rows_dev

time: 90.9 us -> 90.4 us (level)
  starting transfers between devices: 20.8 us -> 28.4 us
  waiting for transfers between devices: 35.7 us -> 28.3 us
    ppermute x12 -> x6, waiting for transfers between devices: 26 us -> 9.17 us  [passed(): return lax.ppermute(values, axis, pairs)]
    ppermute x0 -> x6, waiting for transfers between devices: none -> 10.8 us  [round_ring(): lax.ppermute(values, 'tok', [(i, 2 * following[i // 2] + i % 2) for i in...]
    ppermute x0 -> x6, starting transfers between devices: none -> 9.34 us  [round_ring(): lax.ppermute(values, 'tok', [(i, 2 * following[i // 2] + i % 2) for i in...]
    ppermute x12 -> x6, starting transfers between devices: 14.7 us -> 12.9 us  [passed(): return lax.ppermute(values, axis, pairs)]
    ppermute x11, waiting for transfers between devices: 9.66 us -> 8.31 us  [swapped(): return lax.ppermute(values, axis, [(i, i ^ 1) for i in range(size)])]
  transfers between devices with their start and end apart: 23 -> 23, of which waited for: 17 -> 15; matrix products, arithmetic and copies ran while one was open for 6% -> 6% of each run, Pallas kernels for 17% -> 17%
where the time goes in v6:
time: 90.4 us; the launch traced here: 90.2 us
  starting transfers between devices  28.4 us (31%)
  waiting for transfers between devices  28.3 us (31%)
  Pallas kernels  23.5 us (26%)
  local copies, waits for them, and re-layouts  4.95 us (5%)
  matrix products  2.92 us (3%)
  other arithmetic  1.09 us (1%)
  between operations  1.04 us (1%)
    pallas_call x8, Pallas kernels, absorb(): pl.pallas_call(functools.partial(absorb_kernel, first), out_shape=shapes,...  16.3 us
    ppermute x6, starting transfers between devices, passed(): return lax.ppermute(values, axis, pairs)  12.9 us
    ppermute x6, waiting for transfers between devices, round_ring(): lax.ppermute(values, 'tok', [(i, 2 * following[i // 2] + i % 2) for i in...  10.8 us
    ppermute x6, starting transfers between devices, round_ring(): lax.ppermute(values, 'tok', [(i, 2 * following[i // 2] + i % 2) for i in...  9.34 us
    ppermute x6, waiting for transfers between devices, passed(): return lax.ppermute(values, axis, pairs)  9.17 us
    ppermute x11, waiting for transfers between devices, swapped(): return lax.ppermute(values, axis, [(i, i ^ 1) for i in range(size)])  8.31 us
    ppermute x11, starting transfers between devices, swapped(): return lax.ppermute(values, axis, [(i, i ^ 1) for i in range(size)])  6.16 us
    pallas_call x1, Pallas kernels, network(): pl.pallas_call(functools.partial(network_kernel, cols, frame_rows), out_s...  3.77 us
  transfers between devices with their start and end apart: 23, of which 15 were waited for; matrix products, arithmetic and copies ran while one was open for 6% of the time, Pallas kernels for 17%

profile of v6, /device:TPU:0, one launch (start us, length us, event | category | flops | bytes accessed | tf_op | source)
XLA Modules:
  0.0 90.2 jit_solution(14131962655138941238)
XLA Ops:
  0.7 1.4 %copy-done.2 = bf16[1,512,1024]{2,1,0:T(8,128)(2,1)S(1)} copy-done((bf16[1,512,1024]{2,1,0:T(8,128)(2,1)S(1)}, bf16[1,512,1024]{2,1,0:T(8,128)(2,1)}, u32[]{:S(2)}) %copy-start.2) | copy-done | bytes 1048600
  3.5 1.4 %project.2 = (bf16[2,128,512]{2,1,0:T(8,128)(2,1)S(1)}, bf16[2,128,512]{2,1,0:T(8,128)(2,1)S(1)}) custom-call(s32[3]{0:T(128)S(1)} %pad_add_fusion.place, bf16[512,1024]{1,0:T(8,128)(2,1)S(1)} %normalize.1.normed, bf16[3,1024,256]{2,1,0:T(8,128)(2,1)S(1)} %copy-done.1), custom_call_target="tpu_custom_call" | custom-call | tf_op jit(solution)/shard_map/project/pallas_call | solution.py:70
  8.0 2.8 %collective-permute-start.3 = (bf16[128,1024]{1,0:T(8,128)(2,1)S(1)}, bf16[128,1024]{1,0:T(8,128)(2,1)S(1)}, u32[]{:S(2)}, u32[]{:S(2)}) collective-permute-start(bf16[128,1024]{1,0:T(8,128)(2,1)S(1)} %pad_maximum_fusion.1.refs_1_), channel_id=1, source_target_pairs={{0,4},{2,6},{4,12},{6,14},{8,0},{10,2},{12,8},{14,10},{1,5},{3,7},... | collective-permute-start | bytes 786440 | tf_op jit(solution)/shard_map/ppermute | solution.py:275
  10.8 2.0 %absorb.8 = (f32[80,1024]{1,0:T(8,128)S(1)}, f32[8,1024]{1,0:T(8,128)S(1)}) custom-call(bf16[64,1024]{1,0:T(8,128)(2,1)S(1)} %get-tuple-element.162.refs_0_, bf16[128,1024]{1,0:T(8,128)(2,1)S(1)} %pad_maximum_fusion.1.refs_1_), custom_call_target="tpu_custom_call" | custom-call | tf_op jit(solution)/shard_map/absorb/pallas_call | solution.py:112
  12.8 2.6 %collective-permute-start.1 = (bf16[128,1024]{1,0:T(8,128)(2,1)S(1)}, bf16[128,1024]{1,0:T(8,128)(2,1)S(1)}, u32[]{:S(2)}, u32[]{:S(2)}) collective-permute-start(bf16[128,1024]{1,0:T(8,128)(2,1)S(1)} %pad_maximum_fusion.refs_1_), channel_id=1, source_target_pairs={{0,4},{2,6},{4,12},{6,14},{8,0},{10,2},{12,8},{14,10},{1,5},{3,7},... | collective-permute-start | bytes 786440 | tf_op jit(solution)/shard_map/ppermute | solution.py:275
  15.4 1.5 %collective-permute-start.6 = (f32[2,2,128]{2,1,0:T(2,128)S(1)}, f32[2,2,128]{2,1,0:T(2,128)S(1)}, u32[]{:S(2)}, u32[]{:S(2)}) collective-permute-start(f32[2,2,128]{2,1,0:T(2,128)S(1)} %bitcast.52), channel_id=1, source_target_pairs={{0,1},{1,0},{2,3},{3,2},{4,5},{5,4},{6,7},{7,6},{8,9},{9,8},{10,11... | collective-permute-start | bytes 6152 | tf_op jit(solution)/shard_map/ppermute | solution.py:259
  20.1 2.0 %absorb.9 = (f32[80,1024]{1,0:T(8,128)S(1)}, f32[8,1024]{1,0:T(8,128)S(1)}) custom-call(bf16[64,1024]{1,0:T(8,128)(2,1)S(1)} %get-tuple-element.161.refs_0_, bf16[128,1024]{1,0:T(8,128)(2,1)S(1)} %pad_maximum_fusion.refs_1_), custom_call_target="tpu_custom_call" | custom-call | tf_op jit(solution)/shard_map/absorb/pallas_call | solution.py:112
  22.1 2.5 %collective-permute-done.1.refs_1_ = bf16[128,1024]{1,0:T(8,128)(2,1)S(1)} collective-permute-done((bf16[128,1024]{1,0:T(8,128)(2,1)S(1)}, bf16[128,1024]{1,0:T(8,128)(2,1)S(1)}, u32[]{:S(2)}, u32[]{:S(2)}) %collective-permute-start.1) | collective-permute-done | bytes 262176 | tf_op jit(solution)/shard_map/ppermute | solution.py:275
  25.7 2.1 %absorb.10 = (f32[80,1024]{1,0:T(8,128)S(1)}, f32[8,1024]{1,0:T(8,128)S(1)}) custom-call(bf16[64,1024]{1,0:T(8,128)(2,1)S(1)} %get-tuple-element.162.refs_0_, bf16[128,1024]{1,0:T(8,128)(2,1)S(1)} %collective-permute-done.3.refs_1_, f32[80,1024]{1,0:T(8,128)S(1)} %get-tuple-element.91.refs_2_, ...), custom_call_target="tpu_custom_call", output_to_operand_aliasing={{0}: (2, {}), {1}: (3, {})} | custom-call | tf_op jit(solution)/shard_map/absorb/pallas_call | solution.py:112
  27.7 2.4 %collective-permute-done.5.refs_1_ = bf16[128,1024]{1,0:T(8,128)(2,1)S(1)} collective-permute-done((bf16[128,1024]{1,0:T(8,128)(2,1)S(1)}, bf16[128,1024]{1,0:T(8,128)(2,1)S(1)}, u32[]{:S(2)}, u32[]{:S(2)}) %collective-permute-start.5) | collective-permute-done | bytes 262176 | tf_op jit(solution)/shard_map/ppermute | solution.py:275
  31.3 2.1 %absorb.11 = (f32[80,1024]{1,0:T(8,128)S(1)}, f32[8,1024]{1,0:T(8,128)S(1)}) custom-call(bf16[64,1024]{1,0:T(8,128)(2,1)S(1)} %get-tuple-element.161.refs_0_, bf16[128,1024]{1,0:T(8,128)(2,1)S(1)} %collective-permute-done.1.refs_1_, f32[80,1024]{1,0:T(8,128)S(1)} %get-tuple-element.97.refs_2_, ...), custom_call_target="tpu_custom_call", output_to_operand_aliasing={{0}: (2, {}), {1}: (3, {})} | custom-call | tf_op jit(solution)/shard_map/absorb/pallas_call | solution.py:112
  33.4 2.4 %collective-permute-done.4.refs_1_ = bf16[128,1024]{1,0:T(8,128)(2,1)S(1)} collective-permute-done((bf16[128,1024]{1,0:T(8,128)(2,1)S(1)}, bf16[128,1024]{1,0:T(8,128)(2,1)S(1)}, u32[]{:S(2)}, u32[]{:S(2)}) %collective-permute-start.4) | collective-permute-done | bytes 262176 | tf_op jit(solution)/shard_map/ppermute | solution.py:275
  37.0 2.1 %absorb.12 = (f32[80,1024]{1,0:T(8,128)S(1)}, f32[8,1024]{1,0:T(8,128)S(1)}) custom-call(bf16[64,1024]{1,0:T(8,128)(2,1)S(1)} %get-tuple-element.162.refs_0_, bf16[128,1024]{1,0:T(8,128)(2,1)S(1)} %collective-permute-done.5.refs_1_, f32[80,1024]{1,0:T(8,128)S(1)} %get-tuple-element.110.refs_2_, ...), custom_call_target="tpu_custom_call", output_to_operand_aliasing={{0}: (2, {}), {1}: (3, {})} | custom-call | tf_op jit(solution)/shard_map/absorb/pallas_call | solution.py:112
  39.1 2.4 %collective-permute-done.8.refs_1_ = bf16[128,1024]{1,0:T(8,128)(2,1)S(1)} collective-permute-done((bf16[128,1024]{1,0:T(8,128)(2,1)S(1)}, bf16[128,1024]{1,0:T(8,128)(2,1)S(1)}, u32[]{:S(2)}, u32[]{:S(2)}) %collective-permute-start.8) | collective-permute-done | bytes 262176 | tf_op jit(solution)/shard_map/ppermute | solution.py:275
  41.4 2.1 %absorb.14 = (f32[80,1024]{1,0:T(8,128)S(1)}, f32[8,1024]{1,0:T(8,128)S(1)}) custom-call(bf16[64,1024]{1,0:T(8,128)(2,1)S(1)} %get-tuple-element.162.refs_0_, bf16[128,1024]{1,0:T(8,128)(2,1)S(1)} %collective-permute-done.8.refs_1_, f32[80,1024]{1,0:T(8,128)S(1)} %get-tuple-element.122.refs_2_, ...), custom_call_target="tpu_custom_call", output_to_operand_aliasing={{0}: (2, {}), {1}: (3, {})} | custom-call | tf_op jit(solution)/shard_map/absorb/pallas_call | solution.py:112
  43.5 2.1 %absorb.13 = (f32[80,1024]{1,0:T(8,128)S(1)}, f32[8,1024]{1,0:T(8,128)S(1)}) custom-call(bf16[64,1024]{1,0:T(8,128)(2,1)S(1)} %get-tuple-element.161.refs_0_, bf16[128,1024]{1,0:T(8,128)(2,1)S(1)} %collective-permute-done.4.refs_1_, f32[80,1024]{1,0:T(8,128)S(1)} %get-tuple-element.116.refs_2_, ...), custom_call_target="tpu_custom_call", output_to_operand_aliasing={{0}: (2, {}), {1}: (3, {})} | custom-call | tf_op jit(solution)/shard_map/absorb/pallas_call | solution.py:112
  46.7 2.1 %absorb.15 = (f32[80,1024]{1,0:T(8,128)S(1)}, f32[8,1024]{1,0:T(8,128)S(1)}) custom-call(bf16[64,1024]{1,0:T(8,128)(2,1)S(1)} %get-tuple-element.161.refs_0_, bf16[128,1024]{1,0:T(8,128)(2,1)S(1)} %collective-permute-done.7.refs_1_, f32[80,1024]{1,0:T(8,128)S(1)} %get-tuple-element.128.refs_2_, ...), custom_call_target="tpu_custom_call", output_to_operand_aliasing={{0}: (2, {}), {1}: (3, {})} | custom-call | tf_op jit(solution)/shard_map/absorb/pallas_call | solution.py:112
  49.2 1.3 %collective-permute-done.9 = f32[64,512]{1,0:T(8,128)S(1)} collective-permute-done((f32[64,512]{1,0:T(8,128)S(1)}, f32[64,512]{1,0:T(8,128)S(1)}, u32[]{:S(2)}, u32[]{:S(2)}) %collective-permute-start.9) | collective-permute-done | bytes 131104 | tf_op jit(solution)/shard_map/ppermute | solution.py:259
  50.5 1.6 %collective-permute-start.10 = (bf16[64,512]{1,0:T(8,128)(2,1)S(1)}, bf16[64,512]{1,0:T(8,128)(2,1)S(1)}, u32[]{:S(2)}, u32[]{:S(2)}) collective-permute-start(bf16[64,512]{1,0:T(8,128)(2,1)S(1)} %add_convert_fusion.1), channel_id=1, source_target_pairs={{0,1},{1,0},{2,3},{3,2},{4,5},{5,4},{6,7},{7,6},{8,9},{9,8},{10,11... | collective-permute-start | bytes 196616 | tf_op jit(solution)/shard_map/ppermute | solution.py:259
  52.1 2.7 %collective-permute-done.10 = bf16[64,512]{1,0:T(8,128)(2,1)S(1)} collective-permute-done((bf16[64,512]{1,0:T(8,128)(2,1)S(1)}, bf16[64,512]{1,0:T(8,128)(2,1)S(1)}, u32[]{:S(2)}, u32[]{:S(2)}) %collective-permute-start.10) | collective-permute-done | bytes 65568 | tf_op jit(solution)/shard_map/ppermute | solution.py:259
  54.9 2.7 %collective-permute-start.12 = (bf16[80,512]{1,0:T(8,128)(2,1)S(1)}, bf16[80,512]{1,0:T(8,128)(2,1)S(1)}, u32[]{:S(2)}, u32[]{:S(2)}) collective-permute-start(bf16[80,512]{1,0:T(8,128)(2,1)S(1)} %pad_maximum_fusion.4.own_map), channel_id=1, source_target_pairs={{0,4},{2,6},{4,8},{6,10},{8,12},{10,14},{1,5},{3,7},{5,9},{7,11},{... | collective-permute-start | bytes 245768 | tf_op jit(solution)/shard_map/ppermute | solution.py:265
  57.6 1.3 %collective-permute-start.13 = (bf16[80,512]{1,0:T(8,128)(2,1)S(1)}, bf16[80,512]{1,0:T(8,128)(2,1)S(1)}, u32[]{:S(2)}, u32[]{:S(2)}) collective-permute-start(bf16[80,512]{1,0:T(8,128)(2,1)S(1)} %pad_maximum_fusion.4.own_map), channel_id=1, source_target_pairs={{4,0},{6,2},{8,4},{10,6},{12,8},{14,10},{5,1},{7,3},{9,5},{11,7},{... | collective-permute-start | bytes 245768 | tf_op jit(solution)/shard_map/ppermute | solution.py:265
  59.7 4.3 %collective-permute-done.13 = bf16[80,512]{1,0:T(8,128)(2,1)S(1)} collective-permute-done((bf16[80,512]{1,0:T(8,128)(2,1)S(1)}, bf16[80,512]{1,0:T(8,128)(2,1)S(1)}, u32[]{:S(2)}, u32[]{:S(2)}) %collective-permute-start.13) | collective-permute-done | bytes 81952 | tf_op jit(solution)/shard_map/ppermute | solution.py:265
  65.5 3.8 %network.1 = (f32[2,1024]{1,0:T(2,128)S(1)}, f32[32,576]{1,0:T(8,128)S(1)}, f32[64,128]{1,0:T(8,128)S(1)}) custom-call(s32[3]{0:T(128)S(1)} %pad_add_fusion.place, bf16[80,512]{1,0:T(8,128)(2,1)S(1)} %pad_maximum_fusion.4.own_map, bf16[80,512]{1,0:T(8,128)(2,1)S(1)} %collective-permute-done.11.other_map, ...), custom_call_target="tpu_custom_call" | custom-call | tf_op jit(solution)/shard_map/network/pallas_call | solution.py:242
  69.3 1.6 %collective-permute-start.15 = (bf16[32,896]{1,0:T(8,128)(2,1)S(1)}, bf16[32,896]{1,0:T(8,128)(2,1)S(1)}, u32[]{:S(2)}, u32[]{:S(2)}) collective-permute-start(bf16[32,896]{1,0:T(8,128)(2,1)S(1)} %fusion.14), channel_id=1, source_target_pairs={{0,16},{16,0},{1,17},{17,1},{2,18},{18,2},{3,19},{19,3},{4,20},{20... | collective-permute-start | bytes 172040 | tf_op jit(solution)/shard_map/ppermute | solution.py:265
  70.9 2.6 %collective-permute-done.15 = bf16[32,896]{1,0:T(8,128)(2,1)S(1)} collective-permute-done((bf16[32,896]{1,0:T(8,128)(2,1)S(1)}, bf16[32,896]{1,0:T(8,128)(2,1)S(1)}, u32[]{:S(2)}, u32[]{:S(2)}) %collective-permute-start.15) | collective-permute-done | bytes 57376 | tf_op jit(solution)/shard_map/ppermute | solution.py:265
  73.6 3.4 %collective-permute-start.16 = (bf16[32,896]{1,0:T(8,128)(2,1)S(1)}, bf16[32,896]{1,0:T(8,128)(2,1)S(1)}, u32[]{:S(2)}, u32[]{:S(2)}) collective-permute-start(bf16[32,896]{1,0:T(8,128)(2,1)S(1)} %add_convert_fusion.2), channel_id=1, source_target_pairs={{0,8},{2,10},{4,12},{6,14},{8,0},{10,2},{12,4},{14,6},{1,9},{3,11}... | collective-permute-start | bytes 172040 | tf_op jit(solution)/shard_map/ppermute | solution.py:265
  77.1 3.8 %collective-permute-start.18 = (bf16[32,896]{1,0:T(8,128)(2,1)S(1)}, bf16[32,896]{1,0:T(8,128)(2,1)S(1)}, u32[]{:S(2)}, u32[]{:S(2)}) collective-permute-start(bf16[32,896]{1,0:T(8,128)(2,1)S(1)} %add_convert_fusion.2), channel_id=1, source_target_pairs={{0,12},{2,14},{4,0},{6,2},{8,4},{10,6},{12,8},{14,10},{1,13},{3,15... | collective-permute-start | bytes 172040 | tf_op jit(solution)/shard_map/ppermute | solution.py:265
  81.5 1.5 %collective-permute-done.17 = bf16[32,896]{1,0:T(8,128)(2,1)S(1)} collective-permute-done((bf16[32,896]{1,0:T(8,128)(2,1)S(1)}, bf16[32,896]{1,0:T(8,128)(2,1)S(1)}, u32[]{:S(2)}, u32[]{:S(2)}) %collective-permute-start.17) | collective-permute-done | bytes 57376 | tf_op jit(solution)/shard_map/ppermute | solution.py:265
  83.2 1.6 %collective-permute-start.19 = (f32[32,576]{1,0:T(8,128)S(1)}, f32[32,576]{1,0:T(8,128)S(1)}, u32[]{:S(2)}, u32[]{:S(2)}) collective-permute-start(f32[32,576]{1,0:T(8,128)S(1)} %get-tuple-element.154), channel_id=1, source_target_pairs={{0,1},{1,0},{2,3},{3,2},{4,5},{5,4},{6,7},{7,6},{8,9},{9,8},{10,11... | collective-permute-start | bytes 221192 | tf_op jit(solution)/shard_map/ppermute | solution.py:259
  85.0 1.6 %fusion.3 = f32[256,1024]{1,0:T(8,128)} fusion(bf16[1024,64]{0,1:T(8,128)(2,1)S(1)} %copy-done.6, f32[64,128]{1,0:T(8,128)S(1)} %collective-permute-done.20, f32[32,128]{1,0:T(8,128)S(1)} %get-tuple-element.156, f32[32,128]{1,0:T(8,128)S(1)} %get-tuple-element.155, pred[]{:T(512)S(6)} %eq.5), kind=kOutput, calls=%fused_computation.25 | convolution fusion | flops 201408512 | bytes 1245185 | tf_op jit(solution)/shard_map/dot_general | solution.py:388
  86.6 1.5 %collective-permute-done.19 = f32[32,576]{1,0:T(8,128)S(1)} collective-permute-done((f32[32,576]{1,0:T(8,128)S(1)}, f32[32,576]{1,0:T(8,128)S(1)}, u32[]{:S(2)}, u32[]{:S(2)}) %collective-permute-start.19) | collective-permute-done | bytes 73760 | tf_op jit(solution)/shard_map/ppermute | solution.py:259
  (93 shorter events, 18.1 us)
Async XLA Ops:
  0.6 17.4 %copy-start = (bf16[256,1024]{1,0:T(8,128)(2,1)S(1)}, bf16[256,1024]{1,0:T(8,128)(2,1)}, u32[]{:S(2)}) copy-start(bf16[256,1024]{1,0:T(8,128)(2,1)} %param.11) | copy-start | bytes 1572868
  4.9 3.1 %collective-permute-start = (bf16[2,128,512]{2,1,0:T(8,128)(2,1)S(1)}, bf16[2,128,512]{2,1,0:T(8,128)(2,1)S(1)}, u32[]{:S(2)}, u32[]{:S(2)}) collective-permute-start(bf16[2,128,512]{2,1,0:T(8,128)(2,1)S(1)} %get-tuple-element.77), channel_id=1, source_target_pairs={{0,2},{2,0},{4,6},{6,4},{8,10},{10,8},{12,14},{14,12},{1,3},{3,1},... | collective-permute-start | bytes 786440 | tf_op jit(solution)/shard_map/ppermute | solution.py:259
  6.5 1.4 %collective-permute-start.2 = (bf16[2,64,512]{2,1,0:T(8,128)(2,1)S(1)}, bf16[2,64,512]{2,1,0:T(8,128)(2,1)S(1)}, u32[]{:S(2)}, u32[]{:S(2)}) collective-permute-start(bf16[2,64,512]{2,1,0:T(8,128)(2,1)S(1)} %get-tuple-element.80), channel_id=1, source_target_pairs={{0,2},{2,0},{4,6},{6,4},{8,10},{10,8},{12,14},{14,12},{1,3},{3,1},... | collective-permute-start | bytes 393224 | tf_op jit(solution)/shard_map/ppermute | solution.py:259
  7.2 8.2 %copy-start.11 = (f32[1,2,2,128]{3,2,1,0:T(2,128)S(1)}, f32[1,2,2,128]{3,2,1,0:T(2,128)}, u32[]{:S(2)}) copy-start(f32[1,2,2,128]{3,2,1,0:T(2,128)} %param.15) | copy-start | bytes 6148
  7.2 9.7 %copy-start.3 = (bf16[1,512,1024]{2,1,0:T(8,128)(2,1)S(1)}, bf16[1,512,1024]{2,1,0:T(8,128)(2,1)}, u32[]{:S(2)}) copy-start(bf16[1,512,1024]{2,1,0:T(8,128)(2,1)} %param.8) | copy-start | bytes 3145732
  7.2 9.7 %copy-start.6 = (bf16[1024,64]{0,1:T(8,128)(2,1)S(1)}, bf16[1024,64]{0,1:T(8,128)(2,1)}, u32[]{:S(2)}) copy-start(bf16[1024,64]{0,1:T(8,128)(2,1)} %param.12) | copy-start | bytes 393220
  7.2 5.5 %copy-start.10 = (bf16[128,512]{1,0:T(8,128)(2,1)S(1)}, bf16[128,512]{1,0:T(8,128)(2,1)}, u32[]{:S(2)}) copy-start(bf16[128,512]{1,0:T(8,128)(2,1)} %get-tuple-element.146) | copy-start | bytes 393220
  8.0 10.3 %copy-start.8 = (bf16[2,64,576]{2,1,0:T(8,128)(2,1)S(1)}, bf16[2,64,576]{2,1,0:T(8,128)(2,1)}, u32[]{:S(2)}) copy-start(bf16[2,64,576]{2,1,0:T(8,128)(2,1)} %param.13) | copy-start | bytes 442372
  8.0 11.6 %collective-permute-start.3 = (bf16[128,1024]{1,0:T(8,128)(2,1)S(1)}, bf16[128,1024]{1,0:T(8,128)(2,1)S(1)}, u32[]{:S(2)}, u32[]{:S(2)}) collective-permute-start(bf16[128,1024]{1,0:T(8,128)(2,1)S(1)} %pad_maximum_fusion.1.refs_1_), channel_id=1, source_target_pairs={{0,4},{2,6},{4,12},{6,14},{8,0},{10,2},{12,8},{14,10},{1,5},{3,7},... | collective-permute-start | bytes 786440 | tf_op jit(solution)/shard_map/ppermute | solution.py:275
  12.8 11.8 %collective-permute-start.1 = (bf16[128,1024]{1,0:T(8,128)(2,1)S(1)}, bf16[128,1024]{1,0:T(8,128)(2,1)S(1)}, u32[]{:S(2)}, u32[]{:S(2)}) collective-permute-start(bf16[128,1024]{1,0:T(8,128)(2,1)S(1)} %pad_maximum_fusion.refs_1_), channel_id=1, source_target_pairs={{0,4},{2,6},{4,12},{6,14},{8,0},{10,2},{12,8},{14,10},{1,5},{3,7},... | collective-permute-start | bytes 786440 | tf_op jit(solution)/shard_map/ppermute | solution.py:275
  15.4 4.6 %collective-permute-start.6 = (f32[2,2,128]{2,1,0:T(2,128)S(1)}, f32[2,2,128]{2,1,0:T(2,128)S(1)}, u32[]{:S(2)}, u32[]{:S(2)}) collective-permute-start(f32[2,2,128]{2,1,0:T(2,128)S(1)} %bitcast.52), channel_id=1, source_target_pairs={{0,1},{1,0},{2,3},{3,2},{4,5},{5,4},{6,7},{7,6},{8,9},{9,8},{10,11... | collective-permute-start | bytes 6152 | tf_op jit(solution)/shard_map/ppermute | solution.py:259
  19.6 10.6 %collective-permute-start.5 = (bf16[128,1024]{1,0:T(8,128)(2,1)S(1)}, bf16[128,1024]{1,0:T(8,128)(2,1)S(1)}, u32[]{:S(2)}, u32[]{:S(2)}) collective-permute-start(bf16[128,1024]{1,0:T(8,128)(2,1)S(1)} %collective-permute-done.3.refs_1_), channel_id=1, source_target_pairs={{0,4},{2,6},{4,12},{6,14},{8,0},{10,2},{12,8},{14,10},{1,5},{3,7},... | collective-permute-start | bytes 786440 | tf_op jit(solution)/shard_map/ppermute | solution.py:275
  24.6 11.2 %collective-permute-start.4 = (bf16[128,1024]{1,0:T(8,128)(2,1)S(1)}, bf16[128,1024]{1,0:T(8,128)(2,1)S(1)}, u32[]{:S(2)}, u32[]{:S(2)}) collective-permute-start(bf16[128,1024]{1,0:T(8,128)(2,1)S(1)} %collective-permute-done.1.refs_1_), channel_id=1, source_target_pairs={{0,4},{2,6},{4,12},{6,14},{8,0},{10,2},{12,8},{14,10},{1,5},{3,7},... | collective-permute-start | bytes 786440 | tf_op jit(solution)/shard_map/ppermute | solution.py:275
  30.2 11.2 %collective-permute-start.8 = (bf16[128,1024]{1,0:T(8,128)(2,1)S(1)}, bf16[128,1024]{1,0:T(8,128)(2,1)S(1)}, u32[]{:S(2)}, u32[]{:S(2)}) collective-permute-start(bf16[128,1024]{1,0:T(8,128)(2,1)S(1)} %collective-permute-done.5.refs_1_), channel_id=1, source_target_pairs={{0,4},{2,6},{4,12},{6,14},{8,0},{10,2},{12,8},{14,10},{1,5},{3,7},... | collective-permute-start | bytes 786440 | tf_op jit(solution)/shard_map/ppermute | solution.py:275
  35.8 10.9 %collective-permute-start.7 = (bf16[128,1024]{1,0:T(8,128)(2,1)S(1)}, bf16[128,1024]{1,0:T(8,128)(2,1)S(1)}, u32[]{:S(2)}, u32[]{:S(2)}) collective-permute-start(bf16[128,1024]{1,0:T(8,128)(2,1)S(1)} %collective-permute-done.4.refs_1_), channel_id=1, source_target_pairs={{0,4},{2,6},{4,12},{6,14},{8,0},{10,2},{12,8},{14,10},{1,5},{3,7},... | collective-permute-start | bytes 786440 | tf_op jit(solution)/shard_map/ppermute | solution.py:275
  41.4 9.1 %copy-start.9 = (f32[64,512]{1,0:T(8,128)S(1)}, f32[64,512]{1,0:T(8,128)}, u32[]{:S(2)}) copy-start(f32[64,512]{1,0:T(8,128)} %fusion.27) | copy-start | bytes 393220
  45.5 19.0 %copy-start.7 = (bf16[2,3,64,3,64]{2,4,3,1,0:T(8,128)(2,1)S(1)}, bf16[2,3,64,3,64]{2,4,3,1,0:T(8,128)(2,1)}, u32[]{:S(2)}) copy-start(bf16[2,3,64,3,64]{2,4,3,1,0:T(8,128)(2,1)} %copy.26) | copy-start | bytes 442372
  46.7 18.8 %copy-start.5 = (bf16[2,64]{1,0:T(2,128)(2,1)S(1)}, bf16[2,64]{1,0:T(2,128)(2,1)}, u32[]{:S(2)}) copy-start(bf16[2,64]{1,0:T(2,128)(2,1)} %head.1) | copy-start | bytes 772
  49.1 1.4 %collective-permute-start.9 = (f32[64,512]{1,0:T(8,128)S(1)}, f32[64,512]{1,0:T(8,128)S(1)}, u32[]{:S(2)}, u32[]{:S(2)}) collective-permute-start(f32[64,512]{1,0:T(8,128)S(1)} %slice.56), channel_id=1, source_target_pairs={{0,2},{2,0},{4,6},{6,4},{8,10},{10,8},{12,14},{14,12},{1,3},{3,1},... | collective-permute-start | bytes 393224 | tf_op jit(solution)/shard_map/ppermute | solution.py:259
  50.5 4.3 %collective-permute-start.10 = (bf16[64,512]{1,0:T(8,128)(2,1)S(1)}, bf16[64,512]{1,0:T(8,128)(2,1)S(1)}, u32[]{:S(2)}, u32[]{:S(2)}) collective-permute-start(bf16[64,512]{1,0:T(8,128)(2,1)S(1)} %add_convert_fusion.1), channel_id=1, source_target_pairs={{0,1},{1,0},{2,3},{3,2},{4,5},{5,4},{6,7},{7,6},{8,9},{9,8},{10,11... | collective-permute-start | bytes 196616 | tf_op jit(solution)/shard_map/ppermute | solution.py:259
  54.9 4.8 %collective-permute-start.12 = (bf16[80,512]{1,0:T(8,128)(2,1)S(1)}, bf16[80,512]{1,0:T(8,128)(2,1)S(1)}, u32[]{:S(2)}, u32[]{:S(2)}) collective-permute-start(bf16[80,512]{1,0:T(8,128)(2,1)S(1)} %pad_maximum_fusion.4.own_map), channel_id=1, source_target_pairs={{0,4},{2,6},{4,8},{6,10},{8,12},{10,14},{1,5},{3,7},{5,9},{7,11},{... | collective-permute-start | bytes 245768 | tf_op jit(solution)/shard_map/ppermute | solution.py:265
  57.6 6.3 %collective-permute-start.13 = (bf16[80,512]{1,0:T(8,128)(2,1)S(1)}, bf16[80,512]{1,0:T(8,128)(2,1)S(1)}, u32[]{:S(2)}, u32[]{:S(2)}) collective-permute-start(bf16[80,512]{1,0:T(8,128)(2,1)S(1)} %pad_maximum_fusion.4.own_map), channel_id=1, source_target_pairs={{4,0},{6,2},{8,4},{10,6},{12,8},{14,10},{5,1},{7,3},{9,5},{11,7},{... | collective-permute-start | bytes 245768 | tf_op jit(solution)/shard_map/ppermute | solution.py:265
  64.0 1.5 %collective-permute-start.14 = (bf16[80,1024]{1,0:T(8,128)(2,1)S(1)}, bf16[80,1024]{1,0:T(8,128)(2,1)S(1)}, u32[]{:S(2)}, u32[]{:S(2)}) collective-permute-start(bf16[80,1024]{1,0:T(8,128)(2,1)S(1)} %constant_dynamic-update-slice_fusion.rims), channel_id=1, source_target_pairs={{0,2},{2,0},{4,6},{6,4},{8,10},{10,8},{12,14},{14,12},{1,3},{3,1},... | collective-permute-start | bytes 491528 | tf_op jit(solution)/shard_map/ppermute | solution.py:259
  64.0 1.5 %collective-permute-start.11 = (bf16[80,512]{1,0:T(8,128)(2,1)S(1)}, bf16[80,512]{1,0:T(8,128)(2,1)S(1)}, u32[]{:S(2)}, u32[]{:S(2)}) collective-permute-start(bf16[80,512]{1,0:T(8,128)(2,1)S(1)} %pad_maximum_fusion.4.own_map), channel_id=1, source_target_pairs={{0,2},{2,0},{4,6},{6,4},{8,10},{10,8},{12,14},{14,12},{1,3},{3,1},... | collective-permute-start | bytes 245768 | tf_op jit(solution)/shard_map/ppermute | solution.py:259
  69.3 4.2 %collective-permute-start.15 = (bf16[32,896]{1,0:T(8,128)(2,1)S(1)}, bf16[32,896]{1,0:T(8,128)(2,1)S(1)}, u32[]{:S(2)}, u32[]{:S(2)}) collective-permute-start(bf16[32,896]{1,0:T(8,128)(2,1)S(1)} %fusion.14), channel_id=1, source_target_pairs={{0,16},{16,0},{1,17},{17,1},{2,18},{18,2},{3,19},{19,3},{4,20},{20... | collective-permute-start | bytes 172040 | tf_op jit(solution)/shard_map/ppermute | solution.py:265
  73.6 7.9 %collective-permute-start.16 = (bf16[32,896]{1,0:T(8,128)(2,1)S(1)}, bf16[32,896]{1,0:T(8,128)(2,1)S(1)}, u32[]{:S(2)}, u32[]{:S(2)}) collective-permute-start(bf16[32,896]{1,0:T(8,128)(2,1)S(1)} %add_convert_fusion.2), channel_id=1, source_target_pairs={{0,8},{2,10},{4,12},{6,14},{8,0},{10,2},{12,4},{14,6},{1,9},{3,11}... | collective-permute-start | bytes 172040 | tf_op jit(solution)/shard_map/ppermute | solution.py:265
  77.1 6.0 %collective-permute-start.17 = (bf16[32,896]{1,0:T(8,128)(2,1)S(1)}, bf16[32,896]{1,0:T(8,128)(2,1)S(1)}, u32[]{:S(2)}, u32[]{:S(2)}) collective-permute-start(bf16[32,896]{1,0:T(8,128)(2,1)S(1)} %add_convert_fusion.2), channel_id=1, source_target_pairs={{0,4},{2,6},{4,8},{6,10},{8,12},{10,14},{12,0},{14,2},{1,5},{3,7},... | collective-permute-start | bytes 172040 | tf_op jit(solution)/shard_map/ppermute | solution.py:265
  77.1 6.0 %collective-permute-start.18 = (bf16[32,896]{1,0:T(8,128)(2,1)S(1)}, bf16[32,896]{1,0:T(8,128)(2,1)S(1)}, u32[]{:S(2)}, u32[]{:S(2)}) collective-permute-start(bf16[32,896]{1,0:T(8,128)(2,1)S(1)} %add_convert_fusion.2), channel_id=1, source_target_pairs={{0,12},{2,14},{4,0},{6,2},{8,4},{10,6},{12,8},{14,10},{1,13},{3,15... | collective-permute-start | bytes 172040 | tf_op jit(solution)/shard_map/ppermute | solution.py:265
  83.1 1.9 %collective-permute-start.20 = (f32[64,128]{1,0:T(8,128)S(1)}, f32[64,128]{1,0:T(8,128)S(1)}, u32[]{:S(2)}, u32[]{:S(2)}) collective-permute-start(f32[64,128]{1,0:T(8,128)S(1)} %pad_maximum_fusion.5), channel_id=1, source_target_pairs={{0,2},{2,0},{4,6},{6,4},{8,10},{10,8},{12,14},{14,12},{1,3},{3,1},... | collective-permute-start | bytes 98312 | tf_op jit(solution)/shard_map/ppermute | solution.py:259
  83.2 4.9 %collective-permute-start.19 = (f32[32,576]{1,0:T(8,128)S(1)}, f32[32,576]{1,0:T(8,128)S(1)}, u32[]{:S(2)}, u32[]{:S(2)}) collective-permute-start(f32[32,576]{1,0:T(8,128)S(1)} %get-tuple-element.154), channel_id=1, source_target_pairs={{0,1},{1,0},{2,3},{3,2},{4,5},{5,4},{6,7},{7,6},{8,9},{9,8},{10,11... | collective-permute-start | bytes 221192 | tf_op jit(solution)/shard_map/ppermute | solution.py:259
  84.8 3.3 %collective-permute-start.21 = (f32[32,576]{1,0:T(8,128)S(1)}, f32[32,576]{1,0:T(8,128)S(1)}, u32[]{:S(2)}, u32[]{:S(2)}) collective-permute-start(f32[32,576]{1,0:T(8,128)S(1)} %get-tuple-element.154), channel_id=1, source_target_pairs={{0,2},{2,0},{4,6},{6,4},{8,10},{10,8},{12,14},{14,12},{1,3},{3,1},... | collective-permute-start | bytes 221192 | tf_op jit(solution)/shard_map/ppermute | solution.py:259
  88.1 1.3 %collective-permute-start.22 = (f32[32,576]{1,0:T(8,128)S(1)}, f32[32,576]{1,0:T(8,128)S(1)}, u32[]{:S(2)}, u32[]{:S(2)}) collective-permute-start(f32[32,576]{1,0:T(8,128)S(1)} %collective-permute-done.19), channel_id=1, source_target_pairs={{0,2},{2,0},{4,6},{6,4},{8,10},{10,8},{12,14},{14,12},{1,3},{3,1},... | collective-permute-start | bytes 221192 | tf_op jit(solution)/shard_map/ppermute | solution.py:259
  (3 other events, 4.9 us)

commit v7 on v6

--- a/solution.py
+++ b/solution.py
@@ -6,6 +6,7 @@
 from jax.experimental import pallas as pl
 from jax.experimental.pallas import tpu as pltpu
 from jax.sharding import PartitionSpec as P
+
 
 HEAD = 64
 EPSILON = 1e-05
@@ -34,8 +35,7 @@
     values = tokens[...].astype(F32)
     center = values - jnp.mean(values, axis=-1, keepdims=True)
     spread = jnp.mean(center * center, axis=-1, keepdims=True)
-    wide_gain = gain[...].astype(F32)[None, :]
-    normed[...] = (center * lax.rsqrt(spread + EPSILON) * wide_gain).astype(BF16)
+    normed[...] = (center * lax.rsqrt(spread + EPSILON) * gain[...]).astype(BF16)
 
 
 def normalize(tokens, gain):
@@ -120,27 +120,41 @@
     )(queries, block, *(() if first else state))
 
 
-def finish_kernel(*refs):
+def closing_kernel(start, queries, block, *refs):
     states, (folded, context, share) = refs[:-3], refs[-3:]
-    for head, state in enumerate(states):
-        context[head * HEAD : (head + 1) * HEAD, :] = (state[:HEAD, :] / state[HEAD : HEAD + 1, :]).astype(BF16)
+    carried, carried_top = states[-2:]
+    length = context.shape[1]
+    where = slice(start, start + length)
+    keys = block[:HEAD, :].T
+    values = jnp.concatenate([block[HEAD:, :], jnp.ones((16, block.shape[1]), BF16)], axis=0)
+    depth = min(512, block.shape[1])
+    running, best = carried[:, where], carried_top[0:1, where]
+    for below in range(0, block.shape[1], depth):
+        scores = dot(keys[below : below + depth], queries[:, where])
+        raised_top = jnp.maximum(best, jnp.max(scores, axis=0, keepdims=True))
+        weights = jnp.exp(scores - raised_top).astype(BF16)
+        running = running * jnp.exp(best - raised_top) + dot(values[:, below : below + depth], weights)
+        best = raised_top
+    sums = [state[:, where] for state in states[:-2]] + [running]
+    for head, state in enumerate(sums):
+        context[head * HEAD : (head + 1) * HEAD, :] = (state[:HEAD] / state[HEAD : HEAD + 1]).astype(BF16)
     whole = context[...]
     share[...] = sum(dot(part, whole) for part in split3(folded[...]))
 
 
-def finish(states, folded):
-    count = states[0].shape[1]
+def closing(start, length, queries, block, states, folded):
+    sums = [state[0] for state in states[:-1]] + list(states[-1])
     return pl.pallas_call(
-        finish_kernel,
+        functools.partial(closing_kernel, start),
         out_shape=(
-            jax.ShapeDtypeStruct((len(states) * HEAD, count), BF16),
-            jax.ShapeDtypeStruct((folded.shape[0], count), F32),
+            jax.ShapeDtypeStruct((len(states) * HEAD, length), BF16),
+            jax.ShapeDtypeStruct((folded.shape[0], length), F32),
         ),
-        in_specs=[VMEM] * (len(states) + 1),
+        in_specs=[VMEM] * (len(sums) + 3),
         out_specs=(VMEM, VMEM),
         compiler_params=PARAMS,
-        name="finish",
-    )(*states, folded)
+        name="closing",
+    )(queries, block, *sums, folded)
 
 
 def turned(values, step):
@@ -162,23 +176,22 @@
 
 
 def network_kernel(
-    cols, frame_rows, place, own_map, other_map, rims, other_rims, forward, backward, head, context, holo, sums,
-    gradient, hidden, pre_one, pre_two,
+    cols, frame_rows, place, chip_map, near, far, forward, backward, head, own_context, their_context, holo, sums,
+    gradient, hidden, pre_one, pre_two, grads,
 ):
     core, half, row_at = place[0], place[1], place[2]
-    own = context.shape[1]
+    own = chip_map.shape[1]
     cells = hidden.shape[1]
     rim = (cells - own) // 2
     row_count = cells // cols
     above = rim // cols
     first_row = row_at - above
     piece = own // 2
-    for order, (mine, theirs, at) in enumerate(
-        ((rims, other_rims, 0), (own_map, other_map, 0), (rims, other_rims, piece))
-    ):
-        for which, source in ((core, mine), (1 - core, theirs)):
-            start = pl.multiple_of(order * own + which * piece, 128)
-            hidden[:, pl.ds(start, piece)] = source[:, at : at + piece]
+    down = (core == place[3]).astype(jnp.int32)
+    for source, base, lead in ((chip_map, own, core), (near, 2 * own * down, core), (far, 2 * own * (1 - down), 1 - core)):
+        for side in range(2):
+            start = pl.multiple_of(base + lax.rem(lead + side, 2) * piece, 128)
+            hidden[:, pl.ds(start, piece)] = source[:, side * piece : (side + 1) * piece]
 
     def inside(start_row, rows):
         lane = lax.broadcasted_iota(jnp.int32, (1, rows * cols), 1)
@@ -225,33 +238,31 @@
             rows = pre[pl.ds(pl.multiple_of(half * share, 16), share), :]
             sums[:, :taps] = lax.dot_general(rows, stacked, NT, preferred_element_type=F32)
 
-    total = None
-    for side in range(2):
-        where = lax.rem(core + side, 2)
-        seen = context[:, pl.ds(pl.multiple_of(where * piece, 128), piece)]
-        term = lax.dot_general(
-            grad_zero[:, side * piece : (side + 1) * piece], seen, NT, preferred_element_type=F32
+    grads[...] = grad_zero
+    gradient[...] = sum(
+        lax.dot_general(
+            grads[:, pl.ds(pl.multiple_of(at * piece, 128), piece)], seen[...], NT, preferred_element_type=F32
         )
-        total = term if total is None else total + term
-    gradient[...] = total
-
-
-def network(place, maps, forward, backward, head, context, cols, frame_rows, col_count):
-    own = context.shape[1]
+        for at, seen in ((core, own_context), (1 - core, their_context))
+    )
+
+
+def network(place, maps, forward, backward, head, own_context, their_context, cols, frame_rows, col_count):
+    own = maps[0].shape[1]
     channels = forward.shape[2]
     return pl.pallas_call(
         functools.partial(network_kernel, cols, frame_rows),
         out_shape=(
             jax.ShapeDtypeStruct((head.shape[0], own), F32),
             jax.ShapeDtypeStruct((channels // col_count, 9 * channels), F32),
-            jax.ShapeDtypeStruct((channels, context.shape[0]), F32),
+            jax.ShapeDtypeStruct((channels, own_context.shape[0]), F32),
         ),
         in_specs=[SMEM] + [VMEM] * 8,
         out_specs=(VMEM,) * 3,
-        scratch_shapes=[pltpu.VMEM((maps[0].shape[0], 3 * own), BF16)] + [pltpu.VMEM((channels, own), BF16)] * 2,
+        scratch_shapes=[pltpu.VMEM((maps[0].shape[0], 3 * own), BF16)] + [pltpu.VMEM((channels, own), BF16)] * 3,
         compiler_params=PARAMS,
         name="network",
-    )(place, *maps, forward, backward, head, context)
+    )(place, *maps, forward, backward, head, own_context, their_context)
 
 
 def swapped(values, axis):
@@ -263,6 +274,17 @@
     size = lax.axis_size(axis)
     pairs = [(i, (i + step) % size) for i in range(size) if wrap or 0 <= i + step < size]
     return lax.ppermute(values, axis, pairs)
+
+
+def beside(values):
+    size = lax.axis_size("tok")
+    chips = size // 2
+    pairs = []
+    for at in range(chips):
+        for core, other in ((0, at ^ 1), (1, ((at + 1) ^ 1) - 1)):
+            if 0 <= other < chips:
+                pairs.append((2 * at + core, 2 * other + core))
+    return lax.ppermute(values, "tok", pairs)
 
 
 def round_ring(values):
@@ -290,7 +312,7 @@
     )
 
 
-def shards(
+def step(
     tokens, ln_gain, qkv_weight, out_weight, readout_weight, conv_weight, head_weight, holo_cot
 ):
     frame_rows = tokens[0]
@@ -301,20 +323,20 @@
     tok_at, half = lax.axis_index("tok"), lax.axis_index("col")
     core = lax.rem(tok_at, 2)
     chip_row = (tok_at - core) * rows_dev
-    place = jnp.stack([core, half, chip_row]).astype(jnp.int32)
+    place = jnp.stack([core, half, chip_row, lax.rem(tok_at // 2, 2)]).astype(jnp.int32)
     layers, channels = conv_weight.shape[:2]
     cols = cols_dev * col_count
     length = frame_rows.shape[0]
 
-    normed = normalize(frame_rows, ln_gain)
+    normed = normalize(frame_rows, ln_gain.astype(F32).reshape(1, -1))
     own_keyed, their_keyed = project((1, 2), place, normed, qkv_weight)
-    own_keyed, their_keyed, normed = lax.optimization_barrier((own_keyed, their_keyed, normed))
     got_keyed = swapped(their_keyed, "tok")
-    own_queries, their_queries = project((0,), place, normed, qkv_weight)
-    got_queries = swapped(their_queries, "tok")
     count = got_keyed.shape[0]
     kept = count * HEAD
     blocks = [jnp.concatenate([own_keyed[head], got_keyed[head]], axis=1) for head in range(count)]
+    blocks, normed = lax.optimization_barrier((blocks, normed))
+    own_queries, their_queries = project((0,), place, normed, qkv_weight)
+    got_queries = swapped(their_queries, "tok")
     queries = [jnp.concatenate([own_queries[head], got_queries[head]], axis=1) for head in range(count)]
     states = [None] * count
 
@@ -333,15 +355,21 @@
         return (forward, backward, folded, direct, exact_cot)
 
     for turn in range(chips):
-        arriving = [round_ring(block) for block in blocks] if turn < chips - 1 else blocks
+        arriving = blocks
+        if turn < chips - 1:
+            arriving = []
+            for block in blocks:
+                arriving.append(round_ring(block))
         for head in range(count):
+            if turn == chips - 1 and head == count - 1:
+                break
             states[head] = absorb(queries[head], blocks[head], states[head])
             if turn == 0 and head == 0:
                 states[head], given = lax.optimization_barrier(
                     (states[head], (conv_weight, out_weight, readout_weight, frame_rows, cotangent))
                 )
                 prepared = prepare(*given)
-            if turn == min(1, chips - 1) and head == count - 1:
+            if turn == min(1, chips - 2) and head == count - 1:
                 states[head], prepared = lax.optimization_barrier((states[head], prepared))
             arriving[head], states[head] = lax.optimization_barrier((arriving[head], states[head]))
             if head + 1 < count:
@@ -354,16 +382,19 @@
         blocks = arriving
     forward, backward, folded, direct, exact_cot = prepared
 
-    context, share = finish([state[0] for state in states], folded)
-    partial = share[:, :length] + swapped(share[:, length:], "tok")
+    last = (queries[-1], blocks[-1], states, folded)
+    their_context, their_share = closing(length, length, *last)
+    own_context, own_share = closing(0, length, *last)
+    partial = own_share + swapped(their_share, "tok")
     partial = (partial + jnp.where(half == 0, direct, 0.0)).astype(BF16)
     own_map = (partial.astype(F32) + swapped(partial, "col").astype(F32)).astype(BF16)
     own_map = jnp.concatenate([own_map, exact_cot], axis=0)
-    rims = jnp.concatenate([passed(own_map, "tok", 2, False), passed(own_map, "tok", -2, False)], axis=1)
+    chip_map = jnp.concatenate([own_map, swapped(own_map, "tok")], axis=1)
+    near = beside(chip_map)
     rows_chip = 2 * rows_dev
-    maps = (own_map, swapped(own_map, "tok"), rims, swapped(rims, "tok"))
+    maps = (chip_map, near, swapped(near, "tok"))
     holo, sums, gradient = network(
-        place, maps, forward, backward, head_weight, context, cols, tok_count * rows_dev, col_count
+        place, maps, forward, backward, head_weight, own_context, their_context, cols, tok_count * rows_dev, col_count
     )
     holo = holo.reshape(-1, rows_chip, cols)
     hologram = lax.dynamic_slice(
@@ -409,4 +440,4 @@
         P("dp", None, "tok", "col"),
     )
     out_specs = (P("dp", None, "tok", "col"), P(), P("col", None))
-    return jax.shard_map(shards, mesh=mesh, in_specs=in_specs, out_specs=out_specs, check_vma=False)
+    return jax.shard_map(step, mesh=mesh, in_specs=in_specs, out_specs=out_specs, check_vma=False)

time: 90.4 us -> 91.4 us (1.011)
  starting transfers between devices: 28.4 us -> 26.4 us
  Pallas kernels: 23.5 us -> 25.3 us
  other arithmetic: 1.09 us -> 2.65 us
  waiting for transfers between devices: 28.3 us -> 29.8 us
  local copies, waits for them, and re-layouts: 4.95 us -> 3.72 us
    ppermute x6 -> x4, starting transfers between devices: 12.9 us -> 7.74 us  [passed(): return lax.ppermute(values, axis, pairs)]
    ppermute x0 -> x1, waiting for transfers between devices: none -> 4.46 us  [beside(): return lax.ppermute(values, 'tok', pairs)]
    ppermute x6 -> x4, waiting for transfers between devices: 9.17 us -> 4.8 us  [passed(): return lax.ppermute(values, axis, pairs)]
    ppermute x0 -> x1, starting transfers between devices: none -> 2.74 us  [beside(): return lax.ppermute(values, 'tok', pairs)]
    pallas_call x1 -> x2, Pallas kernels: 0.29 us -> 2.6 us  [closing(): pl.pallas_call(functools.partial(closing_kernel, start), out_shape=(jax.S...]
    ppermute x11, waiting for transfers between devices: 8.31 us -> 9.74 us  [swapped(): return lax.ppermute(values, axis, [(i, i ^ 1) for i in range(size)])]
    pallas_call x8 -> x7, Pallas kernels: 16.3 us -> 15.2 us  [absorb(): pl.pallas_call(functools.partial(absorb_kernel, first), out_shape=shapes,...]
    unnamed x26 -> x17, local copies, waits for them, and re-layouts: 2.1 us -> 1.27 us
  transfers between devices with their start and end apart: 23 -> 22, of which waited for: 15 -> 15; matrix products, arithmetic and copies ran while one was open for 6% -> 4% of each run, Pallas kernels for 17% -> 18%
where the time goes in v7:
time: 91.4 us; the launch traced here: 91.2 us
  waiting for transfers between devices  29.8 us (33%)
  starting transfers between devices  26.4 us (29%)
  Pallas kernels  25.3 us (28%)
  local copies, waits for them, and re-layouts  3.72 us (4%)
  other arithmetic  2.65 us (3%)
  matrix products  2.25 us (2%)
  between operations  1.04 us (1%)
    pallas_call x7, Pallas kernels, absorb(): pl.pallas_call(functools.partial(absorb_kernel, first), out_shape=shapes,...  15.2 us
    ppermute x6, waiting for transfers between devices, round_ring(): lax.ppermute(values, 'tok', [(i, 2 * following[i // 2] + i % 2) for i in...  10.8 us
    ppermute x6, starting transfers between devices, round_ring(): lax.ppermute(values, 'tok', [(i, 2 * following[i // 2] + i % 2) for i in...  9.84 us
    ppermute x11, waiting for transfers between devices, swapped(): return lax.ppermute(values, axis, [(i, i ^ 1) for i in range(size)])  9.74 us
    ppermute x4, starting transfers between devices, passed(): return lax.ppermute(values, axis, pairs)  7.74 us
    ppermute x11, starting transfers between devices, swapped(): return lax.ppermute(values, axis, [(i, i ^ 1) for i in range(size)])  6.08 us
    ppermute x4, waiting for transfers between devices, passed(): return lax.ppermute(values, axis, pairs)  4.8 us
    ppermute x1, waiting for transfers between devices, beside(): return lax.ppermute(values, 'tok', pairs)  4.46 us
  transfers between devices with their start and end apart: 22, of which 15 were waited for; matrix products, arithmetic and copies ran while one was open for 4% of the time, Pallas kernels for 18%

profile of v7, /device:TPU:0, one launch (start us, length us, event | category | flops | bytes accessed | tf_op | source)
XLA Modules:
  0.0 91.2 jit_solution(9697488285809656591)
XLA Ops:
  3.5 2.1 %project.2 = (bf16[2,128,512]{2,1,0:T(8,128)(2,1)S(1)}, bf16[2,128,512]{2,1,0:T(8,128)(2,1)}) custom-call(s32[4]{0:T(128)S(1)} %pad_add_fusion.place, bf16[512,1024]{1,0:T(8,128)(2,1)S(1)} %normalize.1.normed, bf16[3,1024,256]{2,1,0:T(8,128)(2,1)S(1)} %copy-done.1), custom_call_target="tpu_custom_call" | custom-call | tf_op jit(solution)/shard_map/project/pallas_call | solution.py:70
  6.1 1.5 %collective-permute-done = bf16[2,128,512]{2,1,0:T(8,128)(2,1)} collective-permute-done((bf16[2,128,512]{2,1,0:T(8,128)(2,1)}, bf16[2,128,512]{2,1,0:T(8,128)(2,1)}, u32[]{:S(2)}, u32[]{:S(2)}) %collective-permute-start) | collective-permute-done | bytes 262176 | tf_op jit(solution)/shard_map/ppermute | solution.py:270
  10.8 2.7 %collective-permute-start.3 = (bf16[128,1024]{1,0:T(8,128)(2,1)}, bf16[128,1024]{1,0:T(8,128)(2,1)S(1)}, u32[]{:S(2)}, u32[]{:S(2)}) collective-permute-start(bf16[128,1024]{1,0:T(8,128)(2,1)} %get-tuple-element.80.refs_1_), channel_id=1, source_target_pairs={{0,4},{2,6},{4,12},{6,14},{8,0},{10,2},{12,8},{14,10},{1,5},{3,7},... | collective-permute-start | bytes 786440 | tf_op jit(solution)/shard_map/ppermute | solution.py:297
  13.5 2.6 %collective-permute-start.2 = (bf16[128,1024]{1,0:T(8,128)(2,1)S(1)}, bf16[128,1024]{1,0:T(8,128)(2,1)S(1)}, u32[]{:S(2)}, u32[]{:S(2)}) collective-permute-start(bf16[128,1024]{1,0:T(8,128)(2,1)S(1)} %get-tuple-element.86.refs_1_), channel_id=1, source_target_pairs={{0,4},{2,6},{4,12},{6,14},{8,0},{10,2},{12,8},{14,10},{1,5},{3,7},... | collective-permute-start | bytes 786440 | tf_op jit(solution)/shard_map/ppermute | solution.py:297
  16.2 2.9 %absorb.7 = (f32[80,1024]{1,0:T(8,128)S(1)}, f32[8,1024]{1,0:T(8,128)S(1)}) custom-call(bf16[64,1024]{1,0:T(8,128)(2,1)S(1)} %pad_maximum_fusion.4.refs_0_, bf16[128,1024]{1,0:T(8,128)(2,1)} %get-tuple-element.80.refs_1_), custom_call_target="tpu_custom_call" | custom-call | tf_op jit(solution)/shard_map/absorb/pallas_call | solution.py:112
  19.1 1.6 %collective-permute-start.6 = (f32[2,2,128]{2,1,0:T(2,128)S(1)}, f32[2,2,128]{2,1,0:T(2,128)S(1)}, u32[]{:S(2)}, u32[]{:S(2)}) collective-permute-start(f32[2,2,128]{2,1,0:T(2,128)S(1)} %bitcast.55), channel_id=1, source_target_pairs={{0,1},{1,0},{2,3},{3,2},{4,5},{5,4},{6,7},{7,6},{8,9},{9,8},{10,11... | collective-permute-start | bytes 6152 | tf_op jit(solution)/shard_map/ppermute | solution.py:270
  23.2 2.0 %absorb.8 = (f32[80,1024]{1,0:T(8,128)S(1)}, f32[8,1024]{1,0:T(8,128)S(1)}) custom-call(bf16[64,1024]{1,0:T(8,128)(2,1)S(1)} %pad_maximum_fusion.3.refs_0_.queries, bf16[128,1024]{1,0:T(8,128)(2,1)S(1)} %get-tuple-element.86.refs_1_), custom_call_target="tpu_custom_call" | custom-call | tf_op jit(solution)/shard_map/absorb/pallas_call | solution.py:112
  25.1 2.4 %collective-permute-done.2.refs_1_ = bf16[128,1024]{1,0:T(8,128)(2,1)S(1)} collective-permute-done((bf16[128,1024]{1,0:T(8,128)(2,1)S(1)}, bf16[128,1024]{1,0:T(8,128)(2,1)S(1)}, u32[]{:S(2)}, u32[]{:S(2)}) %collective-permute-start.2) | collective-permute-done | bytes 262176 | tf_op jit(solution)/shard_map/ppermute | solution.py:297
  28.6 2.0 %absorb.9 = (f32[80,1024]{1,0:T(8,128)S(1)}, f32[8,1024]{1,0:T(8,128)S(1)}) custom-call(bf16[64,1024]{1,0:T(8,128)(2,1)S(1)} %pad_maximum_fusion.4.refs_0_, bf16[128,1024]{1,0:T(8,128)(2,1)S(1)} %collective-permute-done.3.refs_1_, f32[80,1024]{1,0:T(8,128)S(1)} %get-tuple-element.91.refs_2_, ...), custom_call_target="tpu_custom_call", output_to_operand_aliasing={{0}: (2, {}), {1}: (3, {})} | custom-call | tf_op jit(solution)/shard_map/absorb/pallas_call | solution.py:112
  30.7 2.4 %collective-permute-done.5.refs_1_ = bf16[128,1024]{1,0:T(8,128)(2,1)S(1)} collective-permute-done((bf16[128,1024]{1,0:T(8,128)(2,1)S(1)}, bf16[128,1024]{1,0:T(8,128)(2,1)S(1)}, u32[]{:S(2)}, u32[]{:S(2)}) %collective-permute-start.5) | collective-permute-done | bytes 262176 | tf_op jit(solution)/shard_map/ppermute | solution.py:297
  34.3 2.1 %absorb.10 = (f32[80,1024]{1,0:T(8,128)S(1)}, f32[8,1024]{1,0:T(8,128)S(1)}) custom-call(bf16[64,1024]{1,0:T(8,128)(2,1)S(1)} %pad_maximum_fusion.3.refs_0_.queries, bf16[128,1024]{1,0:T(8,128)(2,1)S(1)} %collective-permute-done.2.refs_1_, f32[80,1024]{1,0:T(8,128)S(1)} %get-tuple-element.97.refs_2_, ...), custom_call_target="tpu_custom_call", output_to_operand_aliasing={{0}: (2, {}), {1}: (3, {})} | custom-call | tf_op jit(solution)/shard_map/absorb/pallas_call | solution.py:112
  36.3 2.4 %collective-permute-done.4.refs_1_ = bf16[128,1024]{1,0:T(8,128)(2,1)S(1)} collective-permute-done((bf16[128,1024]{1,0:T(8,128)(2,1)S(1)}, bf16[128,1024]{1,0:T(8,128)(2,1)S(1)}, u32[]{:S(2)}, u32[]{:S(2)}) %collective-permute-start.4) | collective-permute-done | bytes 262176 | tf_op jit(solution)/shard_map/ppermute | solution.py:297
  40.0 2.0 %absorb.11 = (f32[80,1024]{1,0:T(8,128)S(1)}, f32[8,1024]{1,0:T(8,128)S(1)}) custom-call(bf16[64,1024]{1,0:T(8,128)(2,1)S(1)} %pad_maximum_fusion.4.refs_0_, bf16[128,1024]{1,0:T(8,128)(2,1)S(1)} %collective-permute-done.5.refs_1_, f32[80,1024]{1,0:T(8,128)S(1)} %get-tuple-element.110.refs_2_, ...), custom_call_target="tpu_custom_call", output_to_operand_aliasing={{0}: (2, {}), {1}: (3, {})} | custom-call | tf_op jit(solution)/shard_map/absorb/pallas_call | solution.py:112
  42.0 2.4 %collective-permute-done.8.refs_1_ = bf16[128,1024]{1,0:T(8,128)(2,1)S(1)} collective-permute-done((bf16[128,1024]{1,0:T(8,128)(2,1)S(1)}, bf16[128,1024]{1,0:T(8,128)(2,1)S(1)}, u32[]{:S(2)}, u32[]{:S(2)}) %collective-permute-start.8) | collective-permute-done | bytes 262176 | tf_op jit(solution)/shard_map/ppermute | solution.py:297
  44.4 2.1 %absorb.13 = (f32[80,1024]{1,0:T(8,128)S(1)}, f32[8,1024]{1,0:T(8,128)S(1)}) custom-call(bf16[64,1024]{1,0:T(8,128)(2,1)S(1)} %pad_maximum_fusion.4.refs_0_, bf16[128,1024]{1,0:T(8,128)(2,1)S(1)} %collective-permute-done.8.refs_1_, f32[80,1024]{1,0:T(8,128)S(1)} %get-tuple-element.122.refs_2_, ...), custom_call_target="tpu_custom_call", output_to_operand_aliasing={{0}: (2, {}), {1}: (3, {})} | custom-call | tf_op jit(solution)/shard_map/absorb/pallas_call | solution.py:112
  46.4 2.1 %absorb.12 = (f32[80,1024]{1,0:T(8,128)S(1)}, f32[8,1024]{1,0:T(8,128)S(1)}) custom-call(bf16[64,1024]{1,0:T(8,128)(2,1)S(1)} %pad_maximum_fusion.3.refs_0_.queries, bf16[128,1024]{1,0:T(8,128)(2,1)S(1)} %collective-permute-done.4.refs_1_, f32[80,1024]{1,0:T(8,128)S(1)} %get-tuple-element.116.refs_2_, ...), custom_call_target="tpu_custom_call", output_to_operand_aliasing={{0}: (2, {}), {1}: (3, {})} | custom-call | tf_op jit(solution)/shard_map/absorb/pallas_call | solution.py:112
  49.7 1.3 %closing.3 = (bf16[128,512]{1,0:T(8,128)(2,1)S(1)}, f32[64,512]{1,0:T(8,128)S(1)}) custom-call(bf16[64,1024]{1,0:T(8,128)(2,1)S(1)} %pad_maximum_fusion.3.refs_0_.queries, bf16[128,1024]{1,0:T(8,128)(2,1)S(1)} %collective-permute-done.7.block, f32[80,1024]{1,0:T(8,128)S(1)} %get-tuple-element.127.refs_0_, f32[80,1024]{1,0:T(8,128)S(1)} %get-tuple-element.128.refs_1_, ...), custom_call_target="tpu_custom_call" | custom-call | tf_op jit(solution)/shard_map/closing/pallas_call | solution.py:147
  51.1 1.3 %closing.2 = (bf16[128,512]{1,0:T(8,128)(2,1)S(1)}, f32[64,512]{1,0:T(8,128)S(1)}) custom-call(bf16[64,1024]{1,0:T(8,128)(2,1)S(1)} %pad_maximum_fusion.3.refs_0_.queries, bf16[128,1024]{1,0:T(8,128)(2,1)S(1)} %collective-permute-done.7.block, f32[80,1024]{1,0:T(8,128)S(1)} %get-tuple-element.127.refs_0_, f32[80,1024]{1,0:T(8,128)S(1)} %get-tuple-element.128.refs_1_, ...), custom_call_target="tpu_custom_call" | custom-call | tf_op jit(solution)/shard_map/closing/pallas_call | solution.py:147
  52.4 1.6 %collective-permute-start.10 = (bf16[64,512]{1,0:T(8,128)(2,1)S(1)}, bf16[64,512]{1,0:T(8,128)(2,1)S(1)}, u32[]{:S(2)}, u32[]{:S(2)}) collective-permute-start(bf16[64,512]{1,0:T(8,128)(2,1)S(1)} %add_convert_fusion.1), channel_id=1, source_target_pairs={{0,1},{1,0},{2,3},{3,2},{4,5},{5,4},{6,7},{7,6},{8,9},{9,8},{10,11... | collective-permute-start | bytes 196616 | tf_op jit(solution)/shard_map/ppermute | solution.py:270
  54.1 2.9 %collective-permute-done.10 = bf16[64,512]{1,0:T(8,128)(2,1)S(1)} collective-permute-done((bf16[64,512]{1,0:T(8,128)(2,1)S(1)}, bf16[64,512]{1,0:T(8,128)(2,1)S(1)}, u32[]{:S(2)}, u32[]{:S(2)}) %collective-permute-start.10) | collective-permute-done | bytes 65568 | tf_op jit(solution)/shard_map/ppermute | solution.py:270
  58.4 2.7 %collective-permute-start.12 = (bf16[80,1024]{1,0:T(8,128)(2,1)S(1)}, bf16[80,1024]{1,0:T(8,128)(2,1)S(1)}, u32[]{:S(2)}, u32[]{:S(2)}) collective-permute-start(bf16[80,1024]{1,0:T(8,128)(2,1)S(1)} %pad_maximum_fusion.2.chip_map), channel_id=1, source_target_pairs={{0,4},{4,0},{6,10},{8,12},{10,6},{12,8},{1,5},{5,1},{7,11},{9,13},... | collective-permute-start | bytes 491528 | tf_op jit(solution)/shard_map/ppermute | solution.py:287
  61.1 4.5 %collective-permute-done.12.near = bf16[80,1024]{1,0:T(8,128)(2,1)S(1)} collective-permute-done((bf16[80,1024]{1,0:T(8,128)(2,1)S(1)}, bf16[80,1024]{1,0:T(8,128)(2,1)S(1)}, u32[]{:S(2)}, u32[]{:S(2)}) %collective-permute-start.12) | collective-permute-done | bytes 163872 | tf_op jit(solution)/shard_map/ppermute | solution.py:287
  67.0 3.8 %network.1 = (f32[2,1024]{1,0:T(2,128)S(1)}, f32[32,576]{1,0:T(8,128)S(1)}, f32[64,128]{1,0:T(8,128)S(1)}) custom-call(s32[4]{0:T(128)S(1)} %pad_add_fusion.place, bf16[80,1024]{1,0:T(8,128)(2,1)S(1)} %pad_maximum_fusion.2.chip_map, bf16[80,1024]{1,0:T(8,128)(2,1)S(1)} %collective-permute-done.12.near, bf16[80,1024]{1,0:T(8,128)(2,1)S(1)} %collective-permute-done.13.far, ...), custom_call_target="tpu_custom_call" | custom-call | tf_op jit(solution)/shard_map/network/pallas_call | solution.py:253
  70.8 1.6 %collective-permute-start.14 = (bf16[32,896]{1,0:T(8,128)(2,1)S(1)}, bf16[32,896]{1,0:T(8,128)(2,1)S(1)}, u32[]{:S(2)}, u32[]{:S(2)}) collective-permute-start(bf16[32,896]{1,0:T(8,128)(2,1)S(1)} %fusion.14), channel_id=1, source_target_pairs={{0,16},{16,0},{1,17},{17,1},{2,18},{18,2},{3,19},{19,3},{4,20},{20... | collective-permute-start | bytes 172040 | tf_op jit(solution)/shard_map/ppermute | solution.py:276
  72.5 2.6 %collective-permute-done.14 = bf16[32,896]{1,0:T(8,128)(2,1)S(1)} collective-permute-done((bf16[32,896]{1,0:T(8,128)(2,1)S(1)}, bf16[32,896]{1,0:T(8,128)(2,1)S(1)}, u32[]{:S(2)}, u32[]{:S(2)}) %collective-permute-start.14) | collective-permute-done | bytes 57376 | tf_op jit(solution)/shard_map/ppermute | solution.py:276
  75.1 2.3 %collective-permute-start.15 = (bf16[32,896]{1,0:T(8,128)(2,1)S(1)}, bf16[32,896]{1,0:T(8,128)(2,1)S(1)}, u32[]{:S(2)}, u32[]{:S(2)}) collective-permute-start(bf16[32,896]{1,0:T(8,128)(2,1)S(1)} %add_convert_fusion.2), channel_id=1, source_target_pairs={{0,8},{2,10},{4,12},{6,14},{8,0},{10,2},{12,4},{14,6},{1,9},{3,11}... | collective-permute-start | bytes 172040 | tf_op jit(solution)/shard_map/ppermute | solution.py:276
  77.4 2.0 %collective-permute-start.16 = (bf16[32,896]{1,0:T(8,128)(2,1)S(1)}, bf16[32,896]{1,0:T(8,128)(2,1)S(1)}, u32[]{:S(2)}, u32[]{:S(2)}) collective-permute-start(bf16[32,896]{1,0:T(8,128)(2,1)S(1)} %add_convert_fusion.2), channel_id=1, source_target_pairs={{0,4},{2,6},{4,8},{6,10},{8,12},{10,14},{12,0},{14,2},{1,5},{3,7},... | collective-permute-start | bytes 172040 | tf_op jit(solution)/shard_map/ppermute | solution.py:276
  79.4 1.8 %collective-permute-start.17 = (bf16[32,896]{1,0:T(8,128)(2,1)S(1)}, bf16[32,896]{1,0:T(8,128)(2,1)S(1)}, u32[]{:S(2)}, u32[]{:S(2)}) collective-permute-start(bf16[32,896]{1,0:T(8,128)(2,1)S(1)} %add_convert_fusion.2), channel_id=1, source_target_pairs={{0,12},{2,14},{4,0},{6,2},{8,4},{10,6},{12,8},{14,10},{1,13},{3,15... | collective-permute-start | bytes 172040 | tf_op jit(solution)/shard_map/ppermute | solution.py:276
  81.9 1.7 %collective-permute-done.16 = bf16[32,896]{1,0:T(8,128)(2,1)S(1)} collective-permute-done((bf16[32,896]{1,0:T(8,128)(2,1)S(1)}, bf16[32,896]{1,0:T(8,128)(2,1)S(1)}, u32[]{:S(2)}, u32[]{:S(2)}) %collective-permute-start.16) | collective-permute-done | bytes 57376 | tf_op jit(solution)/shard_map/ppermute | solution.py:276
  84.2 1.6 %collective-permute-start.18 = (f32[32,576]{1,0:T(8,128)S(1)}, f32[32,576]{1,0:T(8,128)S(1)}, u32[]{:S(2)}, u32[]{:S(2)}) collective-permute-start(f32[32,576]{1,0:T(8,128)S(1)} %get-tuple-element.154), channel_id=1, source_target_pairs={{0,1},{1,0},{2,3},{3,2},{4,5},{5,4},{6,7},{7,6},{8,9},{9,8},{10,11... | collective-permute-start | bytes 221192 | tf_op jit(solution)/shard_map/ppermute | solution.py:270
  86.0 1.6 %fusion.3 = f32[256,1024]{1,0:T(8,128)} fusion(bf16[1024,64]{0,1:T(8,128)(2,1)S(1)} %copy-done.5, f32[64,128]{1,0:T(8,128)S(1)} %collective-permute-done.19, f32[32,128]{1,0:T(8,128)S(1)} %get-tuple-element.156, f32[32,128]{1,0:T(8,128)S(1)} %get-tuple-element.155, pred[]{:T(512)S(6)} %eq.5), kind=kOutput, calls=%fused_computation.26 | convolution fusion | flops 201408512 | bytes 1245185 | tf_op jit(solution)/shard_map/dot_general | solution.py:419
  87.6 1.5 %collective-permute-done.18 = f32[32,576]{1,0:T(8,128)S(1)} collective-permute-done((f32[32,576]{1,0:T(8,128)S(1)}, f32[32,576]{1,0:T(8,128)S(1)}, u32[]{:S(2)}, u32[]{:S(2)}) %collective-permute-start.18) | collective-permute-done | bytes 73760 | tf_op jit(solution)/shard_map/ppermute | solution.py:270
  (82 shorter events, 20.2 us)
Async XLA Ops:
  0.6 20.5 %copy-start = (bf16[256,1024]{1,0:T(8,128)(2,1)S(1)}, bf16[256,1024]{1,0:T(8,128)(2,1)}, u32[]{:S(2)}) copy-start(bf16[256,1024]{1,0:T(8,128)(2,1)} %param.11) | copy-start | bytes 1572868
  0.6 2.8 %copy-start.1 = (bf16[3,1024,256]{2,1,0:T(8,128)(2,1)S(1)}, bf16[3,1024,256]{2,1,0:T(8,128)(2,1)}, u32[]{:S(2)}) copy-start(bf16[3,1024,256]{2,1,0:T(8,128)(2,1)} %weight.3) | copy-start | bytes 4718596
  1.5 1.2 %copy-start.2 = (bf16[1,512,1024]{2,1,0:T(8,128)(2,1)S(1)}, bf16[1,512,1024]{2,1,0:T(8,128)(2,1)}, u32[]{:S(2)}) copy-start(bf16[1,512,1024]{2,1,0:T(8,128)(2,1)} %param.8) | copy-start | bytes 3145732
  5.6 2.0 %collective-permute-start = (bf16[2,128,512]{2,1,0:T(8,128)(2,1)}, bf16[2,128,512]{2,1,0:T(8,128)(2,1)}, u32[]{:S(2)}, u32[]{:S(2)}) collective-permute-start(bf16[2,128,512]{2,1,0:T(8,128)(2,1)} %get-tuple-element.75), channel_id=1, source_target_pairs={{0,2},{2,0},{4,6},{6,4},{8,10},{10,8},{12,14},{14,12},{1,3},{3,1},... | collective-permute-start | bytes 786440 | tf_op jit(solution)/shard_map/ppermute | solution.py:270
  9.3 9.8 %copy-start.7 = (f32[1,2,2,128]{3,2,1,0:T(2,128)S(1)}, f32[1,2,2,128]{3,2,1,0:T(2,128)}, u32[]{:S(2)}) copy-start(f32[1,2,2,128]{3,2,1,0:T(2,128)} %param.15) | copy-start | bytes 6148
  9.3 11.4 %copy-start.3 = (bf16[1,512,1024]{2,1,0:T(8,128)(2,1)S(1)}, bf16[1,512,1024]{2,1,0:T(8,128)(2,1)}, u32[]{:S(2)}) copy-start(bf16[1,512,1024]{2,1,0:T(8,128)(2,1)} %param.8) | copy-start | bytes 3145732
  9.3 11.4 %copy-start.5 = (bf16[1024,64]{0,1:T(8,128)(2,1)S(1)}, bf16[1024,64]{0,1:T(8,128)(2,1)}, u32[]{:S(2)}) copy-start(bf16[1024,64]{0,1:T(8,128)(2,1)} %param.12) | copy-start | bytes 393220
  10.4 11.0 %copy-start.6 = (bf16[2,64,576]{2,1,0:T(8,128)(2,1)S(1)}, bf16[2,64,576]{2,1,0:T(8,128)(2,1)}, u32[]{:S(2)}) copy-start(bf16[2,64,576]{2,1,0:T(8,128)(2,1)} %param.13) | copy-start | bytes 442372
  10.4 5.7 %collective-permute-start.1 = (bf16[2,64,512]{2,1,0:T(8,128)(2,1)S(1)}, bf16[2,64,512]{2,1,0:T(8,128)(2,1)S(1)}, u32[]{:S(2)}, u32[]{:S(2)}) collective-permute-start(bf16[2,64,512]{2,1,0:T(8,128)(2,1)S(1)} %get-tuple-element.78), channel_id=1, source_target_pairs={{0,2},{2,0},{4,6},{6,4},{8,10},{10,8},{12,14},{14,12},{1,3},{3,1},... | collective-permute-start | bytes 393224 | tf_op jit(solution)/shard_map/ppermute | solution.py:270
  10.8 11.2 %collective-permute-start.3 = (bf16[128,1024]{1,0:T(8,128)(2,1)}, bf16[128,1024]{1,0:T(8,128)(2,1)S(1)}, u32[]{:S(2)}, u32[]{:S(2)}) collective-permute-start(bf16[128,1024]{1,0:T(8,128)(2,1)} %get-tuple-element.80.refs_1_), channel_id=1, source_target_pairs={{0,4},{2,6},{4,12},{6,14},{8,0},{10,2},{12,8},{14,10},{1,5},{3,7},... | collective-permute-start | bytes 786440 | tf_op jit(solution)/shard_map/ppermute | solution.py:297
  13.5 14.0 %collective-permute-start.2 = (bf16[128,1024]{1,0:T(8,128)(2,1)S(1)}, bf16[128,1024]{1,0:T(8,128)(2,1)S(1)}, u32[]{:S(2)}, u32[]{:S(2)}) collective-permute-start(bf16[128,1024]{1,0:T(8,128)(2,1)S(1)} %get-tuple-element.86.refs_1_), channel_id=1, source_target_pairs={{0,4},{2,6},{4,12},{6,14},{8,0},{10,2},{12,8},{14,10},{1,5},{3,7},... | collective-permute-start | bytes 786440 | tf_op jit(solution)/shard_map/ppermute | solution.py:297
  19.1 4.0 %collective-permute-start.6 = (f32[2,2,128]{2,1,0:T(2,128)S(1)}, f32[2,2,128]{2,1,0:T(2,128)S(1)}, u32[]{:S(2)}, u32[]{:S(2)}) collective-permute-start(f32[2,2,128]{2,1,0:T(2,128)S(1)} %bitcast.55), channel_id=1, source_target_pairs={{0,1},{1,0},{2,3},{3,2},{4,5},{5,4},{6,7},{7,6},{8,9},{9,8},{10,11... | collective-permute-start | bytes 6152 | tf_op jit(solution)/shard_map/ppermute | solution.py:270
  22.0 11.1 %collective-permute-start.5 = (bf16[128,1024]{1,0:T(8,128)(2,1)S(1)}, bf16[128,1024]{1,0:T(8,128)(2,1)S(1)}, u32[]{:S(2)}, u32[]{:S(2)}) collective-permute-start(bf16[128,1024]{1,0:T(8,128)(2,1)S(1)} %collective-permute-done.3.refs_1_), channel_id=1, source_target_pairs={{0,4},{2,6},{4,12},{6,14},{8,0},{10,2},{12,8},{14,10},{1,5},{3,7},... | collective-permute-start | bytes 786440 | tf_op jit(solution)/shard_map/ppermute | solution.py:297
  27.5 11.2 %collective-permute-start.4 = (bf16[128,1024]{1,0:T(8,128)(2,1)S(1)}, bf16[128,1024]{1,0:T(8,128)(2,1)S(1)}, u32[]{:S(2)}, u32[]{:S(2)}) collective-permute-start(bf16[128,1024]{1,0:T(8,128)(2,1)S(1)} %collective-permute-done.2.refs_1_), channel_id=1, source_target_pairs={{0,4},{2,6},{4,12},{6,14},{8,0},{10,2},{12,8},{14,10},{1,5},{3,7},... | collective-permute-start | bytes 786440 | tf_op jit(solution)/shard_map/ppermute | solution.py:297
  33.1 11.2 %collective-permute-start.8 = (bf16[128,1024]{1,0:T(8,128)(2,1)S(1)}, bf16[128,1024]{1,0:T(8,128)(2,1)S(1)}, u32[]{:S(2)}, u32[]{:S(2)}) collective-permute-start(bf16[128,1024]{1,0:T(8,128)(2,1)S(1)} %collective-permute-done.5.refs_1_), channel_id=1, source_target_pairs={{0,4},{2,6},{4,12},{6,14},{8,0},{10,2},{12,8},{14,10},{1,5},{3,7},... | collective-permute-start | bytes 786440 | tf_op jit(solution)/shard_map/ppermute | solution.py:297
  38.8 10.9 %collective-permute-start.7 = (bf16[128,1024]{1,0:T(8,128)(2,1)S(1)}, bf16[128,1024]{1,0:T(8,128)(2,1)S(1)}, u32[]{:S(2)}, u32[]{:S(2)}) collective-permute-start(bf16[128,1024]{1,0:T(8,128)(2,1)S(1)} %collective-permute-done.4.refs_1_), channel_id=1, source_target_pairs={{0,4},{2,6},{4,12},{6,14},{8,0},{10,2},{12,8},{14,10},{1,5},{3,7},... | collective-permute-start | bytes 786440 | tf_op jit(solution)/shard_map/ppermute | solution.py:297
  51.0 16.0 %copy-start.4 = (bf16[2,64]{1,0:T(2,128)(2,1)S(1)}, bf16[2,64]{1,0:T(2,128)(2,1)}, u32[]{:S(2)}) copy-start(bf16[2,64]{1,0:T(2,128)(2,1)} %head.1) | copy-start | bytes 772
  51.0 1.4 %collective-permute-start.9 = (f32[64,512]{1,0:T(8,128)S(1)}, f32[64,512]{1,0:T(8,128)S(1)}, u32[]{:S(2)}, u32[]{:S(2)}) collective-permute-start(f32[64,512]{1,0:T(8,128)S(1)} %get-tuple-element.132), channel_id=1, source_target_pairs={{0,2},{2,0},{4,6},{6,4},{8,10},{10,8},{12,14},{14,12},{1,3},{3,1},... | collective-permute-start | bytes 393224 | tf_op jit(solution)/shard_map/ppermute | solution.py:270
  52.4 4.6 %collective-permute-start.10 = (bf16[64,512]{1,0:T(8,128)(2,1)S(1)}, bf16[64,512]{1,0:T(8,128)(2,1)S(1)}, u32[]{:S(2)}, u32[]{:S(2)}) collective-permute-start(bf16[64,512]{1,0:T(8,128)(2,1)S(1)} %add_convert_fusion.1), channel_id=1, source_target_pairs={{0,1},{1,0},{2,3},{3,2},{4,5},{5,4},{6,7},{7,6},{8,9},{9,8},{10,11... | collective-permute-start | bytes 196616 | tf_op jit(solution)/shard_map/ppermute | solution.py:270
  57.0 1.3 %collective-permute-start.11 = (bf16[80,512]{1,0:T(8,128)(2,1)S(1)}, bf16[80,512]{1,0:T(8,128)(2,1)S(1)}, u32[]{:S(2)}, u32[]{:S(2)}) collective-permute-start(bf16[80,512]{1,0:T(8,128)(2,1)S(1)} %pad_maximum_fusion.5), channel_id=1, source_target_pairs={{0,2},{2,0},{4,6},{6,4},{8,10},{10,8},{12,14},{14,12},{1,3},{3,1},... | collective-permute-start | bytes 245768 | tf_op jit(solution)/shard_map/ppermute | solution.py:270
  58.4 7.2 %collective-permute-start.12 = (bf16[80,1024]{1,0:T(8,128)(2,1)S(1)}, bf16[80,1024]{1,0:T(8,128)(2,1)S(1)}, u32[]{:S(2)}, u32[]{:S(2)}) collective-permute-start(bf16[80,1024]{1,0:T(8,128)(2,1)S(1)} %pad_maximum_fusion.2.chip_map), channel_id=1, source_target_pairs={{0,4},{4,0},{6,10},{8,12},{10,6},{12,8},{1,5},{5,1},{7,11},{9,13},... | collective-permute-start | bytes 491528 | tf_op jit(solution)/shard_map/ppermute | solution.py:287
  65.6 1.4 %collective-permute-start.13 = (bf16[80,1024]{1,0:T(8,128)(2,1)S(1)}, bf16[80,1024]{1,0:T(8,128)(2,1)S(1)}, u32[]{:S(2)}, u32[]{:S(2)}) collective-permute-start(bf16[80,1024]{1,0:T(8,128)(2,1)S(1)} %collective-permute-done.12.near), channel_id=1, source_target_pairs={{0,2},{2,0},{4,6},{6,4},{8,10},{10,8},{12,14},{14,12},{1,3},{3,1},... | collective-permute-start | bytes 491528 | tf_op jit(solution)/shard_map/ppermute | solution.py:270
  70.8 4.2 %collective-permute-start.14 = (bf16[32,896]{1,0:T(8,128)(2,1)S(1)}, bf16[32,896]{1,0:T(8,128)(2,1)S(1)}, u32[]{:S(2)}, u32[]{:S(2)}) collective-permute-start(bf16[32,896]{1,0:T(8,128)(2,1)S(1)} %fusion.14), channel_id=1, source_target_pairs={{0,16},{16,0},{1,17},{17,1},{2,18},{18,2},{3,19},{19,3},{4,20},{20... | collective-permute-start | bytes 172040 | tf_op jit(solution)/shard_map/ppermute | solution.py:276
  75.1 6.8 %collective-permute-start.15 = (bf16[32,896]{1,0:T(8,128)(2,1)S(1)}, bf16[32,896]{1,0:T(8,128)(2,1)S(1)}, u32[]{:S(2)}, u32[]{:S(2)}) collective-permute-start(bf16[32,896]{1,0:T(8,128)(2,1)S(1)} %add_convert_fusion.2), channel_id=1, source_target_pairs={{0,8},{2,10},{4,12},{6,14},{8,0},{10,2},{12,4},{14,6},{1,9},{3,11}... | collective-permute-start | bytes 172040 | tf_op jit(solution)/shard_map/ppermute | solution.py:276
  77.4 6.1 %collective-permute-start.16 = (bf16[32,896]{1,0:T(8,128)(2,1)S(1)}, bf16[32,896]{1,0:T(8,128)(2,1)S(1)}, u32[]{:S(2)}, u32[]{:S(2)}) collective-permute-start(bf16[32,896]{1,0:T(8,128)(2,1)S(1)} %add_convert_fusion.2), channel_id=1, source_target_pairs={{0,4},{2,6},{4,8},{6,10},{8,12},{10,14},{12,0},{14,2},{1,5},{3,7},... | collective-permute-start | bytes 172040 | tf_op jit(solution)/shard_map/ppermute | solution.py:276
  79.4 4.7 %collective-permute-start.17 = (bf16[32,896]{1,0:T(8,128)(2,1)S(1)}, bf16[32,896]{1,0:T(8,128)(2,1)S(1)}, u32[]{:S(2)}, u32[]{:S(2)}) collective-permute-start(bf16[32,896]{1,0:T(8,128)(2,1)S(1)} %add_convert_fusion.2), channel_id=1, source_target_pairs={{0,12},{2,14},{4,0},{6,2},{8,4},{10,6},{12,8},{14,10},{1,13},{3,15... | collective-permute-start | bytes 172040 | tf_op jit(solution)/shard_map/ppermute | solution.py:276
  84.1 1.9 %collective-permute-start.19 = (f32[64,128]{1,0:T(8,128)S(1)}, f32[64,128]{1,0:T(8,128)S(1)}, u32[]{:S(2)}, u32[]{:S(2)}) collective-permute-start(f32[64,128]{1,0:T(8,128)S(1)} %pad_maximum_fusion.6), channel_id=1, source_target_pairs={{0,2},{2,0},{4,6},{6,4},{8,10},{10,8},{12,14},{14,12},{1,3},{3,1},... | collective-permute-start | bytes 98312 | tf_op jit(solution)/shard_map/ppermute | solution.py:270
  84.2 4.9 %collective-permute-start.18 = (f32[32,576]{1,0:T(8,128)S(1)}, f32[32,576]{1,0:T(8,128)S(1)}, u32[]{:S(2)}, u32[]{:S(2)}) collective-permute-start(f32[32,576]{1,0:T(8,128)S(1)} %get-tuple-element.154), channel_id=1, source_target_pairs={{0,1},{1,0},{2,3},{3,2},{4,5},{5,4},{6,7},{7,6},{8,9},{9,8},{10,11... | collective-permute-start | bytes 221192 | tf_op jit(solution)/shard_map/ppermute | solution.py:270
  85.8 3.4 %collective-permute-start.20 = (f32[32,576]{1,0:T(8,128)S(1)}, f32[32,576]{1,0:T(8,128)S(1)}, u32[]{:S(2)}, u32[]{:S(2)}) collective-permute-start(f32[32,576]{1,0:T(8,128)S(1)} %get-tuple-element.154), channel_id=1, source_target_pairs={{0,2},{2,0},{4,6},{6,4},{8,10},{10,8},{12,14},{14,12},{1,3},{3,1},... | collective-permute-start | bytes 221192 | tf_op jit(solution)/shard_map/ppermute | solution.py:270
  89.2 1.3 %collective-permute-start.21 = (f32[32,576]{1,0:T(8,128)S(1)}, f32[32,576]{1,0:T(8,128)S(1)}, u32[]{:S(2)}, u32[]{:S(2)}) collective-permute-start(f32[32,576]{1,0:T(8,128)S(1)} %collective-permute-done.18), channel_id=1, source_target_pairs={{0,2},{2,0},{4,6},{6,4},{8,10},{10,8},{12,14},{14,12},{1,3},{3,1},... | collective-permute-start | bytes 221192 | tf_op jit(solution)/shard_map/ppermute | solution.py:270

commit v8 on v7

--- a/solution.py
+++ b/solution.py
@@ -78,83 +78,75 @@
     )(place, normed, weight)
 
 
-def absorb_kernel(first, *refs):
-    if first:
-        queries, block, out, top = refs
-    else:
-        queries, block, carried, carried_top, out, top = refs
-    keys = block[:HEAD, :].T
+def attend(queries, block, running, best):
     length = block.shape[1]
-    values = jnp.concatenate([block[HEAD:, :], jnp.ones((16, length), BF16)], axis=0)
-    width = min(512, queries.shape[1])
+    keys = block[:HEAD].T
+    values = jnp.concatenate([block[HEAD:], jnp.ones((16, length), BF16)], axis=0)
     depth = min(512, length)
-    for at in range(0, queries.shape[1], width):
-        part = queries[:, at : at + width]
-        running = None if first else carried[:, at : at + width]
-        best = None if first else carried_top[0:1, at : at + width]
-        for below in range(0, length, depth):
-            scores = dot(keys[below : below + depth], part)
-            raised_top = jnp.max(scores, axis=0, keepdims=True)
-            if best is not None:
-                raised_top = jnp.maximum(best, raised_top)
-            weights = jnp.exp(scores - raised_top).astype(BF16)
-            added = dot(values[:, below : below + depth], weights)
-            running = added if best is None else running * jnp.exp(best - raised_top) + added
-            best = raised_top
-        out[:, at : at + width] = running
-        top[:, at : at + width] = jnp.broadcast_to(best, (8, width))
+    for below in range(0, length, depth):
+        scores = dot(keys[below : below + depth], queries)
+        raised_top = jnp.max(scores, axis=0, keepdims=True)
+        if best is not None:
+            raised_top = jnp.maximum(best, raised_top)
+        weights = jnp.exp(scores - raised_top).astype(BF16)
+        added = dot(values[:, below : below + depth], weights)
+        running = added if best is None else running * jnp.exp(best - raised_top) + added
+        best = raised_top
+    return running, best
+
+
+def absorb_kernel(first, own, got, block, *refs):
+    carried, carried_top = (None, None) if first else refs[:2]
+    out, top = refs[-2:]
+    length = own.shape[2]
+    for head in range(own.shape[0]):
+        for side, queries in enumerate((own, got)):
+            where = slice(side * length, (side + 1) * length)
+            running = None if first else carried[head, :, where]
+            best = None if first else carried_top[head, 0:1, where]
+            running, best = attend(queries[head], block[head], running, best)
+            out[head, :, where] = running
+            top[head, :, where] = jnp.broadcast_to(best, (8, length))
 
 
 def absorb(queries, block, state):
-    count = queries.shape[1]
-    shapes = (jax.ShapeDtypeStruct((HEAD + 16, count), F32), jax.ShapeDtypeStruct((8, count), F32))
+    heads, _, length = queries[0].shape
+    shapes = tuple(jax.ShapeDtypeStruct((heads, rows, 2 * length), F32) for rows in (HEAD + 16, 8))
     first = state is None
     return pl.pallas_call(
         functools.partial(absorb_kernel, first),
         out_shape=shapes,
-        in_specs=[VMEM] * (2 if first else 4),
+        in_specs=[VMEM] * (3 if first else 5),
         out_specs=(VMEM, VMEM),
-        input_output_aliases={} if first else {2: 0, 3: 1},
+        input_output_aliases={} if first else {3: 0, 4: 1},
         compiler_params=PARAMS,
         name="absorb",
-    )(queries, block, *(() if first else state))
-
-
-def closing_kernel(start, queries, block, *refs):
-    states, (folded, context, share) = refs[:-3], refs[-3:]
-    carried, carried_top = states[-2:]
+    )(*queries, block, *(() if first else state))
+
+
+def closing_kernel(side, queries, block, carried, carried_top, folded, context, share):
     length = context.shape[1]
-    where = slice(start, start + length)
-    keys = block[:HEAD, :].T
-    values = jnp.concatenate([block[HEAD:, :], jnp.ones((16, block.shape[1]), BF16)], axis=0)
-    depth = min(512, block.shape[1])
-    running, best = carried[:, where], carried_top[0:1, where]
-    for below in range(0, block.shape[1], depth):
-        scores = dot(keys[below : below + depth], queries[:, where])
-        raised_top = jnp.maximum(best, jnp.max(scores, axis=0, keepdims=True))
-        weights = jnp.exp(scores - raised_top).astype(BF16)
-        running = running * jnp.exp(best - raised_top) + dot(values[:, below : below + depth], weights)
-        best = raised_top
-    sums = [state[:, where] for state in states[:-2]] + [running]
-    for head, state in enumerate(sums):
-        context[head * HEAD : (head + 1) * HEAD, :] = (state[:HEAD] / state[HEAD : HEAD + 1]).astype(BF16)
+    where = slice(side * length, (side + 1) * length)
+    for head in range(queries.shape[0]):
+        running, _ = attend(queries[head], block[head], carried[head, :, where], carried_top[head, 0:1, where])
+        context[head * HEAD : (head + 1) * HEAD, :] = (running[:HEAD] / running[HEAD : HEAD + 1]).astype(BF16)
     whole = context[...]
     share[...] = sum(dot(part, whole) for part in split3(folded[...]))
 
 
-def closing(start, length, queries, block, states, folded):
-    sums = [state[0] for state in states[:-1]] + list(states[-1])
+def closing(side, queries, block, state, folded):
+    heads, _, length = queries[side].shape
     return pl.pallas_call(
-        functools.partial(closing_kernel, start),
+        functools.partial(closing_kernel, side),
         out_shape=(
-            jax.ShapeDtypeStruct((len(states) * HEAD, length), BF16),
+            jax.ShapeDtypeStruct((heads * HEAD, length), BF16),
             jax.ShapeDtypeStruct((folded.shape[0], length), F32),
         ),
-        in_specs=[VMEM] * (len(sums) + 3),
+        in_specs=[VMEM] * 5,
         out_specs=(VMEM, VMEM),
         compiler_params=PARAMS,
         name="closing",
-    )(queries, block, *sums, folded)
+    )(queries[side], block, *state, folded)
 
 
 def turned(values, step):
@@ -199,7 +191,7 @@
         return jnp.logical_and(frame_lane >= 0, frame_lane < frame_rows * cols)
 
     channels, outputs = forward.shape[2], head.shape[0]
-    columns_zero = three_columns(hidden[:channels, :], cols)
+    columns_zero = three_columns(jnp.where(inside(0, row_count), hidden[:channels, :].astype(F32), 0.0), cols)
     first = three_rows(forward[0], columns_zero, cols)
     rows_one = row_count - 2
     one = jnp.where(inside(1, rows_one), first * jax.nn.sigmoid(first), 0.0)
@@ -277,14 +269,15 @@
 
 
 def beside(values):
-    size = lax.axis_size("tok")
-    chips = size // 2
+    size, cols = lax.axis_size("tok"), lax.axis_size("col")
     pairs = []
-    for at in range(chips):
+    for at in range(size // 2):
         for core, other in ((0, at ^ 1), (1, ((at + 1) ^ 1) - 1)):
-            if 0 <= other < chips:
-                pairs.append((2 * at + core, 2 * other + core))
-    return lax.ppermute(values, "tok", pairs)
+            inside = 0 <= other < size // 2
+            for col in range(cols):
+                target = (other if inside else at, col if inside or cols == 1 else col ^ 1)
+                pairs.append(((2 * at + core) * cols + col, (2 * target[0] + core) * cols + target[1]))
+    return lax.ppermute(values, ("tok", "col"), pairs)
 
 
 def round_ring(values):
@@ -326,19 +319,14 @@
     place = jnp.stack([core, half, chip_row, lax.rem(tok_at // 2, 2)]).astype(jnp.int32)
     layers, channels = conv_weight.shape[:2]
     cols = cols_dev * col_count
-    length = frame_rows.shape[0]
 
     normed = normalize(frame_rows, ln_gain.astype(F32).reshape(1, -1))
     own_keyed, their_keyed = project((1, 2), place, normed, qkv_weight)
+    own_keyed, their_keyed, normed = lax.optimization_barrier((own_keyed, their_keyed, normed))
     got_keyed = swapped(their_keyed, "tok")
-    count = got_keyed.shape[0]
-    kept = count * HEAD
-    blocks = [jnp.concatenate([own_keyed[head], got_keyed[head]], axis=1) for head in range(count)]
-    blocks, normed = lax.optimization_barrier((blocks, normed))
     own_queries, their_queries = project((0,), place, normed, qkv_weight)
-    got_queries = swapped(their_queries, "tok")
-    queries = [jnp.concatenate([own_queries[head], got_queries[head]], axis=1) for head in range(count)]
-    states = [None] * count
+    queries = (own_queries, swapped(their_queries, "tok"))
+    kept = own_keyed.shape[0] * HEAD
 
     def prepare(conv_weight, out_weight, readout_weight, frame_rows, cotangent):
         taps = conv_weight.reshape(layers, channels, 3, 3, channels)
@@ -354,37 +342,30 @@
         exact_cot = jnp.pad(exact_cot, ((0, -exact_cot.shape[0] % 16), (0, 0)))
         return (forward, backward, folded, direct, exact_cot)
 
+    state, blocks = None, [own_keyed, got_keyed]
     for turn in range(chips):
-        arriving = blocks
+        arriving = []
         if turn < chips - 1:
-            arriving = []
             for block in blocks:
                 arriving.append(round_ring(block))
-        for head in range(count):
-            if turn == chips - 1 and head == count - 1:
+        for at, block in enumerate(blocks):
+            if turn == chips - 1 and at == 1:
                 break
-            states[head] = absorb(queries[head], blocks[head], states[head])
-            if turn == 0 and head == 0:
-                states[head], given = lax.optimization_barrier(
-                    (states[head], (conv_weight, out_weight, readout_weight, frame_rows, cotangent))
+            state = absorb(queries, block, state)
+            if at == 0 and turn == min(1, chips - 2):
+                state, given = lax.optimization_barrier(
+                    (state, (conv_weight, out_weight, readout_weight, frame_rows, cotangent))
                 )
                 prepared = prepare(*given)
-            if turn == min(1, chips - 2) and head == count - 1:
-                states[head], prepared = lax.optimization_barrier((states[head], prepared))
-            arriving[head], states[head] = lax.optimization_barrier((arriving[head], states[head]))
-            if head + 1 < count:
-                gate = arriving[head] if turn < chips - 1 else states[head]
-                blocks[head + 1], gate = lax.optimization_barrier((blocks[head + 1], gate))
-                if turn < chips - 1:
-                    arriving[head] = gate
-                else:
-                    states[head] = gate
-        blocks = arriving
+            if at == 0 and turn == chips - 2:
+                state, prepared = lax.optimization_barrier((state, prepared))
+            if turn < chips - 2:
+                arriving[at], state = lax.optimization_barrier((arriving[at], state))
+        blocks = arriving if turn < chips - 1 else blocks
     forward, backward, folded, direct, exact_cot = prepared
 
-    last = (queries[-1], blocks[-1], states, folded)
-    their_context, their_share = closing(length, length, *last)
-    own_context, own_share = closing(0, length, *last)
+    their_context, their_share = closing(1, queries, blocks[1], state, folded)
+    own_context, own_share = closing(0, queries, blocks[1], state, folded)
     partial = own_share + swapped(their_share, "tok")
     partial = (partial + jnp.where(half == 0, direct, 0.0)).astype(BF16)
     own_map = (partial.astype(F32) + swapped(partial, "col").astype(F32)).astype(BF16)

time: 91.4 us -> 88.8 us (0.972)
  waiting for transfers between devices: 29.8 us -> 23.6 us
  local copies, waits for them, and re-layouts: 3.72 us -> 8.52 us
  starting transfers between devices: 26.4 us -> 24.8 us
    ppermute x6, waiting for transfers between devices: 10.8 us -> 6.08 us  [round_ring(): lax.ppermute(values, 'tok', [(i, 2 * following[i // 2] + i % 2) for i in...]
    transpose x2, local copies, waits for them, and re-layouts: 0.22 us -> 3.52 us  [prepare(): jnp.transpose(taps[:, :, ::-1, ::-1, :], (0, 2, 4, 3, 1))]
    ppermute x1, starting transfers between devices: 2.74 us -> 0.28 us  [beside(): return lax.ppermute(values, ('tok', 'col'), pairs)]
    optimization_barrier x2, local copies, waits for them, and re-layouts: 0.35 us -> 1.95 us  [the longest x1 1.78 us: step(): lax.optimization_barrier((state, (conv_weight, out_weight, readout_weight...]
    ppermute x11, waiting for transfers between devices: 9.74 us -> 8.31 us  [swapped(): return lax.ppermute(values, axis, [(i, i ^ 1) for i in range(size)])]
    pallas_call x7, Pallas kernels: 15.2 us -> 16.2 us  [absorb(): pl.pallas_call(functools.partial(absorb_kernel, first), out_shape=shapes,...]
    squeeze x4 -> x0, local copies, waits for them, and re-layouts: 1.02 us -> none  [the longest x1 0.98 us: step(): got_keyed[head]]
    ppermute x6, starting transfers between devices: 9.84 us -> 10.8 us  [round_ring(): lax.ppermute(values, 'tok', [(i, 2 * following[i // 2] + i % 2) for i in...]
  transfers between devices with their start and end apart: 22 -> 22, of which waited for: 15 -> 12; matrix products, arithmetic and copies ran while one was open for 4% -> 12% of each run, Pallas kernels for 18% -> 21%
where the time goes in v8:
time: 88.8 us; the launch traced here: 88.5 us
  Pallas kernels  25.7 us (29%)
  starting transfers between devices  24.8 us (28%)
  waiting for transfers between devices  23.6 us (27%)
  local copies, waits for them, and re-layouts  8.52 us (10%)
  matrix products  2.91 us (3%)
  other arithmetic  1.87 us (2%)
  between operations  1.05 us (1%)
    pallas_call x7, Pallas kernels, absorb(): pl.pallas_call(functools.partial(absorb_kernel, first), out_shape=shapes,...  16.2 us
    ppermute x6, starting transfers between devices, round_ring(): lax.ppermute(values, 'tok', [(i, 2 * following[i // 2] + i % 2) for i in...  10.8 us
    ppermute x11, waiting for transfers between devices, swapped(): return lax.ppermute(values, axis, [(i, i ^ 1) for i in range(size)])  8.31 us
    ppermute x4, starting transfers between devices, passed(): return lax.ppermute(values, axis, pairs)  7.49 us
    ppermute x11, starting transfers between devices, swapped(): return lax.ppermute(values, axis, [(i, i ^ 1) for i in range(size)])  6.21 us
    ppermute x6, waiting for transfers between devices, round_ring(): lax.ppermute(values, 'tok', [(i, 2 * following[i // 2] + i % 2) for i in...  6.08 us
    ppermute x1, waiting for transfers between devices, beside(): return lax.ppermute(values, ('tok', 'col'), pairs)  5.11 us
    ppermute x4, waiting for transfers between devices, passed(): return lax.ppermute(values, axis, pairs)  4.14 us
  transfers between devices with their start and end apart: 22, of which 12 were waited for; matrix products, arithmetic and copies ran while one was open for 12% of the time, Pallas kernels for 21%

profile of v8, /device:TPU:0, one launch (start us, length us, event | category | flops | bytes accessed | tf_op | source)
XLA Modules:
  0.0 88.5 jit_solution(3105730899529900623)
XLA Ops:
  3.5 1.4 %project.2 = (bf16[2,128,512]{2,1,0:T(8,128)(2,1)S(1)}, bf16[2,128,512]{2,1,0:T(8,128)(2,1)S(1)}) custom-call(s32[4]{0:T(128)S(1)} %pad_add_fusion.place, bf16[512,1024]{1,0:T(8,128)(2,1)S(1)} %normalize.1.normed, bf16[3,1024,256]{2,1,0:T(8,128)(2,1)S(1)} %copy-done.1), custom_call_target="tpu_custom_call" | custom-call | tf_op jit(solution)/shard_map/project/pallas_call | solution.py:70
  5.4 2.6 %collective-permute-start.3 = (bf16[2,128,512]{2,1,0:T(8,128)(2,1)S(1)}, bf16[2,128,512]{2,1,0:T(8,128)(2,1)S(1)}, u32[]{:S(2)}, u32[]{:S(2)}) collective-permute-start(bf16[2,128,512]{2,1,0:T(8,128)(2,1)S(1)} %get-tuple-element.66.block), channel_id=1, source_target_pairs={{0,4},{2,6},{4,12},{6,14},{8,0},{10,2},{12,8},{14,10},{1,5},{3,7},... | collective-permute-start | bytes 786440 | tf_op jit(solution)/shard_map/ppermute | solution.py:290
  9.4 2.6 %collective-permute-start.1 = (bf16[2,128,512]{2,1,0:T(8,128)(2,1)}, bf16[2,128,512]{2,1,0:T(8,128)(2,1)S(1)}, u32[]{:S(2)}, u32[]{:S(2)}) collective-permute-start(bf16[2,128,512]{2,1,0:T(8,128)(2,1)} %collective-permute-done.block), channel_id=1, source_target_pairs={{0,4},{2,6},{4,12},{6,14},{8,0},{10,2},{12,8},{14,10},{1,5},{3,7},... | collective-permute-start | bytes 786440 | tf_op jit(solution)/shard_map/ppermute | solution.py:290
  11.9 2.0 %absorb.7 = (f32[2,80,1024]{2,1,0:T(8,128)S(1)}, f32[2,8,1024]{2,1,0:T(8,128)S(1)}) custom-call(bf16[2,64,512]{2,1,0:T(8,128)(2,1)S(1)} %get-tuple-element.63.own.queries, bf16[2,64,512]{2,1,0:T(8,128)(2,1)S(1)} %collective-permute-done.2.got.queries, bf16[2,128,512]{2,1,0:T(8,128)(2,1)S(1)} %get-tuple-element.66.block), custom_call_target="tpu_custom_call" | custom-call | tf_op jit(solution)/shard_map/absorb/pallas_call | solution.py:116
  14.0 2.3 %collective-permute-done.3.block = bf16[2,128,512]{2,1,0:T(8,128)(2,1)S(1)} collective-permute-done((bf16[2,128,512]{2,1,0:T(8,128)(2,1)S(1)}, bf16[2,128,512]{2,1,0:T(8,128)(2,1)S(1)}, u32[]{:S(2)}, u32[]{:S(2)}) %collective-permute-start.3) | collective-permute-done | bytes 262176 | tf_op jit(solution)/shard_map/ppermute | solution.py:290
  17.3 3.0 %absorb.8 = (f32[2,80,1024]{2,1,0:T(8,128)S(1)}, f32[2,8,1024]{2,1,0:T(8,128)S(1)}) custom-call(bf16[2,64,512]{2,1,0:T(8,128)(2,1)S(1)} %get-tuple-element.63.own.queries, bf16[2,64,512]{2,1,0:T(8,128)(2,1)S(1)} %collective-permute-done.2.got.queries, bf16[2,128,512]{2,1,0:T(8,128)(2,1)} %collective-permute-done.block, ...), custom_call_target="tpu_custom_call", output_to_operand_aliasing={{0}: (3, {}), {1}: (4, {})} | custom-call | tf_op jit(solution)/shard_map/absorb/pallas_call | solution.py:116
  20.4 1.5 %collective-permute-done.1.block = bf16[2,128,512]{2,1,0:T(8,128)(2,1)S(1)} collective-permute-done((bf16[2,128,512]{2,1,0:T(8,128)(2,1)}, bf16[2,128,512]{2,1,0:T(8,128)(2,1)S(1)}, u32[]{:S(2)}, u32[]{:S(2)}) %collective-permute-start.1) | collective-permute-done | bytes 262176 | tf_op jit(solution)/shard_map/ppermute | solution.py:290
  21.8 2.0 %absorb.9 = (f32[2,80,1024]{2,1,0:T(8,128)S(1)}, f32[2,8,1024]{2,1,0:T(8,128)S(1)}) custom-call(bf16[2,64,512]{2,1,0:T(8,128)(2,1)S(1)} %get-tuple-element.63.own.queries, bf16[2,64,512]{2,1,0:T(8,128)(2,1)S(1)} %collective-permute-done.2.got.queries, ...), custom_call_target="tpu_custom_call", output_to_operand_aliasing={{0}: (3, {}), {1}: (4, {})} | custom-call | tf_op jit(solution)/shard_map/absorb/pallas_call | solution.py:116
  23.9 1.9 %collective-permute-start.8 = (f32[2,2,128]{2,1,0:T(2,128)S(1)}, f32[2,2,128]{2,1,0:T(2,128)S(1)}, u32[]{:S(2)}, u32[]{:S(2)}) collective-permute-start(f32[2,2,128]{2,1,0:T(2,128)S(1)} %bitcast.39), channel_id=1, source_target_pairs={{0,1},{1,0},{2,3},{3,2},{4,5},{5,4},{6,7},{7,6},{8,9},{9,8},{10,11... | collective-permute-start | bytes 6152 | tf_op jit(solution)/shard_map/ppermute | solution.py:262
  25.8 1.4 %collective-permute-done.5.block = bf16[2,128,512]{2,1,0:T(8,128)(2,1)S(1)} collective-permute-done((bf16[2,128,512]{2,1,0:T(8,128)(2,1)S(1)}, bf16[2,128,512]{2,1,0:T(8,128)(2,1)S(1)}, u32[]{:S(2)}, u32[]{:S(2)}) %collective-permute-start.5) | collective-permute-done | bytes 262176 | tf_op jit(solution)/shard_map/ppermute | solution.py:290
  28.1 1.8 %copy.25 = bf16[2,64,576]{1,2,0:T(8,128)(2,1)} copy(bf16[2,64,576]{2,1,0:T(8,128)(2,1)} %param.13) | data formatting | bytes 294912 | tf_op jit(solution)/shard_map/optimization_barrier | solution.py:356
  29.8 1.7 %reverse_bitcast_fusion = bf16[2,3,64,3,64]{4,2,3,1,0:T(8,128)(2,1)} fusion(bf16[2,64,3,3,64]{1,4,3,2,0:T(8,128)(2,1)} %bitcast.32), kind=kLoop, calls=%fused_computation.1 | loop fusion | bytes 294912 | tf_op jit(solution)/shard_map/transpose | solution.py:334
  31.5 1.8 %copy.26 = bf16[2,3,64,3,64]{2,4,3,1,0:T(8,128)(2,1)} copy(bf16[2,3,64,3,64]{4,2,3,1,0:T(8,128)(2,1)} %reverse_bitcast_fusion) | data formatting | bytes 294912 | tf_op jit(solution)/shard_map/transpose | solution.py:334
  33.4 3.4 %collective-permute-start.7 = (bf16[2,128,512]{2,1,0:T(8,128)(2,1)S(1)}, bf16[2,128,512]{2,1,0:T(8,128)(2,1)}, u32[]{:S(2)}, u32[]{:S(2)}) collective-permute-start(bf16[2,128,512]{2,1,0:T(8,128)(2,1)S(1)} %collective-permute-done.5.block), channel_id=1, source_target_pairs={{0,4},{2,6},{4,12},{6,14},{8,0},{10,2},{12,8},{14,10},{1,5},{3,7},... | collective-permute-start | bytes 786440 | tf_op jit(solution)/shard_map/ppermute | solution.py:290
  39.2 2.1 %absorb.10 = (f32[2,80,1024]{2,1,0:T(8,128)S(1)}, f32[2,8,1024]{2,1,0:T(8,128)S(1)}) custom-call(bf16[2,64,512]{2,1,0:T(8,128)(2,1)S(1)} %get-tuple-element.63.own.queries, bf16[2,64,512]{2,1,0:T(8,128)(2,1)S(1)} %collective-permute-done.2.got.queries, ...), custom_call_target="tpu_custom_call", output_to_operand_aliasing={{0}: (3, {}), {1}: (4, {})} | custom-call | tf_op jit(solution)/shard_map/absorb/pallas_call | solution.py:116
  41.6 2.0 %absorb.11 = (f32[2,80,1024]{2,1,0:T(8,128)S(1)}, f32[2,8,1024]{2,1,0:T(8,128)S(1)}) custom-call(bf16[2,64,512]{2,1,0:T(8,128)(2,1)S(1)} %get-tuple-element.63.own.queries, bf16[2,64,512]{2,1,0:T(8,128)(2,1)S(1)} %collective-permute-done.2.got.queries, ...), custom_call_target="tpu_custom_call", output_to_operand_aliasing={{0}: (3, {}), {1}: (4, {})} | custom-call | tf_op jit(solution)/shard_map/absorb/pallas_call | solution.py:116
  43.6 2.0 %absorb.12 = (f32[2,80,1024]{2,1,0:T(8,128)S(1)}, f32[2,8,1024]{2,1,0:T(8,128)S(1)}) custom-call(bf16[2,64,512]{2,1,0:T(8,128)(2,1)S(1)} %get-tuple-element.63.own.queries, bf16[2,64,512]{2,1,0:T(8,128)(2,1)S(1)} %collective-permute-done.2.got.queries, ...), custom_call_target="tpu_custom_call", output_to_operand_aliasing={{0}: (3, {}), {1}: (4, {})} | custom-call | tf_op jit(solution)/shard_map/absorb/pallas_call | solution.py:116
  45.7 3.0 %absorb.13 = (f32[2,80,1024]{2,1,0:T(8,128)S(1)}, f32[2,8,1024]{2,1,0:T(8,128)S(1)}) custom-call(bf16[2,64,512]{2,1,0:T(8,128)(2,1)S(1)} %get-tuple-element.63.own.queries, bf16[2,64,512]{2,1,0:T(8,128)(2,1)S(1)} %collective-permute-done.2.got.queries, ...), custom_call_target="tpu_custom_call", output_to_operand_aliasing={{0}: (3, {}), {1}: (4, {})} | custom-call | tf_op jit(solution)/shard_map/absorb/pallas_call | solution.py:116
  49.7 1.3 %closing.3 = (bf16[128,512]{1,0:T(8,128)(2,1)S(1)}, f32[64,512]{1,0:T(8,128)S(1)}) custom-call(bf16[2,64,512]{2,1,0:T(8,128)(2,1)S(1)} %collective-permute-done.2.got.queries, bf16[2,128,512]{2,1,0:T(8,128)(2,1)S(1)} %collective-permute-done.6.block, f32[2,80,1024]{2,1,0:T(8,128)S(1)} %get-tuple-element.100.carried, ...), custom_call_target="tpu_custom_call" | custom-call | tf_op jit(solution)/shard_map/closing/pallas_call | solution.py:139
  51.0 1.3 %closing.2 = (bf16[128,512]{1,0:T(8,128)(2,1)S(1)}, f32[64,512]{1,0:T(8,128)S(1)}) custom-call(bf16[2,64,512]{2,1,0:T(8,128)(2,1)S(1)} %get-tuple-element.63.own.queries, bf16[2,128,512]{2,1,0:T(8,128)(2,1)S(1)} %collective-permute-done.6.block, f32[2,80,1024]{2,1,0:T(8,128)S(1)} %get-tuple-element.100.carried, ...), custom_call_target="tpu_custom_call" | custom-call | tf_op jit(solution)/shard_map/closing/pallas_call | solution.py:139
  52.4 1.6 %collective-permute-start.10 = (bf16[64,512]{1,0:T(8,128)(2,1)S(1)}, bf16[64,512]{1,0:T(8,128)(2,1)S(1)}, u32[]{:S(2)}, u32[]{:S(2)}) collective-permute-start(bf16[64,512]{1,0:T(8,128)(2,1)S(1)} %add_convert_fusion.1), channel_id=1, source_target_pairs={{0,1},{1,0},{2,3},{3,2},{4,5},{5,4},{6,7},{7,6},{8,9},{9,8},{10,11... | collective-permute-start | bytes 196616 | tf_op jit(solution)/shard_map/ppermute | solution.py:262
  54.0 3.0 %collective-permute-done.10 = bf16[64,512]{1,0:T(8,128)(2,1)S(1)} collective-permute-done((bf16[64,512]{1,0:T(8,128)(2,1)S(1)}, bf16[64,512]{1,0:T(8,128)(2,1)S(1)}, u32[]{:S(2)}, u32[]{:S(2)}) %collective-permute-start.10) | collective-permute-done | bytes 65568 | tf_op jit(solution)/shard_map/ppermute | solution.py:262
  58.6 5.1 %collective-permute-done.12.near = bf16[80,1024]{1,0:T(8,128)(2,1)S(1)} collective-permute-done((bf16[80,1024]{1,0:T(8,128)(2,1)S(1)}, bf16[80,1024]{1,0:T(8,128)(2,1)S(1)}, u32[]{:S(2)}, u32[]{:S(2)}) %collective-permute-start.12) | collective-permute-done | bytes 163872 | tf_op jit(solution)/shard_map/ppermute | solution.py:280
  65.1 3.8 %network.1 = (f32[2,1024]{1,0:T(2,128)S(1)}, f32[32,576]{1,0:T(8,128)S(1)}, f32[64,128]{1,0:T(8,128)S(1)}) custom-call(s32[4]{0:T(128)S(1)} %pad_add_fusion.place, bf16[80,1024]{1,0:T(8,128)(2,1)S(1)} %pad_maximum_fusion.chip_map, bf16[80,1024]{1,0:T(8,128)(2,1)S(1)} %collective-permute-done.12.near, bf16[80,1024]{1,0:T(8,128)(2,1)S(1)} %collective-permute-done.13.far, ...), custom_call_target="tpu_custom_call" | custom-call | tf_op jit(solution)/shard_map/network/pallas_call | solution.py:245
  69.0 1.6 %collective-permute-start.14 = (bf16[32,896]{1,0:T(8,128)(2,1)S(1)}, bf16[32,896]{1,0:T(8,128)(2,1)S(1)}, u32[]{:S(2)}, u32[]{:S(2)}) collective-permute-start(bf16[32,896]{1,0:T(8,128)(2,1)S(1)} %fusion.14), channel_id=1, source_target_pairs={{0,16},{16,0},{1,17},{17,1},{2,18},{18,2},{3,19},{19,3},{4,20},{20... | collective-permute-start | bytes 172040 | tf_op jit(solution)/shard_map/ppermute | solution.py:268
  70.6 2.6 %collective-permute-done.14 = bf16[32,896]{1,0:T(8,128)(2,1)S(1)} collective-permute-done((bf16[32,896]{1,0:T(8,128)(2,1)S(1)}, bf16[32,896]{1,0:T(8,128)(2,1)S(1)}, u32[]{:S(2)}, u32[]{:S(2)}) %collective-permute-start.14) | collective-permute-done | bytes 57376 | tf_op jit(solution)/shard_map/ppermute | solution.py:268
  73.3 2.1 %collective-permute-start.15 = (bf16[32,896]{1,0:T(8,128)(2,1)S(1)}, bf16[32,896]{1,0:T(8,128)(2,1)S(1)}, u32[]{:S(2)}, u32[]{:S(2)}) collective-permute-start(bf16[32,896]{1,0:T(8,128)(2,1)S(1)} %add_convert_fusion.2), channel_id=1, source_target_pairs={{0,8},{2,10},{4,12},{6,14},{8,0},{10,2},{12,4},{14,6},{1,9},{3,11}... | collective-permute-start | bytes 172040 | tf_op jit(solution)/shard_map/ppermute | solution.py:268
  75.4 3.8 %collective-permute-start.17 = (bf16[32,896]{1,0:T(8,128)(2,1)S(1)}, bf16[32,896]{1,0:T(8,128)(2,1)S(1)}, u32[]{:S(2)}, u32[]{:S(2)}) collective-permute-start(bf16[32,896]{1,0:T(8,128)(2,1)S(1)} %add_convert_fusion.2), channel_id=1, source_target_pairs={{0,12},{2,14},{4,0},{6,2},{8,4},{10,6},{12,8},{14,10},{1,13},{3,15... | collective-permute-start | bytes 172040 | tf_op jit(solution)/shard_map/ppermute | solution.py:268
  79.9 1.5 %collective-permute-done.16 = bf16[32,896]{1,0:T(8,128)(2,1)S(1)} collective-permute-done((bf16[32,896]{1,0:T(8,128)(2,1)S(1)}, bf16[32,896]{1,0:T(8,128)(2,1)S(1)}, u32[]{:S(2)}, u32[]{:S(2)}) %collective-permute-start.16) | collective-permute-done | bytes 57376 | tf_op jit(solution)/shard_map/ppermute | solution.py:268
  81.5 1.5 %collective-permute-start.18 = (f32[32,576]{1,0:T(8,128)S(1)}, f32[32,576]{1,0:T(8,128)S(1)}, u32[]{:S(2)}, u32[]{:S(2)}) collective-permute-start(f32[32,576]{1,0:T(8,128)S(1)} %get-tuple-element.118), channel_id=1, source_target_pairs={{0,1},{1,0},{2,3},{3,2},{4,5},{5,4},{6,7},{7,6},{8,9},{9,8},{10,11... | collective-permute-start | bytes 221192 | tf_op jit(solution)/shard_map/ppermute | solution.py:262
  83.3 1.6 %fusion.3 = f32[256,1024]{1,0:T(8,128)} fusion(bf16[1024,64]{0,1:T(8,128)(2,1)S(1)} %copy-done.5, f32[64,128]{1,0:T(8,128)S(1)} %collective-permute-done.19, f32[32,128]{1,0:T(8,128)S(1)} %get-tuple-element.120, f32[32,128]{1,0:T(8,128)S(1)} %get-tuple-element.119, pred[]{:T(512)S(6)} %eq.5), kind=kOutput, calls=%fused_computation.16 | convolution fusion | flops 201408512 | bytes 1245185 | tf_op jit(solution)/shard_map/dot_general | solution.py:400
  84.9 1.5 %collective-permute-done.18 = f32[32,576]{1,0:T(8,128)S(1)} collective-permute-done((f32[32,576]{1,0:T(8,128)S(1)}, f32[32,576]{1,0:T(8,128)S(1)}, u32[]{:S(2)}, u32[]{:S(2)}) %collective-permute-start.18) | collective-permute-done | bytes 73760 | tf_op jit(solution)/shard_map/ppermute | solution.py:262
  (77 shorter events, 16.5 us)
Async XLA Ops:
  0.6 37.2 %copy-start = (bf16[256,1024]{1,0:T(8,128)(2,1)S(1)}, bf16[256,1024]{1,0:T(8,128)(2,1)}, u32[]{:S(2)}) copy-start(bf16[256,1024]{1,0:T(8,128)(2,1)} %param.11) | copy-start | bytes 1572868
  0.6 2.8 %copy-start.1 = (bf16[3,1024,256]{2,1,0:T(8,128)(2,1)S(1)}, bf16[3,1024,256]{2,1,0:T(8,128)(2,1)}, u32[]{:S(2)}) copy-start(bf16[3,1024,256]{2,1,0:T(8,128)(2,1)} %weight.3) | copy-start | bytes 4718596
  1.5 1.2 %copy-start.2 = (bf16[1,512,1024]{2,1,0:T(8,128)(2,1)S(1)}, bf16[1,512,1024]{2,1,0:T(8,128)(2,1)}, u32[]{:S(2)}) copy-start(bf16[1,512,1024]{2,1,0:T(8,128)(2,1)} %param.8) | copy-start | bytes 3145732
  4.9 4.5 %collective-permute-start = (bf16[2,128,512]{2,1,0:T(8,128)(2,1)S(1)}, bf16[2,128,512]{2,1,0:T(8,128)(2,1)}, u32[]{:S(2)}, u32[]{:S(2)}) collective-permute-start(bf16[2,128,512]{2,1,0:T(8,128)(2,1)S(1)} %get-tuple-element.64), channel_id=1, source_target_pairs={{0,2},{2,0},{4,6},{6,4},{8,10},{10,8},{12,14},{14,12},{1,3},{3,1},... | collective-permute-start | bytes 786440 | tf_op jit(solution)/shard_map/ppermute | solution.py:262
  5.4 10.8 %collective-permute-start.3 = (bf16[2,128,512]{2,1,0:T(8,128)(2,1)S(1)}, bf16[2,128,512]{2,1,0:T(8,128)(2,1)S(1)}, u32[]{:S(2)}, u32[]{:S(2)}) collective-permute-start(bf16[2,128,512]{2,1,0:T(8,128)(2,1)S(1)} %get-tuple-element.66.block), channel_id=1, source_target_pairs={{0,4},{2,6},{4,12},{6,14},{8,0},{10,2},{12,8},{14,10},{1,5},{3,7},... | collective-permute-start | bytes 786440 | tf_op jit(solution)/shard_map/ppermute | solution.py:290
  9.1 14.8 %copy-start.8 = (f32[1,2,2,128]{3,2,1,0:T(2,128)S(1)}, f32[1,2,2,128]{3,2,1,0:T(2,128)}, u32[]{:S(2)}) copy-start(f32[1,2,2,128]{3,2,1,0:T(2,128)} %param.15) | copy-start | bytes 6148
  9.1 2.8 %collective-permute-start.2 = (bf16[2,64,512]{2,1,0:T(8,128)(2,1)S(1)}, bf16[2,64,512]{2,1,0:T(8,128)(2,1)S(1)}, u32[]{:S(2)}, u32[]{:S(2)}) collective-permute-start(bf16[2,64,512]{2,1,0:T(8,128)(2,1)S(1)} %get-tuple-element.65), channel_id=1, source_target_pairs={{0,2},{2,0},{4,6},{6,4},{8,10},{10,8},{12,14},{14,12},{1,3},{3,1},... | collective-permute-start | bytes 393224 | tf_op jit(solution)/shard_map/ppermute | solution.py:262
  9.4 12.5 %collective-permute-start.1 = (bf16[2,128,512]{2,1,0:T(8,128)(2,1)}, bf16[2,128,512]{2,1,0:T(8,128)(2,1)S(1)}, u32[]{:S(2)}, u32[]{:S(2)}) collective-permute-start(bf16[2,128,512]{2,1,0:T(8,128)(2,1)} %collective-permute-done.block), channel_id=1, source_target_pairs={{0,4},{2,6},{4,12},{6,14},{8,0},{10,2},{12,8},{14,10},{1,5},{3,7},... | collective-permute-start | bytes 786440 | tf_op jit(solution)/shard_map/ppermute | solution.py:290
  16.2 11.0 %collective-permute-start.5 = (bf16[2,128,512]{2,1,0:T(8,128)(2,1)S(1)}, bf16[2,128,512]{2,1,0:T(8,128)(2,1)S(1)}, u32[]{:S(2)}, u32[]{:S(2)}) collective-permute-start(bf16[2,128,512]{2,1,0:T(8,128)(2,1)S(1)} %collective-permute-done.3.block), channel_id=1, source_target_pairs={{0,4},{2,6},{4,12},{6,14},{8,0},{10,2},{12,8},{14,10},{1,5},{3,7},... | collective-permute-start | bytes 786440 | tf_op jit(solution)/shard_map/ppermute | solution.py:290
  20.3 16.4 %copy-start.3 = (bf16[1,512,1024]{2,1,0:T(8,128)(2,1)S(1)}, bf16[1,512,1024]{2,1,0:T(8,128)(2,1)}, u32[]{:S(2)}) copy-start(bf16[1,512,1024]{2,1,0:T(8,128)(2,1)} %param.8) | copy-start | bytes 3145732
  20.4 16.4 %copy-start.5 = (bf16[1024,64]{0,1:T(8,128)(2,1)S(1)}, bf16[1024,64]{0,1:T(8,128)(2,1)}, u32[]{:S(2)}) copy-start(bf16[1024,64]{0,1:T(8,128)(2,1)} %param.12) | copy-start | bytes 393220
  23.9 17.3 %collective-permute-start.8 = (f32[2,2,128]{2,1,0:T(2,128)S(1)}, f32[2,2,128]{2,1,0:T(2,128)S(1)}, u32[]{:S(2)}, u32[]{:S(2)}) collective-permute-start(f32[2,2,128]{2,1,0:T(2,128)S(1)} %bitcast.39), channel_id=1, source_target_pairs={{0,1},{1,0},{2,3},{3,2},{4,5},{5,4},{6,7},{7,6},{8,9},{9,8},{10,11... | collective-permute-start | bytes 6152 | tf_op jit(solution)/shard_map/ppermute | solution.py:262
  27.2 14.1 %collective-permute-start.4 = (bf16[2,128,512]{2,1,0:T(8,128)(2,1)S(1)}, bf16[2,128,512]{2,1,0:T(8,128)(2,1)S(1)}, u32[]{:S(2)}, u32[]{:S(2)}) collective-permute-start(bf16[2,128,512]{2,1,0:T(8,128)(2,1)S(1)} %collective-permute-done.1.block), channel_id=1, source_target_pairs={{0,4},{2,6},{4,12},{6,14},{8,0},{10,2},{12,8},{14,10},{1,5},{3,7},... | collective-permute-start | bytes 786440 | tf_op jit(solution)/shard_map/ppermute | solution.py:290
  33.4 12.3 %collective-permute-start.7 = (bf16[2,128,512]{2,1,0:T(8,128)(2,1)S(1)}, bf16[2,128,512]{2,1,0:T(8,128)(2,1)}, u32[]{:S(2)}, u32[]{:S(2)}) collective-permute-start(bf16[2,128,512]{2,1,0:T(8,128)(2,1)S(1)} %collective-permute-done.5.block), channel_id=1, source_target_pairs={{0,4},{2,6},{4,12},{6,14},{8,0},{10,2},{12,8},{14,10},{1,5},{3,7},... | collective-permute-start | bytes 786440 | tf_op jit(solution)/shard_map/ppermute | solution.py:290
  41.3 8.4 %collective-permute-start.6 = (bf16[2,128,512]{2,1,0:T(8,128)(2,1)S(1)}, bf16[2,128,512]{2,1,0:T(8,128)(2,1)S(1)}, u32[]{:S(2)}, u32[]{:S(2)}) collective-permute-start(bf16[2,128,512]{2,1,0:T(8,128)(2,1)S(1)} %collective-permute-done.4.block), channel_id=1, source_target_pairs={{0,4},{2,6},{4,12},{6,14},{8,0},{10,2},{12,8},{14,10},{1,5},{3,7},... | collective-permute-start | bytes 786440 | tf_op jit(solution)/shard_map/ppermute | solution.py:290
  45.7 6.7 %copy-start.7 = (f32[64,512]{1,0:T(8,128)S(1)}, f32[64,512]{1,0:T(8,128)}, u32[]{:S(2)}) copy-start(f32[64,512]{1,0:T(8,128)} %fusion.27) | copy-start | bytes 393220
  49.7 14.1 %copy-start.6 = (bf16[2,3,64,3,64]{2,4,3,1,0:T(8,128)(2,1)S(1)}, bf16[2,3,64,3,64]{2,4,3,1,0:T(8,128)(2,1)}, u32[]{:S(2)}) copy-start(bf16[2,3,64,3,64]{2,4,3,1,0:T(8,128)(2,1)} %copy.26) | copy-start | bytes 442372
  51.0 14.2 %copy-start.4 = (bf16[2,64]{1,0:T(2,128)(2,1)S(1)}, bf16[2,64]{1,0:T(2,128)(2,1)}, u32[]{:S(2)}) copy-start(bf16[2,64]{1,0:T(2,128)(2,1)} %head.1) | copy-start | bytes 772
  51.0 1.4 %collective-permute-start.9 = (f32[64,512]{1,0:T(8,128)S(1)}, f32[64,512]{1,0:T(8,128)S(1)}, u32[]{:S(2)}, u32[]{:S(2)}) collective-permute-start(f32[64,512]{1,0:T(8,128)S(1)} %get-tuple-element.104), channel_id=1, source_target_pairs={{0,2},{2,0},{4,6},{6,4},{8,10},{10,8},{12,14},{14,12},{1,3},{3,1},... | collective-permute-start | bytes 393224 | tf_op jit(solution)/shard_map/ppermute | solution.py:262
  52.4 4.5 %collective-permute-start.10 = (bf16[64,512]{1,0:T(8,128)(2,1)S(1)}, bf16[64,512]{1,0:T(8,128)(2,1)S(1)}, u32[]{:S(2)}, u32[]{:S(2)}) collective-permute-start(bf16[64,512]{1,0:T(8,128)(2,1)S(1)} %add_convert_fusion.1), channel_id=1, source_target_pairs={{0,1},{1,0},{2,3},{3,2},{4,5},{5,4},{6,7},{7,6},{8,9},{9,8},{10,11... | collective-permute-start | bytes 196616 | tf_op jit(solution)/shard_map/ppermute | solution.py:262
  57.0 1.3 %collective-permute-start.11 = (bf16[80,512]{1,0:T(8,128)(2,1)S(1)}, bf16[80,512]{1,0:T(8,128)(2,1)S(1)}, u32[]{:S(2)}, u32[]{:S(2)}) collective-permute-start(bf16[80,512]{1,0:T(8,128)(2,1)S(1)} %pad_maximum_fusion.1), channel_id=1, source_target_pairs={{0,2},{2,0},{4,6},{6,4},{8,10},{10,8},{12,14},{14,12},{1,3},{3,1},... | collective-permute-start | bytes 245768 | tf_op jit(solution)/shard_map/ppermute | solution.py:262
  58.4 5.4 %collective-permute-start.12 = (bf16[80,1024]{1,0:T(8,128)(2,1)S(1)}, bf16[80,1024]{1,0:T(8,128)(2,1)S(1)}, u32[]{:S(2)}, u32[]{:S(2)}) collective-permute-start(bf16[80,1024]{1,0:T(8,128)(2,1)S(1)} %pad_maximum_fusion.chip_map), channel_id=1, source_target_pairs={{0,4},{1,5},{2,3},{3,2},{4,0},{5,1},{6,10},{7,11},{8,12},{9,13},{1... | collective-permute-start | bytes 491528 | tf_op jit(solution)/shard_map/ppermute | solution.py:280
  63.7 1.4 %collective-permute-start.13 = (bf16[80,1024]{1,0:T(8,128)(2,1)S(1)}, bf16[80,1024]{1,0:T(8,128)(2,1)S(1)}, u32[]{:S(2)}, u32[]{:S(2)}) collective-permute-start(bf16[80,1024]{1,0:T(8,128)(2,1)S(1)} %collective-permute-done.12.near), channel_id=1, source_target_pairs={{0,2},{2,0},{4,6},{6,4},{8,10},{10,8},{12,14},{14,12},{1,3},{3,1},... | collective-permute-start | bytes 491528 | tf_op jit(solution)/shard_map/ppermute | solution.py:262
  69.0 4.2 %collective-permute-start.14 = (bf16[32,896]{1,0:T(8,128)(2,1)S(1)}, bf16[32,896]{1,0:T(8,128)(2,1)S(1)}, u32[]{:S(2)}, u32[]{:S(2)}) collective-permute-start(bf16[32,896]{1,0:T(8,128)(2,1)S(1)} %fusion.14), channel_id=1, source_target_pairs={{0,16},{16,0},{1,17},{17,1},{2,18},{18,2},{3,19},{19,3},{4,20},{20... | collective-permute-start | bytes 172040 | tf_op jit(solution)/shard_map/ppermute | solution.py:268
  73.3 6.6 %collective-permute-start.15 = (bf16[32,896]{1,0:T(8,128)(2,1)S(1)}, bf16[32,896]{1,0:T(8,128)(2,1)S(1)}, u32[]{:S(2)}, u32[]{:S(2)}) collective-permute-start(bf16[32,896]{1,0:T(8,128)(2,1)S(1)} %add_convert_fusion.2), channel_id=1, source_target_pairs={{0,8},{2,10},{4,12},{6,14},{8,0},{10,2},{12,4},{14,6},{1,9},{3,11}... | collective-permute-start | bytes 172040 | tf_op jit(solution)/shard_map/ppermute | solution.py:268
  75.4 6.0 %collective-permute-start.16 = (bf16[32,896]{1,0:T(8,128)(2,1)S(1)}, bf16[32,896]{1,0:T(8,128)(2,1)S(1)}, u32[]{:S(2)}, u32[]{:S(2)}) collective-permute-start(bf16[32,896]{1,0:T(8,128)(2,1)S(1)} %add_convert_fusion.2), channel_id=1, source_target_pairs={{0,4},{2,6},{4,8},{6,10},{8,12},{10,14},{12,0},{14,2},{1,5},{3,7},... | collective-permute-start | bytes 172040 | tf_op jit(solution)/shard_map/ppermute | solution.py:268
  75.4 6.0 %collective-permute-start.17 = (bf16[32,896]{1,0:T(8,128)(2,1)S(1)}, bf16[32,896]{1,0:T(8,128)(2,1)S(1)}, u32[]{:S(2)}, u32[]{:S(2)}) collective-permute-start(bf16[32,896]{1,0:T(8,128)(2,1)S(1)} %add_convert_fusion.2), channel_id=1, source_target_pairs={{0,12},{2,14},{4,0},{6,2},{8,4},{10,6},{12,8},{14,10},{1,13},{3,15... | collective-permute-start | bytes 172040 | tf_op jit(solution)/shard_map/ppermute | solution.py:268
  81.4 1.9 %collective-permute-start.19 = (f32[64,128]{1,0:T(8,128)S(1)}, f32[64,128]{1,0:T(8,128)S(1)}, u32[]{:S(2)}, u32[]{:S(2)}) collective-permute-start(f32[64,128]{1,0:T(8,128)S(1)} %pad_maximum_fusion.2), channel_id=1, source_target_pairs={{0,2},{2,0},{4,6},{6,4},{8,10},{10,8},{12,14},{14,12},{1,3},{3,1},... | collective-permute-start | bytes 98312 | tf_op jit(solution)/shard_map/ppermute | solution.py:262
  81.5 4.9 %collective-permute-start.18 = (f32[32,576]{1,0:T(8,128)S(1)}, f32[32,576]{1,0:T(8,128)S(1)}, u32[]{:S(2)}, u32[]{:S(2)}) collective-permute-start(f32[32,576]{1,0:T(8,128)S(1)} %get-tuple-element.118), channel_id=1, source_target_pairs={{0,1},{1,0},{2,3},{3,2},{4,5},{5,4},{6,7},{7,6},{8,9},{9,8},{10,11... | collective-permute-start | bytes 221192 | tf_op jit(solution)/shard_map/ppermute | solution.py:262
  83.1 3.4 %collective-permute-start.20 = (f32[32,576]{1,0:T(8,128)S(1)}, f32[32,576]{1,0:T(8,128)S(1)}, u32[]{:S(2)}, u32[]{:S(2)}) collective-permute-start(f32[32,576]{1,0:T(8,128)S(1)} %get-tuple-element.118), channel_id=1, source_target_pairs={{0,2},{2,0},{4,6},{6,4},{8,10},{10,8},{12,14},{14,12},{1,3},{3,1},... | collective-permute-start | bytes 221192 | tf_op jit(solution)/shard_map/ppermute | solution.py:262
  86.4 1.3 %collective-permute-start.21 = (f32[32,576]{1,0:T(8,128)S(1)}, f32[32,576]{1,0:T(8,128)S(1)}, u32[]{:S(2)}, u32[]{:S(2)}) collective-permute-start(f32[32,576]{1,0:T(8,128)S(1)} %collective-permute-done.18), channel_id=1, source_target_pairs={{0,2},{2,0},{4,6},{6,4},{8,10},{10,8},{12,14},{14,12},{1,3},{3,1},... | collective-permute-start | bytes 221192 | tf_op jit(solution)/shard_map/ppermute | solution.py:262
